TPU v7x, 32 devices: a whole 2x2x4 slice. The times are simulated.
32 devices in a mesh: wide: 8 (over z, x), narrow: 4 (over y, core).
Axes of the slice: x: 2, y: 2, z: 4, core: 2. Of those that a mesh axis runs over, the one named last changes fastest.
Arguments:
- tokens: bfloat16 [4096, 1024], P('wide'), may hold values from -6 to 6
- cotangent: bfloat16 [4096, 1024], P('wide'), may hold values from -6 to 6
- seq_spans: int32 [3], replicated, may hold values from 1 to 5, as said below
- w_query: bfloat16 [1024, 1024], P(('wide', 'narrow')), may hold values from -0.1875 to 0.1875
- w_key: bfloat16 [1024, 1024], P(('wide', 'narrow')), may hold values from -0.1875 to 0.1875
- w_value: bfloat16 [1024, 1024], P(('wide', 'narrow')), may hold values from -0.1875 to 0.1875
- conv_kernel: bfloat16 [4, 3072], P(None, ('wide', 'narrow')), may hold values from -3 to 3
- persistent: bfloat16 [2, 16, 1024], P(None, None, ('wide', 'narrow')), may hold values from -6 to 6
- norm_gain: bfloat16 [1024], P(('wide', 'narrow')), may hold values from 0.5 to 1.5
- rate_proj: bfloat16 [1024, 3], P(('wide', 'narrow')), may hold values from -5 to 5
- out_gate: bfloat16 [1024, 1024], P('wide', 'narrow'), may hold values from -0.1875 to 0.1875
- out_proj: bfloat16 [1024, 1024], P('narrow', 'wide'), may hold values from -0.5 to 0.5
- memory_in: bfloat16 [1024, 4096], P('wide', 'narrow'), may hold values from -0.1875 to 0.1875
- memory_out: bfloat16 [4096, 1024], P('narrow', 'wide'), may hold values from -0.1875 to 0.1875
- ffn_gain: bfloat16 [1024], P(('wide', 'narrow')), may hold values from 0.5 to 1.5
- ffn_gate: bfloat16 [1024, 4096], P('wide', 'narrow'), may hold values from -0.1875 to 0.1875
- ffn_up: bfloat16 [1024, 4096], P('wide', 'narrow'), may hold values from -0.1875 to 0.1875
- ffn_down: bfloat16 [4096, 1024], P('narrow', 'wide'), may hold values from -0.1875 to 0.1875
Outputs:
- output: bfloat16 [4096, 1024], P('wide')
- tokens_grad: float32 [4096, 1024], P('wide')
- query_grad: float32 [1024, 1024], P('wide', 'narrow')
- key_grad: float32 [1024, 1024], P('wide', 'narrow')
- value_grad: float32 [1024, 1024], P('wide', 'narrow')
- kernel_grad: float32 [4, 3072], P(None, ('wide', 'narrow'))
- persistent_grad: float32 [2, 16, 1024], P(None, None, ('wide', 'narrow'))
- norm_grad: float32 [1024], P(('wide', 'narrow'))
- rate_grad: float32 [1024, 3], P(('wide', 'narrow'))
- out_gate_grad: float32 [1024, 1024], P('wide', 'narrow')
- out_proj_grad: float32 [1024, 1024], P('narrow', 'wide')
- memory_in_grad: float32 [1024, 4096], P('wide', 'narrow')
- memory_out_grad: float32 [4096, 1024], P('narrow', 'wide')
- ffn_gain_grad: float32 [1024], P(('wide', 'narrow'))
- ffn_gate_grad: float32 [1024, 4096], P('wide', 'narrow')
- ffn_up_grad: float32 [1024, 4096], P('wide', 'narrow')
- ffn_down_grad: float32 [4096, 1024], P('narrow', 'wide')
Inputs may be any that keep to these rules, and one draw needn't show every extreme that they name: `seq_spans`: the sequences fill all 4096 tokens, one has exactly 5 spans, and the span that holds token 2048 never begins a sequence.
All inputs are finite; a program needn't handle non-finite values.
Results may differ from a plain program's by a relative error of at most 0.025.
Values may be sent and summed in bfloat16 or wider, within the bound.
A program may use at most 256 MiB of HBM per device.

v0:
```python
import math

import jax
import jax.numpy as jnp
from jax import lax
from jax.sharding import PartitionSpec as P

HEAD = 64


decay_top = 0.2
moment_top = 0.9
learn_top = 0.1
eps_norm = 1e-05
eps_head = 1e-06
masked_score = -1e30


def from_behind(value, axis, steps):
    count = lax.axis_size(axis)
    first, last = (max(0, -steps), min(count, count - steps))
    return lax.ppermute(value, axis, [(source, source + steps) for source in range(first, last)])


def as_sent(array):
    return jax.tree.map(lambda a: a.astype(jnp.bfloat16) if a.dtype == jnp.float32 else a, array)


def matmul(left_side, right_side):
    return jnp.dot(left_side, right_side, preferred_element_type=jnp.float32)


def inner_left(left_side, right_side):
    return lax.dot_general(
        left_side, right_side, (((0,), (0,)), ((), ())), preferred_element_type=jnp.float32
    )


def inner_right(left_side, right_side):
    return lax.dot_general(
        left_side, right_side, (((1,), (1,)), ((), ())), preferred_element_type=jnp.float32
    )


def split_heads(values, head_size):
    return values.reshape(values.shape[:-1] + (values.shape[-1] // head_size, head_size))


def head_norm(values, head_size):
    shaped = split_heads(values, head_size)
    factor = lax.rsqrt(jnp.sum(shaped * shaped, axis=-1, keepdims=True) + eps_head)
    return (shaped * factor).reshape(values.shape)


def head_norm_back(values, upstream, head_size):
    shaped = split_heads(values, head_size)
    grad_shaped = split_heads(upstream, head_size)
    factor = lax.rsqrt(jnp.sum(shaped * shaped, axis=-1, keepdims=True) + eps_head)
    normed = shaped * factor
    inner_sum = jnp.sum(normed * grad_shaped, axis=-1, keepdims=True)
    return (factor * (grad_shaped - normed * inner_sum)).reshape(values.shape)


def rms_back(scaled, factor, upstream):
    return factor * (upstream - scaled * jnp.mean(upstream * scaled, axis=-1, keepdims=True))


def silu_slope(values):
    sigmoid_val = jax.nn.sigmoid(values)
    return sigmoid_val * (1.0 + values * (1.0 - sigmoid_val))


def silu_curve(values):
    sigmoid_val = jax.nn.sigmoid(values)
    return sigmoid_val * (1.0 - sigmoid_val) * (2.0 + values * (1.0 - 2.0 * sigmoid_val))


def body(
    tokens,
    cotangent,
    seq_spans,
    w_query,
    w_key,
    w_value,
    conv_kernel,
    persistent,
    norm_gain,
    rate_proj,
    out_gate,
    out_proj,
    memory_in,
    memory_out,
    ffn_gain,
    ffn_gate,
    ffn_up,
    ffn_down,
):
    (
        query_full,
        key_full,
        value_full,
        kernel_full,
        persist_full,
        gain_first,
        gain_second,
        rate_full,
    ) = (
        lax.all_gather(w_query, ("wide", "narrow"), axis=0, tiled=True),
        lax.all_gather(w_key, ("wide", "narrow"), axis=0, tiled=True),
        lax.all_gather(w_value, ("wide", "narrow"), axis=0, tiled=True),
        lax.all_gather(conv_kernel, ("wide", "narrow"), axis=1, tiled=True),
        lax.all_gather(persistent, ("wide", "narrow"), axis=2, tiled=True),
        lax.all_gather(norm_gain, ("wide", "narrow"), axis=0, tiled=True),
        lax.all_gather(ffn_gain, ("wide", "narrow"), axis=0, tiled=True),
        lax.all_gather(rate_proj, ("wide", "narrow"), axis=0, tiled=True),
    )
    gate_cols, proj_rows, memory_cols, memory_rows, ffn_gate_cols, ffn_up_cols, ffn_down_rows = (
        lax.all_gather(out_gate, "wide", axis=0, tiled=True),
        lax.all_gather(out_proj, "wide", axis=1, tiled=True),
        lax.all_gather(memory_in, "wide", axis=0, tiled=True),
        lax.all_gather(memory_out, "wide", axis=1, tiled=True),
        lax.all_gather(ffn_gate, "wide", axis=0, tiled=True),
        lax.all_gather(ffn_up, "wide", axis=0, tiled=True),
        lax.all_gather(ffn_down, "wide", axis=1, tiled=True),
    )
    span_rows = tokens.shape[0]
    model_width = tokens.shape[1]
    kernel_size = kernel_full.shape[0]
    persist_count = persist_full.shape[1]
    local_width = gate_cols.shape[1]
    score_scale = math.sqrt(HEAD)
    narrow_pos = lax.axis_index("narrow")
    wide_pos = lax.axis_index("wide")
    chain_turns = min(6, lax.axis_size("wide") * 5 // 8)
    col_offset = narrow_pos * local_width
    lead_narrow = narrow_pos == 0
    seq_ends = jnp.cumsum(seq_spans)
    is_first = jnp.any(seq_ends - seq_spans == wide_pos)

    def own_cols(values, axis_dim):
        return lax.dynamic_slice_in_dim(values, col_offset, local_width, axis_dim)

    def place_cols(piece, axis_dim):
        shape_full = piece.shape[:axis_dim] + (model_width,) + piece.shape[axis_dim + 1 :]
        return lax.dynamic_update_slice_in_dim(
            jnp.zeros(shape_full, jnp.float32), piece, col_offset, axis_dim
        )

    inputs_f = tokens.astype(jnp.float32)
    first_factor = lax.rsqrt(jnp.mean(inputs_f * inputs_f, axis=-1, keepdims=True) + eps_norm)
    first_scaled = inputs_f * first_factor
    gain_one = gain_first.astype(jnp.float32)
    normed = first_scaled * gain_one
    normed_low = normed.astype(jnp.bfloat16)
    qkv_weights = jnp.concatenate([query_full, key_full, value_full], 1)
    projected = matmul(normed_low, qkv_weights)
    tail_rows = from_behind(
        projected[span_rows - kernel_size + 1 :].astype(jnp.bfloat16), "wide", 1
    ).astype(jnp.float32)
    extended = jnp.concatenate([jnp.where(is_first, 0.0, tail_rows), projected], 0)
    kernel_f = kernel_full.astype(jnp.float32)
    mixed_conv = kernel_f[0] * projected
    for offset in range(1, kernel_size):
        start_row = kernel_size - 1 - offset
        mixed_conv = mixed_conv + kernel_f[offset] * extended[start_row : start_row + span_rows]
    activated = jax.nn.silu(mixed_conv)
    query_low = head_norm(activated[:, :model_width], HEAD).astype(jnp.bfloat16)
    key_low = head_norm(activated[:, model_width : 2 * model_width], HEAD).astype(jnp.bfloat16)
    value_act = activated[:, 2 * model_width :]
    value_low = value_act.astype(jnp.bfloat16)
    span_mean = jnp.mean(normed, axis=0)
    rate_f = rate_full.astype(jnp.float32)
    gate_scale = jnp.array([decay_top, moment_top, learn_top], jnp.float32)
    gate_sig = jax.nn.sigmoid(jnp.sum(span_mean[:, None] * rate_f, axis=0))
    gate_vals = gate_sig * gate_scale
    decay_rate = gate_vals[0]
    moment_rate = gate_vals[1]
    learn_rate = gate_vals[2]
    first_init = memory_cols.astype(jnp.float32)
    second_init = memory_rows.astype(jnp.float32)
    zero_first = jnp.zeros_like(first_init)
    zero_second = jnp.zeros_like(second_init)
    incoming = (zero_first, zero_second, zero_first, zero_second)
    for turn_number in range(chain_turns):
        final_turn = turn_number == chain_turns - 1
        state_first = jnp.where(is_first, first_init, incoming[0])
        state_second = jnp.where(is_first, second_init, incoming[1])
        moment_first = jnp.where(is_first, 0.0, incoming[2])
        moment_second = jnp.where(is_first, 0.0, incoming[3])
        first_low = state_first.astype(jnp.bfloat16)
        second_low = state_second.astype(jnp.bfloat16)
        lookups = jnp.concatenate([query_low, key_low], 0) if final_turn else key_low
        hidden_pre = matmul(lookups, first_low)
        hidden_low = jax.nn.silu(hidden_pre).astype(jnp.bfloat16)
        recalled_all = lax.psum(
            matmul(hidden_low, second_low).astype(jnp.bfloat16), "narrow"
        ).astype(jnp.float32)
        key_pre = hidden_pre[-span_rows:]
        key_hidden = hidden_low[-span_rows:]
        error_low = ((recalled_all[-span_rows:] - value_act) / span_rows).astype(jnp.bfloat16)
        grad_second = inner_left(key_hidden, error_low)
        hidden_grad = inner_right(error_low, second_low)
        slope_low = (hidden_grad * silu_slope(key_pre)).astype(jnp.bfloat16)
        grad_first = inner_left(key_low, slope_low)
        new_moment_first = moment_rate * moment_first - learn_rate * grad_first
        new_moment_second = moment_rate * moment_second - learn_rate * grad_second
        new_first = (1.0 - decay_rate) * state_first + new_moment_first
        new_second = (1.0 - decay_rate) * state_second + new_moment_second
        if not final_turn:
            incoming = (
                from_behind(new_first.astype(jnp.bfloat16), "wide", 1).astype(new_first.dtype),
                from_behind(new_second.astype(jnp.bfloat16), "wide", 1).astype(new_second.dtype),
                from_behind(new_moment_first.astype(jnp.bfloat16), "wide", 1).astype(
                    new_moment_first.dtype
                ),
                from_behind(new_moment_second.astype(jnp.bfloat16), "wide", 1).astype(
                    new_moment_second.dtype
                ),
            )
    query_pre = hidden_pre[:span_rows]
    query_hidden = hidden_low[:span_rows]
    recalled = recalled_all[:span_rows]
    recall_own = own_cols(recalled, 1)
    persist_f = own_cols(persist_full, 2).astype(jnp.float32)
    keys_all = jnp.concatenate(
        [
            head_norm(persist_f[0], HEAD).astype(jnp.bfloat16),
            head_norm(recall_own, HEAD).astype(jnp.bfloat16),
            own_cols(key_low, 1),
        ],
        0,
    )
    values_all = jnp.concatenate(
        [
            persist_f[1].astype(jnp.bfloat16),
            recall_own.astype(jnp.bfloat16),
            own_cols(value_low, 1),
        ],
        0,
    )
    query_heads = split_heads(own_cols(query_low, 1), HEAD)
    key_heads = split_heads(keys_all, HEAD)
    value_heads = split_heads(values_all, HEAD)
    key_total = keys_all.shape[0]
    row_index = lax.broadcasted_iota(jnp.int32, (span_rows, key_total), 0)
    col_index = lax.broadcasted_iota(jnp.int32, (span_rows, key_total), 1)
    allowed = (col_index < persist_count + span_rows) | (
        col_index - persist_count - span_rows <= row_index
    )

    def score_block():
        raw_scores = (
            jnp.einsum("thd,jhd->htj", query_heads, key_heads, preferred_element_type=jnp.float32)
            * score_scale
        )
        return jnp.where(allowed[None], raw_scores, masked_score)

    scores = score_block()
    row_top = jnp.max(scores, axis=-1, keepdims=True)
    exponent = jnp.exp(scores - row_top)
    total_sum = jnp.sum(exponent, axis=-1, keepdims=True)
    log_total = row_top + jnp.log(total_sum)
    weights_low = (exponent / total_sum).astype(jnp.bfloat16)
    attended = jnp.einsum(
        "htj,jhd->thd", weights_low, value_heads, preferred_element_type=jnp.float32
    ).reshape(span_rows, local_width)
    gate_pre = matmul(normed_low, gate_cols)
    gate_sigmoid = jax.nn.sigmoid(gate_pre)
    gated_low = (attended * gate_sigmoid).astype(jnp.bfloat16)
    branch = lax.psum(matmul(gated_low, proj_rows).astype(jnp.bfloat16), "narrow").astype(
        jnp.float32
    )
    middle = inputs_f + branch
    second_factor = lax.rsqrt(jnp.mean(middle * middle, axis=-1, keepdims=True) + eps_norm)
    second_scaled = middle * second_factor
    gain_two = gain_second.astype(jnp.float32)
    normed_two = (second_scaled * gain_two).astype(jnp.bfloat16)
    gate_val = matmul(normed_two, ffn_gate_cols)
    up_val = matmul(normed_two, ffn_up_cols)
    gate_silu = jax.nn.silu(gate_val)
    hidden_ffn = (gate_silu * up_val).astype(jnp.bfloat16)
    ffn_out = lax.psum(matmul(hidden_ffn, ffn_down_rows).astype(jnp.bfloat16), "narrow").astype(
        jnp.float32
    )
    output = (middle + ffn_out).astype(jnp.bfloat16)
    upstream = cotangent.astype(jnp.float32)
    down_grad = inner_left(hidden_ffn, cotangent)
    hidden_grad_ffn = inner_right(cotangent, ffn_down_rows)
    gate_sig_ffn = jax.nn.sigmoid(gate_val)
    gate_grad_low = (
        hidden_grad_ffn * up_val * gate_sig_ffn * (1.0 + gate_val * (1.0 - gate_sig_ffn))
    ).astype(jnp.bfloat16)
    up_grad_low = (hidden_grad_ffn * gate_silu).astype(jnp.bfloat16)
    ffn_gate_grad = inner_left(normed_two, gate_grad_low)
    ffn_up_grad = inner_left(normed_two, up_grad_low)
    normed_two_part = inner_right(gate_grad_low, ffn_gate_cols) + inner_right(
        up_grad_low, ffn_up_cols
    )
    gain_two_part = jnp.sum(normed_two_part * second_scaled, axis=0)
    normed_two_grad = lax.psum(normed_two_part.astype(jnp.bfloat16), "narrow").astype(jnp.float32)
    middle_grad = upstream + rms_back(second_scaled, second_factor, normed_two_grad * gain_two)
    branch_low = middle_grad.astype(jnp.bfloat16)
    proj_grad = inner_left(gated_low, branch_low)
    gated_grad = inner_right(branch_low, proj_rows)
    attended_grad_low = (gated_grad * gate_sigmoid).astype(jnp.bfloat16)
    gate_pre_low = (gated_grad * attended * gate_sigmoid * (1.0 - gate_sigmoid)).astype(
        jnp.bfloat16
    )
    out_gate_grad = inner_left(normed_low, gate_pre_low)
    other_part = inner_right(gate_pre_low, gate_cols)
    weights_again = jnp.exp(score_block() - log_total)
    grad_heads = split_heads(attended_grad_low, HEAD)
    weight_grad = jnp.einsum(
        "thd,jhd->htj", grad_heads, value_heads, preferred_element_type=jnp.float32
    )
    row_delta = jnp.sum(weights_again * weight_grad, axis=-1, keepdims=True)
    score_grad_low = (weights_again * (weight_grad - row_delta)).astype(jnp.bfloat16)
    query_att = (
        score_scale
        * jnp.einsum("htj,jhd->thd", score_grad_low, key_heads, preferred_element_type=jnp.float32)
    ).reshape(span_rows, local_width)
    keys_grad = (
        score_scale
        * jnp.einsum(
            "htj,thd->jhd", score_grad_low, query_heads, preferred_element_type=jnp.float32
        )
    ).reshape(key_total, local_width)
    values_grad = jnp.einsum(
        "htj,thd->jhd",
        weights_again.astype(jnp.bfloat16),
        grad_heads,
        preferred_element_type=jnp.float32,
    ).reshape(key_total, local_width)
    recall_end = persist_count + span_rows
    persist_grad_part = place_cols(
        jnp.stack(
            [
                head_norm_back(persist_f[0], keys_grad[:persist_count], HEAD),
                values_grad[:persist_count],
            ]
        ),
        2,
    )
    recall_part = place_cols(
        head_norm_back(recall_own, keys_grad[persist_count:recall_end], HEAD)
        + values_grad[persist_count:recall_end],
        1,
    )
    query_att_full = place_cols(query_att, 1)
    key_att_full = place_cols(keys_grad[recall_end:], 1)
    value_att_full = place_cols(values_grad[recall_end:], 1)
    returning = (zero_first, zero_second, zero_first, zero_second)
    for turn_number in range(chain_turns):
        first_turn = turn_number == 0
        final_turn = turn_number == chain_turns - 1
        total_first = returning[2] + returning[0]
        total_second = returning[3] + returning[1]
        coeff_first = (-learn_rate * total_first).astype(jnp.bfloat16)
        coeff_second = (-learn_rate * total_second).astype(jnp.bfloat16)
        slope_grad = matmul(key_low, coeff_first)
        dh_grad_low = (slope_grad * silu_slope(key_pre)).astype(jnp.bfloat16)
        pre_extra = slope_grad * hidden_grad * silu_curve(key_pre)
        error_part = matmul(key_hidden, coeff_second) + matmul(dh_grad_low, second_low)
        stacked = jnp.concatenate([recall_part, error_part], 0) if first_turn else error_part
        summed = lax.psum(stacked.astype(jnp.bfloat16), "narrow").astype(jnp.float32)
        error_grad = summed[-span_rows:]
        if first_turn:
            recall_low = summed[:span_rows].astype(jnp.bfloat16)
            query_pre_low = (inner_right(recall_low, second_low) * silu_slope(query_pre)).astype(
                jnp.bfloat16
            )
            recall_second = inner_left(query_hidden, recall_low)
            recall_first = inner_left(query_low, query_pre_low)
            query_mem = inner_right(query_pre_low, first_low)
        out_grad_low = (error_grad / span_rows).astype(jnp.bfloat16)
        key_hidden_grad = inner_right(error_low, coeff_second) + inner_right(
            out_grad_low, second_low
        )
        key_pre_low = (key_hidden_grad * silu_slope(key_pre) + pre_extra).astype(jnp.bfloat16)
        first_grad = inner_left(key_low, key_pre_low) + recall_first
        second_grad = (
            inner_left(dh_grad_low, error_low)
            + inner_left(key_hidden, out_grad_low)
            + recall_second
        )
        state_first_grad = (1.0 - decay_rate) * returning[0] + first_grad
        state_second_grad = (1.0 - decay_rate) * returning[1] + second_grad
        moment_first_grad = moment_rate * total_first
        moment_second_grad = moment_rate * total_second
        if not final_turn:
            returning = from_behind(
                (
                    as_sent(jnp.where(is_first, 0.0, state_first_grad)),
                    as_sent(jnp.where(is_first, 0.0, state_second_grad)),
                    as_sent(jnp.where(is_first, 0.0, moment_first_grad)),
                    as_sent(jnp.where(is_first, 0.0, moment_second_grad)),
                ),
                "wide",
                -1,
            )
    value_mem = jnp.where(lead_narrow, -error_grad / span_rows, 0.0)
    key_mem = inner_right(key_pre_low, first_low) + inner_right(slope_low, coeff_first)
    decay_part = -(jnp.sum(returning[0] * state_first) + jnp.sum(returning[1] * state_second))
    moment_part = jnp.sum(total_first * moment_first) + jnp.sum(total_second * moment_second)
    learn_part = -(jnp.sum(total_first * grad_first) + jnp.sum(total_second * grad_second))
    memory_first_grad = jnp.where(is_first, state_first_grad, 0.0)
    memory_second_grad = jnp.where(is_first, state_second_grad, 0.0)
    logit_grad = (
        jnp.stack([decay_part, moment_part, learn_part]) * gate_scale * gate_sig * (1.0 - gate_sig)
    )
    rate_grad_part = span_mean[:, None] * logit_grad[None, :]
    other_part = other_part + jnp.sum(rate_f * logit_grad[None, :], axis=1)[None, :] / span_rows
    act_grad = jnp.concatenate(
        [
            head_norm_back(activated[:, :model_width], query_mem + query_att_full, HEAD),
            head_norm_back(
                activated[:, model_width : 2 * model_width], key_mem + key_att_full, HEAD
            ),
            value_mem + value_att_full,
        ],
        1,
    )
    conv_grad = act_grad * silu_slope(mixed_conv)
    kernel_rows = []
    extended_grad = jnp.zeros_like(extended)
    for offset in range(kernel_size):
        start_row = kernel_size - 1 - offset
        kernel_rows.append(jnp.sum(conv_grad * extended[start_row : start_row + span_rows], axis=0))
        extended_grad = extended_grad + jnp.pad(
            kernel_f[offset] * conv_grad, ((start_row, offset), (0, 0))
        )
    kernel_grad_part = jnp.stack(kernel_rows)
    tail_back = from_behind(
        as_sent(jnp.where(is_first, 0.0, extended_grad[: kernel_size - 1])), "wide", -1
    )
    projected_part = extended_grad[kernel_size - 1 :] + jnp.pad(
        tail_back, ((span_rows - kernel_size + 1, 0), (0, 0))
    )
    projected_grad, other_grad = (
        lax.psum(projected_part.astype(jnp.bfloat16), "narrow").astype(jnp.float32),
        lax.psum(other_part.astype(jnp.bfloat16), "narrow").astype(jnp.float32),
    )
    projected_low = projected_grad.astype(jnp.bfloat16)
    qkv_back = inner_right(projected_low, qkv_weights)
    normed_grad = qkv_back + other_grad
    gain_one_part = jnp.sum(
        (jnp.where(lead_narrow, qkv_back, 0.0) + other_part) * first_scaled, axis=0
    )
    query_grad = inner_left(
        normed_low, lax.dynamic_slice_in_dim(projected_low, col_offset, local_width, 1)
    )
    key_grad = inner_left(
        normed_low,
        lax.dynamic_slice_in_dim(projected_low, model_width + col_offset, local_width, 1),
    )
    value_grad = inner_left(
        normed_low,
        lax.dynamic_slice_in_dim(projected_low, 2 * model_width + col_offset, local_width, 1),
    )
    tokens_grad = middle_grad + rms_back(first_scaled, first_factor, normed_grad * gain_one)
    kernel_grad, persist_grad, norm_grad, ffn_gain_grad, rate_grad = (
        lax.psum_scatter(kernel_grad_part, ("wide", "narrow"), scatter_dimension=1, tiled=True),
        lax.psum_scatter(persist_grad_part, ("wide", "narrow"), scatter_dimension=2, tiled=True),
        lax.psum_scatter(gain_one_part, ("wide", "narrow"), scatter_dimension=0, tiled=True),
        lax.psum_scatter(gain_two_part, ("wide", "narrow"), scatter_dimension=0, tiled=True),
        lax.psum_scatter(rate_grad_part, ("wide", "narrow"), scatter_dimension=0, tiled=True),
    )
    (
        query_out,
        key_out,
        value_out,
        gate_out,
        proj_out,
        first_out,
        second_out,
        ffn_gate_out,
        ffn_up_out,
        ffn_down_out,
    ) = (
        lax.psum_scatter(
            query_grad.astype(jnp.bfloat16), "wide", scatter_dimension=0, tiled=True
        ).astype(jnp.float32),
        lax.psum_scatter(
            key_grad.astype(jnp.bfloat16), "wide", scatter_dimension=0, tiled=True
        ).astype(jnp.float32),
        lax.psum_scatter(
            value_grad.astype(jnp.bfloat16), "wide", scatter_dimension=0, tiled=True
        ).astype(jnp.float32),
        lax.psum_scatter(
            out_gate_grad.astype(jnp.bfloat16), "wide", scatter_dimension=0, tiled=True
        ).astype(jnp.float32),
        lax.psum_scatter(
            proj_grad.astype(jnp.bfloat16), "wide", scatter_dimension=1, tiled=True
        ).astype(jnp.float32),
        lax.psum_scatter(
            memory_first_grad.astype(jnp.bfloat16), "wide", scatter_dimension=0, tiled=True
        ).astype(jnp.float32),
        lax.psum_scatter(
            memory_second_grad.astype(jnp.bfloat16), "wide", scatter_dimension=1, tiled=True
        ).astype(jnp.float32),
        lax.psum_scatter(
            ffn_gate_grad.astype(jnp.bfloat16), "wide", scatter_dimension=0, tiled=True
        ).astype(jnp.float32),
        lax.psum_scatter(
            ffn_up_grad.astype(jnp.bfloat16), "wide", scatter_dimension=0, tiled=True
        ).astype(jnp.float32),
        lax.psum_scatter(
            down_grad.astype(jnp.bfloat16), "wide", scatter_dimension=1, tiled=True
        ).astype(jnp.float32),
    )
    return (
        output,
        tokens_grad,
        query_out,
        key_out,
        value_out,
        kernel_grad,
        persist_grad,
        norm_grad,
        rate_grad,
        gate_out,
        proj_out,
        first_out,
        second_out,
        ffn_gain_grad,
        ffn_gate_out,
        ffn_up_out,
        ffn_down_out,
    )


def solution(mesh):
    return jax.shard_map(
        body,
        mesh=mesh,
        in_specs=(
            P("wide", None),
            P("wide", None),
            P(),
            P(("wide", "narrow"), None),
            P(("wide", "narrow"), None),
            P(("wide", "narrow"), None),
            P(None, ("wide", "narrow")),
            P(None, None, ("wide", "narrow")),
            P(("wide", "narrow")),
            P(("wide", "narrow"), None),
            P("wide", "narrow"),
            P("narrow", "wide"),
            P("wide", "narrow"),
            P("narrow", "wide"),
            P(("wide", "narrow")),
            P("wide", "narrow"),
            P("wide", "narrow"),
            P("narrow", "wide"),
        ),
        out_specs=(
            P("wide", None),
            P("wide", None),
            P("wide", "narrow"),
            P("wide", "narrow"),
            P("wide", "narrow"),
            P(None, ("wide", "narrow")),
            P(None, None, ("wide", "narrow")),
            P(("wide", "narrow")),
            P(("wide", "narrow"), None),
            P("wide", "narrow"),
            P("narrow", "wide"),
            P("wide", "narrow"),
            P("narrow", "wide"),
            P(("wide", "narrow")),
            P("wide", "narrow"),
            P("wide", "narrow"),
            P("narrow", "wide"),
        ),
        check_vma=False,
    )
```

profile of v0, /device:TPU:0, one launch (start us, length us, event | category | flops | bytes accessed | tf_op | source)
XLA Modules:
  0.0 3550.6 jit_solution(14251354325047720069)
XLA Ops:
  13.9 42.1 %all-reduce.10 = (bf16[1024]{0:T(1024)(128)(2,1)S(1)}, bf16[1024]{0:T(1024)(128)(2,1)}) all-reduce(bf16[1024]{0:T(1024)(128)(2,1)S(1)} %dynamic-update-slice.3, bf16[1024]{0:T(1024)(128)(2,1)S(1)} %dynamic-update-slice.4), channel_id=1, replica_groups=mesh['wide'=8,'narrow'=4] {'wide','narrow'}, use_global_device_ids=true, to_apply=%add.5 | all-reduce | flops 2048 | bytes 8192
  55.9 40.8 %all-gather = bf16[32,96,4]{1,2,0:T(4,128)(2,1)S(1)} all-gather(bf16[1,96,4]{1,2,0:T(4,128)(2,1)} %bitcast.247), channel_id=1, replica_groups=mesh['wide'=8,'narrow'=4] {'wide','narrow'}, dimensions={0}, use_global_device_ids=true | all-gather | bytes 25344 | tf_op jit(solution)/shard_map/all_gather | solution.py:111
  140.6 45.9 %all-gather.15.cloned.1.call-done = bf16[1024,1024]{1,0:T(8,128)(2,1)} async-done(((bf16[32,1024]{1,0:T(8,128)(2,1)}), bf16[1024,1024]{1,0:T(8,128)(2,1)}) %all-gather.15.cloned.1.call-update) | async-done | bytes 2097168 | tf_op jit(solution)/shard_map/all_gather | solution.py:110
  242.0 46.7 %all-gather.19.cloned.1.call-done = bf16[1024,1024]{1,0:T(8,128)(2,1)} async-done(((bf16[1024,128]{1,0:T(8,128)(2,1)}), bf16[1024,1024]{1,0:T(8,128)(2,1)}) %all-gather.19.cloned.1.call-update) | async-done | bytes 2097168 | tf_op jit(solution)/shard_map/all_gather | solution.py:121
  389.8 42.9 %collective-permute-done.3 = bf16[1024,1024]{1,0:T(8,128)(2,1)S(1)} collective-permute-done((bf16[1024,1024]{1,0:T(8,128)(2,1)S(1)}, bf16[1024,1024]{1,0:T(8,128)(2,1)S(1)}, u32[]{:S(2)}, u32[]{:S(2)}) %collective-permute-start.3) | collective-permute-done | bytes 2097184 | tf_op jit(solution)/shard_map/ppermute | solution.py:22
  569.6 42.9 %collective-permute-done.7 = bf16[1024,1024]{1,0:T(8,128)(2,1)S(1)} collective-permute-done((bf16[1024,1024]{1,0:T(8,128)(2,1)S(1)}, bf16[1024,1024]{1,0:T(8,128)(2,1)S(1)}, u32[]{:S(2)}, u32[]{:S(2)}) %collective-permute-start.7) | collective-permute-done | bytes 2097184 | tf_op jit(solution)/shard_map/ppermute | solution.py:22
  617.1 40.5 %collective-permute-done.5 = bf16[1024,1024]{1,0:T(8,128)(2,1)} collective-permute-done((bf16[1024,1024]{1,0:T(8,128)(2,1)}, bf16[1024,1024]{1,0:T(8,128)(2,1)}, u32[]{:S(2)}, u32[]{:S(2)}) %collective-permute-start.5) | collective-permute-done | bytes 2097184 | tf_op jit(solution)/shard_map/ppermute | solution.py:22
  749.4 42.8 %collective-permute-done.11 = bf16[1024,1024]{1,0:T(8,128)(2,1)S(1)} collective-permute-done((bf16[1024,1024]{1,0:T(8,128)(2,1)S(1)}, bf16[1024,1024]{1,0:T(8,128)(2,1)S(1)}, u32[]{:S(2)}, u32[]{:S(2)}) %collective-permute-start.11) | collective-permute-done | bytes 2097184 | tf_op jit(solution)/shard_map/ppermute | solution.py:22
  802.6 114.1 %all_gather.45 = bf16[2,16,1024]{1,0,2:T(2,128)(2,1)} all-gather(bf16[2,16,32]{1,0,2:T(2,128)(2,1)S(1)} %copy.102), channel_id=1, replica_groups=mesh['wide'=8,'narrow'=4] {'wide','narrow'}, dimensions={2}, use_global_device_ids=true | all-gather | bytes 67584 | tf_op jit(solution)/shard_map/all_gather | solution.py:112
  947.0 100.5 %all_gather.54 = bf16[1024,256]{1,0:T(8,128)(2,1)} all-gather(bf16[128,256]{1,0:T(8,128)(2,1)S(1)} %copy-done.119), channel_id=1, replica_groups=mesh['wide'=8,'narrow'=4] {'wide'}, dimensions={0}, use_global_device_ids=true | all-gather | bytes 589824 | tf_op jit(solution)/shard_map/all_gather | solution.py:118
  1180.4 48.6 %all-gather.23.cloned.1.call-done = bf16[1024,1024]{1,0:T(8,128)(2,1)} async-done(((bf16[128,1024]{1,0:T(8,128)(2,1)}), bf16[1024,1024]{1,0:T(8,128)(2,1)}) %all-gather.23.cloned.1.call-update) | async-done | bytes 2097168 | tf_op jit(solution)/shard_map/all_gather | solution.py:123
  1233.5 45.4 %all-gather.21.cloned.1.call-done = bf16[1024,1024]{1,0:T(8,128)(2,1)} async-done(((bf16[128,1024]{1,0:T(8,128)(2,1)}), bf16[1024,1024]{1,0:T(8,128)(2,1)}) %all-gather.21.cloned.1.call-update) | async-done | bytes 2097168 | tf_op jit(solution)/shard_map/all_gather | solution.py:122
  1283.4 47.0 %all-gather.25.cloned.1.call-done = bf16[1024,1024]{1,0:T(8,128)(2,1)} async-done(((bf16[1024,128]{1,0:T(8,128)(2,1)}), bf16[1024,1024]{1,0:T(8,128)(2,1)}) %all-gather.25.cloned.1.call-update) | async-done | bytes 2097168 | tf_op jit(solution)/shard_map/all_gather | solution.py:124
  1414.4 42.0 %all-reduce.40.cloned.1.call-done = bf16[1024,1024]{1,0:T(8,128)(2,1)} async-done(((bf16[1024,1024]{1,0:T(8,128)(2,1)}), bf16[1024,1024]{1,0:T(8,128)(2,1)}) %all-reduce.40.cloned.1.call-update) | async-done | bytes 2097168 | tf_op jit(solution)/shard_map/psum | solution.py:365
  1509.5 42.7 %collective-permute-done.18 = bf16[1024,1024]{1,0:T(8,128)(2,1)S(1)} collective-permute-done((bf16[1024,1024]{1,0:T(8,128)(2,1)}, bf16[1024,1024]{1,0:T(8,128)(2,1)S(1)}, u32[]{:S(2)}, u32[]{:S(2)}) %collective-permute-start.18) | collective-permute-done | bytes 2097184 | tf_op jit(solution)/shard_map/ppermute | solution.py:22
  1749.9 43.3 %collective-permute-done.19 = bf16[1024,1024]{1,0:T(8,128)(2,1)S(1)} collective-permute-done((bf16[1024,1024]{1,0:T(8,128)(2,1)S(1)}, bf16[1024,1024]{1,0:T(8,128)(2,1)S(1)}, u32[]{:S(2)}, u32[]{:S(2)}) %collective-permute-start.19) | collective-permute-done | bytes 2097184 | tf_op jit(solution)/shard_map/ppermute | solution.py:22
  1945.9 43.2 %collective-permute-done.23 = bf16[1024,1024]{1,0:T(8,128)(2,1)S(1)} collective-permute-done((bf16[1024,1024]{1,0:T(8,128)(2,1)S(1)}, bf16[1024,1024]{1,0:T(8,128)(2,1)S(1)}, u32[]{:S(2)}, u32[]{:S(2)}) %collective-permute-start.23) | collective-permute-done | bytes 2097184 | tf_op jit(solution)/shard_map/ppermute | solution.py:22
  2072.9 105.4 %collective-permute-done.31 = bf16[1024,1024]{1,0:T(8,128)(2,1)} collective-permute-done((bf16[1024,1024]{1,0:T(8,128)(2,1)}, bf16[1024,1024]{1,0:T(8,128)(2,1)}, u32[]{:S(2)}, u32[]{:S(2)}) %collective-permute-start.31) | collective-permute-done | bytes 2097184 | tf_op jit(solution)/shard_map/ppermute | solution.py:22
  2196.1 69.4 %collective-permute-done.32 = bf16[1024,1024]{1,0:T(8,128)(2,1)} collective-permute-done((bf16[1024,1024]{1,0:T(8,128)(2,1)}, bf16[1024,1024]{1,0:T(8,128)(2,1)}, u32[]{:S(2)}, u32[]{:S(2)}) %collective-permute-start.32) | collective-permute-done | bytes 2097184 | tf_op jit(solution)/shard_map/ppermute | solution.py:22
  2420.7 75.2 %all-reduce.50.cloned.1.call-done = (bf16[512,1024]{1,0:T(8,128)(2,1)}, bf16[512,3072]{1,0:T(8,128)(2,1)}, bf16[512,1024]{1,0:T(8,128)(2,1)}) async-done(((bf16[512,1024]{1,0:T(8,128)(2,1)}, bf16[512,3072]{1,0:T(8,128)(2,1)}, bf16[512,1024]{1,0:T(8,128)(2,1)}), (bf16[512,1024]{1,0:T(8,128)(2,1)}, bf16[512,3072]{1,0:T(8,128)(2,1)}, bf16[512,1024]{1,0:T(8,128)(2,1)})) %all-reduce.50.cloned.1.call-update) | async-done | bytes 5242896 | tf_op jit(solution)/shard_map/psum | solution.py:282
  2521.6 111.4 %reduce-scatter.42.cloned.1.call-done = f32[32,32]{1,0:T(8,128)} async-done(((f32[1024,32]{1,0:T(8,128)}), f32[32,32]{1,0:T(8,128)}) %reduce-scatter.42.cloned.1.call-update) | async-done | bytes 4112
  2634.5 60.6 %reduce-scatter.46.cloned.1.call-done = bf16[128,256]{1,0:T(8,128)(2,1)} async-done(((bf16[1024,256]{1,0:T(8,128)(2,1)}), bf16[128,256]{1,0:T(8,128)(2,1)}) %reduce-scatter.46.cloned.1.call-update) | async-done | bytes 65552
  2696.7 63.1 %reduce-scatter.32.cloned.1.call-done = bf16[128,256]{1,0:T(8,128)(2,1)} async-done(((bf16[1024,256]{1,0:T(8,128)(2,1)}), bf16[128,256]{1,0:T(8,128)(2,1)}) %reduce-scatter.32.cloned.1.call-update) | async-done | bytes 65552 | tf_op jit(solution)/shard_map/reduce_scatter | solution.py:489
  2761.3 69.2 %reduce-scatter.50.cloned.1.call-done = bf16[128,1024]{1,0:T(8,128)(2,1)} async-done(((bf16[1024,1024]{1,0:T(8,128)(2,1)}), bf16[128,1024]{1,0:T(8,128)(2,1)}) %reduce-scatter.50.cloned.1.call-update) | async-done | bytes 262160
  2832.5 68.4 %reduce-scatter.38.cloned.1.call-done = bf16[128,1024]{1,0:T(8,128)(2,1)} async-done(((bf16[1024,1024]{1,0:T(8,128)(2,1)}), bf16[128,1024]{1,0:T(8,128)(2,1)}) %reduce-scatter.38.cloned.1.call-update) | async-done | bytes 262160 | tf_op jit(solution)/shard_map/reduce_scatter | solution.py:504
  2902.7 69.2 %reduce-scatter.36.cloned.1.call-done = bf16[128,1024]{1,0:T(8,128)(2,1)} async-done(((bf16[1024,1024]{1,0:T(8,128)(2,1)}), bf16[128,1024]{1,0:T(8,128)(2,1)}) %reduce-scatter.36.cloned.1.call-update) | async-done | bytes 262160 | tf_op jit(solution)/shard_map/reduce_scatter | solution.py:501
  2973.7 134.1 %reduce-scatter.44.cloned.1.call-done = f32[32,3]{1,0:T(8,128)} async-done(((f32[1024,3]{1,0:T(8,128)}), f32[32,3]{1,0:T(8,128)}) %reduce-scatter.44.cloned.1.call-update) | async-done | bytes 400
  3109.2 96.9 %reduce-scatter.40.cloned.1.call-done = f32[96,4]{1,0:T(8,128)} async-done(((f32[3072,4]{1,0:T(8,128)}), f32[96,4]{1,0:T(8,128)}) %reduce-scatter.40.cloned.1.call-update) | async-done | bytes 1552
  3271.7 63.7 %reduce-scatter.28.cloned.1.call-done = bf16[128,256]{1,0:T(8,128)(2,1)} async-done(((bf16[1024,256]{1,0:T(8,128)(2,1)}), bf16[128,256]{1,0:T(8,128)(2,1)}) %reduce-scatter.28.cloned.1.call-update) | async-done | bytes 65552 | tf_op jit(solution)/shard_map/reduce_scatter | solution.py:483
  3336.9 63.5 %reduce-scatter.26.cloned.1.call-done = bf16[128,256]{1,0:T(8,128)(2,1)} async-done(((bf16[1024,256]{1,0:T(8,128)(2,1)}), bf16[128,256]{1,0:T(8,128)(2,1)}) %reduce-scatter.26.cloned.1.call-update) | async-done | bytes 65552 | tf_op jit(solution)/shard_map/reduce_scatter | solution.py:480
  3401.8 69.0 %reduce-scatter.48.cloned.1.call-done = bf16[128,1024]{1,0:T(8,128)(2,1)} async-done(((bf16[1024,1024]{1,0:T(8,128)(2,1)}), bf16[128,1024]{1,0:T(8,128)(2,1)}) %reduce-scatter.48.cloned.1.call-update) | async-done | bytes 262160
  3472.8 68.8 %reduce-scatter.34.cloned.1.call-done = bf16[128,1024]{1,0:T(8,128)(2,1)} async-done(((bf16[1024,1024]{1,0:T(8,128)(2,1)}), bf16[128,1024]{1,0:T(8,128)(2,1)}) %reduce-scatter.34.cloned.1.call-update) | async-done | bytes 262160 | tf_op jit(solution)/shard_map/reduce_scatter | solution.py:495
  (722 shorter events, 1468.0 us)
Async XLA Ops:
  8.7 177.7 %all-gather.15.cloned.1.call-start = ((), (), s32[]{:S(2)}) async-start(), calls=%async_computation.15 | async-start | bytes 2162688 | tf_op jit(solution)/shard_map/all_gather | solution.py:110
  9.4 227.8 %all-gather.17.cloned.1.call-start = ((), (), s32[]{:S(2)}) async-start(), calls=%async_computation.16 | async-start | bytes 2359296 | tf_op jit(solution)/shard_map/all_gather | solution.py:120
  10.0 278.7 %all-gather.19.cloned.1.call-start = ((), (), s32[]{:S(2)}) async-start(), calls=%async_computation.17 | async-start | bytes 2359296 | tf_op jit(solution)/shard_map/all_gather | solution.py:121
  10.6 317.8 %all-reduce.26.cloned.1.call-start = ((), (), s32[]{:S(2)}) async-start(), calls=%async_computation.18 | async-start | bytes 2097152 | tf_op jit(solution)/shard_map/psum | solution.py:195
  294.0 183.8 %all-reduce.28.cloned.1.call-start = ((), (), s32[]{:S(2)}) async-start(), calls=%async_computation.19 | async-start | bytes 2097152 | tf_op jit(solution)/shard_map/psum | solution.py:195
  437.1 220.4 %all-reduce.30.cloned.1.call-start = ((), (), s32[]{:S(2)}) async-start(), calls=%async_computation.20 | async-start | bytes 2097152 | tf_op jit(solution)/shard_map/psum | solution.py:195
  616.8 299.8 %all-reduce.32.cloned.1.call-start = ((), (), s32[]{:S(2)}) async-start(), calls=%async_computation.21 | async-start | bytes 2097152 | tf_op jit(solution)/shard_map/psum | solution.py:195
  716.5 200.2 %collective-permute-start.9 = (bf16[1024,1024]{1,0:T(8,128)(2,1)}, bf16[1024,1024]{1,0:T(8,128)(2,1)}, u32[]{:S(2)}, u32[]{:S(2)}) collective-permute-start(bf16[1024,1024]{1,0:T(8,128)(2,1)} %get-tuple-element.59), channel_id=1, source_target_pairs={{0,4},{4,8},{8,12},{12,16},{16,20},{20,24},{24,28},{1,5},{5,9},{9,... | collective-permute-start | bytes 6291464 | tf_op jit(solution)/shard_map/ppermute | solution.py:22
  796.7 320.5 %all-reduce.34.cloned.1.call-start = ((), (), s32[]{:S(2)}) async-start(), calls=%async_computation.22 | async-start | bytes 4194304 | tf_op jit(solution)/shard_map/psum | solution.py:195
  1142.3 188.1 %all-gather.25.cloned.1.call-start = ((), (), s32[]{:S(2)}) async-start(), calls=%async_computation.26 | async-start | bytes 2359296 | tf_op jit(solution)/shard_map/all_gather | solution.py:124
  1142.9 233.7 %all-reduce.38.cloned.1.call-start = ((), (), s32[]{:S(2)}) async-start(), calls=%async_computation.27 | async-start | bytes 2097152 | tf_op jit(solution)/shard_map/psum | solution.py:300
  1404.5 233.4 %all-reduce.42.cloned.1.call-start = ((), (), s32[]{:S(2)}) async-start(), calls=%async_computation.29 | async-start | bytes 2097152 | tf_op jit(solution)/shard_map/psum | solution.py:365
  1601.3 232.6 %all-reduce.44.cloned.1.call-start = ((), (), s32[]{:S(2)}) async-start(), calls=%async_computation.30 | async-start | bytes 2097152 | tf_op jit(solution)/shard_map/psum | solution.py:365
  1796.9 232.8 %all-reduce.46.cloned.1.call-start = ((), (), s32[]{:S(2)}) async-start(), calls=%async_computation.31 | async-start | bytes 2097152 | tf_op jit(solution)/shard_map/psum | solution.py:365
  1992.8 332.6 %all-reduce.48.cloned.1.call-start = ((), (), s32[]{:S(2)}) async-start(), calls=%async_computation.32 | async-start | bytes 2097152 | tf_op jit(solution)/shard_map/psum | solution.py:365
  1992.8 185.5 %collective-permute-start.31 = (bf16[1024,1024]{1,0:T(8,128)(2,1)}, bf16[1024,1024]{1,0:T(8,128)(2,1)}, u32[]{:S(2)}, u32[]{:S(2)}) collective-permute-start(bf16[1024,1024]{1,0:T(8,128)(2,1)} %get-tuple-element.51), channel_id=1, source_target_pairs={{0,4},{4,8},{8,12},{12,16},{16,20},{20,24},{24,28},{1,5},{5,9},{9,... | collective-permute-start | bytes 6291464 | tf_op jit(solution)/shard_map/ppermute | solution.py:22
  2047.5 218.1 %collective-permute-start.32 = (bf16[1024,1024]{1,0:T(8,128)(2,1)}, bf16[1024,1024]{1,0:T(8,128)(2,1)}, u32[]{:S(2)}, u32[]{:S(2)}) collective-permute-start(bf16[1024,1024]{1,0:T(8,128)(2,1)} %get-tuple-element.49), channel_id=1, source_target_pairs={{0,4},{4,8},{8,12},{12,16},{16,20},{20,24},{24,28},{1,5},{5,9},{9,... | collective-permute-start | bytes 6291464 | tf_op jit(solution)/shard_map/ppermute | solution.py:22
  2067.1 198.5 %collective-permute-start.24 = (bf16[1024,1024]{1,0:T(8,128)(2,1)S(1)}, bf16[1024,1024]{1,0:T(8,128)(2,1)S(1)}, u32[]{:S(2)}, u32[]{:S(2)}) collective-permute-start(bf16[1024,1024]{1,0:T(8,128)(2,1)S(1)} %fusion.35), channel_id=1, source_target_pairs={{4,0},{8,4},{12,8},{16,12},{20,16},{24,20},{28,24},{5,1},{9,5},{13... | collective-permute-start | bytes 6291464 | tf_op jit(solution)/shard_map/ppermute | solution.py:22
  2288.0 207.8 %all-reduce.50.cloned.1.call-start = ((), (), s32[]{:S(2)}) async-start(), calls=%async_computation.46 | async-start | bytes 10485760 | tf_op jit(solution)/shard_map/psum | solution.py:282
  2391.3 241.7 %reduce-scatter.42.cloned.1.call-start = ((), (), s32[]{:S(2)}) async-start(), calls=%async_computation.41 | async-start | bytes 540672
  2395.3 299.8 %reduce-scatter.46.cloned.1.call-start = ((), (), s32[]{:S(2)}) async-start(), calls=%async_computation.43 | async-start | bytes 589824
  2398.5 361.3 %reduce-scatter.32.cloned.1.call-start = ((), (), s32[]{:S(2)}) async-start(), calls=%async_computation.36 | async-start | bytes 589824 | tf_op jit(solution)/shard_map/reduce_scatter | solution.py:489
  2400.1 430.4 %reduce-scatter.50.cloned.1.call-start = ((), (), s32[]{:S(2)}) async-start(), calls=%async_computation.45 | async-start | bytes 2359296
  2408.0 493.0 %reduce-scatter.38.cloned.1.call-start = ((), (), s32[]{:S(2)}) async-start(), calls=%async_computation.39 | async-start | bytes 2359296 | tf_op jit(solution)/shard_map/reduce_scatter | solution.py:504
  2413.1 558.8 %reduce-scatter.36.cloned.1.call-start = ((), (), s32[]{:S(2)}) async-start(), calls=%async_computation.38 | async-start | bytes 2359296 | tf_op jit(solution)/shard_map/reduce_scatter | solution.py:501
  2417.0 690.7 %reduce-scatter.44.cloned.1.call-start = ((), (), s32[]{:S(2)}) async-start(), calls=%async_computation.42 | async-start | bytes 540672
  2418.8 787.2 %reduce-scatter.40.cloned.1.call-start = ((), (), s32[]{:S(2)}) async-start(), calls=%async_computation.40 | async-start | bytes 1622016
  2420.6 849.5 %reduce-scatter.30.cloned.1.call-start = ((), (), s32[]{:S(2)}) async-start(), calls=%async_computation.35 | async-start | bytes 589824 | tf_op jit(solution)/shard_map/reduce_scatter | solution.py:486
  2498.3 837.0 %reduce-scatter.28.cloned.1.call-start = ((), (), s32[]{:S(2)}) async-start(), calls=%async_computation.34 | async-start | bytes 589824 | tf_op jit(solution)/shard_map/reduce_scatter | solution.py:483
  2500.8 899.5 %reduce-scatter.26.cloned.1.call-start = ((), (), s32[]{:S(2)}) async-start(), calls=%async_computation.33 | async-start | bytes 589824 | tf_op jit(solution)/shard_map/reduce_scatter | solution.py:480
  2503.4 967.5 %reduce-scatter.48.cloned.1.call-start = ((), (), s32[]{:S(2)}) async-start(), calls=%async_computation.44 | async-start | bytes 2359296
  2513.6 1027.9 %reduce-scatter.34.cloned.1.call-start = ((), (), s32[]{:S(2)}) async-start(), calls=%async_computation.37 | async-start | bytes 2359296 | tf_op jit(solution)/shard_map/reduce_scatter | solution.py:495
  (203 other events, 7421.7 us)
Sparse Core Ops, SparseCore 0:
  10.9 59.1 all-gather.10
  72.9 55.3 all-gather.12
  131.2 55.2 all-gather.14
  188.4 48.7 all-gather.16
  239.1 49.5 all-gather.18
  437.2 37.2 all-reduce.27
  617.0 37.3 all-reduce.29
  796.8 38.1 all-reduce.31
  1064.6 52.4 all-reduce.33
  1141.1 36.1 all-reduce.35
  1179.3 49.6 all-gather.22
  1231.1 47.7 all-gather.20
  1280.8 49.5 all-gather.24
  1404.6 51.7 all-reduce.39
  1601.4 36.4 all-reduce.41
  1797.0 36.8 all-reduce.43
  1992.9 36.7 all-reduce.45
  2288.2 37.1 all-reduce.47
  2391.4 104.4 all-reduce.49
  2498.7 134.2 reduce-scatter.41
  2637.3 57.7 reduce-scatter.45
  2698.9 60.9 reduce-scatter.31
  2763.8 66.7 reduce-scatter.49
  2834.3 66.5 reduce-scatter.37
  2905.3 66.5 reduce-scatter.35
  2974.8 132.9 reduce-scatter.43
  3113.0 92.9 reduce-scatter.39
  3209.2 60.9 reduce-scatter.29
  3274.5 60.8 reduce-scatter.27
  3339.3 60.9 reduce-scatter.25
  3404.1 66.6 reduce-scatter.47
  3474.8 66.7 reduce-scatter.33
  (2 shorter events, 68.4 us)
where the time goes:
time: 3560 us; the launch traced here: 3550 us
  waiting for transfers between devices  2360 us (66%)
  blocking collectives  403 us (11%)
  matrix products  376 us (11%)
  other arithmetic  179 us (5%)
  local copies, waits for them, and re-layouts  110 us (3%)
  starting transfers between devices  100 us (3%)
    ppermute x33, waiting for transfers between devices, from_behind(): lax.ppermute(value, axis, [(source, source + steps) for source in range(f...  836 us
    unnamed x40, waiting for transfers between devices  546 us
    dot_general x35, matrix products, inner_left(): lax.dot_general(left_side, right_side, (((0,), (0,)), ((), ())), preferre...  193 us
    psum x5, waiting for transfers between devices, body(): lax.psum(stacked.astype(jnp.bfloat16), 'narrow').astype(jnp.float32)  154 us
    all_gather x1, blocking collectives, body(): lax.all_gather(persistent, ('wide', 'narrow'), axis=2, tiled=True)  114 us
    dot_general x31, matrix products, matmul(): return jnp.dot(left_side, right_side, preferred_element_type=jnp.float32)  104 us
    all_gather x1, blocking collectives, body(): lax.all_gather(out_gate, 'wide', axis=0, tiled=True)  100 us
    ppermute x33, starting transfers between devices, from_behind(): lax.ppermute(value, axis, [(source, source + steps) for source in range(f...  96.7 us
  transfers between devices with their start and end apart: 67, of which 50 were waited for; matrix products, arithmetic and copies ran while one was open for 13% of the time, Pallas kernels for 0%

commit v1 on v0

v1 whole, which is shorter than its diff:
```python
import math

import jax
import jax.numpy as jnp
from jax import lax
from jax.experimental import pallas as pl
from jax.experimental.pallas import tpu as pltpu
from jax.sharding import PartitionSpec as P

HEAD = 64
LANE_WIDE = 4
MESH = pl.DeviceIdType.MESH
ANY = pl.BlockSpec(memory_space=pl.ANY)
bf16 = jnp.bfloat16
f32 = jnp.float32

decay_top = 0.2
moment_top = 0.9
learn_top = 0.1
eps_norm = 1e-05
eps_head = 1e-06
masked_score = -1e30


def remote(src, dst, send, recv, device):
    return pltpu.make_async_remote_copy(
        src_ref=src, dst_ref=dst, send_sem=send, recv_sem=recv, device_id=device, device_id_type=MESH
    )


def exchange(arrays, axes, ident):
    wide, narrow = lax.axis_size("wide"), lax.axis_size("narrow")
    peers = {"all": wide * narrow, "wide": wide, "narrow": narrow}[axes]
    picks = [pick for _, pick in arrays]
    operands = [array for array, _ in arrays]
    chunks = [a.shape if pick is None else a.shape[1:] for a, pick in arrays]
    count = len(arrays)

    def kernel(*refs):
        ins, outs, holds = refs[:count], refs[count : 2 * count], refs[2 * count : 3 * count]
        send_sem, recv_sem, local_sem = refs[3 * count :]
        my_wide, my_narrow = lax.axis_index("wide"), lax.axis_index("narrow")
        me = {"all": my_wide * narrow + my_narrow, "wide": my_wide, "narrow": my_narrow}[axes]

        def place(step):
            target = lax.rem(me + step, peers)
            if axes == "all":
                return lax.div(target, narrow), lax.rem(target, narrow)
            return (target, my_narrow) if axes == "wide" else (my_wide, target)

        barrier = pltpu.get_barrier_semaphore()

        def greet(step, carry):
            pl.semaphore_signal(barrier, inc=1, device_id=place(step), device_id_type=MESH)
            return carry

        lax.fori_loop(1, peers, greet, 0)

        def chunk(index, where):
            return ins[index] if picks[index] is None else ins[index].at[picks[index](*where)]

        own = [
            pltpu.make_async_copy(chunk(i, (my_wide, my_narrow)), holds[i], local_sem.at[i]) for i in range(count)
        ]
        for copy in own:
            copy.start()
        pl.semaphore_wait(barrier, peers - 1)

        def send(step, carry):
            where = place(step)
            for i in range(count):
                remote(chunk(i, where), outs[i].at[me], send_sem.at[i], recv_sem.at[i], where).start()
            return carry

        lax.fori_loop(1, peers, send, 0)
        for i in range(count):
            own[i].wait()
            back = pltpu.make_async_copy(holds[i], outs[i].at[me], local_sem.at[i])
            back.start()
            back.wait()
        for i in range(count):
            others = outs[i].at[pl.ds(0, peers - 1)]
            whole = remote(others, others, send_sem.at[i], recv_sem.at[i], place(1))
            whole.wait_send()
            whole.wait_recv()

    return pl.pallas_call(
        kernel,
        out_shape=[jax.ShapeDtypeStruct((peers,) + tuple(c), a.dtype) for a, c in zip(operands, chunks)],
        in_specs=[ANY] * count,
        out_specs=[ANY] * count,
        scratch_shapes=[pltpu.VMEM(tuple(c), a.dtype) for a, c in zip(operands, chunks)]
        + [pltpu.SemaphoreType.DMA((count,))] * 3,
        compiler_params=pltpu.CompilerParams(collective_id=ident, has_side_effects=True),
        name=f"exchange_{ident}",
    )(*operands)


def gather_all(arrays, ident):
    wide, narrow = lax.axis_size("wide"), lax.axis_size("narrow")
    zs = 4 if wide % 4 == 0 else 1
    xs, ys = wide // zs, narrow // 2
    count = len(arrays)
    rows = arrays[0].shape[0]
    half = rows // 2

    def kernel(*refs):
        ins, outs = refs[:count], refs[count : 2 * count]
        hold, local_sem, sent, got, sent_pair, got_pair = refs[2 * count :]
        my_wide, my_narrow = lax.axis_index("wide"), lax.axis_index("narrow")
        mz, mx = lax.div(my_wide, xs), lax.rem(my_wide, xs)
        my, mc = lax.div(my_narrow, 2), lax.rem(my_narrow, 2)

        def dev(z, x, y, c):
            return (z * xs + x, 2 * y + c)

        barrier = pltpu.get_barrier_semaphore()
        friends = [dev(lax.rem(mz + s, zs), mx, my, mc) for s in range(1, zs)]
        friends += [dev(mz, lax.rem(mx + s, xs), my, mc) for s in range(1, xs)]
        friends += [dev(mz, mx, lax.rem(my + s, ys), mc) for s in range(1, ys)]
        friends += [dev(mz, mx, my, 1 - mc)]
        for friend in friends:
            pl.semaphore_signal(barrier, inc=1, device_id=friend, device_id_type=MESH)
        own = [pltpu.make_async_copy(ins[i], hold.at[i], local_sem.at[i]) for i in range(count)]
        for copy in own:
            copy.start()
        pl.semaphore_wait(barrier, len(friends))

        waits = []
        number = [0]

        def piece(i, z, x, y, c, h):
            return outs[i].at[z * xs + x, 2 * y + c, pl.ds(h * half, half)]

        def spot(z, x, y):
            return (z * xs + x) * ys + y

        def push(i, z, x, y, h, target, src=None):
            here = piece(i, z, x, y, mc, h)
            copy = remote(
                here if src is None else src, here, sent.at[number[0]], got.at[i, spot(z, x, y), h], target
            )
            number[0] += 1
            copy.start()
            waits.append(copy)

        def arrived(i, z, x, y, h):
            here = piece(i, z, x, y, mc, h)
            remote(here, here, sent.at[0], got.at[i, spot(z, x, y), h], dev(mz, mx, my, 1 - mc)).wait_recv()

        pairs = []

        def to_partner(i, z, x, y, h, src=None):
            here = piece(i, z, x, y, mc, h)
            copy = remote(
                here if src is None else src,
                here,
                sent_pair.at[len(pairs)],
                got_pair.at[i, spot(z, x, y), h],
                dev(mz, mx, my, 1 - mc),
            )
            copy.start()
            pairs.append(copy)

        def first_fan(i, z, src=(None, None)):
            for s in range(1, ys):
                push(i, z, mx, my, 0, dev(mz, mx, lax.rem(my + s, ys), mc), src[0])
            for s in range(1, xs):
                push(i, z, mx, my, 1, dev(mz, lax.rem(mx + s, xs), my, mc), src[1])
            for s in range(1, xs):
                push(i, z, mx, my, 0, dev(mz, lax.rem(mx + s, xs), my, mc), src[0])
            for s in range(1, ys):
                push(i, z, mx, my, 1, dev(mz, mx, lax.rem(my + s, ys), mc), src[1])
            for h in (0, 1):
                to_partner(i, z, mx, my, h, src[h])

        for i in range(count):
            for s in range(1, zs):
                for h in (0, 1):
                    push(i, mz, mx, my, h, dev(lax.rem(mz + s, zs), mx, my, mc), ins[i].at[pl.ds(h * half, half)])
            first_fan(i, mz, (ins[i].at[pl.ds(0, half)], ins[i].at[pl.ds(half, half)]))
        for i in range(count):
            for s in range(1, zs):
                z = lax.rem(mz + zs - s, zs)
                for h in (0, 1):
                    arrived(i, z, mx, my, h)
                first_fan(i, z)
        for i in range(count):
            for s in range(zs):
                z = lax.rem(mz + zs - s, zs)
                for r in range(1, ys):
                    y = lax.rem(my + r, ys)
                    arrived(i, z, mx, y, 0)
                    for q in range(1, xs):
                        push(i, z, mx, y, 0, dev(mz, lax.rem(mx + q, xs), my, mc))
                    to_partner(i, z, mx, y, 0)
                for r in range(1, xs):
                    x = lax.rem(mx + r, xs)
                    arrived(i, z, x, my, 1)
                    for q in range(1, ys):
                        push(i, z, x, my, 1, dev(mz, mx, lax.rem(my + q, ys), mc))
                    to_partner(i, z, x, my, 1)
        for i in range(count):
            own[i].wait()
            back = pltpu.make_async_copy(hold.at[i], outs[i].at[my_wide, my_narrow], local_sem.at[i])
            back.start()
            back.wait()
        for i in range(count):
            for s in range(zs):
                z = lax.rem(mz + zs - s, zs)
                for q in range(1, xs):
                    x = lax.rem(mx + q, xs)
                    arrived(i, z, x, my, 0)
                    to_partner(i, z, x, my, 0)
                    for r in range(1, ys):
                        y = lax.rem(my + r, ys)
                        arrived(i, z, x, y, 0)
                        to_partner(i, z, x, y, 0)
                for r in range(1, ys):
                    y = lax.rem(my + r, ys)
                    arrived(i, z, mx, y, 1)
                    to_partner(i, z, mx, y, 1)
                    for q in range(1, xs):
                        x = lax.rem(mx + q, xs)
                        arrived(i, z, x, y, 1)
                        to_partner(i, z, x, y, 1)
        for copy in waits + pairs:
            copy.wait_send()
        for i in range(count):
            for z in range(zs):
                for x in range(xs):
                    for y in range(ys):
                        for h in (0, 1):
                            there = piece(i, z, x, y, 1 - mc, h)
                            remote(
                                there, there, sent.at[0], got_pair.at[i, spot(z, x, y), h], dev(mz, mx, my, 1 - mc)
                            ).wait_recv()

    chips = zs * xs * ys
    sends = count * (2 * (zs - 1) + zs * 2 * (xs - 1 + ys - 1) + 2 * zs * (xs - 1) * (ys - 1))
    return pl.pallas_call(
        kernel,
        out_shape=[jax.ShapeDtypeStruct((wide, narrow) + a.shape, a.dtype) for a in arrays],
        in_specs=[ANY] * count,
        out_specs=[ANY] * count,
        scratch_shapes=[
            pltpu.VMEM((count,) + arrays[0].shape, arrays[0].dtype),
            pltpu.SemaphoreType.DMA((count,)),
            pltpu.SemaphoreType.DMA((sends,)),
            pltpu.SemaphoreType.DMA((count, chips, 2)),
            pltpu.SemaphoreType.DMA((count * chips * 2,)),
            pltpu.SemaphoreType.DMA((count, chips, 2)),
        ],
        compiler_params=pltpu.CompilerParams(collective_id=ident, has_side_effects=True),
        name=f"gather_{ident}",
    )(*arrays)


def matmul(left_side, right_side):
    return jnp.dot(left_side, right_side, preferred_element_type=jnp.float32)


def inner_left(left_side, right_side):
    return lax.dot_general(left_side, right_side, (((0,), (0,)), ((), ())), preferred_element_type=jnp.float32)


def inner_right(left_side, right_side):
    return lax.dot_general(left_side, right_side, (((1,), (1,)), ((), ())), preferred_element_type=jnp.float32)


def silu_slope(values):
    sigmoid_val = jax.nn.sigmoid(values)
    return sigmoid_val * (1.0 + values * (1.0 - sigmoid_val))


def silu_curve(values):
    sigmoid_val = jax.nn.sigmoid(values)
    return sigmoid_val * (1.0 - sigmoid_val) * (2.0 + values * (1.0 - 2.0 * sigmoid_val))


class Lane:
    def __init__(self):
        narrow = lax.axis_size("narrow")
        self.ys = narrow // 2
        self.chips = LANE_WIDE * self.ys
        wide_pos, narrow_pos = lax.axis_index("wide"), lax.axis_index("narrow")
        self.base = lax.div(wide_pos, LANE_WIDE) * LANE_WIDE
        self.colour = lax.rem(narrow_pos, 2)
        self.chip = lax.rem(wide_pos, LANE_WIDE) * self.ys + lax.div(narrow_pos, 2)
        self.partner = (wide_pos, narrow_pos + 1 - 2 * self.colour)

    def other(self, step):
        return lax.rem(self.chip + step, self.chips)

    def device(self, chip):
        return self.base + lax.div(chip, self.ys), 2 * lax.rem(chip, self.ys) + self.colour

    def greet(self):
        barrier = pltpu.get_barrier_semaphore()
        for step in range(1, self.chips):
            pl.semaphore_signal(barrier, inc=1, device_id=self.device(self.other(step)), device_id_type=MESH)
        pl.semaphore_signal(barrier, inc=1, device_id=self.partner, device_id_type=MESH)
        pl.semaphore_wait(barrier, self.chips)


class Scatter:
    def __init__(self, lane, part, pair, half, got, sems):
        self.lane, self.part, self.pair, self.half, self.got = lane, part, pair, half, got
        self.pair_send, self.pair_recv, self.send, self.recv = sems

    @staticmethod
    def scratch(chips, rows, width):
        return [
            pltpu.VMEM((2, chips, rows, width), bf16),
            pltpu.VMEM((chips, rows, width), bf16),
            pltpu.VMEM((chips, rows, width), bf16),
            pltpu.VMEM((chips, rows, width), bf16),
            pltpu.SemaphoreType.DMA((1,)),
            pltpu.SemaphoreType.DMA((1,)),
            pltpu.SemaphoreType.DMA((chips,)),
            pltpu.SemaphoreType.DMA((chips,)),
        ]

    @classmethod
    def of(cls, lane, refs):
        return cls(lane, *refs[:4], refs[4:8])

    def pair_copy(self):
        return remote(
            self.part.at[1 - self.lane.colour],
            self.pair,
            self.pair_send.at[0],
            self.pair_recv.at[0],
            self.lane.partner,
        )

    def start_pair(self):
        self.pair_copy().start()

    def take_pair(self):
        self.pair_copy().wait()
        self.half[...] = (
            self.part[self.lane.colour].astype(f32) + self.pair[...].astype(f32)
        ).astype(bf16)

    def copy_to(self, step):
        chip = self.lane.other(step)
        return remote(
            self.half.at[chip],
            self.got.at[self.lane.chip],
            self.send.at[step],
            self.recv.at[self.lane.chip],
            self.lane.device(chip),
        )

    def start_sends(self):
        for step in range(1, self.lane.chips):
            self.copy_to(step).start()

    def total(self):
        result = self.half[self.lane.chip].astype(f32)
        for step in range(1, self.lane.chips):
            chip = self.lane.other(step)
            remote(
                self.got.at[chip], self.got.at[chip], self.send.at[step], self.recv.at[chip], self.lane.device(chip)
            ).wait_recv()
            result = result + self.got[chip].astype(f32)
        return result

    def wait_sends(self):
        for step in range(1, self.lane.chips):
            self.copy_to(step).wait_send()


class Spread:
    def __init__(self, lane, whole, sems):
        self.lane, self.whole = lane, whole
        self.send, self.recv, self.pair_send, self.pair_recv = sems

    @staticmethod
    def scratch(chips, rows, width):
        return [pltpu.VMEM((2, chips, rows, width), bf16)] + [pltpu.SemaphoreType.DMA((chips,))] * 4

    @classmethod
    def of(cls, lane, refs):
        return cls(lane, refs[0], refs[1:5])

    def mine(self):
        return self.whole.at[self.lane.colour, self.lane.chip]

    def copy_to(self, step):
        return remote(
            self.mine(),
            self.mine(),
            self.send.at[step],
            self.recv.at[self.lane.chip],
            self.lane.device(self.lane.other(step)),
        )

    def pair_copy(self, chip, colour):
        place = self.whole.at[colour, chip]
        return remote(place, place, self.pair_send.at[chip], self.pair_recv.at[chip], self.lane.partner)

    def run(self):
        lane = self.lane
        for step in range(1, lane.chips):
            self.copy_to(step).start()
        self.pair_copy(lane.chip, lane.colour).start()
        for step in range(1, lane.chips):
            chip = lane.other(step)
            place = self.whole.at[lane.colour, chip]
            remote(place, place, self.send.at[step], self.recv.at[chip], lane.device(chip)).wait_recv()
            self.pair_copy(chip, lane.colour).start()
        for chip in range(lane.chips):
            self.pair_copy(chip, 1 - lane.colour).wait_recv()
        for step in range(1, lane.chips):
            self.copy_to(step).wait_send()
        for chip in range(lane.chips):
            self.pair_copy(chip, lane.colour).wait_send()


def chain_forward(keys, queries, values, gates, first_init, second_init, ident):
    turns, blocks, span, block = keys.shape
    width, hidden = first_init.shape
    rows = values.shape[1]
    chips = LANE_WIDE * (lax.axis_size("narrow") // 2)
    n_scatter = len(Scatter.scratch(1, 8, 128))
    n_spread = len(Spread.scratch(1, 8, 128))

    def kernel(*refs):
        keys_hbm, queries_hbm, values_hbm, gates_ref, first_hbm, second_hbm = refs[:6]
        recalled_hbm, s1_hbm, s2_hbm, m1_hbm, m2_hbm, g1_hbm, g2_hbm, err_hbm, small_hbm = refs[6:15]
        rest = refs[15:]
        kbuf, qbuf, vbuf, i1, i2, s1, s2, m1, m2, g1, g2, low1, low2, small, khid, rec = rest[:16]
        in_sem, out_sem, init_sem = rest[16:19]
        rest = rest[19:]
        lane = Lane()
        lookup = Scatter.of(lane, rest[:n_scatter])
        recall = Scatter.of(lane, rest[n_scatter : 2 * n_scatter])
        error = Spread.of(lane, rest[2 * n_scatter :])

        def loads(turn, slot):
            return [
                pltpu.make_async_copy(keys_hbm.at[turn], kbuf.at[slot], in_sem.at[slot, 0]),
                pltpu.make_async_copy(queries_hbm.at[turn], qbuf.at[slot], in_sem.at[slot, 1]),
                pltpu.make_async_copy(values_hbm.at[turn], vbuf.at[slot], in_sem.at[slot, 2]),
            ]

        def state_saves(turn):
            return [
                pltpu.make_async_copy(source, target.at[turn], out_sem.at[i])
                for i, (source, target) in enumerate(((s1, s1_hbm), (s2, s2_hbm), (m1, m1_hbm), (m2, m2_hbm)))
            ]

        def other_saves(turn):
            return [
                pltpu.make_async_copy(source, target.at[turn], out_sem.at[4 + i])
                for i, (source, target) in enumerate(
                    ((g1, g1_hbm), (g2, g2_hbm), (error.whole, err_hbm), (small, small_hbm))
                )
            ]

        def rec_save(turn):
            return pltpu.make_async_copy(rec, recalled_hbm.at[turn], out_sem.at[8])

        inits = [
            pltpu.make_async_copy(first_hbm, i1, init_sem.at[0]),
            pltpu.make_async_copy(second_hbm, i2, init_sem.at[1]),
        ]
        for copy in inits + loads(0, 0):
            copy.start()
        lane.greet()
        for copy in inits:
            copy.wait()
        low1[...] = i1[...]
        low2[...] = i2[...]
        s1[...] = i1[...].astype(f32)
        s2[...] = i2[...].astype(f32)
        m1[...] = jnp.zeros_like(m1)
        m2[...] = jnp.zeros_like(m2)

        def finish_recall(turn):
            rec[...] = recall.total().astype(bf16)
            recall.wait_sends()
            rec_save(turn).start()

        def lookup_blocks(buf, slot):
            total = matmul(buf[slot, 0], low1[pl.ds(0, block), :])
            for b in range(1, blocks):
                total = total + matmul(buf[slot, b], low1[pl.ds(b * block, block), :])
            return total

        def turn_body(turn, carry):
            slot = lax.rem(turn, 2)

            @pl.when(turn + 1 < turns)
            def _():
                for copy in loads(turn + 1, 1 - slot):
                    copy.start()

            for copy in state_saves(turn):
                copy.start()
            for copy in loads(turn, slot):
                copy.wait()
            key_pre = lookup_blocks(kbuf, slot)
            small[0] = key_pre
            khid[...] = (key_pre * jax.nn.sigmoid(key_pre)).astype(bf16)
            lookup.part[...] = matmul(khid[...], low2[...]).astype(bf16).reshape(2, chips, rows, width)
            lookup.start_pair()

            @pl.when(turn > 0)
            def _():
                finish_recall(turn - 1)

            query_pre = lookup_blocks(qbuf, slot)
            small[1] = query_pre
            query_hidden = (query_pre * jax.nn.sigmoid(query_pre)).astype(bf16)
            recall.part[...] = matmul(query_hidden, low2[...]).astype(bf16).reshape(2, chips, rows, width)
            recall.start_pair()

            lookup.take_pair()
            lookup.start_sends()
            recall.take_pair()
            total = lookup.total()
            error.whole[lane.colour, lane.chip] = ((total - vbuf[slot].astype(f32)) / span).astype(bf16)
            error.run()
            lookup.wait_sends()
            recall.start_sends()

            err = error.whole[...].reshape(span, width)
            g2[...] = inner_left(khid[...], err)
            hidden_grad = inner_right(err, low2[...])
            small[2] = hidden_grad
            slope = (hidden_grad * silu_slope(small[0])).astype(bf16)
            for b in range(blocks):
                g1[pl.ds(b * block, block), :] = inner_left(kbuf[slot, b], slope)
            saves = other_saves(turn)
            for copy in saves:
                copy.start()
            decay, moment, rate, reset = (gates_ref[turn, i] for i in range(4))
            for copy in state_saves(turn):
                copy.wait()
            for s, m, g, init, low in ((s1, m1, g1, i1, low1), (s2, m2, g2, i2, low2)):
                moment_new = moment * m[...] - rate * g[...]
                state_new = (1.0 - decay) * s[...] + moment_new
                state_new = reset * init[...].astype(f32) + (1.0 - reset) * state_new
                m[...] = (1.0 - reset) * moment_new
                s[...] = state_new
                low[...] = state_new.astype(bf16)
            for copy in saves:
                copy.wait()

            @pl.when(turn > 0)
            def _():
                rec_save(turn - 1).wait()

            return carry

        lax.fori_loop(0, turns, turn_body, 0)
        finish_recall(turns - 1)
        rec_save(turns - 1).wait()

    state = [(width, hidden), (hidden, width)]
    out_shape = (
        [jax.ShapeDtypeStruct((turns, rows, width), bf16)]
        + [jax.ShapeDtypeStruct((turns,) + s, f32) for s in state * 3]
        + [
            jax.ShapeDtypeStruct((turns, 2, chips, rows, width), bf16),
            jax.ShapeDtypeStruct((turns, 3, span, hidden), f32),
        ]
    )
    scratch = (
        [pltpu.VMEM((2, blocks, span, block), bf16)] * 2
        + [pltpu.VMEM((2, rows, width), bf16)]
        + [pltpu.VMEM(s, bf16) for s in state]
        + [pltpu.VMEM(s, f32) for s in state * 3]
        + [pltpu.VMEM(s, bf16) for s in state]
        + [
            pltpu.VMEM((3, span, hidden), f32),
            pltpu.VMEM((span, hidden), bf16),
            pltpu.VMEM((rows, width), bf16),
            pltpu.SemaphoreType.DMA((2, 3)),
            pltpu.SemaphoreType.DMA((9,)),
            pltpu.SemaphoreType.DMA((2,)),
        ]
        + Scatter.scratch(chips, rows, width) * 2
        + Spread.scratch(chips, rows, width)
    )
    return pl.pallas_call(
        kernel,
        out_shape=out_shape,
        in_specs=[ANY] * 3 + [pl.BlockSpec(memory_space=pltpu.SMEM)] + [ANY] * 2,
        out_specs=[ANY] * len(out_shape),
        scratch_shapes=scratch,
        compiler_params=pltpu.CompilerParams(
            collective_id=ident, has_side_effects=True, vmem_limit_bytes=60 * 1024 * 1024
        ),
        cost_estimate=pl.CostEstimate(
            flops=turns * 7 * 2 * span * width * hidden, bytes_accessed=turns * 12 * 2**20, transcendentals=0
        ),
        name="chain_forward",
    )(keys, queries, values, gates, first_init, second_init)


def chain_backward(keys, queries, recall_grads, saved, gates, ident):
    s1_all, s2_all, m1_all, m2_all, g1_all, g2_all, err_all, small_all = saved
    turns, blocks, span, block = keys.shape
    width, hidden = s1_all.shape[1:]
    chips, rows = err_all.shape[2:4]
    n_scatter = len(Scatter.scratch(1, 8, 128))

    def kernel(*refs):
        ins, gates_ref = refs[:11], refs[11]
        qcot_hbm, kcot_hbm, vcot_hbm, sums1_ref, sums2_ref, mg1_hbm, mg2_hbm = refs[12:19]
        rest = refs[19:]
        bufs, rest = rest[:11], rest[11:]
        kbuf, qbuf, rbuf, s1, s2, m1, m2, g1, g2, errs, small = bufs
        cf, cs, cmf, cms, w1, w2, a1, a2, c1, c2, low1, low2, dh, khid, qpl, qhid, sg, qsave, ksave, vsave = rest[:20]
        in_sem, out_sem, end_sem = rest[20:23]
        rest = rest[23:]
        lane = Lane()
        lookup = Scatter.of(lane, rest[:n_scatter])
        qstream = Scatter.of(lane, rest[n_scatter : 2 * n_scatter])
        kstream = Scatter.of(lane, rest[2 * n_scatter : 3 * n_scatter])
        spread = Spread.of(lane, rest[3 * n_scatter :])

        def loads(turn, slot):
            return [
                pltpu.make_async_copy(source.at[turn], target.at[slot], in_sem.at[slot, i])
                for i, (source, target) in enumerate(zip(ins, bufs))
            ]

        for copy in loads(turns - 1, 0):
            copy.start()
        lane.greet()
        for ref in (cf, cs, cmf, cms, a1, a2):
            ref[...] = jnp.zeros_like(ref)

        def qout(turn):
            return pltpu.make_async_copy(qsave, qcot_hbm.at[turn], out_sem.at[0])

        def kout(turn):
            return pltpu.make_async_copy(ksave, kcot_hbm.at[turn], out_sem.at[1])

        def vout(turn):
            return pltpu.make_async_copy(vsave, vcot_hbm.at[turn], out_sem.at[2])

        def finish(stream, save, out):
            save[...] = stream.total().astype(bf16)
            stream.wait_sends()
            out.start()

        def body(step, carry):
            turn = turns - 1 - step
            slot = lax.rem(step, 2)

            @pl.when(step + 1 < turns)
            def _():
                for copy in loads(turn - 1, 1 - slot):
                    copy.start()

            for copy in loads(turn, slot):
                copy.wait()
            decay, moment, rate, reset = (gates_ref[turn, i] for i in range(4))
            c1[...] = (-rate * (cmf[...] + cf[...])).astype(bf16)
            c2[...] = (-rate * (cms[...] + cs[...])).astype(bf16)
            low1[...] = s1[slot].astype(bf16)
            low2[...] = s2[slot].astype(bf16)
            slope_grad = matmul(kbuf[slot, 0], c1[pl.ds(0, block), :])
            for b in range(1, blocks):
                slope_grad = slope_grad + matmul(kbuf[slot, b], c1[pl.ds(b * block, block), :])
            sg[...] = slope_grad
            key_pre = small[slot, 0]
            khid[...] = (key_pre * jax.nn.sigmoid(key_pre)).astype(bf16)
            dh[...] = (slope_grad * silu_slope(key_pre)).astype(bf16)
            lookup.part[...] = (
                (matmul(khid[...], c2[...]) + matmul(dh[...], low2[...])).astype(bf16).reshape(2, chips, rows, width)
            )
            lookup.start_pair()

            @pl.when(step > 0)
            def _():
                finish(qstream, qsave, qout(turn + 1))

            @pl.when(step > 1)
            def _():
                finish(kstream, ksave, kout(turn + 2))

            @pl.when(step > 0)
            def _():
                kstream.take_pair()

            query_pre = small[slot, 1]
            back = inner_right(rbuf[slot, 0], low2[:, pl.ds(0, block)])
            for b in range(1, blocks):
                back = back + inner_right(rbuf[slot, b], low2[:, pl.ds(b * block, block)])
            qpl[...] = (back * silu_slope(query_pre)).astype(bf16)
            qhid[...] = (query_pre * jax.nn.sigmoid(query_pre)).astype(bf16)
            qstream.part[...] = inner_right(qpl[...], low1[...]).astype(bf16).reshape(2, chips, rows, width)
            qstream.start_pair()
            lookup.take_pair()
            lookup.start_sends()
            qstream.take_pair()
            for b in range(blocks):
                w1[pl.ds(b * block, block), :] = inner_left(qbuf[slot, b], qpl[...])
                w2[:, pl.ds(b * block, block)] = inner_left(qhid[...], rbuf[slot, b])

            def sums(first_a, first_b, second_a, second_b, row):
                sums1_ref[turn, pl.ds(row, 1), :] = jnp.sum(first_a * first_b, axis=0, keepdims=True)
                sums2_ref[turn, pl.ds(row, 1), :] = jnp.sum(second_a * second_b, axis=0, keepdims=True)

            sums(cf[...], s1[slot], cs[...], s2[slot], 0)
            sums(cmf[...] + cf[...], m1[slot], cms[...] + cs[...], m2[slot], 1)
            sums(cmf[...] + cf[...], g1[slot], cms[...] + cs[...], g2[slot], 2)
            total = lookup.total()
            mine = (total / span).astype(bf16)
            spread.whole[lane.colour, lane.chip] = mine

            @pl.when(step > 0)
            def _():
                vout(turn + 1).wait()
                qout(turn + 1).wait()

            @pl.when(step > 1)
            def _():
                kout(turn + 2).wait()

            vsave[...] = mine
            vout(turn).start()
            spread.run()
            lookup.wait_sends()
            qstream.start_sends()

            @pl.when(step > 0)
            def _():
                kstream.start_sends()

            out = spread.whole[...].reshape(span, width)
            err = errs[slot].reshape(span, width)
            hidden_back = inner_right(err, c2[...]) + inner_right(out, low2[...])
            key_pre = small[slot, 0]
            hidden_grad = small[slot, 2]
            slope = silu_slope(key_pre)
            kpl = (hidden_back * slope + sg[...] * hidden_grad * silu_curve(key_pre)).astype(bf16)
            slope_low = (hidden_grad * slope).astype(bf16)
            kstream.part[...] = (
                (inner_right(kpl, low1[...]) + inner_right(slope_low, c1[...]))
                .astype(bf16)
                .reshape(2, chips, rows, width)
            )
            kstream.start_pair()
            for b in range(blocks):
                w1[pl.ds(b * block, block), :] += inner_left(kbuf[slot, b], kpl)
            w2[...] += inner_left(dh[...], err) + inner_left(khid[...], out)
            for c, m, w, acc in ((cf, cmf, w1, a1), (cs, cms, w2, a2)):
                both = m[...] + c[...]
                grad = (1.0 - decay) * c[...] + w[...]
                acc[...] += reset * grad
                c[...] = (1.0 - reset) * grad
                m[...] = (1.0 - reset) * (moment * both)
            return carry

        lax.fori_loop(0, turns, body, 0)
        finish(qstream, qsave, qout(0))
        if turns > 1:
            finish(kstream, ksave, kout(1))
            kout(1).wait()
        kstream.take_pair()
        tail = Scatter(
            lane,
            kstream.part,
            kstream.pair,
            kstream.half,
            lookup.got,
            (kstream.pair_send, kstream.pair_recv, lookup.send, lookup.recv),
        )
        tail.start_sends()
        finish(tail, ksave, kout(0))
        ends = [
            pltpu.make_async_copy(a1, mg1_hbm, end_sem.at[0]),
            pltpu.make_async_copy(a2, mg2_hbm, end_sem.at[1]),
        ]
        for copy in ends:
            copy.start()
        for copy in ends + [qout(0), kout(0), vout(0)]:
            copy.wait()

    state = [(width, hidden), (hidden, width)]
    buffers = (
        [((blocks, span, block), bf16)] * 3
        + [(s, f32) for s in state * 3]
        + [((2, chips, rows, width), bf16), ((3, span, hidden), f32)]
    )
    out_shape = (
        [jax.ShapeDtypeStruct((turns, rows, width), bf16)] * 3
        + [jax.ShapeDtypeStruct((turns, 8, hidden), f32), jax.ShapeDtypeStruct((turns, 8, width), f32)]
        + [jax.ShapeDtypeStruct(s, f32) for s in state]
    )
    scratch = (
        [pltpu.VMEM((2,) + s, t) for s, t in buffers]
        + [pltpu.VMEM(s, f32) for s in state * 4]
        + [pltpu.VMEM(s, bf16) for s in state * 2]
        + [pltpu.VMEM((span, hidden), bf16)] * 4
        + [pltpu.VMEM((span, hidden), f32)]
        + [pltpu.VMEM((rows, width), bf16)] * 3
        + [
            pltpu.SemaphoreType.DMA((2, 11)),
            pltpu.SemaphoreType.DMA((3,)),
            pltpu.SemaphoreType.DMA((2,)),
        ]
        + Scatter.scratch(chips, rows, width) * 3
        + Spread.scratch(chips, rows, width)
    )
    vmem = pl.BlockSpec(memory_space=pltpu.VMEM)
    return pl.pallas_call(
        kernel,
        out_shape=out_shape,
        in_specs=[ANY] * 11 + [pl.BlockSpec(memory_space=pltpu.SMEM)],
        out_specs=[ANY] * 3 + [vmem] * 2 + [ANY] * 2,
        scratch_shapes=scratch,
        compiler_params=pltpu.CompilerParams(
            collective_id=ident, has_side_effects=True, vmem_limit_bytes=62 * 1024 * 1024
        ),
        cost_estimate=pl.CostEstimate(
            flops=turns * 14 * 2 * span * width * hidden, bytes_accessed=turns * 16 * 2**20, transcendentals=0
        ),
        name="chain_backward",
    )(keys, queries, recall_grads, s1_all, s2_all, m1_all, m2_all, g1_all, g2_all, err_all, small_all, gates)


def from_behind(value, axis, steps):
    count = lax.axis_size(axis)
    first, last = (max(0, -steps), min(count, count - steps))
    return lax.ppermute(value, axis, [(source, source + steps) for source in range(first, last)])


def split_heads(values, head_size):
    return values.reshape(values.shape[:-1] + (values.shape[-1] // head_size, head_size))


def head_norm(values, head_size):
    shaped = split_heads(values, head_size)
    factor = lax.rsqrt(jnp.sum(shaped * shaped, axis=-1, keepdims=True) + eps_head)
    return (shaped * factor).reshape(values.shape)


def head_norm_back(values, upstream, head_size):
    shaped = split_heads(values, head_size)
    grad_shaped = split_heads(upstream, head_size)
    factor = lax.rsqrt(jnp.sum(shaped * shaped, axis=-1, keepdims=True) + eps_head)
    normed = shaped * factor
    inner_sum = jnp.sum(normed * grad_shaped, axis=-1, keepdims=True)
    return (factor * (grad_shaped - normed * inner_sum)).reshape(values.shape)


def rms_back(scaled, factor, upstream):
    return factor * (upstream - scaled * jnp.mean(upstream * scaled, axis=-1, keepdims=True))


def body(
    tokens,
    cotangent,
    seq_spans,
    w_query,
    w_key,
    w_value,
    conv_kernel,
    persistent,
    norm_gain,
    rate_proj,
    out_gate,
    out_proj,
    memory_in,
    memory_out,
    ffn_gain,
    ffn_gate,
    ffn_up,
    ffn_down,
):
    wide, narrow = lax.axis_size("wide"), lax.axis_size("narrow")
    devices = wide * narrow
    wide_pos, narrow_pos = lax.axis_index("wide"), lax.axis_index("narrow")
    span, width = tokens.shape
    taps = conv_kernel.shape[0]
    persist_count = persistent.shape[1]
    local_width = out_gate.shape[1]
    own_rows = span // narrow
    lanes = wide // LANE_WIDE
    chips = LANE_WIDE * narrow // 2
    shards = 2 * chips
    shard_rows = span // shards
    hidden = memory_in.shape[1] // LANE_WIDE
    score_scale = math.sqrt(HEAD)

    def shard_of(tw, tn):
        return lax.rem(tn, 2) * chips + lax.rem(tw, LANE_WIDE) * (narrow // 2) + lax.div(tn, 2)

    long_turns = min(6, wide * 5 // 8)
    turns = max(long_turns, wide - long_turns)
    seq_ends = jnp.cumsum(seq_spans)
    seq_starts = seq_ends - seq_spans
    long_start = seq_starts[jnp.argmax(seq_spans)]
    order = jnp.arange(wide, dtype=jnp.int32)
    span_first = jnp.any(seq_starts[None, :] == order[:, None], axis=1)
    is_first = span_first[wide_pos]
    in_long = (order >= long_start) & (order < long_start + long_turns)
    lane_of = jnp.where(in_long, 0, 1)
    turn_of = jnp.where(in_long, order - long_start, jnp.where(order < long_start, order, order - long_turns))
    lane_pos = wide_pos // LANE_WIDE
    turn_order = jnp.arange(turns, dtype=jnp.int32)
    rest_order = jnp.where(turn_order < long_start, turn_order, turn_order + long_turns)
    lane_spans = jnp.clip(jnp.where(lane_pos == 0, long_start + turn_order, rest_order), 0, wide - 1)
    lane_count = jnp.where(lane_pos == 0, long_turns, jnp.where(lane_pos == 1, wide - long_turns, 0))
    lane_valid = turn_order < lane_count
    lane_first = span_first[lane_spans] | ~lane_valid

    ffn_gate_cols = lax.all_gather(ffn_gate, "wide", axis=0, tiled=True)
    ffn_up_cols = lax.all_gather(ffn_up, "wide", axis=0, tiled=True)
    ffn_down_rows = lax.all_gather(ffn_down, "wide", axis=1, tiled=True)
    smalls = [conv_kernel, persistent, norm_gain, ffn_gain, rate_proj]
    small_sizes = [a.size for a in smalls]
    packed = jnp.concatenate([a.reshape(-1) for a in smalls])
    padded = -(-packed.size // 2048) * 2048
    packed = jnp.pad(packed, (0, padded - packed.size)).reshape(-1, 128)

    def by_narrow(a):
        return a.reshape(a.shape[0], narrow, local_width).transpose(1, 0, 2)

    small_all, wq, wk, wv = exchange(
        [(packed, None)] + [(by_narrow(a), lambda tw, tn: tn) for a in (w_query, w_key, w_value)], "all", 1
    )
    memory_cols = memory_in.reshape(memory_in.shape[0], LANE_WIDE, hidden).transpose(1, 0, 2)
    memory_rows = memory_out.reshape(LANE_WIDE, hidden, memory_out.shape[1])
    gate_all, proj_all, first_all, second_all = exchange(
        [
            (out_gate, None),
            (out_proj, None),
            (memory_cols, lambda tw, tn: lax.rem(tw, LANE_WIDE)),
            (memory_rows, lambda tw, tn: lax.rem(tw, LANE_WIDE)),
        ],
        "wide",
        2,
    )
    gate_cols = gate_all.reshape(width, local_width)
    proj_rows = proj_all.transpose(1, 0, 2).reshape(local_width, width)
    first_init = first_all.reshape(width, hidden)
    second_init = second_all.transpose(1, 0, 2).reshape(hidden, width)
    small_all = small_all.reshape(devices, padded)
    pieces, at = [], 0
    for a, size in zip(smalls, small_sizes):
        pieces.append(small_all[:, at : at + size].reshape((devices,) + a.shape))
        at += size
    kernel_all = pieces[0].transpose(1, 0, 2).reshape(taps, 3, width)
    persist_all = pieces[1].transpose(1, 2, 0, 3).reshape(2, persist_count, width)
    gain_one = pieces[2].reshape(width).astype(f32)
    gain_two = pieces[3].reshape(width).astype(f32)
    rate_f = pieces[4].reshape(width, 3).astype(f32)
    col_offset = narrow_pos * local_width

    def own_cols(values, axis):
        return lax.dynamic_slice_in_dim(values, col_offset, local_width, axis)

    def own_part(values):
        return lax.dynamic_slice_in_dim(values, narrow_pos * own_rows, own_rows, 0)

    kernel_f = own_cols(kernel_all, 2).reshape(taps, 3 * local_width).astype(f32)
    persist_f = own_cols(persist_all, 2).astype(f32)
    qkv_weights = jnp.concatenate([a.reshape(width, local_width) for a in (wq, wk, wv)], 1)

    inputs_f = tokens.astype(f32)
    first_factor = lax.rsqrt(jnp.mean(inputs_f * inputs_f, axis=-1, keepdims=True) + eps_norm)
    first_scaled = inputs_f * first_factor
    normed = first_scaled * gain_one
    normed_low = normed.astype(bf16)
    projected = matmul(normed_low, qkv_weights)
    tail_rows = from_behind(projected[span - taps + 1 :].astype(bf16), "wide", 1).astype(f32)
    extended = jnp.concatenate([jnp.where(is_first, 0.0, tail_rows), projected], 0)
    mixed_conv = kernel_f[0] * projected
    for offset in range(1, taps):
        start_row = taps - 1 - offset
        mixed_conv = mixed_conv + kernel_f[offset] * extended[start_row : start_row + span]
    activated = jax.nn.silu(mixed_conv)
    query_act = activated[:, :local_width]
    key_act = activated[:, local_width : 2 * local_width]
    query_low = head_norm(query_act, HEAD).astype(bf16)
    key_low = head_norm(key_act, HEAD).astype(bf16)
    value_low = activated[:, 2 * local_width :].astype(bf16)
    span_mean = jnp.mean(normed, axis=0)
    gate_scale = jnp.array([decay_top, moment_top, learn_top], f32)
    gate_sig = jax.nn.sigmoid(jnp.sum(span_mean[:, None] * rate_f, axis=0))
    gate_tile = jnp.broadcast_to(jnp.pad(gate_sig * gate_scale, (0, 125))[None], (8, 128))

    key_all, query_all = gather_all([key_low, query_low], 3)
    value_all, gate_got = exchange(
        [(value_low.reshape(shards, shard_rows, local_width), shard_of), (gate_tile, None)], "all", 4
    )
    value_all = value_all.reshape(wide, narrow, shard_rows, local_width).transpose(0, 2, 1, 3)
    value_all = value_all.reshape(wide, shard_rows, width)
    gate_rows = gate_got[::narrow, 0, :3]
    lane_gates = gate_rows[lane_spans]
    first_f = lane_first.astype(f32)
    next_first = jnp.concatenate([first_f[1:], jnp.ones((1,), f32)])
    keys_lane = key_all[lane_spans]
    queries_lane = query_all[lane_spans]
    chain = chain_forward(
        keys_lane,
        queries_lane,
        value_all[lane_spans],
        jnp.concatenate([lane_gates, next_first[:, None]], 1),
        first_init,
        second_init,
        5,
    )
    recalled_lane, saved = chain[0], chain[1:]

    def by_span(lane_rows):
        spans = lane_rows[turn_of]
        return spans.reshape(wide, shard_rows, narrow, local_width).transpose(0, 2, 1, 3)

    def from_lane(got):
        got = got.reshape(lanes, LANE_WIDE, narrow // 2, 2, shard_rows, local_width)
        own = lax.dynamic_index_in_dim(got, lane_of[wide_pos], 0, keepdims=False)
        return own.transpose(2, 0, 1, 3, 4).reshape(span, local_width)

    recalled_got = exchange(
        [
            (
                by_span(recalled_lane).reshape(devices, shard_rows, local_width),
                lambda tw, tn: tw * narrow + tn,
            )
        ],
        "all",
        6,
    )[0]
    recall_low = from_lane(recalled_got)
    recall_own = recall_low.astype(f32)

    keys_all = jnp.concatenate(
        [head_norm(persist_f[0], HEAD).astype(bf16), head_norm(recall_own, HEAD).astype(bf16), key_low], 0
    )
    values_all = jnp.concatenate([persist_f[1].astype(bf16), recall_low, value_low], 0)
    query_heads = split_heads(query_low, HEAD)
    key_heads = split_heads(keys_all, HEAD)
    value_heads = split_heads(values_all, HEAD)
    key_total = keys_all.shape[0]
    row_index = lax.broadcasted_iota(jnp.int32, (span, key_total), 0)
    col_index = lax.broadcasted_iota(jnp.int32, (span, key_total), 1)
    allowed = (col_index < persist_count + span) | (col_index - persist_count - span <= row_index)

    def score_block():
        raw_scores = (
            jnp.einsum("thd,jhd->htj", query_heads, key_heads, preferred_element_type=f32) * score_scale
        )
        return jnp.where(allowed[None], raw_scores, masked_score)

    scores = score_block()
    row_top = jnp.max(scores, axis=-1, keepdims=True)
    exponent = jnp.exp(scores - row_top)
    total_sum = jnp.sum(exponent, axis=-1, keepdims=True)
    log_total = row_top + jnp.log(total_sum)
    weights_low = (exponent / total_sum).astype(bf16)
    attended = jnp.einsum("htj,jhd->thd", weights_low, value_heads, preferred_element_type=f32).reshape(
        span, local_width
    )
    gate_pre = matmul(normed_low, gate_cols)
    gate_sigmoid = jax.nn.sigmoid(gate_pre)
    gated_low = (attended * gate_sigmoid).astype(bf16)

    def rows_of(parts, ident):
        got = exchange(
            [(a.astype(bf16).reshape(narrow, own_rows, width), lambda tw, tn: tn) for a in parts], "narrow", ident
        )
        return [jnp.sum(a.astype(f32), axis=0) for a in got]

    def all_rows(parts, ident):
        got = exchange([(a, None) for a in parts], "narrow", ident)
        return [a.reshape(span, width) for a in got]

    inputs_own = own_part(inputs_f)
    middle = inputs_own + rows_of([matmul(gated_low, proj_rows)], 7)[0]
    second_factor = lax.rsqrt(jnp.mean(middle * middle, axis=-1, keepdims=True) + eps_norm)
    second_scaled = middle * second_factor
    normed_two = all_rows([(second_scaled * gain_two).astype(bf16)], 8)[0]
    gate_val = matmul(normed_two, ffn_gate_cols)
    up_val = matmul(normed_two, ffn_up_cols)
    gate_silu = jax.nn.silu(gate_val)
    hidden_ffn = (gate_silu * up_val).astype(bf16)
    ffn_part = matmul(hidden_ffn, ffn_down_rows)
    down_grad = inner_left(cotangent, hidden_ffn)
    hidden_grad_ffn = inner_right(cotangent, ffn_down_rows)
    gate_sig_ffn = jax.nn.sigmoid(gate_val)
    gate_grad_low = (
        hidden_grad_ffn * up_val * gate_sig_ffn * (1.0 + gate_val * (1.0 - gate_sig_ffn))
    ).astype(bf16)
    up_grad_low = (hidden_grad_ffn * gate_silu).astype(bf16)
    ffn_gate_grad = inner_left(normed_two, gate_grad_low)
    ffn_up_grad = inner_left(normed_two, up_grad_low)
    normed_two_part = inner_right(gate_grad_low, ffn_gate_cols) + inner_right(up_grad_low, ffn_up_cols)

    def scatter_wide(grad):
        return lax.psum_scatter(grad.astype(bf16), "wide", scatter_dimension=0, tiled=True).astype(f32)

    ffn_gate_out, ffn_up_out, ffn_down_out = [scatter_wide(a) for a in (ffn_gate_grad, ffn_up_grad, down_grad)]
    ffn_rows, normed_two_grad = rows_of([ffn_part, normed_two_part], 9)
    output_own = (middle + ffn_rows).astype(bf16)
    gain_two_part = jnp.sum(normed_two_grad * second_scaled, axis=0)
    upstream = own_part(cotangent).astype(f32)
    middle_grad = upstream + rms_back(second_scaled, second_factor, normed_two_grad * gain_two)
    branch_low, output = all_rows([middle_grad.astype(bf16), output_own], 10)

    gated_grad = inner_right(branch_low, proj_rows)
    attended_grad_low = (gated_grad * gate_sigmoid).astype(bf16)
    gate_pre_low = (gated_grad * attended * gate_sigmoid * (1.0 - gate_sigmoid)).astype(bf16)
    proj_grad = inner_left(branch_low, gated_low)

    weights_again = jnp.exp(score_block() - log_total)
    grad_heads = split_heads(attended_grad_low, HEAD)
    weight_grad = jnp.einsum("thd,jhd->htj", grad_heads, value_heads, preferred_element_type=f32)
    row_delta = jnp.sum(weights_again * weight_grad, axis=-1, keepdims=True)
    score_grad_low = (weights_again * (weight_grad - row_delta)).astype(bf16)
    query_att = (
        score_scale * jnp.einsum("htj,jhd->thd", score_grad_low, key_heads, preferred_element_type=f32)
    ).reshape(span, local_width)
    keys_grad = (
        score_scale * jnp.einsum("htj,thd->jhd", score_grad_low, query_heads, preferred_element_type=f32)
    ).reshape(key_total, local_width)
    values_grad = jnp.einsum(
        "htj,thd->jhd", weights_again.astype(bf16), grad_heads, preferred_element_type=f32
    ).reshape(key_total, local_width)
    recall_end = persist_count + span
    persist_part = jnp.stack(
        [head_norm_back(persist_f[0], keys_grad[:persist_count], HEAD), values_grad[:persist_count]]
    )
    recall_grad_low = (
        head_norm_back(recall_own, keys_grad[persist_count:recall_end], HEAD)
        + values_grad[persist_count:recall_end]
    ).astype(bf16)

    recall_all = gather_all([recall_grad_low], 11)[0]
    recall_lane = jnp.where(lane_valid[:, None, None, None], recall_all[lane_spans], jnp.zeros((), bf16))
    qcot, kcot, vcot, sums1, sums2, first_grad, second_grad = chain_backward(
        keys_lane,
        queries_lane,
        recall_lane,
        saved,
        jnp.concatenate([lane_gates, first_f[:, None]], 1),
        12,
    )
    lane_sums = jnp.sum(sums1[:, :3], axis=2) + jnp.sum(sums2[:, :3], axis=2)
    span_sums = jnp.where((lane_of == lane_pos)[:, None], lane_sums[turn_of], 0.0)
    sums_tile = jnp.pad(span_sums, ((0, 0), (0, 125)))
    cots = jnp.stack([by_span(a) for a in (qcot, kcot, vcot)], 2)
    cots_got, sums_got = exchange(
        [
            (cots.reshape(devices, 3, shard_rows, local_width), lambda tw, tn: tw * narrow + tn),
            (sums_tile, None),
        ],
        "all",
        13,
    )
    query_mem, key_mem, value_mem = [from_lane(cots_got[:, i]).astype(f32) for i in range(3)]
    gate_sums = jnp.sum(sums_got[:, :, :3], axis=0)[wide_pos] * jnp.array([-1.0, 1.0, -1.0], f32)
    first_got, second_got = exchange(
        [
            (first_grad.astype(bf16).reshape(wide, width // wide, hidden), lambda tw, tn: tw),
            (
                second_grad.astype(bf16).reshape(hidden, wide, width // wide).transpose(1, 0, 2),
                lambda tw, tn: tw,
            ),
        ],
        "wide",
        14,
    )

    def over_lanes(got):
        return jnp.sum(got.reshape((lanes, LANE_WIDE) + got.shape[1:]).astype(f32), axis=0)

    first_out = over_lanes(first_got).transpose(1, 0, 2).reshape(width // wide, LANE_WIDE * hidden)
    second_out = over_lanes(second_got).reshape(LANE_WIDE * hidden, width // wide)

    logit_grad = gate_sums * gate_scale * gate_sig * (1.0 - gate_sig)
    rate_part = span_mean[:, None] * logit_grad[None, :]
    gate_row = jnp.sum(rate_f * logit_grad[None, :], axis=1)[None, :] / span
    act_grad = jnp.concatenate(
        [
            head_norm_back(query_act, query_mem + query_att, HEAD),
            head_norm_back(key_act, key_mem + keys_grad[recall_end:], HEAD),
            values_grad[recall_end:] - value_mem,
        ],
        1,
    )
    conv_grad = act_grad * silu_slope(mixed_conv)
    kernel_rows = []
    extended_grad = jnp.zeros_like(extended)
    for offset in range(taps):
        start_row = taps - 1 - offset
        kernel_rows.append(jnp.sum(conv_grad * extended[start_row : start_row + span], axis=0))
        extended_grad = extended_grad + jnp.pad(kernel_f[offset] * conv_grad, ((start_row, offset), (0, 0)))
    tail_back = from_behind(
        jnp.where(is_first, 0.0, extended_grad[: taps - 1]).astype(bf16), "wide", -1
    ).astype(f32)
    projected_grad = extended_grad[taps - 1 :] + jnp.pad(tail_back, ((span - taps + 1, 0), (0, 0)))
    projected_low = projected_grad.astype(bf16)
    normed_part = inner_right(projected_low, qkv_weights) + inner_right(gate_pre_low, gate_cols)
    normed_grad = rows_of([normed_part], 15)[0] + gate_row
    scaled_own = own_part(first_scaled)
    gain_one_part = jnp.sum(normed_grad * scaled_own, axis=0)
    tokens_own = middle_grad + rms_back(scaled_own, own_part(first_factor), normed_grad * gain_one)
    tokens_grad = all_rows([tokens_own.astype(bf16)], 16)[0].astype(f32)
    weight_grads = inner_left(normed_low, jnp.concatenate([projected_low, gate_pre_low], 1))
    weight_out = scatter_wide(weight_grads)
    proj_out = scatter_wide(proj_grad)

    def place_cols(piece, axis):
        full = piece.shape[:axis] + (width,) + piece.shape[axis + 1 :]
        return lax.dynamic_update_slice_in_dim(jnp.zeros(full, f32), piece, col_offset, axis)

    kernel_full = place_cols(jnp.stack(kernel_rows).reshape(taps, 3, local_width), 2).reshape(taps, 3 * width)
    persist_full = place_cols(persist_part, 2)
    rate_part = jnp.where(narrow_pos == 0, rate_part, 0.0)
    chunks = [
        kernel_full.reshape(taps, devices, -1).transpose(1, 0, 2),
        persist_full.reshape(2, persist_count, devices, -1).transpose(2, 0, 1, 3),
        gain_one_part.reshape(devices, -1),
        gain_two_part.reshape(devices, -1),
        rate_part.reshape(devices, -1, 3),
    ]
    flat = jnp.concatenate([a.reshape(devices, -1) for a in chunks], 1)
    flat_size = -(-flat.shape[1] // 1024) * 1024
    flat = jnp.pad(flat, ((0, 0), (0, flat_size - flat.shape[1]))).reshape(devices, -1, 128)
    flat_got = exchange([(flat, lambda tw, tn: tw * narrow + tn)], "all", 17)[0]
    flat_sum = jnp.sum(flat_got, axis=0).reshape(-1)
    small_outs, at = [], 0
    for a in chunks:
        size = a.size // devices
        small_outs.append(flat_sum[at : at + size].reshape(a.shape[1:]))
        at += size
    kernel_grad, persist_grad, norm_grad, ffn_gain_grad, rate_grad = small_outs
    return (
        output,
        tokens_grad,
        weight_out[:, :local_width],
        weight_out[:, local_width : 2 * local_width],
        weight_out[:, 2 * local_width : 3 * local_width],
        kernel_grad,
        persist_grad,
        norm_grad,
        rate_grad,
        weight_out[:, 3 * local_width :],
        proj_out.T,
        first_out,
        second_out,
        ffn_gain_grad,
        ffn_gate_out,
        ffn_up_out,
        ffn_down_out.T,
    )


def solution(mesh):
    rows, both, square, turned = P("wide", None), P(("wide", "narrow"), None), P("wide", "narrow"), P("narrow", "wide")
    flat, taps, heads = P(("wide", "narrow")), P(None, ("wide", "narrow")), P(None, None, ("wide", "narrow"))
    return jax.shard_map(
        body,
        mesh=mesh,
        in_specs=(rows, rows, P(), both, both, both, taps, heads, flat, both)
        + (square, turned, square, turned, flat, square, square, turned),
        out_specs=(rows, rows, square, square, square, taps, heads, flat, both)
        + (square, turned, square, turned, flat, square, square, turned),
        check_vma=False,
    )
```

time: 3560 us -> 1170 us (0.33)
  waiting for transfers between devices: 2360 us -> 3.43 us
  Pallas kernels: 0 us -> 881 us
  blocking collectives: 403 us -> 0 us
  matrix products: 376 us -> 70.4 us
  other arithmetic: 179 us -> 73.4 us
  starting transfers between devices: 100 us -> 5.55 us
    pallas_call x0 -> x17, Pallas kernels: none -> 881 us  [the longest x13 355 us: exchange(): pl.pallas_call(kernel, out_shape=[jax.ShapeDtypeStruct((peers,) + tuple(c...]
    ppermute x33 -> x2, waiting for transfers between devices: 836 us -> 0.01 us  [from_behind(): lax.ppermute(value, axis, [(source, source + steps) for source in range(f...]
    unnamed x40 -> x9, waiting for transfers between devices: 546 us -> 1.48 us
    reduce_scatter x7 -> x4, waiting for transfers between devices: 403 us -> 1.92 us  [scatter_wide(): lax.psum_scatter(grad.astype(bf16), 'wide', scatter_dimension=0, tiled=True)]
    psum x13 -> x0, waiting for transfers between devices: 332 us -> none  [the longest x5 154 us: body(): lax.psum(stacked.astype(jnp.bfloat16), 'narrow').astype(jnp.float32)]
    all_gather x5 -> x0, blocking collectives: 321 us -> none  [the longest x1 114 us: body(): lax.all_gather(persistent, ('wide', 'narrow'), axis=2, tiled=True)]
    all_gather x8 -> x3, waiting for transfers between devices: 241 us -> 0.02 us  [the longest x1 0.02 us: body(): ffn_gate_cols = lax.all_gather(ffn_gate, 'wide', axis=0, tiled=True)]
    dot_general x35 -> x5, matrix products: 193 us -> 16.4 us  [inner_left(): lax.dot_general(left_side, right_side, (((0,), (0,)), ((), ())), preferre...]
  transfers between devices with their start and end apart: 67 -> 10, of which waited for: 50 -> 1; matrix products, arithmetic and copies ran while one was open for 13% -> 19% of each run, Pallas kernels for 0% -> 72%
where the time goes in v1:
time: 1170 us; the launch traced here: 1160 us
  Pallas kernels  881 us (75%)
  local copies, waits for them, and re-layouts  101 us (9%)
  other arithmetic  73.4 us (6%)
  matrix products  70.4 us (6%)
  between operations  21.1 us (2%)
    pallas_call x13, Pallas kernels, exchange(): pl.pallas_call(kernel, out_shape=[jax.ShapeDtypeStruct((peers,) + tuple(c...  355 us
    pallas_call x1, Pallas kernels, chain_backward(): pl.pallas_call(kernel, out_shape=out_shape, in_specs=[ANY] * 11 + [pl.Blo...  201 us
    pallas_call x2, Pallas kernels, gather_all(): pl.pallas_call(kernel, out_shape=[jax.ShapeDtypeStruct((wide, narrow) + a...  179 us
    pallas_call x1, Pallas kernels, chain_forward(): pl.pallas_call(kernel, out_shape=out_shape, in_specs=[ANY] * 3 + [pl.Bloc...  146 us
  transfers between devices with their start and end apart: 10, of which 1 were waited for; matrix products, arithmetic and copies ran while one was open for 19% of the time, Pallas kernels for 72%

profile of v1, /device:TPU:0, one launch (start us, length us, event | category | flops | bytes accessed | tf_op | source)
XLA Modules:
  0.0 1156.7 jit_solution(16953896154810321272)
XLA Ops:
  16.2 42.4 %exchange_1.1 = (bf16[32,16,128]{2,1,0:T(8,128)(2,1)}, bf16[32,32,256]{2,1,0:T(8,128)(2,1)}, bf16[32,32,256]{2,1,0:T(8,128)(2,1)}, bf16[32,32,256]{2,1,0:T(8,128)(2,1)}) custom-call(bf16[16,128]{1,0:T(8,128)(2,1)} %pad_bitcast_fusion.1.refs_0_, bf16[4,32,256]{2,1,0:T(8,128)(2,1)} %bitcast.301, bf16[4,32,256]{2,1,0:T(8,128)(2,1)} %get-tuple-element.257.refs_2_, ...), custom_call_target="tpu_custom_call" | custom-call | tf_op jit(solution)/shard_map/exchange_1/pallas_call | solution.py:87
  63.6 3.8 collective-permute-start
  79.2 60.4 %exchange_2.1 = (bf16[8,128,256]{2,1,0:T(8,128)(2,1)}, bf16[8,256,128]{2,1,0:T(8,128)(2,1)}, bf16[8,128,256]{2,1,0:T(8,128)(2,1)}, bf16[8,256,128]{2,1,0:T(8,128)(2,1)}) custom-call(bf16[128,256]{1,0:T(8,128)(2,1)} %refs_0_.1, bf16[256,128]{1,0:T(8,128)(2,1)} %refs_1_.1, bf16[4,128,256]{2,1,0:T(8,128)(2,1)} %bitcast.278, bf16[4,256,128]{2,1,0:T(8,128)(2,1)} %bitcast.302), custom_call_target="tpu_custom_call" | custom-call | tf_op jit(solution)/shard_map/exchange_2/pallas_call | solution.py:87
  152.5 5.3 fusion.19
  171.0 122.5 %gather_3.1 = (bf16[8,4,512,256]{3,2,1,0:T(8,128)(2,1)}, bf16[8,4,512,256]{3,2,1,0:T(8,128)(2,1)}) custom-call(bf16[512,256]{1,0:T(8,128)(2,1)} %copy-done.24, bf16[512,256]{1,0:T(8,128)(2,1)} %get-tuple-element.220.refs_1_), custom_call_target="tpu_custom_call" | custom-call | tf_op jit(solution)/shard_map/gather_3/pallas_call | solution.py:241
  294.6 7.3 gather_fusion.1
  301.9 7.1 gather_fusion
  310.5 23.5 %exchange_4.1 = (bf16[32,32,256]{2,1,0:T(8,128)(2,1)}, f32[32,8,128]{2,1,0:T(8,128)}) custom-call(bf16[16,32,256]{2,1,0:T(8,128)(2,1)} %bitcast.243, f32[8,128]{1,0:T(8,128)} %broadcast_in_dim.62.refs_1_), custom_call_target="tpu_custom_call" | custom-call | tf_op jit(solution)/shard_map/exchange_4/pallas_call | solution.py:87
  339.1 145.6 %chain_forward.1 = (bf16[5,32,1024]{2,1,0:T(8,128)(2,1)}, f32[5,1024,256]{2,1,0:T(8,128)}, f32[5,256,1024]{2,1,0:T(8,128)}, f32[5,1024,256]{2,1,0:T(8,128)}, f32...) custom-call(bf16[5,4,512,256]{3,2,1,0:T(8,128)(2,1)} %gather_fusion,, ...), custom_call_target="tpu_custom_call" | custom-call | flops 9395240960 | bytes 62914560 | tf_op jit(solution)/shard_map/chain_forward/pallas_call | solution.py:589
  487.2 15.1 %exchange_6.1 = bf16[32,32,256]{2,1,0:T(8,128)(2,1)} custom-call(bf16[32,32,256]{2,1,0:T(8,128)(2,1)} %bitcast.249), custom_call_target="tpu_custom_call" | custom-call | tf_op jit(solution)/shard_map/exchange_6/pallas_call | solution.py:87
  518.8 13.6 %exchange_7.1 = bf16[4,128,1024]{2,1,0:T(8,128)(2,1)} custom-call(bf16[4,128,1024]{2,1,0:T(8,128)(2,1)} %bitcast.237), custom_call_target="tpu_custom_call" | custom-call | tf_op jit(solution)/shard_map/exchange_7/pallas_call | solution.py:87
  535.9 14.0 %exchange_8.1 = bf16[4,128,1024]{2,1,0:T(8,128)(2,1)} custom-call(bf16[128,1024]{1,0:T(8,128)(2,1)} %multiply_convert_fusion.7.refs_0_), custom_call_target="tpu_custom_call" | custom-call | tf_op jit(solution)/shard_map/exchange_8/pallas_call | solution.py:87
  550.0 4.6 fusion.88
  554.6 4.2 fusion.89
  558.8 5.3 multiply_convert_fusion.1
  571.4 25.3 %exchange_9.1 = (bf16[4,128,1024]{2,1,0:T(8,128)(2,1)}, bf16[4,128,1024]{2,1,0:T(8,128)(2,1)}) custom-call(bf16[4,128,1024]{2,1,0:T(8,128)(2,1)} %bitcast.275, bf16[4,128,1024]{2,1,0:T(8,128)(2,1)} %bitcast.276), custom_call_target="tpu_custom_call" | custom-call | tf_op jit(solution)/shard_map/exchange_9/pallas_call | solution.py:87
  601.3 25.3 %exchange_10.1 = (bf16[4,128,1024]{2,1,0:T(8,128)(2,1)}, bf16[4,128,1024]{2,1,0:T(8,128)(2,1)}) custom-call(bf16[128,1024]{1,0:T(8,128)(2,1)} %get-tuple-element.229.refs_0_, bf16[128,1024]{1,0:T(8,128)(2,1)} %get-tuple-element.228.refs_1_), custom_call_target="tpu_custom_call" | custom-call | tf_op jit(solution)/shard_map/exchange_10/pallas_call | solution.py:87
  629.2 3.8 convolution_convert_fusion
  637.8 4.4 convolution_convert_fusion.1
  642.3 7.3 multiply_reduce_fusion
  649.5 8.3 multiply_convert_fusion
  660.5 5.4 fusion.11
  667.8 56.9 %gather_11.1 = bf16[8,4,512,256]{3,2,1,0:T(8,128)(2,1)} custom-call(bf16[512,256]{1,0:T(8,128)(2,1)} %copy.309.refs_0_), custom_call_target="tpu_custom_call" | custom-call | tf_op jit(solution)/shard_map/gather_11/pallas_call | solution.py:241
  724.7 7.5 gather_fusion.6
  737.6 5.4 broadcast_select_fusion.refs_2_
  742.9 201.4 %chain_backward.1 = (bf16[5,32,1024]{2,1,0:T(8,128)(2,1)}, bf16[5,32,1024]{2,1,0:T(8,128)(2,1)}, bf16[5,32,1024]{2,1,0:T(8,128)(2,1)}, f32[5,8,256]{2,1,0:T(8,12...) custom-call(bf16[5,4,512,256]{3,2,1,0:T(8,128)(2,1)} %gather_fusion, ...), custom_call_target="tpu_custom_call" | custom-call | flops 18790481920 | bytes 83886080 | tf_op jit(solution)/shard_map/chain_backward/pallas_call | solution.py:815
  951.3 53.0 %exchange_13.1 = (bf16[32,3,32,256]{3,2,1,0:T(8,128)(2,1)}, f32[32,8,128]{2,1,0:T(8,128)}) custom-call(bf16[32,3,32,256]{3,2,1,0:T(8,128)(2,1)} %pad_maximum_fusion.2.refs_0_, f32[8,128]{1,0:T(8,128)} %pad.41.refs_1_), custom_call_target="tpu_custom_call" | custom-call | tf_op jit(solution)/shard_map/exchange_13/pallas_call | solution.py:87
  1007.9 3.1 fusion.24
  1029.2 37.3 %exchange_14.1 = (bf16[8,128,256]{2,1,0:T(8,128)(2,1)}, bf16[8,256,128]{2,1,0:T(8,128)(2,1)}) custom-call(bf16[8,128,256]{2,1,0:T(8,128)(2,1)} %bitcast.244, bf16[8,256,128]{2,1,0:T(8,128)(2,1)} %bitcast.248), custom_call_target="tpu_custom_call" | custom-call | tf_op jit(solution)/shard_map/exchange_14/pallas_call | solution.py:87
  1080.0 13.8 %exchange_15.1 = bf16[4,128,1024]{2,1,0:T(8,128)(2,1)} custom-call(bf16[4,128,1024]{2,1,0:T(8,128)(2,1)} %bitcast.277), custom_call_target="tpu_custom_call" | custom-call | tf_op jit(solution)/shard_map/exchange_15/pallas_call | solution.py:87
  1097.5 17.1 %exchange_17.1 = f32[32,16,128]{2,1,0:T(8,128)} custom-call(f32[32,16,128]{2,1,0:T(8,128)} %bitcast.279), custom_call_target="tpu_custom_call" | custom-call | tf_op jit(solution)/shard_map/exchange_17/pallas_call | solution.py:87
  1119.9 14.3 %exchange_16.1 = bf16[4,128,1024]{2,1,0:T(8,128)(2,1)} custom-call(bf16[128,1024]{1,0:T(8,128)(2,1)} %add_convert_fusion.2.refs_0_), custom_call_target="tpu_custom_call" | custom-call | tf_op jit(solution)/shard_map/exchange_16/pallas_call | solution.py:87
  (465 shorter events, 171.3 us)
Async XLA Ops:
  7.2 52.5 %copy-start.2 = (bf16[512,1024]{1,0:T(8,128)(2,1)S(1)}, bf16[512,1024]{1,0:T(8,128)(2,1)}, u32[]{:S(2)}) copy-start(bf16[512,1024]{1,0:T(8,128)(2,1)} %param.20) | copy-start | bytes 3145732
  7.2 542.7 %all-gather.4.cloned.1.call-start = ((), (), s32[]{:S(2)}) async-start(), calls=%async_computation.5 | async-start | bytes 2359296 | tf_op jit(solution)/shard_map/all_gather | solution.py:917
  7.9 546.6 %all-gather.6.cloned.1.call-start = ((), (), s32[]{:S(2)}) async-start(), calls=%async_computation.6 | async-start | bytes 2359296 | tf_op jit(solution)/shard_map/all_gather | solution.py:918
  8.7 550.1 %all-gather.8.cloned.1.call-start = ((), (), s32[]{:S(2)}) async-start(), calls=%async_computation.7 | async-start | bytes 2359296 | tf_op jit(solution)/shard_map/all_gather | solution.py:919
  60.0 9.5 copy-start.81
  63.6 88.2 %collective-permute-start = (bf16[3,768]{1,0:T(4,128)(2,1)S(1)}, bf16[3,768]{1,0:T(4,128)(2,1)S(1)}, u32[]{:S(2)}, u32[]{:S(2)}) collective-permute-start(bf16[3,768]{1,0:T(4,128)(2,1)S(1)} %slice.333), channel_id=1, source_target_pairs={{0,4},{4,8},{8,12},{12,16},{16,20},{20,24},{24,28},{1,5},{5,9},{9,... | collective-permute-start | bytes 13832 | tf_op jit(solution)/shard_map/ppermute | solution.py:834
  67.4 1070.2 %reduce-scatter.10.cloned.1.call-start = ((), (), s32[]{:S(2)}) async-start(), calls=%async_computation.9 | async-start | bytes 589824 | tf_op jit(solution)/shard_map/reduce_scatter | solution.py:1101
  69.5 8.7 copy-start.48
  76.2 260.9 %copy-start.75 = (s32[1024]{0:T(1024)}, s32[1024]{0:T(1024)S(1)}, u32[]{:S(2)}) copy-start(s32[1024]{0:T(1024)S(1)} %pad_clamp_fusion.1) | copy-start | bytes 12292
  77.6 65.8 %copy-start.58 = (f32[1024]{0:T(1024)}, f32[1024]{0:T(1024)S(1)}, u32[]{:S(2)}) copy-start(f32[1024]{0:T(1024)S(1)} %broadcast_multiply_fusion.6) | copy-start | bytes 12292
  78.2 65.2 %copy-start.13 = (f32[1024,3]{1,0:T(8,128)}, f32[1024,3]{1,0:T(8,128)S(1)}, u32[]{:S(2)}) copy-start(f32[1024,3]{1,0:T(8,128)S(1)} %reshape.661) | copy-start | bytes 36868
  78.3 65.2 %copy-start.91 = (f32[3]{0:T(128)S(1)}, f32[3]{0:T(128)}, u32[]{:S(2)}) copy-start(f32[3]{0:T(128)} %constant.128.clone) | copy-start | bytes 40
  141.5 343.2 %copy-start.76 = (s32[1024]{0:T(1024)}, s32[1024]{0:T(1024)S(1)}, u32[]{:S(2)}) copy-start(s32[1024]{0:T(1024)S(1)} %pad_clamp_fusion) | copy-start | bytes 12292
  294.5 213.1 %copy-start.23 = (bf16[512,256]{0,1:T(8,128)(2,1)}, bf16[512,256]{0,1:T(8,128)(2,1)S(1)}, u32[]{:S(2)}) copy-start(bf16[512,256]{0,1:T(8,128)(2,1)S(1)} %copy.301) | copy-start | bytes 786436
  487.2 17.5 %copy-start.49 = (bf16[1,16,256]{1,2,0:T(8,128)(2,1)S(1)}, bf16[1,16,256]{1,2,0:T(8,128)(2,1)}, u32[]{:S(2)}) copy-start(bf16[1,16,256]{1,2,0:T(8,128)(2,1)} %get-tuple-element.231) | copy-start | bytes 24580
  535.1 64.2 %copy-start.79 = (f32[128]{0:T(128)}, f32[128]{0:T(128)S(1)}, u32[]{:S(2)}) copy-start(f32[128]{0:T(128)S(1)} %add_rsqrt_fusion.5) | copy-start | bytes 1540
  599.1 27.5 %copy-start.84 = (f32[128]{0:T(128)}, f32[128]{0:T(128)S(1)}, u32[]{:S(2)}) copy-start(f32[128]{0:T(128)S(1)} %broadcast_multiply_fusion.8) | copy-start | bytes 1540
  599.1 27.5 %copy-start.46 = (bf16[512,256]{1,0:T(8,128)(2,1)S(1)}, bf16[512,256]{1,0:T(8,128)(2,1)}, u32[]{:S(2)}) copy-start(bf16[512,256]{1,0:T(8,128)(2,1)} %copy-done.45) | copy-start | bytes 786436
  601.2 27.9 %copy-start.31 = (bf16[4,128,1024]{2,1,0:T(8,128)(2,1)S(1)}, bf16[4,128,1024]{2,1,0:T(8,128)(2,1)}, u32[]{:S(2)}) copy-start(bf16[4,128,1024]{2,1,0:T(8,128)(2,1)} %exchange_8.1) | copy-start | bytes 3145732
  629.1 510.1 %reduce-scatter.14.cloned.1.call-start = ((), (), s32[]{:S(2)}) async-start(), calls=%async_computation.11 | async-start | bytes 2359296 | tf_op jit(solution)/shard_map/reduce_scatter | solution.py:1101
  633.1 507.9 %reduce-scatter.12.cloned.1.call-start = ((), (), s32[]{:S(2)}) async-start(), calls=%async_computation.10 | async-start | bytes 2359296 | tf_op jit(solution)/shard_map/reduce_scatter | solution.py:1101
  642.2 500.6 %reduce-scatter.16.cloned.1.call-start = ((), (), s32[]{:S(2)}) async-start(), calls=%async_computation.12 | async-start | bytes 2359296
  945.5 201.2 %reduce-scatter.8.cloned.1.call-start = ((), (), s32[]{:S(2)}) async-start(), calls=%async_computation.8 | async-start | bytes 2359296 | tf_op jit(solution)/shard_map/reduce_scatter | solution.py:1101
  1024.0 42.6 %collective-permute-start.1 = (bf16[3,768]{1,0:T(4,128)(2,1)S(1)}, bf16[3,768]{1,0:T(4,128)(2,1)S(1)}, u32[]{:S(2)}, u32[]{:S(2)}) collective-permute-start(bf16[3,768]{1,0:T(4,128)(2,1)S(1)} %fusion.63), channel_id=1, source_target_pairs={{4,0},{8,4},{12,8},{16,12},{20,16},{24,20},{28,24},{5,1},{9,5},{13... | collective-permute-start | bytes 13832 | tf_op jit(solution)/shard_map/ppermute | solution.py:834
  1029.2 38.3 %copy-start.3 = (bf16[512,1024]{1,0:T(8,128)(2,1)S(1)}, bf16[512,1024]{1,0:T(8,128)(2,1)}, u32[]{:S(2)}) copy-start(bf16[512,1024]{1,0:T(8,128)(2,1)} %param.20) | copy-start | bytes 3145732
  1029.2 38.3 %copy-start.35 = (bf16[512,256]{1,0:T(8,128)(2,1)S(1)}, bf16[512,256]{1,0:T(8,128)(2,1)}, u32[]{:S(2)}) copy-start(bf16[512,256]{1,0:T(8,128)(2,1)} %get-tuple-element.227) | copy-start | bytes 786436
  1029.2 38.3 %copy-start.83 = (f32[512]{0:T(512)S(1)}, f32[512]{0:T(512)}, u32[]{:S(2)}) copy-start(f32[512]{0:T(512)} %copy-done.81) | copy-start | bytes 6148
  1093.8 24.0 %copy-start.5 = (f32[128,1024]{1,0:T(8,128)S(1)}, f32[128,1024]{1,0:T(8,128)}, u32[]{:S(2)}) copy-start(f32[128,1024]{1,0:T(8,128)} %copy-done.4) | copy-start | bytes 1572868
  1093.8 24.0 %copy-start.80 = (f32[128]{0:T(128)S(1)}, f32[128]{0:T(128)}, u32[]{:S(2)}) copy-start(f32[128]{0:T(128)} %copy-done.79) | copy-start | bytes 1540
  1093.8 24.0 %copy-start.85 = (f32[128]{0:T(128)S(1)}, f32[128]{0:T(128)}, u32[]{:S(2)}) copy-start(f32[128]{0:T(128)} %copy-done.84) | copy-start | bytes 1540
  1093.8 24.0 %copy-start.89 = (f32[128]{0:T(128)S(1)}, f32[128]{0:T(128)}, u32[]{:S(2)}) copy-start(f32[128]{0:T(128)} %dynamic-slice.3) | copy-start | bytes 1540
  1138.4 10.0 copy-start.34
  (81 other events, 245.9 us)
Sparse Core Ops, SparseCore 0:
  10.2 78.0 all-gather.3
  90.3 80.5 all-gather.5
  173.0 77.4 all-gather.7
  629.3 72.5 reduce-scatter.9
  705.6 76.1 reduce-scatter.13
  785.6 87.6 reduce-scatter.11
  945.6 119.6 reduce-scatter.15
  1070.5 76.1 reduce-scatter.7

commit v2 on v1

v2 whole, which is shorter than its diff:
```python
import math

import jax
import jax.numpy as jnp
from jax import lax
from jax.experimental import pallas as pl
from jax.experimental.pallas import tpu as pltpu
from jax.sharding import PartitionSpec as P

HEAD = 64
LANE_WIDE = 4
MESH = pl.DeviceIdType.MESH
ANY = pl.BlockSpec(memory_space=pl.ANY)
bf16 = jnp.bfloat16
f32 = jnp.float32

decay_top = 0.2
moment_top = 0.9
learn_top = 0.1
eps_norm = 1e-05
eps_head = 1e-06
masked_score = -1e30


def remote(src, dst, send, recv, device):
    return pltpu.make_async_remote_copy(
        src_ref=src, dst_ref=dst, send_sem=send, recv_sem=recv, device_id=device, device_id_type=MESH
    )


def exchange(arrays, axes, ident):
    wide, narrow = lax.axis_size("wide"), lax.axis_size("narrow")
    peers = {"all": wide * narrow, "wide": wide, "narrow": narrow}[axes]
    picks = [pick for _, pick in arrays]
    operands = [array for array, _ in arrays]
    chunks = [a.shape if pick is None else a.shape[1:] for a, pick in arrays]
    count = len(arrays)

    def kernel(*refs):
        ins, outs, holds = refs[:count], refs[count : 2 * count], refs[2 * count : 3 * count]
        send_sem, recv_sem, local_sem = refs[3 * count :]
        my_wide, my_narrow = lax.axis_index("wide"), lax.axis_index("narrow")
        me = {"all": my_wide * narrow + my_narrow, "wide": my_wide, "narrow": my_narrow}[axes]

        def place(step):
            target = lax.rem(me + step, peers)
            if axes == "all":
                return lax.div(target, narrow), lax.rem(target, narrow)
            return (target, my_narrow) if axes == "wide" else (my_wide, target)

        barrier = pltpu.get_barrier_semaphore()

        def greet(step, carry):
            pl.semaphore_signal(barrier, inc=1, device_id=place(step), device_id_type=MESH)
            return carry

        lax.fori_loop(1, peers, greet, 0)

        def chunk(index, where):
            return ins[index] if picks[index] is None else ins[index].at[picks[index](*where)]

        own = [
            pltpu.make_async_copy(chunk(i, (my_wide, my_narrow)), holds[i], local_sem.at[i]) for i in range(count)
        ]
        for copy in own:
            copy.start()
        pl.semaphore_wait(barrier, peers - 1)

        def send(step, carry):
            where = place(step)
            for i in range(count):
                remote(chunk(i, where), outs[i].at[me], send_sem.at[i], recv_sem.at[i], where).start()
            return carry

        lax.fori_loop(1, peers, send, 0)
        for i in range(count):
            own[i].wait()
            back = pltpu.make_async_copy(holds[i], outs[i].at[me], local_sem.at[i])
            back.start()
            back.wait()
        for i in range(count):
            others = outs[i].at[pl.ds(0, peers - 1)]
            whole = remote(others, others, send_sem.at[i], recv_sem.at[i], place(1))
            whole.wait_send()
            whole.wait_recv()

    return pl.pallas_call(
        kernel,
        out_shape=[jax.ShapeDtypeStruct((peers,) + tuple(c), a.dtype) for a, c in zip(operands, chunks)],
        in_specs=[ANY] * count,
        out_specs=[ANY] * count,
        scratch_shapes=[pltpu.VMEM(tuple(c), a.dtype) for a, c in zip(operands, chunks)]
        + [pltpu.SemaphoreType.DMA((count,))] * 3,
        compiler_params=pltpu.CompilerParams(collective_id=ident, has_side_effects=True),
        name=f"exchange_{ident}",
    )(*operands)


class Grid:
    def __init__(self):
        wide, narrow = lax.axis_size("wide"), lax.axis_size("narrow")
        self.zs = 4 if wide % 4 == 0 else 1
        self.xs, self.ys = wide // self.zs, narrow // 2
        self.wide, self.narrow = lax.axis_index("wide"), lax.axis_index("narrow")
        self.z, self.x = lax.div(self.wide, self.xs), lax.rem(self.wide, self.xs)
        self.y, self.c = lax.div(self.narrow, 2), lax.rem(self.narrow, 2)
        self.partner = self.device(self.z, self.x, self.y, 1 - self.c)

    def device(self, z, x, y, c):
        return z * self.xs + x, 2 * y + c

    def z_others(self):
        if self.zs != 4:
            return [lax.rem(self.z + s, self.zs) for s in range(1, self.zs)]
        near = self.z + 1 - 2 * lax.div(self.z + 3, 4)
        far = 3 - 3 * lax.div(self.z, 2)
        return [near, 6 - self.z - near - far, far]

    def x_others(self):
        return [lax.rem(self.x + s, self.xs) for s in range(1, self.xs)]

    def y_others(self):
        return [lax.rem(self.y + s, self.ys) for s in range(1, self.ys)]

    def greet_all(self):
        wide, narrow = lax.axis_size("wide"), lax.axis_size("narrow")
        devices = wide * narrow
        me = self.wide * narrow + self.narrow
        barrier = pltpu.get_barrier_semaphore()

        def greet(step, carry):
            target = lax.rem(me + step, devices)
            where = lax.div(target, narrow), lax.rem(target, narrow)
            pl.semaphore_signal(barrier, inc=1, device_id=where, device_id_type=MESH)
            return carry

        lax.fori_loop(1, devices, greet, 0)
        return lambda: pl.semaphore_wait(barrier, devices - 1)


class Gather:
    def __init__(self, grid, source, whole, sems):
        self.grid, self.source, self.whole = grid, source, whole
        self.sent, self.got, self.sent_pair, self.got_pair = sems
        self.rows = whole.shape[2]
        self.pushes, self.pairs = 0, 0

    @staticmethod
    def counts():
        zs = 4 if lax.axis_size("wide") % 4 == 0 else 1
        xs, ys = lax.axis_size("wide") // zs, lax.axis_size("narrow") // 2
        sends = 2 * (zs - 1) + zs * 2 * (xs - 1 + ys - 1) + 2 * zs * (xs - 1) * (ys - 1)
        return zs * xs * ys, sends, 2 * zs * xs * ys

    @classmethod
    def scratch(cls):
        chips, sends, pairs = cls.counts()
        return [
            pltpu.SemaphoreType.DMA((sends,)),
            pltpu.SemaphoreType.DMA((chips, 2)),
            pltpu.SemaphoreType.DMA((pairs,)),
            pltpu.SemaphoreType.DMA((chips, 2)),
        ]

    def half(self, ref, h):
        return ref.at[pl.ds(h * (self.rows // 2), self.rows // 2)]

    def piece(self, z, x, y, c, h):
        wide, narrow = self.grid.device(z, x, y, c)
        return self.half(self.whole.at[wide, narrow], h)

    def spot(self, z, x, y):
        return (z * self.grid.xs + x) * self.grid.ys + y

    def push(self, z, x, y, h, target, own):
        here = self.piece(z, x, y, self.grid.c, h)
        copy = remote(
            self.half(self.source, h) if own else here,
            here,
            self.sent.at[self.pushes],
            self.got.at[self.spot(z, x, y), h],
            target,
        )
        self.pushes += 1
        copy.start()

    def to_partner(self, z, x, y, h, own=False):
        here = self.piece(z, x, y, self.grid.c, h)
        copy = remote(
            self.half(self.source, h) if own else here,
            here,
            self.sent_pair.at[self.pairs],
            self.got_pair.at[self.spot(z, x, y), h],
            self.grid.partner,
        )
        self.pairs += 1
        copy.start()

    def arrived(self, z, x, y, h):
        here = self.piece(z, x, y, self.grid.c, h)
        remote(here, here, self.sent.at[0], self.got.at[self.spot(z, x, y), h], self.grid.partner).wait_recv()

    def fan(self, z, own=False):
        g = self.grid
        to_y = [g.device(g.z, g.x, y, g.c) for y in g.y_others()]
        to_x = [g.device(g.z, x, g.y, g.c) for x in g.x_others()]
        for h, targets in ((0, to_y), (1, to_x), (0, to_x), (1, to_y)):
            for target in targets:
                self.push(z, g.x, g.y, h, target, own)
        for h in (0, 1):
            self.to_partner(z, g.x, g.y, h, own)

    def begin(self):
        g = self.grid
        for z in g.z_others():
            for h in (0, 1):
                self.push(g.z, g.x, g.y, h, g.device(z, g.x, g.y, g.c), True)
        self.fan(g.z, True)

    def level(self, number):
        return ([self.grid.z] + self.grid.z_others())[number]

    def along_z(self, number):
        g, z = self.grid, self.level(number)
        for h in (0, 1):
            self.arrived(z, g.x, g.y, h)
        self.fan(z)

    def across(self, number):
        g, z = self.grid, self.level(number)
        for y in g.y_others():
            self.arrived(z, g.x, y, 0)
            for x in g.x_others():
                self.push(z, g.x, y, 0, g.device(g.z, x, g.y, g.c), False)
            self.to_partner(z, g.x, y, 0)
        for x in g.x_others():
            self.arrived(z, x, g.y, 1)
            for y in g.y_others():
                self.push(z, x, g.y, 1, g.device(g.z, g.x, y, g.c), False)
            self.to_partner(z, x, g.y, 1)

    def last(self, number):
        g, z = self.grid, self.level(number)
        for x in g.x_others():
            self.arrived(z, x, g.y, 0)
            self.to_partner(z, x, g.y, 0)
            for y in g.y_others():
                self.arrived(z, x, y, 0)
                self.to_partner(z, x, y, 0)
        for y in g.y_others():
            self.arrived(z, g.x, y, 1)
            self.to_partner(z, g.x, y, 1)
            for x in g.x_others():
                self.arrived(z, x, y, 1)
                self.to_partner(z, x, y, 1)

    def middle(self):
        for number in range(1, self.grid.zs):
            self.along_z(number)
            self.across(number - 1)
            if number > 1:
                self.last(number - 2)
        self.across(self.grid.zs - 1)
        for number in range(max(0, self.grid.zs - 2), self.grid.zs):
            self.last(number)

    def finish(self):
        g = self.grid
        here = self.piece(g.z, g.x, g.y, g.c, 0)
        _, sends, pairs = self.counts()
        for sems, number in ((self.sent, sends), (self.sent_pair, pairs)):
            for i in range(number):
                remote(here, here, sems.at[i], self.got.at[0, 0], g.partner).wait_send()
        for z in range(g.zs):
            for x in range(g.xs):
                for y in range(g.ys):
                    for h in (0, 1):
                        there = self.piece(z, x, y, 1 - g.c, h)
                        remote(
                            there, there, self.sent.at[0], self.got_pair.at[self.spot(z, x, y), h], g.partner
                        ).wait_recv()


def send_parameters(smalls, weights, blocks, ident):
    wide, narrow = lax.axis_size("wide"), lax.axis_size("narrow")
    devices = wide * narrow
    count = len(blocks)

    def kernel(*refs):
        smalls_ref, weights_ref = refs[:2]
        block_refs, refs = refs[2 : 2 + count], refs[2 + count :]
        smalls_out, weights_out = refs[:2]
        block_outs, refs = refs[2 : 2 + count], refs[2 + count :]
        hold_small, hold_weight, refs = refs[0], refs[1], refs[2:]
        hold_blocks, refs = refs[:count], refs[count:]
        local_sem, all_send, all_recv, near_send, near_recv, z_send, z_recv, x_send, x_recv, b_send, b_recv = refs
        g = Grid()
        me = g.wide * narrow + g.narrow
        wait_all = g.greet_all()
        own = [
            (smalls_ref, hold_small, smalls_out.at[me]),
            (weights_ref.at[g.narrow], hold_weight, weights_out.at[g.wide, g.narrow]),
        ] + [
            (block_refs[i].at[lax.rem(g.wide, LANE_WIDE)], hold_blocks[i], block_outs[i].at[g.wide])
            for i in range(count)
        ]
        into = [pltpu.make_async_copy(a, b, local_sem.at[i]) for i, (a, b, _) in enumerate(own)]
        back = [pltpu.make_async_copy(b, c, local_sem.at[i]) for i, (_, b, c) in enumerate(own)]
        for copy in into:
            copy.start()
        wait_all()
        near = []
        for s in range(1, narrow):
            target = lax.rem(g.narrow + s, narrow)
            copy = remote(
                weights_ref.at[target],
                weights_out.at[g.wide, g.narrow],
                near_send.at[s],
                near_recv.at[g.narrow],
                (g.wide, target),
            )
            copy.start()
            near.append(copy)

        def send_small(step, carry):
            target = lax.rem(me + step, devices)
            remote(
                smalls_ref,
                smalls_out.at[me],
                all_send.at[0],
                all_recv.at[0],
                (lax.div(target, narrow), lax.rem(target, narrow)),
            ).start()
            return carry

        lax.fori_loop(1, devices, send_small, 0)
        for copy in into:
            copy.wait()
        for copy in back:
            copy.start()
        for copy in back:
            copy.wait()
        for s in range(1, narrow):
            source = lax.rem(g.narrow + s, narrow)
            there = weights_out.at[g.wide, source]
            remote(there, there, near_send.at[s], near_recv.at[source], g.partner).wait_recv()

        def row(z, x):
            return weights_out.at[z * g.xs + x]

        sends = []

        def push(z, target, send, recv):
            copy = remote(row(z, g.x), row(z, g.x), send, recv, target)
            copy.start()
            sends.append(copy)

        for i, z in enumerate(g.z_others()):
            push(g.z, g.device(z, g.x, g.y, g.c), z_send.at[i], z_recv.at[g.z])
        for i, x in enumerate(g.x_others()):
            push(g.z, g.device(g.z, x, g.y, g.c), x_send.at[0, i], x_recv.at[g.z, g.x])
        for s in range(1, wide):
            target = lax.rem(g.wide + s, wide)
            for i in range(count):
                copy = remote(
                    block_refs[i].at[lax.rem(target, LANE_WIDE)],
                    block_outs[i].at[g.wide],
                    b_send.at[i, s],
                    b_recv.at[i, g.wide],
                    (target, g.narrow),
                )
                copy.start()
                sends.append(copy)
        for j, z in enumerate(g.z_others()):
            remote(row(z, g.x), row(z, g.x), z_send.at[0], z_recv.at[z], g.partner).wait_recv()
            for i, x in enumerate(g.x_others()):
                push(z, g.device(g.z, x, g.y, g.c), x_send.at[1 + j, i], x_recv.at[z, g.x])
        for x in g.x_others():
            for z in [g.z] + g.z_others():
                remote(row(z, x), row(z, x), z_send.at[0], x_recv.at[z, x], g.partner).wait_recv()
        for s in range(1, wide):
            source = lax.rem(g.wide + s, wide)
            for i in range(count):
                there = block_outs[i].at[source]
                remote(there, there, z_send.at[0], b_recv.at[i, source], g.partner).wait_recv()
        for copy in near + sends:
            copy.wait_send()
        others = smalls_out.at[pl.ds(0, devices - 1)]
        whole = remote(others, others, all_send.at[0], all_recv.at[0], g.partner)
        whole.wait_send()
        whole.wait_recv()

    zs = 4 if wide % 4 == 0 else 1
    xs = wide // zs
    sem = pltpu.SemaphoreType.DMA
    return pl.pallas_call(
        kernel,
        out_shape=[
            jax.ShapeDtypeStruct((devices,) + smalls.shape, smalls.dtype),
            jax.ShapeDtypeStruct((wide, narrow) + weights.shape[1:], weights.dtype),
        ]
        + [jax.ShapeDtypeStruct((wide,) + b.shape[1:], b.dtype) for b in blocks],
        in_specs=[ANY] * (2 + count),
        out_specs=[ANY] * (2 + count),
        scratch_shapes=[pltpu.VMEM(smalls.shape, smalls.dtype), pltpu.VMEM(weights.shape[1:], weights.dtype)]
        + [pltpu.VMEM(b.shape[1:], b.dtype) for b in blocks]
        + [sem((2 + count,)), sem((1,)), sem((1,)), sem((narrow,)), sem((narrow,)), sem((zs,)), sem((zs,))]
        + [sem((zs, xs)), sem((zs, xs)), sem((count, wide)), sem((count, wide))],
        compiler_params=pltpu.CompilerParams(collective_id=ident, has_side_effects=True),
        name="send_parameters",
    )(smalls, weights, *blocks)


def rows_to_lanes(rows, chunks, pick, tile, ident):
    wide, narrow = lax.axis_size("wide"), lax.axis_size("narrow")
    devices = wide * narrow

    def kernel(rows_ref, chunks_ref, tile_ref, rows_out, chunks_out, tile_out, *refs):
        hold_rows, hold_chunk, hold_tile, local_sem, send, recv = refs[:6]
        g = Grid()
        me = g.wide * narrow + g.narrow
        wait_all = g.greet_all()
        own = [
            (rows_ref, hold_rows, rows_out.at[g.wide, g.narrow]),
            (chunks_ref.at[pick(g.wide, g.narrow)], hold_chunk, chunks_out.at[me]),
            (tile_ref, hold_tile, tile_out.at[me]),
        ]
        into = [pltpu.make_async_copy(a, b, local_sem.at[i]) for i, (a, b, _) in enumerate(own)]
        back = [pltpu.make_async_copy(b, c, local_sem.at[i]) for i, (_, b, c) in enumerate(own)]
        for copy in into:
            copy.start()
        wait_all()
        gather = Gather(g, rows_ref, rows_out, refs[6:])
        gather.begin()

        def send_chunks(step, carry):
            target = lax.rem(me + step, devices)
            where = lax.div(target, narrow), lax.rem(target, narrow)
            remote(chunks_ref.at[pick(*where)], chunks_out.at[me], send.at[0], recv.at[0], where).start()
            remote(tile_ref, tile_out.at[me], send.at[1], recv.at[1], where).start()
            return carry

        lax.fori_loop(1, devices, send_chunks, 0)
        for copy in into:
            copy.wait()
        for copy in back:
            copy.start()
        gather.middle()
        for copy in back:
            copy.wait()
        for i, out in enumerate((chunks_out, tile_out)):
            others = out.at[pl.ds(0, devices - 1)]
            whole = remote(others, others, send.at[i], recv.at[i], g.partner)
            whole.wait_send()
            whole.wait_recv()
        gather.finish()

    return pl.pallas_call(
        kernel,
        out_shape=[
            jax.ShapeDtypeStruct((wide, narrow) + rows.shape, rows.dtype),
            jax.ShapeDtypeStruct((devices,) + chunks.shape[1:], chunks.dtype),
            jax.ShapeDtypeStruct((devices,) + tile.shape, tile.dtype),
        ],
        in_specs=[ANY] * 3,
        out_specs=[ANY] * 3,
        scratch_shapes=[
            pltpu.VMEM(rows.shape, rows.dtype),
            pltpu.VMEM(chunks.shape[1:], chunks.dtype),
            pltpu.VMEM(tile.shape, tile.dtype),
            pltpu.SemaphoreType.DMA((3,)),
            pltpu.SemaphoreType.DMA((2,)),
            pltpu.SemaphoreType.DMA((2,)),
        ]
        + Gather.scratch(),
        compiler_params=pltpu.CompilerParams(collective_id=ident, has_side_effects=True),
        name="rows_to_lanes",
    )(rows, chunks, tile)


def narrow_step(parts, extras, work, spread_count, locals_like, ident):
    narrow, rows, width = parts[0].shape
    ys = narrow // 2
    count, extra_count, local_count = len(parts), len(extras), len(locals_like)
    parts = [p.reshape(ys, 2, rows, width) for p in parts]

    def kernel(*refs):
        part_refs, refs = refs[:count], refs[count:]
        extra_refs, refs = refs[:extra_count], refs[extra_count:]
        spread_refs, refs = refs[:spread_count], refs[spread_count:]
        local_refs, refs = refs[:local_count], refs[local_count:]
        mine, pair, half, got, rowbuf, refs = refs[0], refs[1], refs[2], refs[3], refs[4], refs[5:]
        load_sem, pair_send, pair_recv, y_send, y_recv, s_send, s_recv, p_send, p_recv, own_sem = refs
        g = Grid()
        barrier = pltpu.get_barrier_semaphore()
        friends = [g.device(g.z, g.x, y, g.c) for y in g.y_others()] + [g.partner]
        for friend in friends:
            pl.semaphore_signal(barrier, inc=1, device_id=friend, device_id_type=MESH)
        loads = [
            pltpu.make_async_copy(part_refs[i].at[:, g.c], mine.at[i], load_sem.at[i]) for i in range(count)
        ]
        for copy in loads:
            copy.start()
        pl.semaphore_wait(barrier, len(friends))
        pairs = [
            remote(part_refs[i].at[:, 1 - g.c], pair.at[i], pair_send.at[i], pair_recv.at[i], g.partner)
            for i in range(count)
        ]
        for copy in pairs:
            copy.start()
        sends = []
        for i in range(count):
            loads[i].wait()
            pairs[i].wait_recv()
            half[i] = (mine[i].astype(f32) + pair[i].astype(f32)).astype(bf16)
            for s, y in enumerate(g.y_others()):
                copy = remote(
                    half.at[i, y], got.at[i, g.y], y_send.at[i, s], y_recv.at[i, g.y], g.device(g.z, g.x, y, g.c)
                )
                copy.start()
                sends.append(copy)
        totals = []
        for i in range(count):
            total = half[i, g.y].astype(f32)
            for y in g.y_others():
                remote(got.at[i, y], got.at[i, y], y_send.at[i, 0], y_recv.at[i, y], g.partner).wait_recv()
                total = total + got[i, y].astype(f32)
            totals.append(total)
        spreads, locals_out = work(totals, [ref[...] for ref in extra_refs])
        for ref, value in zip(local_refs, locals_out):
            ref[...] = value
        own = []
        for i, value in enumerate(spreads):
            rowbuf[i] = value
            for s, y in enumerate(g.y_others()):
                copy = remote(
                    rowbuf.at[i],
                    spread_refs[i].at[g.narrow],
                    s_send.at[i, s],
                    s_recv.at[i, g.y],
                    g.device(g.z, g.x, y, g.c),
                )
                copy.start()
                sends.append(copy)
            copy = remote(
                rowbuf.at[i], spread_refs[i].at[g.narrow], p_send.at[i, g.y], p_recv.at[i, g.y], g.partner
            )
            copy.start()
            sends.append(copy)
            copy = pltpu.make_async_copy(rowbuf.at[i], spread_refs[i].at[g.narrow], own_sem.at[i])
            copy.start()
            own.append(copy)
        for i in range(spread_count):
            for y in g.y_others():
                there = spread_refs[i].at[2 * y + g.c]
                remote(there, there, s_send.at[i, 0], s_recv.at[i, y], g.partner).wait_recv()
                copy = remote(there, there, p_send.at[i, y], p_recv.at[i, y], g.partner)
                copy.start()
                sends.append(copy)
        for i in range(spread_count):
            for y in range(ys):
                there = spread_refs[i].at[2 * y + 1 - g.c]
                remote(there, there, s_send.at[i, 0], p_recv.at[i, y], g.partner).wait_recv()
        for copy in pairs + sends:
            copy.wait_send()
        for copy in own:
            copy.wait()

    sem = pltpu.SemaphoreType.DMA
    vmem = pl.BlockSpec(memory_space=pltpu.VMEM)
    return pl.pallas_call(
        kernel,
        out_shape=[jax.ShapeDtypeStruct((narrow, rows, width), bf16)] * spread_count
        + [jax.ShapeDtypeStruct(shape, dtype) for shape, dtype in locals_like],
        in_specs=[ANY] * count + [vmem] * extra_count,
        out_specs=[ANY] * spread_count + [vmem] * local_count,
        scratch_shapes=[pltpu.VMEM((count, ys, rows, width), bf16)] * 4
        + [pltpu.VMEM((spread_count, rows, width), bf16)]
        + [sem((count,))] * 3
        + [sem((count, ys))] * 2
        + [sem((spread_count, ys))] * 4
        + [sem((spread_count,))],
        compiler_params=pltpu.CompilerParams(collective_id=ident, has_side_effects=True),
        name=f"narrow_step_{ident}",
    )(*parts, *extras)


def matmul(left_side, right_side):
    return jnp.dot(left_side, right_side, preferred_element_type=jnp.float32)


def inner_left(left_side, right_side):
    return lax.dot_general(left_side, right_side, (((0,), (0,)), ((), ())), preferred_element_type=jnp.float32)


def inner_right(left_side, right_side):
    return lax.dot_general(left_side, right_side, (((1,), (1,)), ((), ())), preferred_element_type=jnp.float32)


def silu_slope(values):
    sigmoid_val = jax.nn.sigmoid(values)
    return sigmoid_val * (1.0 + values * (1.0 - sigmoid_val))


def silu_curve(values):
    sigmoid_val = jax.nn.sigmoid(values)
    return sigmoid_val * (1.0 - sigmoid_val) * (2.0 + values * (1.0 - 2.0 * sigmoid_val))


class Lane:
    def __init__(self):
        narrow = lax.axis_size("narrow")
        self.ys = narrow // 2
        self.chips = LANE_WIDE * self.ys
        wide_pos, narrow_pos = lax.axis_index("wide"), lax.axis_index("narrow")
        self.base = lax.div(wide_pos, LANE_WIDE) * LANE_WIDE
        self.colour = lax.rem(narrow_pos, 2)
        self.chip = lax.rem(wide_pos, LANE_WIDE) * self.ys + lax.div(narrow_pos, 2)
        self.partner = (wide_pos, narrow_pos + 1 - 2 * self.colour)

    def other(self, step):
        return lax.rem(self.chip + step, self.chips)

    def device(self, chip):
        return self.base + lax.div(chip, self.ys), 2 * lax.rem(chip, self.ys) + self.colour

    def greet(self):
        barrier = pltpu.get_barrier_semaphore()
        for step in range(1, self.chips):
            pl.semaphore_signal(barrier, inc=1, device_id=self.device(self.other(step)), device_id_type=MESH)
        pl.semaphore_signal(barrier, inc=1, device_id=self.partner, device_id_type=MESH)
        pl.semaphore_wait(barrier, self.chips)


class Scatter:
    def __init__(self, lane, part, pair, half, got, sems):
        self.lane, self.part, self.pair, self.half, self.got = lane, part, pair, half, got
        self.pair_send, self.pair_recv, self.send, self.recv = sems

    @staticmethod
    def scratch(chips, rows, width):
        return [
            pltpu.VMEM((2, chips, rows, width), bf16),
            pltpu.VMEM((chips, rows, width), bf16),
            pltpu.VMEM((chips, rows, width), bf16),
            pltpu.VMEM((chips, rows, width), bf16),
            pltpu.SemaphoreType.DMA((1,)),
            pltpu.SemaphoreType.DMA((1,)),
            pltpu.SemaphoreType.DMA((chips,)),
            pltpu.SemaphoreType.DMA((chips,)),
        ]

    @classmethod
    def of(cls, lane, refs):
        return cls(lane, *refs[:4], refs[4:8])

    def pair_copy(self):
        return remote(
            self.part.at[1 - self.lane.colour],
            self.pair,
            self.pair_send.at[0],
            self.pair_recv.at[0],
            self.lane.partner,
        )

    def start_pair(self):
        self.pair_copy().start()

    def take_pair(self):
        self.pair_copy().wait()
        self.half[...] = (
            self.part[self.lane.colour].astype(f32) + self.pair[...].astype(f32)
        ).astype(bf16)
        self.got[self.lane.chip] = self.half[self.lane.chip]

    def copy_to(self, step):
        chip = self.lane.other(step)
        return remote(
            self.half.at[chip],
            self.got.at[self.lane.chip],
            self.send.at[step],
            self.recv.at[self.lane.chip],
            self.lane.device(chip),
        )

    def start_sends(self):
        for step in range(1, self.lane.chips):
            self.copy_to(step).start()

    def total(self):
        result = self.got[self.lane.chip].astype(f32)
        for step in range(1, self.lane.chips):
            chip = self.lane.other(step)
            remote(
                self.got.at[chip], self.got.at[chip], self.send.at[step], self.recv.at[chip], self.lane.device(chip)
            ).wait_recv()
            result = result + self.got[chip].astype(f32)
        return result

    def wait_sends(self):
        for step in range(1, self.lane.chips):
            self.copy_to(step).wait_send()


class Spread:
    def __init__(self, lane, whole, sems):
        self.lane, self.whole = lane, whole
        self.send, self.recv, self.pair_send, self.pair_recv = sems

    @staticmethod
    def scratch(chips, rows, width):
        return [pltpu.VMEM((2, chips, rows, width), bf16)] + [pltpu.SemaphoreType.DMA((chips,))] * 4

    @classmethod
    def of(cls, lane, refs):
        return cls(lane, refs[0], refs[1:5])

    def mine(self):
        return self.whole.at[self.lane.colour, self.lane.chip]

    def copy_to(self, step):
        return remote(
            self.mine(),
            self.mine(),
            self.send.at[step],
            self.recv.at[self.lane.chip],
            self.lane.device(self.lane.other(step)),
        )

    def pair_copy(self, chip, colour):
        place = self.whole.at[colour, chip]
        return remote(place, place, self.pair_send.at[chip], self.pair_recv.at[chip], self.lane.partner)

    def run(self):
        lane = self.lane
        for step in range(1, lane.chips):
            self.copy_to(step).start()
        self.pair_copy(lane.chip, lane.colour).start()
        for step in range(1, lane.chips):
            chip = lane.other(step)
            place = self.whole.at[lane.colour, chip]
            remote(place, place, self.send.at[step], self.recv.at[chip], lane.device(chip)).wait_recv()
            self.pair_copy(chip, lane.colour).start()
        for chip in range(lane.chips):
            self.pair_copy(chip, 1 - lane.colour).wait_recv()
        for step in range(1, lane.chips):
            self.copy_to(step).wait_send()
        for chip in range(lane.chips):
            self.pair_copy(chip, lane.colour).wait_send()


def chain_forward(keys, key_index, values, queries, spans, gates, first_init, second_init, ident):
    wide = lax.axis_size("wide")
    blocks, span, block = keys.shape[1:]
    width, hidden = first_init.shape
    rows = values.shape[1]
    turns = spans.shape[0]
    key_turns = turns - 1
    per_turn = 3 if turns <= 5 else 1
    first_left = per_turn * (key_turns - 3)
    slots = 3
    stream_keys = keys.shape[0] == turns
    chips = LANE_WIDE * (lax.axis_size("narrow") // 2)
    n_scatter = len(Scatter.scratch(1, 8, 128))

    def kernel(*refs):
        keys_hbm, values_hbm, own_hbm, index_ref, spans_ref, gates_ref, first_hbm, second_hbm = refs[:8]
        recalled_hbm, low1_hbm, low2_hbm, m1_hbm, m2_hbm, g1_hbm, g2_hbm = refs[8:15]
        err_hbm, pre_hbm, qpre_hbm, klane_hbm, qlane_hbm = refs[15:20]
        rest = refs[20:]
        kall, qall, vall, kcur, qcur, i1, i2, s1, s2, m1, m2, low1, low2, mb1, mb2, gb1, gb2 = rest[:17]
        pre, qpre, khid, rec, qpart, qpair, qhalf, qgot, own_hold = rest[17:26]
        in_sem, out_sem, q_sem, q_pair_send, q_pair_recv, q_send, q_recv = rest[26:33]
        rest = rest[33:]
        lane = Lane()
        grid = Grid()
        lookup = Scatter.of(lane, rest[:n_scatter])
        error = Spread.of(lane, rest[n_scatter : n_scatter + 5])
        gather = Gather(grid, own_hbm, qall, rest[n_scatter + 5 :])

        def recall(q, slot):
            sems = q_pair_send.at[pl.ds(q, 1)], q_pair_recv.at[pl.ds(q, 1)], q_send.at[q], q_recv.at[q]
            return Scatter(lane, qpart.at[slot], qpair.at[q], qhalf.at[slot], qgot.at[q], sems)

        def state_saves(turn):
            return [
                pltpu.make_async_copy(source, target.at[turn], out_sem.at[i])
                for i, (source, target) in enumerate(((mb1, m1_hbm), (mb2, m2_hbm), (kcur, klane_hbm)))
            ]

        def other_saves(turn):
            return [
                pltpu.make_async_copy(source, target.at[turn], out_sem.at[3 + i])
                for i, (source, target) in enumerate(
                    ((gb1, g1_hbm), (gb2, g2_hbm), (error.whole, err_hbm), (pre, pre_hbm))
                )
            ]

        def query_saves(q, slot):
            return [
                pltpu.make_async_copy(source.at[slot], target.at[q], q_sem.at[slot, i])
                for i, (source, target) in enumerate(((qcur, qlane_hbm), (qpre, qpre_hbm)))
            ]

        inputs = [
            pltpu.make_async_copy(source, target, in_sem.at[i])
            for i, (source, target) in enumerate(
                ((first_hbm, i1), (second_hbm, i2), (keys_hbm, kall), (values_hbm, vall), (own_hbm, own_hold))
            )
            if not (stream_keys and i == 2)
        ]
        for copy in inputs:
            copy.start()
        grid.greet_all()()
        gather.begin()
        for copy in inputs:
            copy.wait()
        own_store = pltpu.make_async_copy(own_hold, qall.at[grid.wide, grid.narrow], in_sem.at[4])
        own_store.start()
        low1[0] = i1[...]
        low2[0] = i2[...]
        s1[...] = i1[...].astype(f32)
        s2[...] = i2[...].astype(f32)
        for ref in (m1, m2, mb1, mb2):
            ref[...] = jnp.zeros_like(ref)
        own_store.wait()

        def lookup_blocks(buf, first):
            total = matmul(buf[0], first[pl.ds(0, block), :])
            for b in range(1, blocks):
                total = total + matmul(buf[b], first[pl.ds(b * block, block), :])
            return total

        def ask(q, slot, waits):
            def settle():
                recall(q - slots, slot).wait_sends()
                for copy in query_saves(q - slots, slot):
                    copy.wait()

            if waits is True:
                settle()
            elif waits is not False:
                pl.when(waits)(settle)
            index = spans_ref[q]
            for b in range(blocks):
                qcur[slot, b] = qall[index, b]
            query_pre = lookup_blocks(qcur.at[slot], low1.at[q])
            qpre[slot] = query_pre
            for copy in query_saves(q, slot):
                copy.start()
            query_hidden = (query_pre * jax.nn.sigmoid(query_pre)).astype(bf16)
            qpart[slot] = matmul(query_hidden, low2[q]).astype(bf16).reshape(2, chips, rows, width)
            recall(q, slot).start_pair()

        def turn_body(turn, carry):
            index, place = spans_ref[turn], index_ref[turn]
            if stream_keys:
                one = pltpu.make_async_copy(keys_hbm.at[turn], kcur, in_sem.at[2])
                one.start()
                one.wait()
            else:
                for b in range(blocks):
                    kcur[b] = kall[place, b]
            for copy in state_saves(turn):
                copy.start()
            key_pre = lookup_blocks(kcur, low1.at[turn])
            pre[0] = key_pre
            khid[...] = (key_pre * jax.nn.sigmoid(key_pre)).astype(bf16)
            lookup.part[...] = matmul(khid[...], low2[turn]).astype(bf16).reshape(2, chips, rows, width)
            lookup.start_pair()

            @pl.when(turn == 3)
            def _():
                gather.finish()

            first = per_turn * (turn - 3)

            @pl.when(turn >= 3)
            def _():
                ask(first, lax.rem(first, slots), first >= slots)

            lookup.take_pair()
            lookup.start_sends()

            @pl.when(turn >= 3)
            def _():
                recall(first, lax.rem(first, slots)).take_pair()
                for j in range(1, per_turn):
                    ask(first + j, lax.rem(first + j, slots), first + j >= slots)

            total = lookup.total()
            target = jnp.concatenate([vall[index * blocks + b] for b in range(blocks)], axis=1)
            error.whole[lane.colour, lane.chip] = ((total - target.astype(f32)) / span).astype(bf16)
            error.run()
            lookup.wait_sends()

            @pl.when(turn >= 3)
            def _():
                recall(first, lax.rem(first, slots)).start_sends()
                for j in range(1, per_turn):
                    stream = recall(first + j, lax.rem(first + j, slots))
                    stream.take_pair()
                    stream.start_sends()

            err = error.whole[...].reshape(span, width)
            grad_second = inner_left(khid[...], err)
            hidden_grad = inner_right(err, low2[turn])
            pre[1] = hidden_grad
            slope = (hidden_grad * silu_slope(pre[0])).astype(bf16)
            decay, moment, rate, reset = (gates_ref[turn, i] for i in range(4))
            for copy in state_saves(turn):
                copy.wait()
            following = jnp.minimum(turn + 1, turns - 1)

            def update(s, m, mb, init, low, grad, place):
                moment_new = moment * m[place] - rate * grad
                state_new = (1.0 - decay) * s[place] + moment_new
                state_new = reset * init[place].astype(f32) + (1.0 - reset) * state_new
                moment_new = (1.0 - reset) * moment_new
                m[place] = moment_new
                mb[place] = moment_new.astype(bf16)
                s[place] = state_new
                low[(following,) + place] = state_new.astype(bf16)

            gb2[...] = grad_second.astype(bf16)
            update(s2, m2, mb2, i2, low2, grad_second, (slice(None), slice(None)))
            for b in range(blocks):
                grad_first = inner_left(kcur[b], slope)
                place = (pl.ds(b * block, block), slice(None))
                gb1[place] = grad_first.astype(bf16)
                update(s1, m1, mb1, i1, low1, grad_first, place)
            saves = other_saves(turn)
            for copy in saves:
                copy.start()

            @pl.when(turn == 0)
            def _():
                for number in range(1, grid.zs):
                    gather.along_z(number)
                gather.across(0)

            @pl.when(turn == 1)
            def _():
                for number in range(1, grid.zs):
                    gather.across(number)
                gather.last(0)

            @pl.when(turn == 2)
            def _():
                for number in range(1, grid.zs):
                    gather.last(number)

            for copy in saves:
                copy.wait()
            return carry

        lax.fori_loop(0, key_turns, turn_body, 0)
        ends = [
            pltpu.make_async_copy(low1, low1_hbm, out_sem.at[0]),
            pltpu.make_async_copy(low2, low2_hbm, out_sem.at[1]),
        ]
        for copy in ends:
            copy.start()
        left = list(range(first_left, turns))
        for q in left:
            ask(q, q % slots, q >= slots)
            if q > left[0]:
                stream = recall(q - 1, (q - 1) % slots)
                stream.take_pair()
                stream.start_sends()
        stream = recall(turns - 1, (turns - 1) % slots)
        stream.take_pair()
        stream.start_sends()
        for q in range(turns):
            rec[q] = recall(q, q % slots).total().astype(bf16)
        last = pltpu.make_async_copy(rec, recalled_hbm, out_sem.at[2])
        last.start()
        for q in range(turns - slots, turns):
            recall(q, q % slots).wait_sends()
        for q in range(turns - slots, turns):
            for copy in query_saves(q, q % slots):
                copy.wait()
        for copy in ends + [last]:
            copy.wait()

    state = [(width, hidden), (hidden, width)]
    out_shape = (
        [jax.ShapeDtypeStruct((turns, rows, width), bf16)]
        + [jax.ShapeDtypeStruct((turns,) + s, bf16) for s in state]
        + [jax.ShapeDtypeStruct((key_turns,) + s, bf16) for s in state * 2]
        + [
            jax.ShapeDtypeStruct((key_turns, 2, chips, rows, width), bf16),
            jax.ShapeDtypeStruct((key_turns, 2, span, hidden), f32),
            jax.ShapeDtypeStruct((turns, span, hidden), f32),
            jax.ShapeDtypeStruct((key_turns, blocks, span, block), bf16),
            jax.ShapeDtypeStruct((turns, blocks, span, block), bf16),
        ]
    )
    sem = pltpu.SemaphoreType.DMA
    scratch = (
        [pltpu.VMEM((1 if stream_keys else keys.shape[0], blocks, span, block), bf16), pltpu.VMEM((wide, blocks, span, block), bf16)]
        + [pltpu.VMEM(values.shape, bf16)]
        + [pltpu.VMEM((blocks, span, block), bf16), pltpu.VMEM((slots, blocks, span, block), bf16)]
        + [pltpu.VMEM(s, bf16) for s in state]
        + [pltpu.VMEM(s, f32) for s in state * 2]
        + [pltpu.VMEM((turns,) + s, bf16) for s in state]
        + [pltpu.VMEM(s, bf16) for s in state * 2]
        + [
            pltpu.VMEM((2, span, hidden), f32),
            pltpu.VMEM((slots, span, hidden), f32),
            pltpu.VMEM((span, hidden), bf16),
            pltpu.VMEM((turns, rows, width), bf16),
            pltpu.VMEM((slots, 2, chips, rows, width), bf16),
        ]
        + [pltpu.VMEM((n, chips, rows, width), bf16) for n in (turns, slots, turns)]
        + [pltpu.VMEM((span, block), bf16)]
        + [sem((5,)), sem((7,)), sem((slots, 2)), sem((turns,)), sem((turns,)), sem((turns, chips)), sem((turns, chips))]
        + Scatter.scratch(chips, rows, width)
        + Spread.scratch(chips, rows, width)
        + Gather.scratch()
    )
    smem = pl.BlockSpec(memory_space=pltpu.SMEM)
    return pl.pallas_call(
        kernel,
        out_shape=out_shape,
        in_specs=[ANY] * 3 + [smem] * 3 + [ANY] * 2,
        out_specs=[ANY] * len(out_shape),
        scratch_shapes=scratch,
        compiler_params=pltpu.CompilerParams(
            collective_id=ident, has_side_effects=True, vmem_limit_bytes=62 * 1024 * 1024
        ),
        cost_estimate=pl.CostEstimate(
            flops=40 * turns * 2 * span * width * hidden, bytes_accessed=turns * 40 * 2**20, transcendentals=0
        ),
        name="chain_forward",
    )(keys, values, queries, key_index, spans, gates, first_init, second_init)


def chain_backward(recall_grad, saved, spans, gates, ident):
    low1_all, low2_all, m1_all, m2_all, g1_all, g2_all, err_all, pre_all, qpre_all, keys, queries = saved
    wide = lax.axis_size("wide")
    key_turns, blocks, span, block = keys.shape
    turns = key_turns + 1
    width, hidden = low1_all.shape[1:]
    chips, rows = err_all.shape[2:4]
    n_scatter = len(Scatter.scratch(1, 8, 128))

    def kernel(*refs):
        own_hbm, q_ins, k_ins, spans_ref, gates_ref = refs[0], refs[1:5], refs[5:12], refs[12], refs[13]
        qcot_hbm, kcot_hbm, vcot_hbm, sums1_ref, sums2_ref, mg1_hbm, mg2_hbm = refs[14:21]
        rest = refs[21:]
        q_bufs, k_bufs, rest = rest[:4], rest[4:11], rest[11:]
        qbuf, low1, low2, qpre = q_bufs
        kbuf, m1, m2, g1, g2, errs, pre = k_bufs
        rall, own_hold, cf, cs, cmf, cms, w1, w2, a1, a2, c1, c2 = rest[:12]
        dh, khid, qpl, qhid, kpl, slow, sg, hk, qsave, ksave, vsave = rest[12:23]
        q_sem, k_sem, out_sem, end_sem, own_sem = rest[23:28]
        rest = rest[28:]
        lane = Lane()
        grid = Grid()
        lookup = Scatter.of(lane, rest[:n_scatter])
        qstream = Scatter.of(lane, rest[n_scatter : 2 * n_scatter])
        kstream = Scatter.of(lane, rest[2 * n_scatter : 3 * n_scatter])
        spread = Spread.of(lane, rest[3 * n_scatter : 3 * n_scatter + 5])
        gather = Gather(grid, own_hbm, rall, rest[3 * n_scatter + 5 :])

        def q_loads(turn, slot):
            return [
                pltpu.make_async_copy(source.at[turn], target.at[slot], q_sem.at[slot, i])
                for i, (source, target) in enumerate(zip(q_ins, q_bufs))
            ]

        def k_loads(turn, slot):
            return [
                pltpu.make_async_copy(source.at[turn], target.at[slot], k_sem.at[slot, i])
                for i, (source, target) in enumerate(zip(k_ins, k_bufs))
            ]

        own = pltpu.make_async_copy(own_hbm, own_hold, own_sem.at[0])
        own.start()
        grid.greet_all()()
        gather.begin()
        for copy in q_loads(turns - 1, 0) + q_loads(turns - 2, 1) + k_loads(turns - 2, 1):
            copy.start()
        own.wait()
        own_store = pltpu.make_async_copy(own_hold, rall.at[grid.wide, grid.narrow], own_sem.at[0])
        own_store.start()
        for ref in (cf, cs, cmf, cms, a1, a2):
            ref[...] = jnp.zeros_like(ref)
        gather.middle()
        own_store.wait()
        gather.finish()

        def qout(turn):
            return pltpu.make_async_copy(qsave, qcot_hbm.at[turn], out_sem.at[0])

        def kout(turn):
            return pltpu.make_async_copy(ksave, kcot_hbm.at[turn], out_sem.at[1])

        def vout(turn):
            return pltpu.make_async_copy(vsave, vcot_hbm.at[turn], out_sem.at[2])

        def finish(stream, save, out):
            save[...] = stream.total().astype(bf16)
            stream.wait_sends()
            out.start()

        def query_rows(turn, slot):
            index = spans_ref[turn]
            back = inner_right(rall[index, 0], low2[slot, :, pl.ds(0, block)])
            for b in range(1, blocks):
                back = back + inner_right(rall[index, b], low2[slot, :, pl.ds(b * block, block)])
            query_pre = qpre[slot]
            qpl[...] = (gates_ref[turn, 4] * back * silu_slope(query_pre)).astype(bf16)
            qhid[...] = (query_pre * jax.nn.sigmoid(query_pre)).astype(bf16)
            qstream.part[...] = inner_right(qpl[...], low1[slot]).astype(bf16).reshape(2, chips, rows, width)
            qstream.start_pair()

        def query_weights(turn, slot):
            index = spans_ref[turn]
            valid = gates_ref[turn, 4]
            for b in range(blocks):
                w1[pl.ds(b * block, block), :] = inner_left(qbuf[slot, b], qpl[...])
                w2[:, pl.ds(b * block, block)] = valid * inner_left(qhid[...], rall[index, b])

        def key_rows(slot):
            kstream.part[...] = (
                (inner_right(kpl[...], low1[slot]) + inner_right(slow[...], c1[slot]))
                .astype(bf16)
                .reshape(2, chips, rows, width)
            )

        for copy in q_loads(turns - 1, 0):
            copy.wait()
        query_rows(turns - 1, 0)
        query_weights(turns - 1, 0)
        reset = gates_ref[turns - 1, 3]
        for c, w, acc in ((cf, w1, a1), (cs, w2, a2)):
            acc[...] = reset * w[...]
            c[...] = (1.0 - reset) * w[...]
        qstream.take_pair()
        qstream.start_sends()

        def body(step, carry):
            turn = turns - 1 - step
            slot = lax.rem(step, 2)
            decay, moment, rate, reset = (gates_ref[turn, i] for i in range(4))
            for copy in q_loads(turn, slot) + k_loads(turn, slot):
                copy.wait()
            c1[slot] = (-rate * (cmf[...] + cf[...])).astype(bf16)
            c2[...] = (-rate * (cms[...] + cs[...])).astype(bf16)
            slope_grad = matmul(kbuf[slot, 0], c1[slot, pl.ds(0, block), :])
            for b in range(1, blocks):
                slope_grad = slope_grad + matmul(kbuf[slot, b], c1[slot, pl.ds(b * block, block), :])
            sg[...] = slope_grad
            key_pre = pre[slot, 0]
            khid[...] = (key_pre * jax.nn.sigmoid(key_pre)).astype(bf16)
            dh[...] = (slope_grad * silu_slope(key_pre)).astype(bf16)
            lookup.part[...] = (
                (matmul(khid[...], c2[...]) + matmul(dh[...], low2[slot])).astype(bf16).reshape(2, chips, rows, width)
            )
            lookup.start_pair()
            finish(qstream, qsave, qout(turn + 1))

            @pl.when(step > 2)
            def _():
                finish(kstream, ksave, kout(turn + 2))

            lookup.take_pair()
            lookup.start_sends()
            query_rows(turn, slot)

            @pl.when(step > 1)
            def _():
                key_rows(1 - slot)
                kstream.start_pair()

            @pl.when(step + 1 < turns)
            def _():
                for copy in q_loads(turn - 1, 1 - slot) + k_loads(turn - 1, 1 - slot):
                    copy.start()

            query_weights(turn, slot)
            err = errs[slot].reshape(span, width)
            hk[...] = inner_right(err, c2[...])
            w2[...] += inner_left(dh[...], err)

            def sums(first_a, first_b, second_a, second_b, row):
                sums1_ref[turn, pl.ds(row, 1), :] = jnp.sum(first_a * first_b.astype(f32), axis=0, keepdims=True)
                sums2_ref[turn, pl.ds(row, 1), :] = jnp.sum(second_a * second_b.astype(f32), axis=0, keepdims=True)

            sums(cf[...], low1[slot], cs[...], low2[slot], 0)
            sums(cmf[...] + cf[...], m1[slot], cms[...] + cs[...], m2[slot], 1)
            sums(cmf[...] + cf[...], g1[slot], cms[...] + cs[...], g2[slot], 2)
            qstream.take_pair()
            total = lookup.total()
            mine = (total / span).astype(bf16)
            spread.whole[lane.colour, lane.chip] = mine
            qout(turn + 1).wait()

            @pl.when(step > 1)
            def _():
                vout(turn + 1).wait()

            @pl.when(step > 2)
            def _():
                kout(turn + 2).wait()

            vsave[...] = mine
            vout(turn).start()
            spread.run()
            lookup.wait_sends()
            qstream.start_sends()

            @pl.when(step > 1)
            def _():
                kstream.take_pair()
                kstream.start_sends()

            out = spread.whole[...].reshape(span, width)
            hidden_back = hk[...] + inner_right(out, low2[slot])
            key_pre = pre[slot, 0]
            hidden_grad = pre[slot, 1]
            slope = silu_slope(key_pre)
            kpl[...] = (hidden_back * slope + sg[...] * hidden_grad * silu_curve(key_pre)).astype(bf16)
            slow[...] = (hidden_grad * slope).astype(bf16)

            def update(c, m, acc, grad_new, place):
                grad = (1.0 - decay) * c[place] + grad_new
                both = m[place] + c[place]
                acc[place] += reset * grad
                c[place] = (1.0 - reset) * grad
                m[place] = (1.0 - reset) * (moment * both)

            for b in range(blocks):
                place = (pl.ds(b * block, block), slice(None))
                update(cf, cmf, a1, w1[place] + inner_left(kbuf[slot, b], kpl[...]), place)
            place = (slice(None), slice(None))
            update(cs, cms, a2, w2[...] + inner_left(khid[...], out), place)
            return carry

        lax.fori_loop(1, turns, body, 0)
        tail = Scatter(
            lane,
            kstream.part,
            lookup.pair,
            lookup.half,
            lookup.got,
            (lookup.pair_send, lookup.pair_recv, lookup.send, lookup.recv),
        )
        ends = [
            pltpu.make_async_copy(a1, mg1_hbm, end_sem.at[0]),
            pltpu.make_async_copy(a2, mg2_hbm, end_sem.at[1]),
        ]
        for copy in ends:
            copy.start()
        key_rows((turns - 1) % 2)
        tail.start_pair()
        finish(qstream, qsave, qout(0))
        if turns > 2:
            finish(kstream, ksave, kout(1))
        tail.take_pair()
        tail.start_sends()
        if turns > 2:
            kout(1).wait()
        finish(tail, ksave, kout(0))
        for copy in ends + [qout(0), kout(0), vout(0)]:
            copy.wait()

    state = [(width, hidden), (hidden, width)]
    q_buffers = [((blocks, span, block), bf16)] + [(s, bf16) for s in state] + [((span, hidden), f32)]
    k_buffers = (
        [((blocks, span, block), bf16)]
        + [(s, bf16) for s in state * 2]
        + [((2, chips, rows, width), bf16), ((2, span, hidden), f32)]
    )
    out_shape = (
        [jax.ShapeDtypeStruct((turns, rows, width), bf16)]
        + [jax.ShapeDtypeStruct((key_turns, rows, width), bf16)] * 2
        + [jax.ShapeDtypeStruct((key_turns, 8, hidden), f32), jax.ShapeDtypeStruct((key_turns, 8, width), f32)]
        + [jax.ShapeDtypeStruct(s, f32) for s in state]
    )
    sem = pltpu.SemaphoreType.DMA
    scratch = (
        [pltpu.VMEM((2,) + s, t) for s, t in q_buffers + k_buffers]
        + [pltpu.VMEM((wide, blocks, span, block), bf16), pltpu.VMEM((span, block), bf16)]
        + [pltpu.VMEM(s, f32) for s in state * 4]
        + [pltpu.VMEM((2,) + state[0], bf16), pltpu.VMEM(state[1], bf16)]
        + [pltpu.VMEM((span, hidden), bf16)] * 6
        + [pltpu.VMEM((span, hidden), f32)] * 2
        + [pltpu.VMEM((rows, width), bf16)] * 3
        + [sem((2, 4)), sem((2, 7)), sem((3,)), sem((2,)), sem((1,))]
        + Scatter.scratch(chips, rows, width) * 3
        + Spread.scratch(chips, rows, width)
        + Gather.scratch()
    )
    vmem = pl.BlockSpec(memory_space=pltpu.VMEM)
    smem = pl.BlockSpec(memory_space=pltpu.SMEM)
    return pl.pallas_call(
        kernel,
        out_shape=out_shape,
        in_specs=[ANY] * 12 + [smem] * 2,
        out_specs=[ANY] * 3 + [vmem] * 2 + [ANY] * 2,
        scratch_shapes=scratch,
        compiler_params=pltpu.CompilerParams(
            collective_id=ident, has_side_effects=True, vmem_limit_bytes=62 * 1024 * 1024
        ),
        cost_estimate=pl.CostEstimate(
            flops=80 * turns * 2 * span * width * hidden, bytes_accessed=turns * 60 * 2**20, transcendentals=0
        ),
        name="chain_backward",
    )(
        recall_grad, queries, low1_all, low2_all, qpre_all, keys, m1_all, m2_all, g1_all, g2_all, err_all, pre_all,
        spans, gates,
    )


def from_behind(value, axis, steps):
    count = lax.axis_size(axis)
    first, last = (max(0, -steps), min(count, count - steps))
    return lax.ppermute(value, axis, [(source, source + steps) for source in range(first, last)])


def split_heads(values, head_size):
    return values.reshape(values.shape[:-1] + (values.shape[-1] // head_size, head_size))


def head_norm(values, head_size):
    shaped = split_heads(values, head_size)
    factor = lax.rsqrt(jnp.sum(shaped * shaped, axis=-1, keepdims=True) + eps_head)
    return (shaped * factor).reshape(values.shape)


def head_norm_back(values, upstream, head_size):
    shaped = split_heads(values, head_size)
    grad_shaped = split_heads(upstream, head_size)
    factor = lax.rsqrt(jnp.sum(shaped * shaped, axis=-1, keepdims=True) + eps_head)
    normed = shaped * factor
    inner_sum = jnp.sum(normed * grad_shaped, axis=-1, keepdims=True)
    return (factor * (grad_shaped - normed * inner_sum)).reshape(values.shape)


def rms_back(scaled, factor, upstream):
    return factor * (upstream - scaled * jnp.mean(upstream * scaled, axis=-1, keepdims=True))


def body(
    tokens,
    cotangent,
    seq_spans,
    w_query,
    w_key,
    w_value,
    conv_kernel,
    persistent,
    norm_gain,
    rate_proj,
    out_gate,
    out_proj,
    memory_in,
    memory_out,
    ffn_gain,
    ffn_gate,
    ffn_up,
    ffn_down,
):
    wide, narrow = lax.axis_size("wide"), lax.axis_size("narrow")
    devices = wide * narrow
    wide_pos, narrow_pos = lax.axis_index("wide"), lax.axis_index("narrow")
    span, width = tokens.shape
    taps = conv_kernel.shape[0]
    persist_count = persistent.shape[1]
    local_width = out_gate.shape[1]
    own_rows = span // narrow
    lanes = wide // LANE_WIDE
    chips = LANE_WIDE * narrow // 2
    shards = 2 * chips
    shard_rows = span // shards
    hidden = memory_in.shape[1] // LANE_WIDE
    score_scale = math.sqrt(HEAD)

    def shard_of(tw, tn):
        return lax.rem(tn, 2) * chips + lax.rem(tw, LANE_WIDE) * (narrow // 2) + lax.div(tn, 2)

    long_turns = min(6, wide * 5 // 8)
    turns = max(long_turns, wide - long_turns)
    seq_ends = jnp.cumsum(seq_spans)
    seq_starts = seq_ends - seq_spans
    long_start = seq_starts[jnp.argmax(seq_spans)]
    order = jnp.arange(wide, dtype=jnp.int32)
    span_first = jnp.any(seq_starts[None, :] == order[:, None], axis=1)
    is_first = span_first[wide_pos]
    in_long = (order >= long_start) & (order < long_start + long_turns)
    lane_of = jnp.where(in_long, 0, 1)
    turn_of = jnp.where(in_long, order - long_start, jnp.where(order < long_start, order, order - long_turns))
    lane_pos = wide_pos // LANE_WIDE
    turn_order = jnp.arange(turns, dtype=jnp.int32)
    rest_order = jnp.where(turn_order < long_start, turn_order, turn_order + long_turns)
    lane_spans = jnp.clip(jnp.where(lane_pos == 0, long_start + turn_order, rest_order), 0, wide - 1)
    lane_count = jnp.where(lane_pos == 0, long_turns, jnp.where(lane_pos == 1, wide - long_turns, 0))
    lane_valid = turn_order < lane_count
    lane_first = span_first[lane_spans] | ~lane_valid

    smalls = [conv_kernel, persistent, norm_gain, ffn_gain, rate_proj]
    small_sizes = [a.size for a in smalls]
    packed = jnp.concatenate([a.reshape(-1) for a in smalls])
    padded = -(-packed.size // 2048) * 2048
    packed = jnp.pad(packed, (0, padded - packed.size)).reshape(-1, 128)
    own_weights = jnp.concatenate(
        [a.reshape(a.shape[0], narrow, local_width) for a in (w_query, w_key, w_value)], 2
    ).transpose(1, 0, 2)
    memory_cols = memory_in.reshape(memory_in.shape[0], LANE_WIDE, hidden).transpose(1, 0, 2)
    memory_rows = memory_out.reshape(LANE_WIDE, hidden, memory_out.shape[1])
    small_all, weights_all, first_all, second_all = send_parameters(
        packed, own_weights, [memory_cols, memory_rows], 1
    )
    first_init = first_all.reshape(width, hidden)
    second_init = second_all.transpose(1, 0, 2).reshape(hidden, width)
    small_all = small_all.reshape(devices, padded)
    pieces, at = [], 0
    for a, size in zip(smalls, small_sizes):
        pieces.append(small_all[:, at : at + size].reshape((devices,) + a.shape))
        at += size
    kernel_all = pieces[0].transpose(1, 0, 2).reshape(taps, 3, width)
    persist_all = pieces[1].transpose(1, 2, 0, 3).reshape(2, persist_count, width)
    gain_one = pieces[2].reshape(width).astype(f32)
    gain_two = pieces[3].reshape(width).astype(f32)
    rate_f = pieces[4].reshape(width, 3).astype(f32)
    col_offset = narrow_pos * local_width

    def own_cols(values, axis):
        return lax.dynamic_slice_in_dim(values, col_offset, local_width, axis)

    def own_part(values):
        return lax.dynamic_slice_in_dim(values, narrow_pos * own_rows, own_rows, 0)

    kernel_f = own_cols(kernel_all, 2).reshape(taps, 3 * local_width).astype(f32)
    persist_f = own_cols(persist_all, 2).astype(f32)
    qkv_weights = weights_all.reshape(width, 3 * local_width)

    inputs_f = tokens.astype(f32)
    first_factor = lax.rsqrt(jnp.mean(inputs_f * inputs_f, axis=-1, keepdims=True) + eps_norm)
    first_scaled = inputs_f * first_factor
    normed = first_scaled * gain_one
    normed_low = normed.astype(bf16)
    projected = matmul(normed_low, qkv_weights)
    tail_rows = from_behind(projected[span - taps + 1 :].astype(bf16), "wide", 1).astype(f32)
    extended = jnp.concatenate([jnp.where(is_first, 0.0, tail_rows), projected], 0)
    mixed_conv = kernel_f[0] * projected
    for offset in range(1, taps):
        start_row = taps - 1 - offset
        mixed_conv = mixed_conv + kernel_f[offset] * extended[start_row : start_row + span]
    activated = jax.nn.silu(mixed_conv)
    query_act = activated[:, :local_width]
    key_act = activated[:, local_width : 2 * local_width]
    query_low = head_norm(query_act, HEAD).astype(bf16)
    key_low = head_norm(key_act, HEAD).astype(bf16)
    value_low = activated[:, 2 * local_width :].astype(bf16)
    span_mean = jnp.mean(normed, axis=0)
    gate_scale = jnp.array([decay_top, moment_top, learn_top], f32)
    gate_sig = jax.nn.sigmoid(jnp.sum(span_mean[:, None] * rate_f, axis=0))
    gate_tile = jnp.broadcast_to(jnp.pad(gate_sig * gate_scale, (0, 125))[None], (8, 128))

    key_all, value_got, gate_got = rows_to_lanes(
        key_low, value_low.reshape(shards, shard_rows, local_width), shard_of, gate_tile, 2
    )
    later = (ffn_gate, ffn_up, ffn_down, jnp.concatenate([out_gate, out_proj.T], 1))
    key_all, *later = lax.optimization_barrier((key_all,) + later)
    out_weights = lax.all_gather(later[3], "wide", axis=0, tiled=True)
    ffn_gate_cols = lax.all_gather(later[0], "wide", axis=0, tiled=True)
    ffn_up_cols = lax.all_gather(later[1], "wide", axis=0, tiled=True)
    ffn_down_rows = lax.all_gather(later[2], "wide", axis=1, tiled=True)
    gate_cols = out_weights[:, :local_width]
    proj_cols = out_weights[:, local_width:]
    gate_rows = gate_got[::narrow, 0, :3]
    lane_gates = gate_rows[lane_spans]
    first_f = lane_first.astype(f32)
    next_first = jnp.concatenate([first_f[1:], jnp.ones((1,), f32)])
    key_index = lane_spans
    if wide > 8:
        key_all, key_index = key_all[lane_spans], turn_order
    chain = chain_forward(
        key_all,
        key_index,
        value_got,
        query_low,
        lane_spans,
        jnp.concatenate([lane_gates, next_first[:, None]], 1),
        first_init,
        second_init,
        3,
    )
    recalled_lane, saved = chain[0], chain[1:]

    def by_span(lane_rows):
        spans = lane_rows[turn_of]
        return spans.reshape(wide, shard_rows, narrow, local_width).transpose(0, 2, 1, 3)

    def from_lane(got):
        got = got.reshape(lanes, LANE_WIDE, narrow // 2, 2, shard_rows, local_width)
        own = lax.dynamic_index_in_dim(got, lane_of[wide_pos], 0, keepdims=False)
        return own.transpose(2, 0, 1, 3, 4).reshape(span, local_width)

    recalled_got = exchange(
        [
            (
                by_span(recalled_lane).reshape(devices, shard_rows, local_width),
                lambda tw, tn: tw * narrow + tn,
            )
        ],
        "all",
        6,
    )[0]
    recall_low = from_lane(recalled_got)
    recall_own = recall_low.astype(f32)

    keys_all = jnp.concatenate(
        [head_norm(persist_f[0], HEAD).astype(bf16), head_norm(recall_own, HEAD).astype(bf16), key_low], 0
    )
    values_all = jnp.concatenate([persist_f[1].astype(bf16), recall_low, value_low], 0)
    query_heads = split_heads(query_low, HEAD)
    key_heads = split_heads(keys_all, HEAD)
    value_heads = split_heads(values_all, HEAD)
    key_total = keys_all.shape[0]
    row_index = lax.broadcasted_iota(jnp.int32, (span, key_total), 0)
    col_index = lax.broadcasted_iota(jnp.int32, (span, key_total), 1)
    allowed = (col_index < persist_count + span) | (col_index - persist_count - span <= row_index)

    def score_block():
        raw_scores = (
            jnp.einsum("thd,jhd->htj", query_heads, key_heads, preferred_element_type=f32) * score_scale
        )
        return jnp.where(allowed[None], raw_scores, masked_score)

    scores = score_block()
    row_top = jnp.max(scores, axis=-1, keepdims=True)
    exponent = jnp.exp(scores - row_top)
    total_sum = jnp.sum(exponent, axis=-1, keepdims=True)
    log_total = row_top + jnp.log(total_sum)
    weights_low = (exponent / total_sum).astype(bf16)
    attended = jnp.einsum("htj,jhd->thd", weights_low, value_heads, preferred_element_type=f32).reshape(
        span, local_width
    )
    gate_pre = matmul(normed_low, gate_cols)
    gate_sigmoid = jax.nn.sigmoid(gate_pre)
    gated_low = (attended * gate_sigmoid).astype(bf16)

    def by_rows(part):
        return part.astype(bf16).reshape(narrow, own_rows, width)

    tokens_own, cotangent_own = own_part(tokens), own_part(cotangent)
    rows_f32, row_f32 = ((own_rows, width), f32), ((1, width), f32)

    def scaled_of(values):
        factor = lax.rsqrt(jnp.mean(values * values, axis=-1, keepdims=True) + eps_norm)
        return values * factor, factor

    def after_branch(totals, extras):
        tokens_rows, gain = extras
        middle = tokens_rows.astype(f32) + totals[0]
        return [(scaled_of(middle)[0] * gain).astype(bf16)], [middle]

    normed_two, middle = narrow_step(
        [by_rows(inner_right(gated_low, proj_cols))],
        [tokens_own, gain_two[None]],
        after_branch,
        1,
        [rows_f32],
        7,
    )
    normed_two = normed_two.reshape(span, width)
    gate_val = matmul(normed_two, ffn_gate_cols)
    up_val = matmul(normed_two, ffn_up_cols)
    gate_silu = jax.nn.silu(gate_val)
    hidden_ffn = (gate_silu * up_val).astype(bf16)
    ffn_part = matmul(hidden_ffn, ffn_down_rows)
    down_grad = inner_left(cotangent, hidden_ffn).astype(bf16)
    hidden_grad_ffn = inner_right(cotangent, ffn_down_rows)
    gate_sig_ffn = jax.nn.sigmoid(gate_val)
    gate_grad_low = (
        hidden_grad_ffn * up_val * gate_sig_ffn * (1.0 + gate_val * (1.0 - gate_sig_ffn))
    ).astype(bf16)
    up_grad_low = (hidden_grad_ffn * gate_silu).astype(bf16)
    ffn_gate_grad = inner_left(normed_two, gate_grad_low).astype(bf16)
    ffn_up_grad = inner_left(normed_two, up_grad_low).astype(bf16)
    normed_two_part = inner_right(gate_grad_low, ffn_gate_cols) + inner_right(up_grad_low, ffn_up_cols)

    def scatter_wide(grad):
        return lax.psum_scatter(grad.astype(bf16), "wide", scatter_dimension=0, tiled=True).astype(f32)

    ffn_sums = (by_rows(ffn_part), by_rows(normed_two_part))
    ffn_sums, ffn_grads = lax.optimization_barrier((ffn_sums, (ffn_gate_grad, ffn_up_grad, down_grad)))
    ffn_gate_out, ffn_up_out, ffn_down_out = [scatter_wide(a) for a in ffn_grads]

    def after_ffn(totals, extras):
        middle_rows, cotangent_rows, gain = extras
        scaled, factor = scaled_of(middle_rows)
        grad = cotangent_rows.astype(f32) + rms_back(scaled, factor, totals[1] * gain)
        gain_part = jnp.sum(totals[1] * scaled, axis=0, keepdims=True)
        return [grad.astype(bf16), (middle_rows + totals[0]).astype(bf16)], [grad, gain_part]

    branch_low, output, middle_grad, gain_two_part = narrow_step(
        list(ffn_sums), [middle, cotangent_own, gain_two[None]], after_ffn, 2, [rows_f32, row_f32], 9
    )
    branch_low, output = branch_low.reshape(span, width), output.reshape(span, width)

    gated_grad = matmul(branch_low, proj_cols)
    attended_grad_low = (gated_grad * gate_sigmoid).astype(bf16)
    gate_pre_low = (gated_grad * attended * gate_sigmoid * (1.0 - gate_sigmoid)).astype(bf16)
    proj_grad = inner_left(branch_low, gated_low)

    weights_again = jnp.exp(score_block() - log_total)
    grad_heads = split_heads(attended_grad_low, HEAD)
    weight_grad = jnp.einsum("thd,jhd->htj", grad_heads, value_heads, preferred_element_type=f32)
    row_delta = jnp.sum(weights_again * weight_grad, axis=-1, keepdims=True)
    score_grad_low = (weights_again * (weight_grad - row_delta)).astype(bf16)
    query_att = (
        score_scale * jnp.einsum("htj,jhd->thd", score_grad_low, key_heads, preferred_element_type=f32)
    ).reshape(span, local_width)
    keys_grad = (
        score_scale * jnp.einsum("htj,thd->jhd", score_grad_low, query_heads, preferred_element_type=f32)
    ).reshape(key_total, local_width)
    values_grad = jnp.einsum(
        "htj,thd->jhd", weights_again.astype(bf16), grad_heads, preferred_element_type=f32
    ).reshape(key_total, local_width)
    recall_end = persist_count + span
    persist_part = jnp.stack(
        [head_norm_back(persist_f[0], keys_grad[:persist_count], HEAD), values_grad[:persist_count]]
    )
    recall_grad_low = (
        head_norm_back(recall_own, keys_grad[persist_count:recall_end], HEAD)
        + values_grad[persist_count:recall_end]
    ).astype(bf16)

    qcot, kcot, vcot, sums1, sums2, first_grad, second_grad = chain_backward(
        recall_grad_low,
        saved,
        lane_spans,
        jnp.concatenate([lane_gates, first_f[:, None], lane_valid.astype(f32)[:, None]], 1),
        12,
    )
    kcot, vcot = [jnp.concatenate([a, jnp.zeros_like(a[:1])], 0) for a in (kcot, vcot)]
    lane_sums = jnp.sum(sums1[:, :3], axis=2) + jnp.sum(sums2[:, :3], axis=2)
    lane_sums = jnp.pad(lane_sums, ((0, 1), (0, 0)))
    span_sums = jnp.where((lane_of == lane_pos)[:, None], lane_sums[turn_of], 0.0)
    sums_tile = jnp.pad(span_sums, ((0, 0), (0, 125)))
    cots = jnp.stack([by_span(a) for a in (qcot, kcot, vcot)], 2)
    cots_got, sums_got = exchange(
        [
            (cots.reshape(devices, 3, shard_rows, local_width), lambda tw, tn: tw * narrow + tn),
            (sums_tile, None),
        ],
        "all",
        13,
    )
    query_mem, key_mem, value_mem = [from_lane(cots_got[:, i]).astype(f32) for i in range(3)]
    gate_sums = jnp.sum(sums_got[:, :, :3], axis=0)[wide_pos] * jnp.array([-1.0, 1.0, -1.0], f32)
    first_got, second_got = exchange(
        [
            (first_grad.astype(bf16).reshape(wide, width // wide, hidden), lambda tw, tn: tw),
            (
                second_grad.astype(bf16).reshape(hidden, wide, width // wide).transpose(1, 0, 2),
                lambda tw, tn: tw,
            ),
        ],
        "wide",
        14,
    )

    def over_lanes(got):
        return jnp.sum(got.reshape((lanes, LANE_WIDE) + got.shape[1:]).astype(f32), axis=0)

    first_out = over_lanes(first_got).transpose(1, 0, 2).reshape(width // wide, LANE_WIDE * hidden)
    second_out = over_lanes(second_got).reshape(LANE_WIDE * hidden, width // wide)

    logit_grad = gate_sums * gate_scale * gate_sig * (1.0 - gate_sig)
    rate_part = span_mean[:, None] * logit_grad[None, :]
    gate_row = jnp.sum(rate_f * logit_grad[None, :], axis=1)[None, :] / span
    act_grad = jnp.concatenate(
        [
            head_norm_back(query_act, query_mem + query_att, HEAD),
            head_norm_back(key_act, key_mem + keys_grad[recall_end:], HEAD),
            values_grad[recall_end:] - value_mem,
        ],
        1,
    )
    conv_grad = act_grad * silu_slope(mixed_conv)
    kernel_rows = []
    extended_grad = jnp.zeros_like(extended)
    for offset in range(taps):
        start_row = taps - 1 - offset
        kernel_rows.append(jnp.sum(conv_grad * extended[start_row : start_row + span], axis=0))
        extended_grad = extended_grad + jnp.pad(kernel_f[offset] * conv_grad, ((start_row, offset), (0, 0)))
    tail_back = from_behind(
        jnp.where(is_first, 0.0, extended_grad[: taps - 1]).astype(bf16), "wide", -1
    ).astype(f32)
    projected_grad = extended_grad[taps - 1 :] + jnp.pad(tail_back, ((span - taps + 1, 0), (0, 0)))
    projected_low = projected_grad.astype(bf16)
    normed_part = inner_right(projected_low, qkv_weights) + inner_right(gate_pre_low, gate_cols)

    def after_all(totals, extras):
        tokens_rows, grad_rows, gain, row = extras
        scaled, factor = scaled_of(tokens_rows.astype(f32))
        normed_grad = totals[0] + row
        gain_part = jnp.sum(normed_grad * scaled, axis=0, keepdims=True)
        return [(grad_rows + rms_back(scaled, factor, normed_grad * gain)).astype(bf16)], [gain_part]

    tokens_grad, gain_one_part = narrow_step(
        [by_rows(normed_part)], [tokens_own, middle_grad, gain_one[None], gate_row], after_all, 1, [row_f32], 15
    )
    tokens_grad = tokens_grad.reshape(span, width).astype(f32)
    weight_grads = inner_left(normed_low, jnp.concatenate([projected_low, gate_pre_low], 1))
    weight_out = scatter_wide(weight_grads)
    proj_out = scatter_wide(proj_grad)

    def place_cols(piece, axis):
        full = piece.shape[:axis] + (width,) + piece.shape[axis + 1 :]
        return lax.dynamic_update_slice_in_dim(jnp.zeros(full, f32), piece, col_offset, axis)

    kernel_full = place_cols(jnp.stack(kernel_rows).reshape(taps, 3, local_width), 2).reshape(taps, 3 * width)
    persist_full = place_cols(persist_part, 2)
    rate_part = jnp.where(narrow_pos == 0, rate_part, 0.0)
    chunks = [
        kernel_full.reshape(taps, devices, -1).transpose(1, 0, 2),
        persist_full.reshape(2, persist_count, devices, -1).transpose(2, 0, 1, 3),
        gain_one_part.reshape(devices, -1),
        gain_two_part.reshape(devices, -1),
        rate_part.reshape(devices, -1, 3),
    ]
    flat = jnp.concatenate([a.reshape(devices, -1) for a in chunks], 1)
    flat_size = -(-flat.shape[1] // 1024) * 1024
    flat = jnp.pad(flat, ((0, 0), (0, flat_size - flat.shape[1]))).reshape(devices, -1, 128)
    flat_got = exchange([(flat, lambda tw, tn: tw * narrow + tn)], "all", 17)[0]
    flat_sum = jnp.sum(flat_got, axis=0).reshape(-1)
    small_outs, at = [], 0
    for a in chunks:
        size = a.size // devices
        small_outs.append(flat_sum[at : at + size].reshape(a.shape[1:]))
        at += size
    kernel_grad, persist_grad, norm_grad, ffn_gain_grad, rate_grad = small_outs
    return (
        output,
        tokens_grad,
        weight_out[:, :local_width],
        weight_out[:, local_width : 2 * local_width],
        weight_out[:, 2 * local_width : 3 * local_width],
        kernel_grad,
        persist_grad,
        norm_grad,
        rate_grad,
        weight_out[:, 3 * local_width :],
        proj_out.T,
        first_out,
        second_out,
        ffn_gain_grad,
        ffn_gate_out,
        ffn_up_out,
        ffn_down_out.T,
    )


def solution(mesh):
    rows, both, square, turned = P("wide", None), P(("wide", "narrow"), None), P("wide", "narrow"), P("narrow", "wide")
    flat, taps, heads = P(("wide", "narrow")), P(None, ("wide", "narrow")), P(None, None, ("wide", "narrow"))
    return jax.shard_map(
        body,
        mesh=mesh,
        in_specs=(rows, rows, P(), both, both, both, taps, heads, flat, both)
        + (square, turned, square, turned, flat, square, square, turned),
        out_specs=(rows, rows, square, square, square, taps, heads, flat, both)
        + (square, turned, square, turned, flat, square, square, turned),
        check_vma=False,
    )
```

time: 1170 us -> 1010 us (0.86)
  Pallas kernels: 881 us -> 751 us
  local copies, waits for them, and re-layouts: 101 us -> 80.9 us
  other arithmetic: 73.4 us -> 58.5 us
    pallas_call x13 -> x4, Pallas kernels: 355 us -> 123 us  [exchange(): pl.pallas_call(kernel, out_shape=[jax.ShapeDtypeStruct((peers,) + tuple(c...]
    pallas_call x4 -> x7, Pallas kernels: 526 us -> 627 us  [the longest x1 235 us: chain_backward(): pl.pallas_call(kernel, out_shape=out_shape, in_specs=[ANY] * 12 + [smem]...]
    gather x4 -> x0, local copies, waits for them, and re-layouts: 23.3 us -> none  [the longest x1 7.49 us: body(): recall_all[lane_spans]]
  transfers between devices with their start and end apart: 10 -> 11, of which waited for: 1 -> 2; matrix products, arithmetic and copies ran while one was open for 19% -> 14% of each run, Pallas kernels for 72% -> 60%
where the time goes in v2:
time: 1010 us; the launch traced here: 1000 us
  Pallas kernels  751 us (74%)
  local copies, waits for them, and re-layouts  80.9 us (8%)
  matrix products  72.2 us (7%)
  other arithmetic  58.5 us (6%)
  between operations  20.3 us (2%)
  waiting for transfers between devices  12 us (1%)
    pallas_call x1, Pallas kernels, chain_backward(): pl.pallas_call(kernel, out_shape=out_shape, in_specs=[ANY] * 12 + [smem]...  235 us
    pallas_call x1, Pallas kernels, chain_forward(): pl.pallas_call(kernel, out_shape=out_shape, in_specs=[ANY] * 3 + [smem] *...  200 us
    pallas_call x4, Pallas kernels, exchange(): pl.pallas_call(kernel, out_shape=[jax.ShapeDtypeStruct((peers,) + tuple(c...  123 us
    pallas_call x3, Pallas kernels, narrow_step(): pl.pallas_call(kernel, out_shape=[jax.ShapeDtypeStruct((narrow, rows, wid...  77 us
    pallas_call x1, Pallas kernels, rows_to_lanes(): pl.pallas_call(kernel, out_shape=[jax.ShapeDtypeStruct((wide, narrow) + r...  60.2 us
    pallas_call x1, Pallas kernels, send_parameters(): pl.pallas_call(kernel, out_shape=[jax.ShapeDtypeStruct((devices,) + small...  54.7 us
    unnamed x212, local copies, waits for them, and re-layouts  21.5 us
  transfers between devices with their start and end apart: 11, of which 2 were waited for; matrix products, arithmetic and copies ran while one was open for 14% of the time, Pallas kernels for 60%

profile of v2, /device:TPU:0, one launch (start us, length us, event | category | flops | bytes accessed | tf_op | source)
XLA Modules:
  0.0 1001.0 jit_solution(6243060069636243459)
XLA Ops:
  16.9 54.7 %send_parameters.1 = (bf16[32,16,128]{2,1,0:T(8,128)(2,1)}, bf16[8,4,32,768]{3,2,1,0:T(8,128)(2,1)}, bf16[8,128,256]{2,1,0:T(8,128)(2,1)}, bf16[8,256,128]{2,1,0:T(8,128)(2,1)}) custom-call(bf16[16,128]{1,0:T(8,128)(2,1)} %pad_bitcast_fusion.1.refs_0_, bf16[4,32,768]{2,1,0:T(8,128)(2,1)} %maximum_bitcast_fusion.refs_1_, bf16[4,128,256]{2,1,0:T(8,128)(2,1)} %bitcast.277, ...), custom_call_target="tpu_custom_call" | custom-call | tf_op jit(solution)/shard_map/send_parameters/pallas_call | solution.py:396
  76.4 4.6 collective-permute-start
  85.5 5.3 fusion.27
  105.4 60.2 %rows_to_lanes.1 = (bf16[8,4,512,256]{3,2,1,0:T(8,128)(2,1)}, bf16[32,32,256]{2,1,0:T(8,128)(2,1)}, f32[32,8,128]{2,1,0:T(8,128)}) custom-call(bf16[512,256]{1,0:T(8,128)(2,1)} %get-tuple-element.239.rows_ref, bf16[16,32,256]{2,1,0:T(8,128)(2,1)} %bitcast.240, f32[8,128]{1,0:T(8,128)} %broadcast_in_dim.50.tile_ref), custom_call_target="tpu_custom_call" | custom-call | tf_op jit(solution)/shard_map/rows_to_lanes/pallas_call | solution.py:458
  189.0 200.3 %chain_forward.1 = (bf16[5,32,1024]{2,1,0:T(8,128)(2,1)}, bf16[5,1024,256]{2,1,0:T(8,128)(2,1)}, bf16[5,256,1024]{2,1,0:T(8,128)(2,1)}, bf16[4,1024,256]{2,1,0:T...) custom-call(bf16[8,4,512,256]{3,2,1,0:T(8,128)(2,1)} %get-tuple-elem, ...), custom_call_target="tpu_custom_call" | custom-call | flops 53687091200 | bytes 209715200 | tf_op jit(solution)/shard_map/chain_forward/pallas_call | solution.py:1023
  391.8 15.6 %exchange_6.1 = bf16[32,32,256]{2,1,0:T(8,128)(2,1)} custom-call(bf16[32,32,256]{2,1,0:T(8,128)(2,1)} %bitcast.244), custom_call_target="tpu_custom_call" | custom-call | tf_op jit(solution)/shard_map/exchange_6/pallas_call | solution.py:87
  410.8 2.9 fusion.103
  421.6 2.6 multiply_convert_fusion.4
  425.6 22.7 %narrow_step_7.1 = (bf16[4,128,1024]{2,1,0:T(8,128)(2,1)}, f32[128,1024]{1,0:T(8,128)}) custom-call(bf16[2,2,128,1024]{3,2,1,0:T(8,128)(2,1)} %bitcast.234, bf16[128,1024]{1,0:T(8,128)(2,1)} %constant_dynamic-slice_fusion.5.refs_1_, f32[1,1024]{1,0:T(1,128)} %reshape.628.refs_2_.refs_4_), custom_call_target="tpu_custom_call" | custom-call | tf_op jit(solution)/shard_map/narrow_step_7/pallas_call | solution.py:571
  448.3 4.6 fusion.105
  452.9 4.2 fusion.104
  457.1 6.9 all-gather.11.cloned.1.call-done
  464.0 6.2 fusion.22
  471.2 2.6 convolution_convert_fusion.1
  473.7 3.8 convolution_convert_fusion.2
  477.6 4.2 convert_bitcast_fusion
  488.1 33.2 %narrow_step_9.1 = (bf16[4,128,1024]{2,1,0:T(8,128)(2,1)}, bf16[4,128,1024]{2,1,0:T(8,128)(2,1)}, f32[128,1024]{1,0:T(8,128)}, f32[1,1024]{1,0:T(1,128)}) custom-call(bf16[2,2,128,1024]{3,2,1,0:T(8,128)(2,1)} %bitcast.268, bf16[2,2,128,1024]{3,2,1,0:T(8,128)(2,1)} %bitcast.269, f32[128,1024]{1,0:T(8,128)} %get-tuple-element.83.refs_2_, ...), custom_call_target="tpu_custom_call" | custom-call | tf_op jit(solution)/shard_map/narrow_step_9/pallas_call | solution.py:571
  521.4 2.6 convolution_convert_fusion.5
  528.2 6.6 multiply_reduce_fusion
  534.8 10.3 %multiply_convert_fusion = bf16[4,512,1040]{1,2,0:T(8,128)(2,1)} fusion(f32[4,512,1040]{1,2,0:T(8,128)} %get-tuple-element.267, f32[4,512,1040]{1,2,0:T(8,128)} %copy-done.2, f32[4,512]{1,0:T(4,128)S(1)} %get-tuple-element.266, f32[4,512]{1,0:T(4,128)S(1)} %log_add_fusion), kind=kLoop, calls=%fused_computation.11 | loop fusion | flops 8519680 | bytes 21315584 | tf_op jit(solution)/shard_map/convert_element_type | solution.py:1616
  545.0 3.6 fusion.10
  548.7 5.3 fusion.11
  556.0 235.1 %chain_backward.1 = (bf16[5,32,1024]{2,1,0:T(8,128)(2,1)}, bf16[4,32,1024]{2,1,0:T(8,128)(2,1)}, bf16[4,32,1024]{2,1,0:T(8,128)(2,1)}, f32[4,8,256]{2,1,0:T(8,12...) custom-call(bf16[512,256]{1,0:T(8,128)(2,1)} %copy.312.refs_0_, ...), custom_call_target="tpu_custom_call" | custom-call | flops 107374182400 | bytes 314572800 | tf_op jit(solution)/shard_map/chain_backward/pallas_call | solution.py:1299
  791.1 4.0 copy.342
  801.4 44.3 %exchange_13.1 = (bf16[32,3,32,256]{3,2,1,0:T(8,128)(2,1)}, f32[32,8,128]{2,1,0:T(8,128)}) custom-call(bf16[32,3,32,256]{3,2,1,0:T(8,128)(2,1)} %pad_maximum_fusion.1.refs_0_, f32[8,128]{1,0:T(8,128)} %pad.48.refs_1_), custom_call_target="tpu_custom_call" | custom-call | tf_op jit(solution)/shard_map/exchange_13/pallas_call | solution.py:87
  853.8 3.2 fusion.32
  858.9 3.2 multiply_reduce_fusion.3
  865.1 3.7 collective-permute-done.1
  869.8 2.7 convolution_convert_fusion
  884.6 39.4 %exchange_14.1 = (bf16[8,128,256]{2,1,0:T(8,128)(2,1)}, bf16[8,256,128]{2,1,0:T(8,128)(2,1)}) custom-call(bf16[8,128,256]{2,1,0:T(8,128)(2,1)} %bitcast.241, bf16[8,256,128]{2,1,0:T(8,128)(2,1)} %bitcast.245), custom_call_target="tpu_custom_call" | custom-call | tf_op jit(solution)/shard_map/exchange_14/pallas_call | solution.py:87
  931.3 21.2 %narrow_step_15.1 = (bf16[4,128,1024]{2,1,0:T(8,128)(2,1)}, f32[1,1024]{1,0:T(1,128)}) custom-call(bf16[2,2,128,1024]{3,2,1,0:T(8,128)(2,1)} %bitcast.266, bf16[128,1024]{1,0:T(8,128)(2,1)} %constant_dynamic-slice_fusion.5.refs_1_, f32[128,1024]{1,0:T(8,128)} %get-tuple-element.103.refs_2_, f32[1,1024]{1,0:T(1,128)} %reshape.632.refs_3_, f32[1,1024]{1,0:T(1,128)} %bitcast.302), custom_call_target="tpu_custom_call" | custom-call | tf_op jit(solution)/shard_map/narrow_step_15/pallas_call | solution.py:571
  954.9 24.0 %exchange_17.1 = f32[32,16,128]{2,1,0:T(8,128)} custom-call(f32[32,16,128]{2,1,0:T(8,128)} %bitcast.270), custom_call_target="tpu_custom_call" | custom-call | tf_op jit(solution)/shard_map/exchange_17/pallas_call | solution.py:87
  (449 shorter events, 137.0 us)
Async XLA Ops:
  7.2 174.6 %copy-start = (bf16[512,1024]{1,0:T(8,128)(2,1)S(1)}, bf16[512,1024]{1,0:T(8,128)(2,1)}, u32[]{:S(2)}) copy-start(bf16[512,1024]{1,0:T(8,128)(2,1)} %param.21) | copy-start | bytes 3145732
  7.2 65.6 %copy-start.7 = (bf16[512,1024]{1,0:T(8,128)(2,1)S(1)}, bf16[512,1024]{1,0:T(8,128)(2,1)}, u32[]{:S(2)}) copy-start(bf16[512,1024]{1,0:T(8,128)(2,1)} %param.20) | copy-start | bytes 3145732
  7.2 9.0 copy-start.57
  7.2 9.0 copy-start.58
  7.2 414.4 %all-gather.5.cloned.1.call-start = ((), (), s32[]{:S(2)}) async-start(), calls=%async_computation.5 | async-start | bytes 1179648 | tf_op jit(solution)/shard_map/all_gather | solution.py:1469
  10.5 70.6 %copy-start.77 = (f32[512]{0:T(512)}, f32[512]{0:T(512)S(1)}, u32[]{:S(2)}) copy-start(f32[512]{0:T(512)S(1)} %add_rsqrt_fusion.4) | copy-start | bytes 6148
  72.6 8.5 copy-start.41
  72.8 348.9 %copy-start.73 = (f32[1024]{0:T(1024)}, f32[1024]{0:T(1024)S(1)}, u32[]{:S(2)}) copy-start(f32[1024]{0:T(1024)S(1)} %reshape.624) | copy-start | bytes 12292
  72.8 8.7 copy-start.95
  72.8 8.9 copy-start.55
  76.4 8.4 collective-permute-start
  94.0 8.9 copy-start.51
  104.7 81.9 %copy-start.27 = (bf16[512,256]{1,0:T(8,128)(2,1)}, bf16[512,256]{1,0:T(8,128)(2,1)S(1)}, u32[]{:S(2)}) copy-start(bf16[512,256]{1,0:T(8,128)(2,1)S(1)} %get-tuple-element.238.refs_2_) | copy-start | bytes 786436
  105.4 77.2 %copy-start.39 = (bf16[8,256,128]{2,1,0:T(8,128)(2,1)S(1)}, bf16[8,256,128]{2,1,0:T(8,128)(2,1)}, u32[]{:S(2)}) copy-start(bf16[8,256,128]{2,1,0:T(8,128)(2,1)} %get-tuple-element.74) | copy-start | bytes 1572868
  165.6 282.8 %all-gather.9.cloned.1.call-start = ((), (), s32[]{:S(2)}) async-start(), calls=%async_computation.7 | async-start | bytes 2359296 | tf_op jit(solution)/shard_map/all_gather | solution.py:1471
  166.3 286.6 %all-gather.7.cloned.1.call-start = ((), (), s32[]{:S(2)}) async-start(), calls=%async_computation.6 | async-start | bytes 2359296 | tf_op jit(solution)/shard_map/all_gather | solution.py:1470
  176.4 8.6 copy-start.19
  176.5 9.3 copy-start.18
  179.4 209.9 %copy-start.75 = (s32[1024]{0:T(1024)}, s32[1024]{0:T(1024)S(1)}, u32[]{:S(2)}) copy-start(s32[1024]{0:T(1024)S(1)} %pad_clamp_fusion) | copy-start | bytes 12292
  182.5 206.8 %copy-start.71 = (f32[16,4]{0,1:T(4,128)}, f32[16,4]{0,1:T(4,128)S(1)}, u32[]{:S(2)}) copy-start(f32[16,4]{0,1:T(4,128)S(1)} %add_rsqrt_fusion.3) | copy-start | bytes 772
  188.2 275.9 %all-gather.11.cloned.1.call-start = ((), (), s32[]{:S(2)}) async-start(), calls=%async_computation.8 | async-start | bytes 2359296 | tf_op jit(solution)/shard_map/all_gather | solution.py:1472
  391.8 17.3 %copy-start.34 = (bf16[512,256]{0,1:T(8,128)(2,1)S(1)}, bf16[512,256]{0,1:T(8,128)(2,1)}, u32[]{:S(2)}) copy-start(bf16[512,256]{0,1:T(8,128)(2,1)} %copy.301) | copy-start | bytes 786436
  391.8 17.4 %copy-start.42 = (bf16[1,16,256]{1,2,0:T(8,128)(2,1)S(1)}, bf16[1,16,256]{1,2,0:T(8,128)(2,1)}, u32[]{:S(2)}) copy-start(bf16[1,16,256]{1,2,0:T(8,128)(2,1)} %get-tuple-element.245) | copy-start | bytes 24580
  409.1 575.2 %reduce-scatter.10.cloned.1.call-start = ((), (), s32[]{:S(2)}) async-start(), calls=%async_computation.10 | async-start | bytes 589824 | tf_op jit(solution)/shard_map/reduce_scatter | solution.py:1589
  524.0 461.9 %reduce-scatter.14.cloned.1.call-start = ((), (), s32[]{:S(2)}) async-start(), calls=%async_computation.12 | async-start | bytes 2359296 | tf_op jit(solution)/shard_map/reduce_scatter | solution.py:1589
  524.6 463.1 %reduce-scatter.12.cloned.1.call-start = ((), (), s32[]{:S(2)}) async-start(), calls=%async_computation.11 | async-start | bytes 2359296 | tf_op jit(solution)/shard_map/reduce_scatter | solution.py:1589
  555.9 433.6 %reduce-scatter.16.cloned.1.call-start = ((), (), s32[]{:S(2)}) async-start(), calls=%async_computation.13 | async-start | bytes 2359296
  795.2 196.3 %reduce-scatter.8.cloned.1.call-start = ((), (), s32[]{:S(2)}) async-start(), calls=%async_computation.9 | async-start | bytes 2359296 | tf_op jit(solution)/shard_map/reduce_scatter | solution.py:1589
  863.3 5.5 collective-permute-start.1
  884.6 41.9 %copy-start.13 = (f32[1024,3]{1,0:T(8,128)S(1)}, f32[1024,3]{1,0:T(8,128)}, u32[]{:S(2)}) copy-start(f32[1024,3]{1,0:T(8,128)} %copy-done.12) | copy-start | bytes 36868
  929.3 24.7 %copy-start.45 = (f32[32,384]{1,0:T(8,128)S(1)}, f32[32,384]{1,0:T(8,128)}, u32[]{:S(2)}) copy-start(f32[32,384]{1,0:T(8,128)} %reshape.610) | copy-start | bytes 147460
  952.5 30.1 %copy-start.26 = (bf16[4,128,1024]{2,1,0:T(8,128)(2,1)S(1)}, bf16[4,128,1024]{2,1,0:T(8,128)(2,1)}, u32[]{:S(2)}) copy-start(bf16[4,128,1024]{2,1,0:T(8,128)(2,1)} %get-tuple-element.105) | copy-start | bytes 3145732
  (80 other events, 271.1 us)
Sparse Core Ops, SparseCore 0:
  165.7 54.7 all-gather.4
  222.6 63.7 all-gather.8
  288.5 64.8 all-gather.6
  409.2 54.7 all-gather.10
  524.2 66.1 reduce-scatter.9
  594.1 81.2 reduce-scatter.13
  679.3 88.8 reduce-scatter.11
  795.3 99.5 reduce-scatter.15
  898.9 84.2 reduce-scatter.7

commit v3 on v2

--- a/solution.py
+++ b/solution.py
@@ -26,74 +26,6 @@
     return pltpu.make_async_remote_copy(
         src_ref=src, dst_ref=dst, send_sem=send, recv_sem=recv, device_id=device, device_id_type=MESH
     )
-
-
-def exchange(arrays, axes, ident):
-    wide, narrow = lax.axis_size("wide"), lax.axis_size("narrow")
-    peers = {"all": wide * narrow, "wide": wide, "narrow": narrow}[axes]
-    picks = [pick for _, pick in arrays]
-    operands = [array for array, _ in arrays]
-    chunks = [a.shape if pick is None else a.shape[1:] for a, pick in arrays]
-    count = len(arrays)
-
-    def kernel(*refs):
-        ins, outs, holds = refs[:count], refs[count : 2 * count], refs[2 * count : 3 * count]
-        send_sem, recv_sem, local_sem = refs[3 * count :]
-        my_wide, my_narrow = lax.axis_index("wide"), lax.axis_index("narrow")
-        me = {"all": my_wide * narrow + my_narrow, "wide": my_wide, "narrow": my_narrow}[axes]
-
-        def place(step):
-            target = lax.rem(me + step, peers)
-            if axes == "all":
-                return lax.div(target, narrow), lax.rem(target, narrow)
-            return (target, my_narrow) if axes == "wide" else (my_wide, target)
-
-        barrier = pltpu.get_barrier_semaphore()
-
-        def greet(step, carry):
-            pl.semaphore_signal(barrier, inc=1, device_id=place(step), device_id_type=MESH)
-            return carry
-
-        lax.fori_loop(1, peers, greet, 0)
-
-        def chunk(index, where):
-            return ins[index] if picks[index] is None else ins[index].at[picks[index](*where)]
-
-        own = [
-            pltpu.make_async_copy(chunk(i, (my_wide, my_narrow)), holds[i], local_sem.at[i]) for i in range(count)
-        ]
-        for copy in own:
-            copy.start()
-        pl.semaphore_wait(barrier, peers - 1)
-
-        def send(step, carry):
-            where = place(step)
-            for i in range(count):
-                remote(chunk(i, where), outs[i].at[me], send_sem.at[i], recv_sem.at[i], where).start()
-            return carry
-
-        lax.fori_loop(1, peers, send, 0)
-        for i in range(count):
-            own[i].wait()
-            back = pltpu.make_async_copy(holds[i], outs[i].at[me], local_sem.at[i])
-            back.start()
-            back.wait()
-        for i in range(count):
-            others = outs[i].at[pl.ds(0, peers - 1)]
-            whole = remote(others, others, send_sem.at[i], recv_sem.at[i], place(1))
-            whole.wait_send()
-            whole.wait_recv()
-
-    return pl.pallas_call(
-        kernel,
-        out_shape=[jax.ShapeDtypeStruct((peers,) + tuple(c), a.dtype) for a, c in zip(operands, chunks)],
-        in_specs=[ANY] * count,
-        out_specs=[ANY] * count,
-        scratch_shapes=[pltpu.VMEM(tuple(c), a.dtype) for a, c in zip(operands, chunks)]
-        + [pltpu.SemaphoreType.DMA((count,))] * 3,
-        compiler_params=pltpu.CompilerParams(collective_id=ident, has_side_effects=True),
-        name=f"exchange_{ident}",
-    )(*operands)
 
 
 class Grid:
@@ -585,6 +517,212 @@
     )(*parts, *extras)
 
 
+def last_step(part, extras, work, grads, chunks, flat, ident):
+    narrow, rows, width = part.shape
+    wide = lax.axis_size("wide")
+    devices = wide * narrow
+    ys = narrow // 2
+    zs = 4 if wide % 4 == 0 else 1
+    xs = wide // zs
+    lanes = wide // LANE_WIDE
+    extra_count = len(extras)
+    part = part.reshape(ys, 2, rows, width)
+    own_grad = grads.shape[1:]
+    grads = grads.reshape((zs, xs) + own_grad)
+    first_shape, second_shape, flat_shape = chunks[0].shape[1:], chunks[1].shape[1:], flat.shape[1:]
+
+    def kernel(*refs):
+        part_ref, grads_ref, first_ref, second_ref, flat_ref = refs[:5]
+        extra_refs, refs = refs[5 : 5 + extra_count], refs[5 + extra_count :]
+        spread_ref, grads_out, first_out, second_out, flat_out, row_out, refs = refs[:6] + (refs[6:],)
+        mine, pair, half, got, rowbuf, rowtile, rowgot, refs = refs[:7] + (refs[7:],)
+        gown, gx, ghalf, gz, fgot, sgot, flatgot, refs = refs[:7] + (refs[7:],)
+        load_sem, pair_sem, y_send, y_recv, s_send, s_recv, p_send, p_recv, refs = refs[:8] + (refs[8:],)
+        gx_send, gx_recv, gz_send, gz_recv, c_send, c_recv, all_send, all_recv = refs
+        g = Grid()
+        me = g.wide * narrow + g.narrow
+        wait_all = g.greet_all()
+        loads = [
+            pltpu.make_async_copy(part_ref.at[:, g.c], mine, load_sem.at[0]),
+            pltpu.make_async_copy(grads_ref.at[:, g.x], gown, load_sem.at[1]),
+            pltpu.make_async_copy(first_ref.at[g.wide], fgot.at[g.wide], load_sem.at[2]),
+            pltpu.make_async_copy(second_ref.at[g.wide], sgot.at[g.wide], load_sem.at[3]),
+            pltpu.make_async_copy(flat_ref.at[me], flatgot.at[me], load_sem.at[4]),
+        ]
+        for copy in loads:
+            copy.start()
+        wait_all()
+        pair_copy = remote(part_ref.at[:, 1 - g.c], pair, pair_sem.at[0], pair_sem.at[1], g.partner)
+        pair_copy.start()
+        sends = []
+        order = g.z_others()[::-1] + [g.z]
+        for z in order:
+            for i, x in enumerate(g.x_others()):
+                copy = remote(
+                    grads_ref.at[z, x],
+                    gx.at[g.x, z],
+                    gx_send.at[i, z],
+                    gx_recv.at[g.x, z],
+                    g.device(g.z, x, g.y, g.c),
+                )
+                copy.start()
+                sends.append(copy)
+        for s in range(1, wide):
+            target = lax.rem(g.wide + s, wide)
+            for i, (source, place) in enumerate(((first_ref, fgot), (second_ref, sgot))):
+                copy = remote(
+                    source.at[target],
+                    place.at[g.wide],
+                    c_send.at[i, s],
+                    c_recv.at[i, g.wide],
+                    (target, g.narrow),
+                )
+                copy.start()
+                sends.append(copy)
+
+        def send_flat(step, carry):
+            target = lax.rem(me + step, devices)
+            where = lax.div(target, narrow), lax.rem(target, narrow)
+            remote(flat_ref.at[target], flatgot.at[me], all_send.at[0], all_recv.at[0], where).start()
+            return carry
+
+        lax.fori_loop(1, devices, send_flat, 0)
+        loads[0].wait()
+        pair_copy.wait()
+        half[...] = (mine[...].astype(f32) + pair[...].astype(f32)).astype(bf16)
+        for s, y in enumerate(g.y_others()):
+            copy = remote(half.at[y], got.at[g.y], y_send.at[s], y_recv.at[g.y], g.device(g.z, g.x, y, g.c))
+            copy.start()
+            sends.append(copy)
+        for copy in loads[1:]:
+            copy.wait()
+
+        def grad_along_z(z):
+            total = gown[z].astype(f32)
+            for x in g.x_others():
+                place = gx.at[x, z]
+                remote(place, place, gx_send.at[0, 0], gx_recv.at[x, z], g.partner).wait_recv()
+                total = total + gx[x, z].astype(f32)
+            ghalf[z] = total.astype(bf16)
+
+        for i, z in enumerate(order[:-1]):
+            grad_along_z(z)
+            copy = remote(
+                ghalf.at[z], gz.at[g.z], gz_send.at[i], gz_recv.at[g.z], g.device(z, g.x, g.y, g.c)
+            )
+            copy.start()
+            sends.append(copy)
+            if i == 0:
+                total = half[g.y].astype(f32)
+                for y in g.y_others():
+                    remote(got.at[y], got.at[y], y_send.at[0], y_recv.at[y], g.partner).wait_recv()
+                    total = total + got[y].astype(f32)
+                spreads, locals_out = work([total], [ref[...] for ref in extra_refs])
+                rowbuf[...] = spreads[0]
+                for j in range(8):
+                    rowtile[pl.ds(j, 1), :] = locals_out[0][:, j * width // 8 : (j + 1) * width // 8]
+                for s, y in enumerate(g.y_others()):
+                    copy = remote(
+                        rowbuf,
+                        spread_ref.at[g.narrow],
+                        s_send.at[s],
+                        s_recv.at[g.y],
+                        g.device(g.z, g.x, y, g.c),
+                    )
+                    copy.start()
+                    sends.append(copy)
+                copy = remote(rowbuf, spread_ref.at[g.narrow], p_send.at[g.y], p_recv.at[g.y], g.partner)
+                copy.start()
+                sends.append(copy)
+                own = pltpu.make_async_copy(rowbuf, spread_ref.at[g.narrow], load_sem.at[0])
+                own.start()
+
+                def send_row(step, carry):
+                    target = lax.rem(me + step, devices)
+                    where = lax.div(target, narrow), lax.rem(target, narrow)
+                    remote(rowtile, rowgot.at[me], all_send.at[1], all_recv.at[1], where).start()
+                    return carry
+
+                lax.fori_loop(1, devices, send_row, 0)
+                rowgot[me] = rowtile[...]
+        for y in g.y_others():
+            there = spread_ref.at[2 * y + g.c]
+            remote(there, there, s_send.at[0], s_recv.at[y], g.partner).wait_recv()
+            copy = remote(there, there, p_send.at[y], p_recv.at[y], g.partner)
+            copy.start()
+            sends.append(copy)
+        grad_along_z(g.z)
+        for s in range(1, wide):
+            source = lax.rem(g.wide + s, wide)
+            for i, place in enumerate((fgot, sgot)):
+                there = place.at[source]
+                remote(there, there, c_send.at[i, 0], c_recv.at[i, source], g.partner).wait_recv()
+        for p in range(LANE_WIDE):
+            first_sum, second_sum = fgot[p].astype(f32), sgot[p].astype(f32)
+            for lane in range(1, lanes):
+                first_sum = first_sum + fgot[lane * LANE_WIDE + p].astype(f32)
+                second_sum = second_sum + sgot[lane * LANE_WIDE + p].astype(f32)
+            first_out[:, p * first_shape[1] : (p + 1) * first_shape[1]] = first_sum
+            second_out[p * second_shape[0] : (p + 1) * second_shape[0], :] = second_sum
+        total = ghalf[g.z].astype(f32)
+        for z in order[:-1]:
+            place = gz.at[z]
+            remote(place, place, gz_send.at[0], gz_recv.at[z], g.partner).wait_recv()
+            total = total + gz[z].astype(f32)
+        grads_out[...] = total
+        for i, place in enumerate((flatgot, rowgot)):
+            others = place.at[pl.ds(0, devices - 1)]
+            whole = remote(others, others, all_send.at[i], all_recv.at[i], g.partner)
+            whole.wait_send()
+            whole.wait_recv()
+        flat_out[...] = jnp.sum(flatgot[...], axis=0)
+        row_out[...] = jnp.sum(rowgot[...], axis=0)
+        for y in range(ys):
+            there = spread_ref.at[2 * y + 1 - g.c]
+            remote(there, there, s_send.at[0], p_recv.at[y], g.partner).wait_recv()
+        for copy in sends:
+            copy.wait_send()
+        own.wait()
+
+    sem = pltpu.SemaphoreType.DMA
+    vmem = pl.BlockSpec(memory_space=pltpu.VMEM)
+    return pl.pallas_call(
+        kernel,
+        out_shape=[
+            jax.ShapeDtypeStruct((narrow, rows, width), bf16),
+            jax.ShapeDtypeStruct(own_grad, f32),
+            jax.ShapeDtypeStruct((first_shape[0], LANE_WIDE * first_shape[1]), f32),
+            jax.ShapeDtypeStruct((LANE_WIDE * second_shape[0], second_shape[1]), f32),
+            jax.ShapeDtypeStruct(flat_shape, f32),
+            jax.ShapeDtypeStruct((8, width // 8), f32),
+        ],
+        in_specs=[ANY] * 5 + [vmem] * extra_count,
+        out_specs=[ANY] + [vmem] * 5,
+        scratch_shapes=[pltpu.VMEM((ys, rows, width), bf16)] * 4
+        + [pltpu.VMEM((rows, width), bf16)]
+        + [pltpu.VMEM((8, width // 8), f32), pltpu.VMEM((devices, 8, width // 8), f32)]
+        + [
+            pltpu.VMEM((zs,) + own_grad, bf16),
+            pltpu.VMEM((xs, zs) + own_grad, bf16),
+            pltpu.VMEM((zs,) + own_grad, bf16),
+            pltpu.VMEM((zs,) + own_grad, bf16),
+            pltpu.VMEM((wide,) + first_shape, bf16),
+            pltpu.VMEM((wide,) + second_shape, bf16),
+            pltpu.VMEM((devices,) + flat_shape, f32),
+        ]
+        + [sem((5,)), sem((2,))]
+        + [sem((ys,))] * 6
+        + [sem((xs, zs))] * 2
+        + [sem((zs,))] * 2
+        + [sem((2, wide))] * 2
+        + [sem((2,))] * 2,
+        compiler_params=pltpu.CompilerParams(
+            collective_id=ident, has_side_effects=True, vmem_limit_bytes=48 * 1024 * 1024
+        ),
+        name="last_step",
+    )(part, grads, chunks[0], chunks[1], flat, *extras)
+
+
 def matmul(left_side, right_side):
     return jnp.dot(left_side, right_side, preferred_element_type=jnp.float32)
 
@@ -749,12 +887,103 @@
             self.pair_copy(chip, lane.colour).wait_send()
 
 
-def chain_forward(keys, key_index, values, queries, spans, gates, first_init, second_init, ident):
+class Plan:
+    def __init__(self, spans_ref, gates_ref, count):
+        self.wide = lax.axis_size("wide")
+        self.long = min(6, self.wide * 5 // 8)
+        self.gates = gates_ref
+        lengths = [spans_ref[i] for i in range(count)]
+        self.starts, at = [], 0
+        for length in lengths:
+            self.starts.append(at)
+            at = at + length
+        longest, self.start = lengths[0], 0
+        for i in range(1, count):
+            more = lengths[i] > longest
+            longest = jnp.where(more, lengths[i], longest)
+            self.start = jnp.where(more, self.starts[i], self.start)
+        self.lane = lax.div(lax.axis_index("wide"), LANE_WIDE)
+
+    def span(self, turn):
+        rest = jnp.where(turn < self.start, turn, turn + self.long)
+        return jnp.clip(jnp.where(self.lane == 0, self.start + turn, rest), 0, self.wide - 1)
+
+    def valid(self, turn):
+        count = jnp.where(self.lane == 0, self.long, jnp.where(self.lane == 1, self.wide - self.long, 0))
+        return jnp.where(turn < count, 1.0, 0.0)
+
+    def first(self, turn):
+        span = self.span(turn)
+        found = jnp.where(span == self.starts[0], 1.0, 0.0)
+        for start in self.starts[1:]:
+            found = jnp.maximum(found, jnp.where(span == start, 1.0, 0.0))
+        return jnp.maximum(found, 1.0 - self.valid(turn))
+
+    def rates(self, turn):
+        span = self.span(turn)
+        return self.gates[span, 0], self.gates[span, 1], self.gates[span, 2]
+
+    def lane_of(self, span):
+        inside = (span >= self.start) & (span < self.start + self.long)
+        return jnp.where(inside, 0, 1)
+
+    def turn_of(self, span):
+        inside = (span >= self.start) & (span < self.start + self.long)
+        outside = jnp.where(span < self.start, span, span - self.long)
+        return jnp.where(inside, span - self.start, outside)
+
+
+class Deliver:
+    def __init__(self, grid, plan, chips, out, got, sems):
+        self.grid, self.plan, self.chips, self.out, self.got = grid, plan, chips, out, got
+        self.send, self.recv = sems
+        self.wide, self.narrow = lax.axis_size("wide"), lax.axis_size("narrow")
+        self.me = grid.wide * self.narrow + grid.narrow
+
+    @staticmethod
+    def scratch(kinds, rows, block):
+        devices = lax.axis_size("wide") * lax.axis_size("narrow")
+        return [pltpu.VMEM((devices, kinds, rows, block), bf16)] * 2 + [pltpu.SemaphoreType.DMA((1,))] * 2
+
+    def start(self, kinds):
+        block = self.out.shape[3]
+        for span in range(self.wide):
+            turn = self.plan.turn_of(span)
+            for i, kind in enumerate(kinds):
+                lane_rows = kind[turn]
+                for n in range(self.narrow):
+                    self.out[span * self.narrow + n, i] = lane_rows[:, n * block : (n + 1) * block]
+
+        def push(step, carry):
+            target = lax.rem(self.me + step, self.wide * self.narrow)
+            where = lax.div(target, self.narrow), lax.rem(target, self.narrow)
+            remote(self.out.at[target], self.got.at[self.me], self.send.at[0], self.recv.at[0], where).start()
+            return carry
+
+        lax.fori_loop(1, self.wide * self.narrow, push, 0)
+        self.got[self.me] = self.out[self.me]
+
+    def finish(self, result):
+        others = self.got.at[pl.ds(0, self.wide * self.narrow - 1)]
+        whole = remote(others, others, self.send.at[0], self.recv.at[0], self.grid.partner)
+        whole.wait_send()
+        whole.wait_recv()
+        base = self.plan.lane_of(self.grid.wide) * LANE_WIDE
+        ys = self.narrow // 2
+        for p in range(LANE_WIDE):
+            for y in range(ys):
+                for colour in range(2):
+                    source = (base + p) * self.narrow + 2 * y + colour
+                    for i in range(result.shape[0]):
+                        result[i, colour, p * ys + y] = self.got[source, i]
+
+
+def chain_forward(keys, values, queries, lengths, gates, turns, first_init, second_init, ident):
     wide = lax.axis_size("wide")
     blocks, span, block = keys.shape[1:]
     width, hidden = first_init.shape
     rows = values.shape[1]
-    turns = spans.shape[0]
+    sequences = lengths.shape[0]
     key_turns = turns - 1
     per_turn = 3 if turns <= 5 else 1
     first_left = per_turn * (key_turns - 3)
@@ -764,19 +993,22 @@
     n_scatter = len(Scatter.scratch(1, 8, 128))
 
     def kernel(*refs):
-        keys_hbm, values_hbm, own_hbm, index_ref, spans_ref, gates_ref, first_hbm, second_hbm = refs[:8]
-        recalled_hbm, low1_hbm, low2_hbm, m1_hbm, m2_hbm, g1_hbm, g2_hbm = refs[8:15]
-        err_hbm, pre_hbm, qpre_hbm, klane_hbm, qlane_hbm = refs[15:20]
-        rest = refs[20:]
+        keys_hbm, values_hbm, own_hbm, lengths_ref, gates_ref, first_hbm, second_hbm = refs[:7]
+        recalled_hbm, low1_hbm, low2_hbm, m1_hbm, m2_hbm, g1_hbm, g2_hbm = refs[7:14]
+        err_hbm, pre_hbm, qpre_hbm, klane_hbm, qlane_hbm = refs[14:19]
+        rest = refs[19:]
         kall, qall, vall, kcur, qcur, i1, i2, s1, s2, m1, m2, low1, low2, mb1, mb2, gb1, gb2 = rest[:17]
         pre, qpre, khid, rec, qpart, qpair, qhalf, qgot, own_hold = rest[17:26]
         in_sem, out_sem, q_sem, q_pair_send, q_pair_recv, q_send, q_recv = rest[26:33]
         rest = rest[33:]
         lane = Lane()
         grid = Grid()
+        plan = Plan(lengths_ref, gates_ref, sequences)
         lookup = Scatter.of(lane, rest[:n_scatter])
         error = Spread.of(lane, rest[n_scatter : n_scatter + 5])
-        gather = Gather(grid, own_hbm, qall, rest[n_scatter + 5 :])
+        gather = Gather(grid, own_hbm, qall, rest[n_scatter + 5 : n_scatter + 9])
+        deliver = Deliver(grid, plan, chips, *rest[n_scatter + 9 : n_scatter + 11], rest[n_scatter + 11 : n_scatter + 13])
+        result = rest[n_scatter + 13]
 
         def recall(q, slot):
             sems = q_pair_send.at[pl.ds(q, 1)], q_pair_recv.at[pl.ds(q, 1)], q_send.at[q], q_recv.at[q]
@@ -841,7 +1073,7 @@
                 settle()
             elif waits is not False:
                 pl.when(waits)(settle)
-            index = spans_ref[q]
+            index = plan.span(q)
             for b in range(blocks):
                 qcur[slot, b] = qall[index, b]
             query_pre = lookup_blocks(qcur.at[slot], low1.at[q])
@@ -853,14 +1085,14 @@
             recall(q, slot).start_pair()
 
         def turn_body(turn, carry):
-            index, place = spans_ref[turn], index_ref[turn]
+            index = plan.span(turn)
             if stream_keys:
                 one = pltpu.make_async_copy(keys_hbm.at[turn], kcur, in_sem.at[2])
                 one.start()
                 one.wait()
             else:
                 for b in range(blocks):
-                    kcur[b] = kall[place, b]
+                    kcur[b] = kall[index, b]
             for copy in state_saves(turn):
                 copy.start()
             key_pre = lookup_blocks(kcur, low1.at[turn])
@@ -907,7 +1139,8 @@
             hidden_grad = inner_right(err, low2[turn])
             pre[1] = hidden_grad
             slope = (hidden_grad * silu_slope(pre[0])).astype(bf16)
-            decay, moment, rate, reset = (gates_ref[turn, i] for i in range(4))
+            decay, moment, rate = plan.rates(turn)
+            reset = plan.first(turn + 1)
             for copy in state_saves(turn):
                 copy.wait()
             following = jnp.minimum(turn + 1, turns - 1)
@@ -973,19 +1206,21 @@
         stream.start_sends()
         for q in range(turns):
             rec[q] = recall(q, q % slots).total().astype(bf16)
-        last = pltpu.make_async_copy(rec, recalled_hbm, out_sem.at[2])
-        last.start()
+        deliver.start([rec])
         for q in range(turns - slots, turns):
             recall(q, q % slots).wait_sends()
         for q in range(turns - slots, turns):
             for copy in query_saves(q, q % slots):
                 copy.wait()
+        deliver.finish(result)
+        last = pltpu.make_async_copy(result.at[0], recalled_hbm, out_sem.at[2])
+        last.start()
         for copy in ends + [last]:
             copy.wait()
 
     state = [(width, hidden), (hidden, width)]
     out_shape = (
-        [jax.ShapeDtypeStruct((turns, rows, width), bf16)]
+        [jax.ShapeDtypeStruct((2, chips, rows, block), bf16)]
         + [jax.ShapeDtypeStruct((turns,) + s, bf16) for s in state]
         + [jax.ShapeDtypeStruct((key_turns,) + s, bf16) for s in state * 2]
         + [
@@ -1018,12 +1253,14 @@
         + Scatter.scratch(chips, rows, width)
         + Spread.scratch(chips, rows, width)
         + Gather.scratch()
+        + Deliver.scratch(1, rows, block)
+        + [pltpu.VMEM((1, 2, chips, rows, block), bf16)]
     )
     smem = pl.BlockSpec(memory_space=pltpu.SMEM)
     return pl.pallas_call(
         kernel,
         out_shape=out_shape,
-        in_specs=[ANY] * 3 + [smem] * 3 + [ANY] * 2,
+        in_specs=[ANY] * 3 + [smem] * 2 + [ANY] * 2,
         out_specs=[ANY] * len(out_shape),
         scratch_shapes=scratch,
         compiler_params=pltpu.CompilerParams(
@@ -1033,12 +1270,13 @@
             flops=40 * turns * 2 * span * width * hidden, bytes_accessed=turns * 40 * 2**20, transcendentals=0
         ),
         name="chain_forward",
-    )(keys, values, queries, key_index, spans, gates, first_init, second_init)
-
-
-def chain_backward(recall_grad, saved, spans, gates, ident):
+    )(keys, values, queries, lengths, gates, first_init, second_init)
+
+
+def chain_backward(recall_grad, saved, lengths, gates, ident):
     low1_all, low2_all, m1_all, m2_all, g1_all, g2_all, err_all, pre_all, qpre_all, keys, queries = saved
     wide = lax.axis_size("wide")
+    devices = wide * lax.axis_size("narrow")
     key_turns, blocks, span, block = keys.shape
     turns = key_turns + 1
     width, hidden = low1_all.shape[1:]
@@ -1046,23 +1284,26 @@
     n_scatter = len(Scatter.scratch(1, 8, 128))
 
     def kernel(*refs):
-        own_hbm, q_ins, k_ins, spans_ref, gates_ref = refs[0], refs[1:5], refs[5:12], refs[12], refs[13]
-        qcot_hbm, kcot_hbm, vcot_hbm, sums1_ref, sums2_ref, mg1_hbm, mg2_hbm = refs[14:21]
-        rest = refs[21:]
+        own_hbm, q_ins, k_ins, lengths_ref, gates_ref = refs[0], refs[1:5], refs[5:12], refs[12], refs[13]
+        cots_hbm, sums_out, mg1_hbm, mg2_hbm = refs[14:18]
+        rest = refs[18:]
         q_bufs, k_bufs, rest = rest[:4], rest[4:11], rest[11:]
         qbuf, low1, low2, qpre = q_bufs
         kbuf, m1, m2, g1, g2, errs, pre = k_bufs
         rall, own_hold, cf, cs, cmf, cms, w1, w2, a1, a2, c1, c2 = rest[:12]
-        dh, khid, qpl, qhid, kpl, slow, sg, hk, qsave, ksave, vsave = rest[12:23]
-        q_sem, k_sem, out_sem, end_sem, own_sem = rest[23:28]
-        rest = rest[28:]
+        dh, khid, qpl, qhid, kpl, slow, sg, hk, qcots, kcots, vcots, sumrows, tile, mb1, mb2, result = rest[12:28]
+        q_sem, k_sem, end_sem, own_sem, tile_send, tile_recv = rest[28:34]
+        rest = rest[34:]
         lane = Lane()
         grid = Grid()
+        plan = Plan(lengths_ref, gates_ref, lengths.shape[0])
         lookup = Scatter.of(lane, rest[:n_scatter])
         qstream = Scatter.of(lane, rest[n_scatter : 2 * n_scatter])
         kstream = Scatter.of(lane, rest[2 * n_scatter : 3 * n_scatter])
         spread = Spread.of(lane, rest[3 * n_scatter : 3 * n_scatter + 5])
-        gather = Gather(grid, own_hbm, rall, rest[3 * n_scatter + 5 :])
+        gather = Gather(grid, own_hbm, rall, rest[3 * n_scatter + 5 : 3 * n_scatter + 9])
+        rest = rest[3 * n_scatter + 9 :]
+        deliver = Deliver(grid, plan, chips, *rest[:2], rest[2:4])
 
         def q_loads(turn, slot):
             return [
@@ -1091,34 +1332,28 @@
         own_store.wait()
         gather.finish()
 
-        def qout(turn):
-            return pltpu.make_async_copy(qsave, qcot_hbm.at[turn], out_sem.at[0])
-
-        def kout(turn):
-            return pltpu.make_async_copy(ksave, kcot_hbm.at[turn], out_sem.at[1])
-
-        def vout(turn):
-            return pltpu.make_async_copy(vsave, vcot_hbm.at[turn], out_sem.at[2])
-
-        def finish(stream, save, out):
-            save[...] = stream.total().astype(bf16)
+        kcots[turns - 1] = jnp.zeros((rows, width), bf16)
+        vcots[turns - 1] = jnp.zeros((rows, width), bf16)
+        sumrows[turns - 1] = jnp.zeros((8, 128), f32)
+
+        def finish(stream, save, turn):
+            save[turn] = stream.total().astype(bf16)
             stream.wait_sends()
-            out.start()
 
         def query_rows(turn, slot):
-            index = spans_ref[turn]
+            index = plan.span(turn)
             back = inner_right(rall[index, 0], low2[slot, :, pl.ds(0, block)])
             for b in range(1, blocks):
                 back = back + inner_right(rall[index, b], low2[slot, :, pl.ds(b * block, block)])
             query_pre = qpre[slot]
-            qpl[...] = (gates_ref[turn, 4] * back * silu_slope(query_pre)).astype(bf16)
+            qpl[...] = (plan.valid(turn) * back * silu_slope(query_pre)).astype(bf16)
             qhid[...] = (query_pre * jax.nn.sigmoid(query_pre)).astype(bf16)
             qstream.part[...] = inner_right(qpl[...], low1[slot]).astype(bf16).reshape(2, chips, rows, width)
             qstream.start_pair()
 
         def query_weights(turn, slot):
-            index = spans_ref[turn]
-            valid = gates_ref[turn, 4]
+            index = plan.span(turn)
+            valid = plan.valid(turn)
             for b in range(blocks):
                 w1[pl.ds(b * block, block), :] = inner_left(qbuf[slot, b], qpl[...])
                 w2[:, pl.ds(b * block, block)] = valid * inner_left(qhid[...], rall[index, b])
@@ -1134,7 +1369,7 @@
             copy.wait()
         query_rows(turns - 1, 0)
         query_weights(turns - 1, 0)
-        reset = gates_ref[turns - 1, 3]
+        reset = plan.first(turns - 1)
         for c, w, acc in ((cf, w1, a1), (cs, w2, a2)):
             acc[...] = reset * w[...]
             c[...] = (1.0 - reset) * w[...]
@@ -1144,7 +1379,8 @@
         def body(step, carry):
             turn = turns - 1 - step
             slot = lax.rem(step, 2)
-            decay, moment, rate, reset = (gates_ref[turn, i] for i in range(4))
+            decay, moment, rate = plan.rates(turn)
+            reset = plan.first(turn)
             for copy in q_loads(turn, slot) + k_loads(turn, slot):
                 copy.wait()
             c1[slot] = (-rate * (cmf[...] + cf[...])).astype(bf16)
@@ -1160,11 +1396,11 @@
                 (matmul(khid[...], c2[...]) + matmul(dh[...], low2[slot])).astype(bf16).reshape(2, chips, rows, width)
             )
             lookup.start_pair()
-            finish(qstream, qsave, qout(turn + 1))
+            finish(qstream, qcots, turn + 1)
 
             @pl.when(step > 2)
             def _():
-                finish(kstream, ksave, kout(turn + 2))
+                finish(kstream, kcots, turn + 2)
 
             lookup.take_pair()
             lookup.start_sends()
@@ -1185,29 +1421,26 @@
             hk[...] = inner_right(err, c2[...])
             w2[...] += inner_left(dh[...], err)
 
-            def sums(first_a, first_b, second_a, second_b, row):
-                sums1_ref[turn, pl.ds(row, 1), :] = jnp.sum(first_a * first_b.astype(f32), axis=0, keepdims=True)
-                sums2_ref[turn, pl.ds(row, 1), :] = jnp.sum(second_a * second_b.astype(f32), axis=0, keepdims=True)
-
-            sums(cf[...], low1[slot], cs[...], low2[slot], 0)
-            sums(cmf[...] + cf[...], m1[slot], cms[...] + cs[...], m2[slot], 1)
-            sums(cmf[...] + cf[...], g1[slot], cms[...] + cs[...], g2[slot], 2)
+            def whole_sum(first_a, first_b, second_a, second_b):
+                first = jnp.sum(first_a * first_b.astype(f32), axis=0, keepdims=True)
+                second = jnp.sum(second_a * second_b.astype(f32), axis=0, keepdims=True)
+                return jnp.sum(first, axis=1, keepdims=True) + jnp.sum(second, axis=1, keepdims=True)
+
+            kinds = (
+                whole_sum(cf[...], low1[slot], cs[...], low2[slot]),
+                whole_sum(cmf[...] + cf[...], m1[slot], cms[...] + cs[...], m2[slot]),
+                whole_sum(cmf[...] + cf[...], g1[slot], cms[...] + cs[...], g2[slot]),
+            )
+            column = lax.broadcasted_iota(jnp.int32, (8, 128), 1)
+            sumrow = jnp.zeros((8, 128), f32)
+            for i, kind in enumerate(kinds):
+                sumrow = jnp.where(column == i, kind, sumrow)
+            sumrows[turn] = sumrow
             qstream.take_pair()
             total = lookup.total()
             mine = (total / span).astype(bf16)
             spread.whole[lane.colour, lane.chip] = mine
-            qout(turn + 1).wait()
-
-            @pl.when(step > 1)
-            def _():
-                vout(turn + 1).wait()
-
-            @pl.when(step > 2)
-            def _():
-                kout(turn + 2).wait()
-
-            vsave[...] = mine
-            vout(turn).start()
+            vcots[turn] = mine
             spread.run()
             lookup.wait_sends()
             qstream.start_sends()
@@ -1248,23 +1481,44 @@
             lookup.got,
             (lookup.pair_send, lookup.pair_recv, lookup.send, lookup.recv),
         )
+        key_rows((turns - 1) % 2)
+        tail.start_pair()
+        mb1[...] = a1[...].astype(bf16).reshape(mb1.shape)
+        for owner in range(wide):
+            mb2[owner] = a2[:, owner * (width // wide) : (owner + 1) * (width // wide)].astype(bf16)
         ends = [
-            pltpu.make_async_copy(a1, mg1_hbm, end_sem.at[0]),
-            pltpu.make_async_copy(a2, mg2_hbm, end_sem.at[1]),
+            pltpu.make_async_copy(mb1, mg1_hbm, end_sem.at[0]),
+            pltpu.make_async_copy(mb2, mg2_hbm, end_sem.at[1]),
         ]
         for copy in ends:
             copy.start()
-        key_rows((turns - 1) % 2)
-        tail.start_pair()
-        finish(qstream, qsave, qout(0))
+        for span_number in range(wide):
+            here = jnp.where(plan.lane_of(span_number) == plan.lane, 1.0, 0.0)
+            tile[pl.ds(span_number, 1), :] = here * sumrows[plan.turn_of(span_number)][:1]
+
+        def send_tile(step, carry):
+            target = lax.rem(deliver.me + step, devices)
+            where = lax.div(target, blocks), lax.rem(target, blocks)
+            remote(tile, sums_out.at[deliver.me], tile_send.at[0], tile_recv.at[0], where).start()
+            return carry
+
+        lax.fori_loop(1, devices, send_tile, 0)
+        sums_out[deliver.me] = tile[...]
+        finish(qstream, qcots, 0)
         if turns > 2:
-            finish(kstream, ksave, kout(1))
+            finish(kstream, kcots, 1)
         tail.take_pair()
         tail.start_sends()
-        if turns > 2:
-            kout(1).wait()
-        finish(tail, ksave, kout(0))
-        for copy in ends + [qout(0), kout(0), vout(0)]:
+        finish(tail, kcots, 0)
+        deliver.start([qcots, kcots, vcots])
+        others = sums_out.at[pl.ds(0, devices - 1)]
+        tiles = remote(others, others, tile_send.at[0], tile_recv.at[0], grid.partner)
+        tiles.wait_send()
+        tiles.wait_recv()
+        deliver.finish(result)
+        ends.append(pltpu.make_async_copy(result, cots_hbm, end_sem.at[2]))
+        ends[2].start()
+        for copy in ends:
             copy.wait()
 
     state = [(width, hidden), (hidden, width)]
@@ -1274,12 +1528,11 @@
         + [(s, bf16) for s in state * 2]
         + [((2, chips, rows, width), bf16), ((2, span, hidden), f32)]
     )
-    out_shape = (
-        [jax.ShapeDtypeStruct((turns, rows, width), bf16)]
-        + [jax.ShapeDtypeStruct((key_turns, rows, width), bf16)] * 2
-        + [jax.ShapeDtypeStruct((key_turns, 8, hidden), f32), jax.ShapeDtypeStruct((key_turns, 8, width), f32)]
-        + [jax.ShapeDtypeStruct(s, f32) for s in state]
-    )
+    by_owner = [(wide, width // wide, hidden), (wide, hidden, width // wide)]
+    out_shape = [
+        jax.ShapeDtypeStruct((3, 2, chips, rows, block), bf16),
+        jax.ShapeDtypeStruct((devices, wide, 128), f32),
+    ] + [jax.ShapeDtypeStruct(s, bf16) for s in by_owner]
     sem = pltpu.SemaphoreType.DMA
     scratch = (
         [pltpu.VMEM((2,) + s, t) for s, t in q_buffers + k_buffers]
@@ -1288,11 +1541,15 @@
         + [pltpu.VMEM((2,) + state[0], bf16), pltpu.VMEM(state[1], bf16)]
         + [pltpu.VMEM((span, hidden), bf16)] * 6
         + [pltpu.VMEM((span, hidden), f32)] * 2
-        + [pltpu.VMEM((rows, width), bf16)] * 3
-        + [sem((2, 4)), sem((2, 7)), sem((3,)), sem((2,)), sem((1,))]
+        + [pltpu.VMEM((turns, rows, width), bf16)] * 3
+        + [pltpu.VMEM((turns, 8, 128), f32), pltpu.VMEM((wide, 128), f32)]
+        + [pltpu.VMEM(s, bf16) for s in by_owner]
+        + [pltpu.VMEM((3, 2, chips, rows, block), bf16)]
+        + [sem((2, 4)), sem((2, 7)), sem((3,)), sem((1,)), sem((1,)), sem((1,))]
         + Scatter.scratch(chips, rows, width) * 3
         + Spread.scratch(chips, rows, width)
         + Gather.scratch()
+        + Deliver.scratch(3, rows, block)
     )
     vmem = pl.BlockSpec(memory_space=pltpu.VMEM)
     smem = pl.BlockSpec(memory_space=pltpu.SMEM)
@@ -1300,7 +1557,7 @@
         kernel,
         out_shape=out_shape,
         in_specs=[ANY] * 12 + [smem] * 2,
-        out_specs=[ANY] * 3 + [vmem] * 2 + [ANY] * 2,
+        out_specs=[ANY, vmem, ANY, ANY],
         scratch_shapes=scratch,
         compiler_params=pltpu.CompilerParams(
             collective_id=ident, has_side_effects=True, vmem_limit_bytes=62 * 1024 * 1024
@@ -1311,7 +1568,7 @@
         name="chain_backward",
     )(
         recall_grad, queries, low1_all, low2_all, qpre_all, keys, m1_all, m2_all, g1_all, g2_all, err_all, pre_all,
-        spans, gates,
+        lengths, gates,
     )
 
 
@@ -1384,22 +1641,11 @@
 
     long_turns = min(6, wide * 5 // 8)
     turns = max(long_turns, wide - long_turns)
-    seq_ends = jnp.cumsum(seq_spans)
-    seq_starts = seq_ends - seq_spans
-    long_start = seq_starts[jnp.argmax(seq_spans)]
-    order = jnp.arange(wide, dtype=jnp.int32)
-    span_first = jnp.any(seq_starts[None, :] == order[:, None], axis=1)
-    is_first = span_first[wide_pos]
-    in_long = (order >= long_start) & (order < long_start + long_turns)
-    lane_of = jnp.where(in_long, 0, 1)
-    turn_of = jnp.where(in_long, order - long_start, jnp.where(order < long_start, order, order - long_turns))
-    lane_pos = wide_pos // LANE_WIDE
-    turn_order = jnp.arange(turns, dtype=jnp.int32)
-    rest_order = jnp.where(turn_order < long_start, turn_order, turn_order + long_turns)
-    lane_spans = jnp.clip(jnp.where(lane_pos == 0, long_start + turn_order, rest_order), 0, wide - 1)
-    lane_count = jnp.where(lane_pos == 0, long_turns, jnp.where(lane_pos == 1, wide - long_turns, 0))
-    lane_valid = turn_order < lane_count
-    lane_first = span_first[lane_spans] | ~lane_valid
+    is_first = False
+    start = 0
+    for i in range(seq_spans.shape[0]):
+        is_first = is_first | (wide_pos == start)
+        start = start + seq_spans[i]
 
     smalls = [conv_kernel, persistent, norm_gain, ffn_gain, rate_proj]
     small_sizes = [a.size for a in smalls]
@@ -1473,45 +1719,16 @@
     gate_cols = out_weights[:, :local_width]
     proj_cols = out_weights[:, local_width:]
     gate_rows = gate_got[::narrow, 0, :3]
-    lane_gates = gate_rows[lane_spans]
-    first_f = lane_first.astype(f32)
-    next_first = jnp.concatenate([first_f[1:], jnp.ones((1,), f32)])
-    key_index = lane_spans
     if wide > 8:
-        key_all, key_index = key_all[lane_spans], turn_order
+        long_start = (jnp.cumsum(seq_spans) - seq_spans)[jnp.argmax(seq_spans)]
+        turn_order = jnp.arange(turns, dtype=jnp.int32)
+        rest_order = jnp.where(turn_order < long_start, turn_order, turn_order + long_turns)
+        lane_spans = jnp.where(wide_pos // LANE_WIDE == 0, long_start + turn_order, rest_order)
+        key_all = key_all[jnp.clip(lane_spans, 0, wide - 1)]
     chain = chain_forward(
-        key_all,
-        key_index,
-        value_got,
-        query_low,
-        lane_spans,
-        jnp.concatenate([lane_gates, next_first[:, None]], 1),
-        first_init,
-        second_init,
-        3,
+        key_all, value_got, query_low, seq_spans, gate_rows, turns, first_init, second_init, 3
     )
-    recalled_lane, saved = chain[0], chain[1:]
-
-    def by_span(lane_rows):
-        spans = lane_rows[turn_of]
-        return spans.reshape(wide, shard_rows, narrow, local_width).transpose(0, 2, 1, 3)
-
-    def from_lane(got):
-        got = got.reshape(lanes, LANE_WIDE, narrow // 2, 2, shard_rows, local_width)
-        own = lax.dynamic_index_in_dim(got, lane_of[wide_pos], 0, keepdims=False)
-        return own.transpose(2, 0, 1, 3, 4).reshape(span, local_width)
-
-    recalled_got = exchange(
-        [
-            (
-                by_span(recalled_lane).reshape(devices, shard_rows, local_width),
-                lambda tw, tn: tw * narrow + tn,
-            )
-        ],
-        "all",
-        6,
-    )[0]
-    recall_low = from_lane(recalled_got)
+    recall_low, saved = chain[0].reshape(span, local_width), chain[1:]
     recall_own = recall_low.astype(f32)
 
     keys_all = jnp.concatenate(
@@ -1607,7 +1824,8 @@
     gated_grad = matmul(branch_low, proj_cols)
     attended_grad_low = (gated_grad * gate_sigmoid).astype(bf16)
     gate_pre_low = (gated_grad * attended * gate_sigmoid * (1.0 - gate_sigmoid)).astype(bf16)
-    proj_grad = inner_left(branch_low, gated_low)
+    early_grads = jnp.concatenate([inner_left(normed_low, gate_pre_low), inner_left(branch_low, gated_low)], 1)
+    early_out = scatter_wide(early_grads)
 
     weights_again = jnp.exp(score_block() - log_total)
     grad_heads = split_heads(attended_grad_low, HEAD)
@@ -1632,46 +1850,9 @@
         + values_grad[persist_count:recall_end]
     ).astype(bf16)
 
-    qcot, kcot, vcot, sums1, sums2, first_grad, second_grad = chain_backward(
-        recall_grad_low,
-        saved,
-        lane_spans,
-        jnp.concatenate([lane_gates, first_f[:, None], lane_valid.astype(f32)[:, None]], 1),
-        12,
-    )
-    kcot, vcot = [jnp.concatenate([a, jnp.zeros_like(a[:1])], 0) for a in (kcot, vcot)]
-    lane_sums = jnp.sum(sums1[:, :3], axis=2) + jnp.sum(sums2[:, :3], axis=2)
-    lane_sums = jnp.pad(lane_sums, ((0, 1), (0, 0)))
-    span_sums = jnp.where((lane_of == lane_pos)[:, None], lane_sums[turn_of], 0.0)
-    sums_tile = jnp.pad(span_sums, ((0, 0), (0, 125)))
-    cots = jnp.stack([by_span(a) for a in (qcot, kcot, vcot)], 2)
-    cots_got, sums_got = exchange(
-        [
-            (cots.reshape(devices, 3, shard_rows, local_width), lambda tw, tn: tw * narrow + tn),
-            (sums_tile, None),
-        ],
-        "all",
-        13,
-    )
-    query_mem, key_mem, value_mem = [from_lane(cots_got[:, i]).astype(f32) for i in range(3)]
+    cots, sums_got, first_chunks, second_chunks = chain_backward(recall_grad_low, saved, seq_spans, gate_rows, 12)
+    query_mem, key_mem, value_mem = [cots[i].reshape(span, local_width).astype(f32) for i in range(3)]
     gate_sums = jnp.sum(sums_got[:, :, :3], axis=0)[wide_pos] * jnp.array([-1.0, 1.0, -1.0], f32)
-    first_got, second_got = exchange(
-        [
-            (first_grad.astype(bf16).reshape(wide, width // wide, hidden), lambda tw, tn: tw),
-            (
-                second_grad.astype(bf16).reshape(hidden, wide, width // wide).transpose(1, 0, 2),
-                lambda tw, tn: tw,
-            ),
-        ],
-        "wide",
-        14,
-    )
-
-    def over_lanes(got):
-        return jnp.sum(got.reshape((lanes, LANE_WIDE) + got.shape[1:]).astype(f32), axis=0)
-
-    first_out = over_lanes(first_got).transpose(1, 0, 2).reshape(width // wide, LANE_WIDE * hidden)
-    second_out = over_lanes(second_got).reshape(LANE_WIDE * hidden, width // wide)
 
     logit_grad = gate_sums * gate_scale * gate_sig * (1.0 - gate_sig)
     rate_part = span_mean[:, None] * logit_grad[None, :]
@@ -1705,13 +1886,7 @@
         gain_part = jnp.sum(normed_grad * scaled, axis=0, keepdims=True)
         return [(grad_rows + rms_back(scaled, factor, normed_grad * gain)).astype(bf16)], [gain_part]
 
-    tokens_grad, gain_one_part = narrow_step(
-        [by_rows(normed_part)], [tokens_own, middle_grad, gain_one[None], gate_row], after_all, 1, [row_f32], 15
-    )
-    tokens_grad = tokens_grad.reshape(span, width).astype(f32)
-    weight_grads = inner_left(normed_low, jnp.concatenate([projected_low, gate_pre_low], 1))
-    weight_out = scatter_wide(weight_grads)
-    proj_out = scatter_wide(proj_grad)
+    weight_grads = inner_left(normed_low, projected_low).astype(bf16)
 
     def place_cols(piece, axis):
         full = piece.shape[:axis] + (width,) + piece.shape[axis + 1 :]
@@ -1723,21 +1898,31 @@
     chunks = [
         kernel_full.reshape(taps, devices, -1).transpose(1, 0, 2),
         persist_full.reshape(2, persist_count, devices, -1).transpose(2, 0, 1, 3),
-        gain_one_part.reshape(devices, -1),
         gain_two_part.reshape(devices, -1),
         rate_part.reshape(devices, -1, 3),
     ]
     flat = jnp.concatenate([a.reshape(devices, -1) for a in chunks], 1)
     flat_size = -(-flat.shape[1] // 1024) * 1024
     flat = jnp.pad(flat, ((0, 0), (0, flat_size - flat.shape[1]))).reshape(devices, -1, 128)
-    flat_got = exchange([(flat, lambda tw, tn: tw * narrow + tn)], "all", 17)[0]
-    flat_sum = jnp.sum(flat_got, axis=0).reshape(-1)
+    tokens_grad, weight_out, first_out, second_out, flat_sum, gain_sum = last_step(
+        by_rows(normed_part),
+        [tokens_own, middle_grad, gain_one[None], gate_row],
+        after_all,
+        weight_grads.reshape(wide, width // wide, 3 * local_width),
+        [first_chunks, second_chunks],
+        flat,
+        15,
+    )
+    tokens_grad = tokens_grad.reshape(span, width).astype(f32)
+    flat_sum = flat_sum.reshape(-1)
+    own_start = (wide_pos * narrow + narrow_pos) * (width // devices)
+    norm_grad = lax.dynamic_slice_in_dim(gain_sum.reshape(-1), own_start, width // devices, 0)
     small_outs, at = [], 0
     for a in chunks:
         size = a.size // devices
         small_outs.append(flat_sum[at : at + size].reshape(a.shape[1:]))
         at += size
-    kernel_grad, persist_grad, norm_grad, ffn_gain_grad, rate_grad = small_outs
+    kernel_grad, persist_grad, ffn_gain_grad, rate_grad = small_outs
     return (
         output,
         tokens_grad,
@@ -1748,8 +1933,8 @@
         persist_grad,
         norm_grad,
         rate_grad,
-        weight_out[:, 3 * local_width :],
-        proj_out.T,
+        early_out[:, :local_width],
+        early_out[:, local_width:].T,
         first_out,
         second_out,
         ffn_gain_grad,

time: 1010 us -> 954 us (0.945)
  Pallas kernels: 751 us -> 714 us
  local copies, waits for them, and re-layouts: 80.9 us -> 67.2 us
  other arithmetic: 58.5 us -> 48.1 us
    pallas_call x4 -> x1, Pallas kernels: 123 us -> 65.6 us  [last_step(): pl.pallas_call(kernel, out_shape=[jax.ShapeDtypeStruct((narrow, rows, wid...]
    pallas_call x1, Pallas kernels: 235 us -> 266 us  [chain_backward(): pl.pallas_call(kernel, out_shape=out_shape, in_specs=[ANY] * 12 + [smem]...]
    pallas_call x3 -> x2, Pallas kernels: 77 us -> 55.7 us  [narrow_step(): pl.pallas_call(kernel, out_shape=[jax.ShapeDtypeStruct((narrow, rows, wid...]
    pallas_call x1, Pallas kernels: 200 us -> 212 us  [chain_forward(): pl.pallas_call(kernel, out_shape=out_shape, in_specs=[ANY] * 3 + [smem] *...]
    unnamed x212 -> x189, local copies, waits for them, and re-layouts: 21.5 us -> 24.5 us
  transfers between devices with their start and end apart: 11 -> 10, of which waited for: 2 -> 3; matrix products, arithmetic and copies ran while one was open for 14% -> 12% of each run, Pallas kernels for 60% -> 60%
where the time goes in v3:
time: 954 us; the launch traced here: 942 us
  Pallas kernels  714 us (75%)
  matrix products  70.5 us (7%)
  local copies, waits for them, and re-layouts  67.2 us (7%)
  other arithmetic  48.1 us (5%)
  waiting for transfers between devices  17.9 us (2%)
  between operations  17.8 us (2%)
    pallas_call x1, Pallas kernels, chain_backward(): pl.pallas_call(kernel, out_shape=out_shape, in_specs=[ANY] * 12 + [smem]...  266 us
    pallas_call x1, Pallas kernels, chain_forward(): pl.pallas_call(kernel, out_shape=out_shape, in_specs=[ANY] * 3 + [smem] *...  212 us
    pallas_call x1, Pallas kernels, last_step(): pl.pallas_call(kernel, out_shape=[jax.ShapeDtypeStruct((narrow, rows, wid...  65.6 us
    pallas_call x1, Pallas kernels, rows_to_lanes(): pl.pallas_call(kernel, out_shape=[jax.ShapeDtypeStruct((wide, narrow) + r...  60.1 us
    pallas_call x2, Pallas kernels, narrow_step(): pl.pallas_call(kernel, out_shape=[jax.ShapeDtypeStruct((narrow, rows, wid...  55.7 us
    pallas_call x1, Pallas kernels, send_parameters(): pl.pallas_call(kernel, out_shape=[jax.ShapeDtypeStruct((devices,) + small...  54.7 us
    unnamed x189, local copies, waits for them, and re-layouts  24.5 us
  transfers between devices with their start and end apart: 10, of which 3 were waited for; matrix products, arithmetic and copies ran while one was open for 12% of the time, Pallas kernels for 60%

profile of v3, /device:TPU:0, one launch (start us, length us, event | category | flops | bytes accessed | tf_op | source)
XLA Modules:
  0.0 941.8 jit_solution(15025749565592305577)
XLA Ops:
  16.9 54.7 %send_parameters.1 = (bf16[32,16,128]{2,1,0:T(8,128)(2,1)}, bf16[8,4,32,768]{3,2,1,0:T(8,128)(2,1)}, bf16[8,128,256]{2,1,0:T(8,128)(2,1)}, bf16[8,256,128]{2,1,0:T(8,128)(2,1)}) custom-call(bf16[16,128]{1,0:T(8,128)(2,1)} %pad_bitcast_fusion.1.refs_0_, bf16[4,32,768]{2,1,0:T(8,128)(2,1)} %maximum_bitcast_fusion.refs_1_, bf16[4,128,256]{2,1,0:T(8,128)(2,1)} %bitcast.210, ...), custom_call_target="tpu_custom_call" | custom-call | tf_op jit(solution)/shard_map/send_parameters/pallas_call | solution.py:328
  72.8 2.5 fusion.89
  76.4 4.6 collective-permute-start
  86.6 5.3 fusion.27
  105.9 60.1 %rows_to_lanes.1 = (bf16[8,4,512,256]{3,2,1,0:T(8,128)(2,1)}, bf16[32,32,256]{2,1,0:T(8,128)(2,1)}, f32[32,8,128]{2,1,0:T(8,128)}) custom-call(bf16[512,256]{1,0:T(8,128)(2,1)} %get-tuple-element.192.rows_ref, bf16[16,32,256]{2,1,0:T(8,128)(2,1)} %bitcast.192, f32[8,128]{1,0:T(8,128)} %broadcast_in_dim.31.tile_ref), custom_call_target="tpu_custom_call" | custom-call | tf_op jit(solution)/shard_map/rows_to_lanes/pallas_call | solution.py:390
  177.2 211.8 %chain_forward.1 = (bf16[2,8,32,256]{3,2,1,0:T(8,128)(2,1)}, bf16[5,1024,256]{2,1,0:T(8,128)(2,1)}, bf16[5,256,1024]{2,1,0:T(8,128)(2,1)}, bf16[4,1024,256]{2,1,...) custom-call(bf16[8,4,512,256]{3,2,1,0:T(8,128)(2,1)} %get-tuple-elem, ...), custom_call_target="tpu_custom_call" | custom-call | flops 53687091200 | bytes 209715200 | tf_op jit(solution)/shard_map/chain_forward/pallas_call | solution.py:1260
  392.5 2.9 fusion.96
  398.8 2.4 fusion.9
  401.3 2.7 fusion.52
  405.4 22.5 %narrow_step_7.1 = (bf16[4,128,1024]{2,1,0:T(8,128)(2,1)}, f32[128,1024]{1,0:T(8,128)}) custom-call(bf16[2,2,128,1024]{3,2,1,0:T(8,128)(2,1)} %bitcast.186, bf16[128,1024]{1,0:T(8,128)(2,1)} %constant_dynamic-slice_fusion.3.refs_1_.refs_5_, f32[1,1024]{1,0:T(1,128)} %reshape.419.refs_2_.refs_4_), custom_call_target="tpu_custom_call" | custom-call | tf_op jit(solution)/shard_map/narrow_step_7/pallas_call | solution.py:503
  427.9 4.5 fusion.98
  432.4 4.5 fusion.97
  436.9 6.4 all-gather.11.cloned.1.call-done
  443.3 6.2 fusion.22
  450.6 2.6 convolution_convert_fusion
  453.2 4.2 convolution_convert_fusion.1
  457.3 4.2 convert_bitcast_fusion
  465.6 2.3 add_convert_fusion.1
  467.9 33.2 %narrow_step_9.1 = (bf16[4,128,1024]{2,1,0:T(8,128)(2,1)}, bf16[4,128,1024]{2,1,0:T(8,128)(2,1)}, f32[128,1024]{1,0:T(8,128)}, f32[1,1024]{1,0:T(1,128)}) custom-call(bf16[2,2,128,1024]{3,2,1,0:T(8,128)(2,1)} %bitcast.202, bf16[2,2,128,1024]{3,2,1,0:T(8,128)(2,1)} %bitcast.203, f32[128,1024]{1,0:T(8,128)} %get-tuple-element.78.refs_2_, ...), custom_call_target="tpu_custom_call" | custom-call | tf_op jit(solution)/shard_map/narrow_step_9/pallas_call | solution.py:503
  508.3 4.0 copy.174
  512.3 6.5 multiply_reduce_fusion
  518.8 10.3 %multiply_convert_fusion = bf16[4,512,1040]{1,2,0:T(8,128)(2,1)} fusion(f32[4,512,1040]{1,2,0:T(8,128)} %get-tuple-element.218, f32[4,512,1040]{1,2,0:T(8,128)} %copy-done.8, f32[4,512]{1,0:T(4,128)S(1)} %get-tuple-element.217, f32[4,512]{1,0:T(4,128)S(1)} %log_add_fusion), kind=kLoop, calls=%fused_computation.4 | loop fusion | flops 8519680 | bytes 21315584 | tf_op jit(solution)/shard_map/convert_element_type | solution.py:1834
  529.2 3.6 fusion.10
  532.8 5.4 fusion.11
  540.2 266.1 %chain_backward.1 = (bf16[3,2,8,32,256]{4,3,2,1,0:T(8,128)(2,1)}, f32[32,8,128]{2,1,0:T(8,128)}, bf16[8,128,256]{2,1,0:T(8,128)(2,1)}, bf16[8,256,128]{2,1,0:T(8,128)(2,1)}) custom-call(bf16[512,256]{1,0:T(8,128)(2,1)} %copy.156.refs_0_, bf16[5,4,512,256]{3,2,1,0:T(8,128)(2,1)} %get-tuple-element.81.refs_1_, ...), custom_call_target="tpu_custom_call" | custom-call | flops 107374182400 | bytes 314572800 | tf_op jit(solution)/shard_map/chain_backward/pallas_call | solution.py:1556
  814.4 3.2 fusion.32
  820.2 2.6 fusion.42
  825.2 3.4 multiply_reduce_fusion.3
  834.6 2.9 pad_add_fusion
  838.1 8.5 collective-permute-done.1
  846.6 2.3 convolution_convert_fusion.2
  850.4 65.6 %last_step.1 = (bf16[4,128,1024]{2,1,0:T(8,128)(2,1)S(1)}, f32[128,768]{1,0:T(8,128)S(1)}, f32[128,1024]{1,0:T(8,128)S(1)}, f32[1024,128]{1,0:T(8,128)S(1)}, f32...) custom-call(bf16[2,2,128,1024]{3,2,1,0:T(8,128)(2,1)S(1)} %bitcast.177, bf16[4,2,128,768]{3,2,1,0:T(8,128)(2,1)} %bitcast.199, ...), custom_call_target="tpu_custom_call" | custom-call | tf_op jit(solution)/shard_map/last_step/pallas_call | solution.py:689
  (366 shorter events, 102.0 us)
Async XLA Ops:
  7.2 163.2 %copy-start = (bf16[512,1024]{1,0:T(8,128)(2,1)S(1)}, bf16[512,1024]{1,0:T(8,128)(2,1)}, u32[]{:S(2)}) copy-start(bf16[512,1024]{1,0:T(8,128)(2,1)} %param.21) | copy-start | bytes 3145732
  7.2 65.5 %copy-start.16 = (bf16[512,1024]{1,0:T(8,128)(2,1)S(1)}, bf16[512,1024]{1,0:T(8,128)(2,1)}, u32[]{:S(2)}) copy-start(bf16[512,1024]{1,0:T(8,128)(2,1)} %param.20) | copy-start | bytes 3145732
  7.2 9.0 copy-start.52
  7.2 9.0 copy-start.53
  7.2 394.0 %all-gather.5.cloned.1.call-start = ((), (), s32[]{:S(2)}) async-start(), calls=%async_computation.4 | async-start | bytes 1179648 | tf_op jit(solution)/shard_map/all_gather | solution.py:1715
  10.5 70.6 %copy-start.71 = (f32[512]{0:T(512)}, f32[512]{0:T(512)S(1)}, u32[]{:S(2)}) copy-start(f32[512]{0:T(512)S(1)} %add_rsqrt_fusion.4) | copy-start | bytes 6148
  72.7 8.3 copy-start.69
  72.8 8.7 copy-start.51
  76.4 7.0 copy-start.77
  76.4 7.5 copy-start.74
  76.4 10.1 %collective-permute-start = (bf16[3,768]{1,0:T(4,128)(2,1)S(1)}, bf16[3,768]{1,0:T(4,128)(2,1)S(1)}, u32[]{:S(2)}, u32[]{:S(2)}) collective-permute-start(bf16[3,768]{1,0:T(4,128)(2,1)S(1)} %slice.302), channel_id=1, source_target_pairs={{0,4},{4,8},{8,12},{12,16},{16,20},{20,24},{24,28},{1,5},{5,9},{9,... | collective-permute-start | bytes 13832 | tf_op jit(solution)/shard_map/ppermute | solution.py:1578
  95.0 7.1 copy-start.19
  95.1 8.3 copy-start.49
  98.3 7.0 copy-start.47
  105.3 65.9 %copy-start.41 = (bf16[8,256,128]{2,1,0:T(8,128)(2,1)S(1)}, bf16[8,256,128]{2,1,0:T(8,128)(2,1)}, u32[]{:S(2)}) copy-start(bf16[8,256,128]{2,1,0:T(8,128)(2,1)} %get-tuple-element.69) | copy-start | bytes 1572868
  166.0 261.9 %all-gather.9.cloned.1.call-start = ((), (), s32[]{:S(2)}) async-start(), calls=%async_computation.6 | async-start | bytes 2359296 | tf_op jit(solution)/shard_map/all_gather | solution.py:1717
  166.8 265.7 %all-gather.7.cloned.1.call-start = ((), (), s32[]{:S(2)}) async-start(), calls=%async_computation.5 | async-start | bytes 2359296 | tf_op jit(solution)/shard_map/all_gather | solution.py:1716
  167.7 6.7 copy-start.27
  168.0 7.3 copy-start.33
  168.7 6.7 copy-start.35
  176.9 266.4 %all-gather.11.cloned.1.call-start = ((), (), s32[]{:S(2)}) async-start(), calls=%async_computation.7 | async-start | bytes 2359296 | tf_op jit(solution)/shard_map/all_gather | solution.py:1718
  390.8 531.7 %reduce-scatter.13.cloned.1.call-start = ((), (), s32[]{:S(2)}) async-start(), calls=%async_computation.10 | async-start | bytes 1179648
  443.3 7.3 copy-start.82
  507.3 417.6 %reduce-scatter.11.cloned.1.call-start = ((), (), s32[]{:S(2)}) async-start(), calls=%async_computation.9 | async-start | bytes 2359296 | tf_op jit(solution)/shard_map/reduce_scatter | solution.py:1806
  507.9 418.8 %reduce-scatter.15.cloned.1.call-start = ((), (), s32[]{:S(2)}) async-start(), calls=%async_computation.11 | async-start | bytes 2359296
  540.1 390.3 %reduce-scatter.9.cloned.1.call-start = ((), (), s32[]{:S(2)}) async-start(), calls=%async_computation.8 | async-start | bytes 2359296 | tf_op jit(solution)/shard_map/reduce_scatter | solution.py:1806
  540.2 268.1 %copy-start.73 = (f32[1,1024]{1,0:T(1,128)S(1)}, f32[1,1024]{1,0:T(1,128)}, u32[]{:S(2)}) copy-start(f32[1,1024]{1,0:T(1,128)} %get-tuple-element.95) | copy-start | bytes 12292
  540.2 268.8 %slice-start = ((f32[1040,4,64]{0,2,1:T(8,128)}), f32[16,4,64]{0,2,1:T(8,128)S(1)}, s32[]{:S(2)}) async-start(f32[1040,4,64]{0,2,1:T(8,128)} %copy-done.25), calls=%async_computation.12 | async-start | bytes 262144 | tf_op jit(solution)/shard_map/slice | solution.py:1846
  833.0 13.6 %collective-permute-start.1 = (bf16[3,768]{1,0:T(4,128)(2,1)S(1)}, bf16[3,768]{1,0:T(4,128)(2,1)S(1)}, u32[]{:S(2)}, u32[]{:S(2)}) collective-permute-start(bf16[3,768]{1,0:T(4,128)(2,1)S(1)} %fusion.79), channel_id=1, source_target_pairs={{4,0},{8,4},{12,8},{16,12},{20,16},{24,20},{28,24},{5,1},{9,5},{13... | collective-permute-start | bytes 13832 | tf_op jit(solution)/shard_map/ppermute | solution.py:1578
  837.5 9.1 copy-start.18
  838.1 10.8 %copy-start.81 = (bf16[8,4,32,768]{3,2,1,0:T(8,128)(2,1)S(1)}, bf16[8,4,32,768]{3,2,1,0:T(8,128)(2,1)}, u32[]{:S(2)}) copy-start(bf16[8,4,32,768]{3,2,1,0:T(8,128)(2,1)} %get-tuple-element.63) | copy-start | bytes 4718596
  923.5 8.7 copy-start.34
  (66 other events, 193.9 us)
Sparse Core Ops, SparseCore 0:
  166.1 51.9 all-gather.4
  220.3 63.5 all-gather.8
  286.0 58.8 all-gather.6
  390.9 52.3 all-gather.10
  507.5 68.0 reduce-scatter.12
  579.3 83.4 reduce-scatter.10
  666.7 88.8 reduce-scatter.14
  825.2 105.2 reduce-scatter.8

commit v4 on v3

--- a/solution.py
+++ b/solution.py
@@ -341,73 +341,6 @@
         compiler_params=pltpu.CompilerParams(collective_id=ident, has_side_effects=True),
         name="send_parameters",
     )(smalls, weights, *blocks)
-
-
-def rows_to_lanes(rows, chunks, pick, tile, ident):
-    wide, narrow = lax.axis_size("wide"), lax.axis_size("narrow")
-    devices = wide * narrow
-
-    def kernel(rows_ref, chunks_ref, tile_ref, rows_out, chunks_out, tile_out, *refs):
-        hold_rows, hold_chunk, hold_tile, local_sem, send, recv = refs[:6]
-        g = Grid()
-        me = g.wide * narrow + g.narrow
-        wait_all = g.greet_all()
-        own = [
-            (rows_ref, hold_rows, rows_out.at[g.wide, g.narrow]),
-            (chunks_ref.at[pick(g.wide, g.narrow)], hold_chunk, chunks_out.at[me]),
-            (tile_ref, hold_tile, tile_out.at[me]),
-        ]
-        into = [pltpu.make_async_copy(a, b, local_sem.at[i]) for i, (a, b, _) in enumerate(own)]
-        back = [pltpu.make_async_copy(b, c, local_sem.at[i]) for i, (_, b, c) in enumerate(own)]
-        for copy in into:
-            copy.start()
-        wait_all()
-        gather = Gather(g, rows_ref, rows_out, refs[6:])
-        gather.begin()
-
-        def send_chunks(step, carry):
-            target = lax.rem(me + step, devices)
-            where = lax.div(target, narrow), lax.rem(target, narrow)
-            remote(chunks_ref.at[pick(*where)], chunks_out.at[me], send.at[0], recv.at[0], where).start()
-            remote(tile_ref, tile_out.at[me], send.at[1], recv.at[1], where).start()
-            return carry
-
-        lax.fori_loop(1, devices, send_chunks, 0)
-        for copy in into:
-            copy.wait()
-        for copy in back:
-            copy.start()
-        gather.middle()
-        for copy in back:
-            copy.wait()
-        for i, out in enumerate((chunks_out, tile_out)):
-            others = out.at[pl.ds(0, devices - 1)]
-            whole = remote(others, others, send.at[i], recv.at[i], g.partner)
-            whole.wait_send()
-            whole.wait_recv()
-        gather.finish()
-
-    return pl.pallas_call(
-        kernel,
-        out_shape=[
-            jax.ShapeDtypeStruct((wide, narrow) + rows.shape, rows.dtype),
-            jax.ShapeDtypeStruct((devices,) + chunks.shape[1:], chunks.dtype),
-            jax.ShapeDtypeStruct((devices,) + tile.shape, tile.dtype),
-        ],
-        in_specs=[ANY] * 3,
-        out_specs=[ANY] * 3,
-        scratch_shapes=[
-            pltpu.VMEM(rows.shape, rows.dtype),
-            pltpu.VMEM(chunks.shape[1:], chunks.dtype),
-            pltpu.VMEM(tile.shape, tile.dtype),
-            pltpu.SemaphoreType.DMA((3,)),
-            pltpu.SemaphoreType.DMA((2,)),
-            pltpu.SemaphoreType.DMA((2,)),
-        ]
-        + Gather.scratch(),
-        compiler_params=pltpu.CompilerParams(collective_id=ident, has_side_effects=True),
-        name="rows_to_lanes",
-    )(rows, chunks, tile)
 
 
 def narrow_step(parts, extras, work, spread_count, locals_like, ident):
@@ -723,6 +656,386 @@
     )(part, grads, chunks[0], chunks[1], flat, *extras)
 
 
+class Plan:
+    def __init__(self, spans_ref, gates_ref, count):
+        self.wide = lax.axis_size("wide")
+        self.long = min(6, self.wide * 5 // 8)
+        self.gates = gates_ref
+        lengths = [spans_ref[i] for i in range(count)]
+        self.starts, at = [], 0
+        for length in lengths:
+            self.starts.append(at)
+            at = at + length
+        longest, self.start = lengths[0], 0
+        for i in range(1, count):
+            more = lengths[i] > longest
+            longest = jnp.where(more, lengths[i], longest)
+            self.start = jnp.where(more, self.starts[i], self.start)
+        self.lane = lax.div(lax.axis_index("wide"), LANE_WIDE)
+
+    def span(self, turn):
+        rest = jnp.where(turn < self.start, turn, turn + self.long)
+        return jnp.clip(jnp.where(self.lane == 0, self.start + turn, rest), 0, self.wide - 1)
+
+    def valid(self, turn):
+        count = jnp.where(self.lane == 0, self.long, jnp.where(self.lane == 1, self.wide - self.long, 0))
+        return jnp.where(turn < count, 1.0, 0.0)
+
+    def first(self, turn):
+        span = self.span(turn)
+        found = jnp.where(span == self.starts[0], 1.0, 0.0)
+        for start in self.starts[1:]:
+            found = jnp.maximum(found, jnp.where(span == start, 1.0, 0.0))
+        return jnp.maximum(found, 1.0 - self.valid(turn))
+
+    def rates(self, turn):
+        span = self.span(turn)
+        return self.gates[span, 0], self.gates[span, 1], self.gates[span, 2]
+
+    def lane_of(self, span):
+        inside = (span >= self.start) & (span < self.start + self.long)
+        return jnp.where(inside, 0, 1)
+
+    def turn_of(self, span):
+        inside = (span >= self.start) & (span < self.start + self.long)
+        outside = jnp.where(span < self.start, span, span - self.long)
+        return jnp.where(inside, span - self.start, outside)
+
+
+def paired_lanes():
+    wide = lax.axis_size("wide")
+    long = min(6, wide * 5 // 8)
+    return wide == 2 * LANE_WIDE and long == LANE_WIDE + 1 and lax.axis_size("narrow") == 4
+
+
+class LaneGather:
+    def __init__(self, grid, plan, source, whole, refs):
+        self.grid, self.plan, self.source, self.whole = grid, plan, source, whole
+        self.own, self.taken, self.mine = refs[:3]
+        self.sent, self.got, self.sent_pair, self.got_pair, self.swap_sent, self.swap_got, self.local = refs[3:]
+        self.rows = whole.shape[2]
+        self.quarter = self.rows // LANE_WIDE
+        third = (self.rows + self.quarter) // 3 // 16 * 16
+        self.cuts = [(0, third), (third, third), (2 * third, self.rows - 2 * third)]
+        self.side = lax.div(grid.wide, LANE_WIDE)
+        self.spot = lax.rem(grid.wide, LANE_WIDE)
+        long = plan.long
+        lone = jnp.where((grid.wide >= plan.wide - long) & (grid.wide < long), 1, 0)
+        self.paired = lone == 0
+        self.pair = (grid.wide + long - 2 * long * self.side, grid.narrow)
+        self.here = (lax.div(self.spot, 2), lax.rem(self.spot, 2), grid.y)
+
+    @staticmethod
+    def scratch(rows, cols):
+        sem = pltpu.SemaphoreType.DMA
+        return [
+            pltpu.VMEM((rows, cols), bf16),
+            pltpu.VMEM((rows, cols), bf16),
+            pltpu.VMEM((rows + rows // LANE_WIDE, cols), bf16),
+            sem((4, 7)),
+            sem((4, 8)),
+            sem((4, 8)),
+            sem((4, 8)),
+            sem((4,)),
+            sem((4,)),
+            sem((5,)),
+        ]
+
+    @staticmethod
+    def shape(rows, cols):
+        return (LANE_WIDE + 1, lax.axis_size("narrow"), rows, cols)
+
+    def order(self, part):
+        return ((0, 1, 2), (1, 2, 0), (2, 0, 1))[part]
+
+    def place(self, mask):
+        return [1 - v if mask >> i & 1 else v for i, v in enumerate(self.here)]
+
+    def device(self, mask, colour):
+        z, x, y = self.place(mask)
+        return self.side * LANE_WIDE + 2 * z + x, 2 * y + colour
+
+    def pieces(self, part, mask, colour):
+        z, x, y = self.place(mask)
+        spot, narrow = 2 * z + x, 2 * y + colour
+        start, size = self.cuts[part]
+        result = [(part, self.whole.at[spot, narrow, pl.ds(start, size)], self.mine.at[pl.ds(start, size)])]
+        if part == 2:
+            there = self.whole.at[LANE_WIDE, narrow, pl.ds(spot * self.quarter, self.quarter)]
+            result.append((3, there, self.mine.at[pl.ds(self.rows, self.quarter)]))
+        return result
+
+    def push(self, part, mask, axis, number):
+        for i, there, own in self.pieces(part, mask, self.grid.c):
+            remote(
+                there if mask else own,
+                there,
+                self.sent.at[i, number],
+                self.got.at[i, mask | 1 << axis],
+                self.device(1 << axis, self.grid.c),
+            ).start()
+
+    def to_partner(self, part, mask):
+        for i, there, own in self.pieces(part, mask, self.grid.c):
+            remote(
+                there if mask else own,
+                there,
+                self.sent_pair.at[i, mask],
+                self.got_pair.at[i, mask],
+                self.grid.partner,
+            ).start()
+
+    def arrived(self, part, mask):
+        for i, there, _ in self.pieces(part, mask, self.grid.c):
+            remote(there, there, self.sent.at[i, 0], self.got.at[i, mask], self.grid.partner).wait_recv()
+
+    def swaps(self):
+        return [
+            remote(
+                self.source.at[pl.ds(start, size)],
+                self.taken.at[pl.ds(start, size)],
+                self.swap_sent.at[i],
+                self.swap_got.at[i],
+                self.pair,
+            )
+            for i, (start, size) in enumerate(self.cuts)
+        ]
+
+    def quarters(self):
+        return [
+            remote(
+                self.source.at[pl.ds(q * self.quarter, self.quarter)],
+                self.mine.at[pl.ds(self.rows, self.quarter)],
+                self.swap_sent.at[q],
+                self.swap_got.at[3],
+                (q, self.grid.narrow),
+            )
+            for q in range(LANE_WIDE)
+        ]
+
+    def begin(self):
+        @pl.when(self.paired)
+        def _():
+            for copy in self.swaps():
+                copy.start()
+
+        @pl.when(self.grid.wide == LANE_WIDE)
+        def _():
+            for copy in self.quarters():
+                copy.start()
+
+        pltpu.make_async_copy(self.source, self.own, self.local.at[4]).start()
+
+        @pl.when(self.side == 1)
+        def _():
+            self.mine[pl.ds(self.rows, self.quarter), :] = jnp.zeros((self.quarter, self.mine.shape[1]), bf16)
+
+    def stage_a(self):
+        pltpu.make_async_copy(self.source, self.own, self.local.at[4]).wait()
+        keep = self.plan.lane_of(self.grid.wide) == self.side
+        for part in range(3):
+            start, size = self.cuts[part]
+            place = (pl.ds(start, size), slice(None))
+
+            @pl.when(self.paired)
+            def _():
+                self.swaps()[part].wait_recv()
+                self.mine[place] = jnp.where(keep, self.own[place], self.taken[place])
+
+            @pl.when(jnp.logical_not(self.paired))
+            def _():
+                self.mine[place] = self.own[place]
+
+            if part == 2:
+
+                @pl.when(self.side == 0)
+                def _():
+                    self.quarters()[0].wait_recv()
+
+            for number, axis in enumerate(self.order(part)):
+                self.push(part, 0, axis, number)
+            self.to_partner(part, 0)
+            for i, there, own in self.pieces(part, 0, self.grid.c):
+                pltpu.make_async_copy(own, there, self.local.at[i]).start()
+
+    def stage_b(self):
+        for part in range(3):
+            a, b, c = self.order(part)
+            self.arrived(part, 1 << a)
+            self.push(part, 1 << a, b, 3)
+            self.push(part, 1 << a, c, 4)
+            self.to_partner(part, 1 << a)
+            self.arrived(part, 1 << b)
+            self.push(part, 1 << b, c, 5)
+            self.to_partner(part, 1 << b)
+        for part in range(3):
+            a, b, c = self.order(part)
+            self.arrived(part, 1 << a | 1 << b)
+            self.push(part, 1 << a | 1 << b, c, 6)
+            self.to_partner(part, 1 << a | 1 << b)
+
+    def stage_c(self):
+        for part in range(3):
+            a, b, c = self.order(part)
+            for mask in (1 << c, 1 << a | 1 << c, 1 << b | 1 << c, 7):
+                self.arrived(part, mask)
+                self.to_partner(part, mask)
+
+    def finish(self):
+        for part in range(3):
+            for i, there, own in self.pieces(part, 0, self.grid.c):
+                for number in range(7):
+                    remote(own, there, self.sent.at[i, number], self.got.at[i, 0], self.grid.partner).wait_send()
+                for mask in range(8):
+                    remote(own, there, self.sent_pair.at[i, mask], self.got.at[i, 0], self.grid.partner).wait_send()
+                pltpu.make_async_copy(own, there, self.local.at[i]).wait()
+            for mask in range(8):
+                for i, there, _ in self.pieces(part, mask, 1 - self.grid.c):
+                    remote(there, there, self.sent.at[i, 0], self.got_pair.at[i, mask], self.grid.partner).wait_recv()
+
+        @pl.when(self.paired)
+        def _():
+            for copy in self.swaps():
+                copy.wait_send()
+
+        @pl.when(self.grid.wide == LANE_WIDE)
+        def _():
+            for copy in self.quarters():
+                copy.wait_send()
+
+    def middle(self):
+        self.stage_a()
+        self.stage_b()
+        self.stage_c()
+
+    def index(self, turn):
+        start = lax.rem(self.plan.start + turn, self.plan.long)
+        return jnp.where(self.plan.lane == 0, start, jnp.minimum(turn + 1, LANE_WIDE - 1))
+
+
+class SpanGather(Gather):
+    def __init__(self, grid, plan, source, whole, refs):
+        super().__init__(grid, source, whole, refs[1:5])
+        self.plan, self.own, self.local = plan, refs[0], refs[5]
+
+    @classmethod
+    def scratch(cls, rows, cols):
+        return [pltpu.VMEM((rows, cols), bf16)] + Gather.scratch() + [pltpu.SemaphoreType.DMA((1,))]
+
+    @staticmethod
+    def shape(rows, cols):
+        return (lax.axis_size("wide"), lax.axis_size("narrow"), rows, cols)
+
+    def own_copies(self):
+        there = self.whole.at[self.grid.wide, self.grid.narrow]
+        return (
+            pltpu.make_async_copy(self.source, self.own, self.local.at[0]),
+            pltpu.make_async_copy(self.own, there, self.local.at[0]),
+        )
+
+    def begin(self):
+        super().begin()
+        self.own_copies()[0].start()
+
+    def stage_a(self):
+        self.own_copies()[0].wait()
+        self.own_copies()[1].start()
+        for number in range(1, self.grid.zs):
+            self.along_z(number)
+        self.across(0)
+
+    def stage_b(self):
+        for number in range(1, self.grid.zs):
+            self.across(number)
+        self.last(0)
+
+    def stage_c(self):
+        for number in range(1, self.grid.zs):
+            self.last(number)
+
+    def finish(self):
+        super().finish()
+        self.own_copies()[1].wait()
+
+    def middle(self):
+        self.stage_a()
+        self.stage_b()
+        self.stage_c()
+
+    def index(self, turn):
+        return self.plan.span(turn)
+
+
+def lane_gather():
+    return LaneGather if paired_lanes() else SpanGather
+
+
+def rows_to_lanes(rows, lengths, chunks, pick, tile, ident):
+    wide, narrow = lax.axis_size("wide"), lax.axis_size("narrow")
+    devices = wide * narrow
+    kind = lane_gather()
+
+    def kernel(rows_ref, lengths_ref, chunks_ref, tile_ref, rows_out, chunks_out, tile_out, *refs):
+        hold_chunk, hold_tile, local_sem, send, recv = refs[:5]
+        g = Grid()
+        me = g.wide * narrow + g.narrow
+        wait_all = g.greet_all()
+        own = [
+            (chunks_ref.at[pick(g.wide, g.narrow)], hold_chunk, chunks_out.at[me]),
+            (tile_ref, hold_tile, tile_out.at[me]),
+        ]
+        into = [pltpu.make_async_copy(a, b, local_sem.at[i]) for i, (a, b, _) in enumerate(own)]
+        back = [pltpu.make_async_copy(b, c, local_sem.at[i]) for i, (_, b, c) in enumerate(own)]
+        for copy in into:
+            copy.start()
+        wait_all()
+        gather = kind(g, Plan(lengths_ref, None, lengths.shape[0]), rows_ref, rows_out, refs[5:])
+        gather.begin()
+
+        def send_chunks(step, carry):
+            target = lax.rem(me + step, devices)
+            where = lax.div(target, narrow), lax.rem(target, narrow)
+            remote(chunks_ref.at[pick(*where)], chunks_out.at[me], send.at[0], recv.at[0], where).start()
+            remote(tile_ref, tile_out.at[me], send.at[1], recv.at[1], where).start()
+            return carry
+
+        lax.fori_loop(1, devices, send_chunks, 0)
+        for copy in into:
+            copy.wait()
+        for copy in back:
+            copy.start()
+        gather.middle()
+        for copy in back:
+            copy.wait()
+        for i, out in enumerate((chunks_out, tile_out)):
+            others = out.at[pl.ds(0, devices - 1)]
+            whole = remote(others, others, send.at[i], recv.at[i], g.partner)
+            whole.wait_send()
+            whole.wait_recv()
+        gather.finish()
+
+    return pl.pallas_call(
+        kernel,
+        out_shape=[
+            jax.ShapeDtypeStruct(kind.shape(*rows.shape), rows.dtype),
+            jax.ShapeDtypeStruct((devices,) + chunks.shape[1:], chunks.dtype),
+            jax.ShapeDtypeStruct((devices,) + tile.shape, tile.dtype),
+        ],
+        in_specs=[ANY, pl.BlockSpec(memory_space=pltpu.SMEM), ANY, ANY],
+        out_specs=[ANY] * 3,
+        scratch_shapes=[
+            pltpu.VMEM(chunks.shape[1:], chunks.dtype),
+            pltpu.VMEM(tile.shape, tile.dtype),
+            pltpu.SemaphoreType.DMA((2,)),
+            pltpu.SemaphoreType.DMA((2,)),
+            pltpu.SemaphoreType.DMA((2,)),
+        ]
+        + kind.scratch(*rows.shape),
+        compiler_params=pltpu.CompilerParams(collective_id=ident, has_side_effects=True),
+        name="rows_to_lanes",
+    )(rows, lengths, chunks, tile)
+
+
 def matmul(left_side, right_side):
     return jnp.dot(left_side, right_side, preferred_element_type=jnp.float32)
 
@@ -887,52 +1200,6 @@
             self.pair_copy(chip, lane.colour).wait_send()
 
 
-class Plan:
-    def __init__(self, spans_ref, gates_ref, count):
-        self.wide = lax.axis_size("wide")
-        self.long = min(6, self.wide * 5 // 8)
-        self.gates = gates_ref
-        lengths = [spans_ref[i] for i in range(count)]
-        self.starts, at = [], 0
-        for length in lengths:
-            self.starts.append(at)
-            at = at + length
-        longest, self.start = lengths[0], 0
-        for i in range(1, count):
-            more = lengths[i] > longest
-            longest = jnp.where(more, lengths[i], longest)
-            self.start = jnp.where(more, self.starts[i], self.start)
-        self.lane = lax.div(lax.axis_index("wide"), LANE_WIDE)
-
-    def span(self, turn):
-        rest = jnp.where(turn < self.start, turn, turn + self.long)
-        return jnp.clip(jnp.where(self.lane == 0, self.start + turn, rest), 0, self.wide - 1)
-
-    def valid(self, turn):
-        count = jnp.where(self.lane == 0, self.long, jnp.where(self.lane == 1, self.wide - self.long, 0))
-        return jnp.where(turn < count, 1.0, 0.0)
-
-    def first(self, turn):
-        span = self.span(turn)
-        found = jnp.where(span == self.starts[0], 1.0, 0.0)
-        for start in self.starts[1:]:
-            found = jnp.maximum(found, jnp.where(span == start, 1.0, 0.0))
-        return jnp.maximum(found, 1.0 - self.valid(turn))
-
-    def rates(self, turn):
-        span = self.span(turn)
-        return self.gates[span, 0], self.gates[span, 1], self.gates[span, 2]
-
-    def lane_of(self, span):
-        inside = (span >= self.start) & (span < self.start + self.long)
-        return jnp.where(inside, 0, 1)
-
-    def turn_of(self, span):
-        inside = (span >= self.start) & (span < self.start + self.long)
-        outside = jnp.where(span < self.start, span, span - self.long)
-        return jnp.where(inside, span - self.start, outside)
-
-
 class Deliver:
     def __init__(self, grid, plan, chips, out, got, sems):
         self.grid, self.plan, self.chips, self.out, self.got = grid, plan, chips, out, got
@@ -985,10 +1252,12 @@
     rows = values.shape[1]
     sequences = lengths.shape[0]
     key_turns = turns - 1
-    per_turn = 3 if turns <= 5 else 1
-    first_left = per_turn * (key_turns - 3)
+    kind = lane_gather()
+    own_rows = kind.scratch(span, block)
+    per_turn, ask_from = (2, 2) if paired_lanes() else (1, 3)
+    first_left = per_turn * (key_turns - ask_from)
     slots = 3
-    stream_keys = keys.shape[0] == turns
+    stream_keys = not paired_lanes()
     chips = LANE_WIDE * (lax.axis_size("narrow") // 2)
     n_scatter = len(Scatter.scratch(1, 8, 128))
 
@@ -998,17 +1267,19 @@
         err_hbm, pre_hbm, qpre_hbm, klane_hbm, qlane_hbm = refs[14:19]
         rest = refs[19:]
         kall, qall, vall, kcur, qcur, i1, i2, s1, s2, m1, m2, low1, low2, mb1, mb2, gb1, gb2 = rest[:17]
-        pre, qpre, khid, rec, qpart, qpair, qhalf, qgot, own_hold = rest[17:26]
-        in_sem, out_sem, q_sem, q_pair_send, q_pair_recv, q_send, q_recv = rest[26:33]
-        rest = rest[33:]
+        pre, qpre, khid, rec, qpart, qpair, qhalf, qgot = rest[17:25]
+        in_sem, out_sem, q_sem, q_pair_send, q_pair_recv, q_send, q_recv = rest[25:32]
+        rest = rest[32:]
         lane = Lane()
         grid = Grid()
         plan = Plan(lengths_ref, gates_ref, sequences)
         lookup = Scatter.of(lane, rest[:n_scatter])
         error = Spread.of(lane, rest[n_scatter : n_scatter + 5])
-        gather = Gather(grid, own_hbm, qall, rest[n_scatter + 5 : n_scatter + 9])
-        deliver = Deliver(grid, plan, chips, *rest[n_scatter + 9 : n_scatter + 11], rest[n_scatter + 11 : n_scatter + 13])
-        result = rest[n_scatter + 13]
+        rest = rest[n_scatter + 5 :]
+        gather = kind(grid, plan, own_hbm, qall, rest[: len(own_rows)])
+        rest = rest[len(own_rows) :]
+        deliver = Deliver(grid, plan, chips, *rest[:2], rest[2:4])
+        result = rest[4]
 
         def recall(q, slot):
             sems = q_pair_send.at[pl.ds(q, 1)], q_pair_recv.at[pl.ds(q, 1)], q_send.at[q], q_recv.at[q]
@@ -1037,7 +1308,7 @@
         inputs = [
             pltpu.make_async_copy(source, target, in_sem.at[i])
             for i, (source, target) in enumerate(
-                ((first_hbm, i1), (second_hbm, i2), (keys_hbm, kall), (values_hbm, vall), (own_hbm, own_hold))
+                ((first_hbm, i1), (second_hbm, i2), (keys_hbm, kall), (values_hbm, vall))
             )
             if not (stream_keys and i == 2)
         ]
@@ -1047,15 +1318,12 @@
         gather.begin()
         for copy in inputs:
             copy.wait()
-        own_store = pltpu.make_async_copy(own_hold, qall.at[grid.wide, grid.narrow], in_sem.at[4])
-        own_store.start()
         low1[0] = i1[...]
         low2[0] = i2[...]
         s1[...] = i1[...].astype(f32)
         s2[...] = i2[...].astype(f32)
         for ref in (m1, m2, mb1, mb2):
             ref[...] = jnp.zeros_like(ref)
-        own_store.wait()
 
         def lookup_blocks(buf, first):
             total = matmul(buf[0], first[pl.ds(0, block), :])
@@ -1073,7 +1341,7 @@
                 settle()
             elif waits is not False:
                 pl.when(waits)(settle)
-            index = plan.span(q)
+            index = gather.index(q)
             for b in range(blocks):
                 qcur[slot, b] = qall[index, b]
             query_pre = lookup_blocks(qcur.at[slot], low1.at[q])
@@ -1092,7 +1360,7 @@
                 one.wait()
             else:
                 for b in range(blocks):
-                    kcur[b] = kall[index, b]
+                    kcur[b] = kall[gather.index(turn), b]
             for copy in state_saves(turn):
                 copy.start()
             key_pre = lookup_blocks(kcur, low1.at[turn])
@@ -1101,24 +1369,27 @@
             lookup.part[...] = matmul(khid[...], low2[turn]).astype(bf16).reshape(2, chips, rows, width)
             lookup.start_pair()
 
-            @pl.when(turn == 3)
+            @pl.when(turn == ask_from)
             def _():
                 gather.finish()
 
-            first = per_turn * (turn - 3)
-
-            @pl.when(turn >= 3)
+            first = per_turn * (turn - ask_from)
+
+            @pl.when(turn >= ask_from)
             def _():
                 ask(first, lax.rem(first, slots), first >= slots)
 
             lookup.take_pair()
             lookup.start_sends()
 
-            @pl.when(turn >= 3)
+            @pl.when(turn >= ask_from)
             def _():
                 recall(first, lax.rem(first, slots)).take_pair()
                 for j in range(1, per_turn):
                     ask(first + j, lax.rem(first + j, slots), first + j >= slots)
+
+            if paired_lanes():
+                pl.when(turn == 1)(gather.stage_b)
 
             total = lookup.total()
             target = jnp.concatenate([vall[index * blocks + b] for b in range(blocks)], axis=1)
@@ -1126,13 +1397,17 @@
             error.run()
             lookup.wait_sends()
 
-            @pl.when(turn >= 3)
+            @pl.when(turn >= ask_from)
             def _():
                 recall(first, lax.rem(first, slots)).start_sends()
                 for j in range(1, per_turn):
                     stream = recall(first + j, lax.rem(first + j, slots))
                     stream.take_pair()
                     stream.start_sends()
+
+            if paired_lanes():
+                pl.when(turn == 0)(gather.stage_a)
+                pl.when(turn == 1)(gather.stage_c)
 
             err = error.whole[...].reshape(span, width)
             grad_second = inner_left(khid[...], err)
@@ -1166,22 +1441,10 @@
             for copy in saves:
                 copy.start()
 
-            @pl.when(turn == 0)
-            def _():
-                for number in range(1, grid.zs):
-                    gather.along_z(number)
-                gather.across(0)
-
-            @pl.when(turn == 1)
-            def _():
-                for number in range(1, grid.zs):
-                    gather.across(number)
-                gather.last(0)
-
-            @pl.when(turn == 2)
-            def _():
-                for number in range(1, grid.zs):
-                    gather.last(number)
+            if not paired_lanes():
+                pl.when(turn == 0)(gather.stage_a)
+                pl.when(turn == 1)(gather.stage_b)
+                pl.when(turn == 2)(gather.stage_c)
 
             for copy in saves:
                 copy.wait()
@@ -1233,7 +1496,7 @@
     )
     sem = pltpu.SemaphoreType.DMA
     scratch = (
-        [pltpu.VMEM((1 if stream_keys else keys.shape[0], blocks, span, block), bf16), pltpu.VMEM((wide, blocks, span, block), bf16)]
+        [pltpu.VMEM((1 if stream_keys else keys.shape[0], blocks, span, block), bf16), pltpu.VMEM(kind.shape(span, block), bf16)]
         + [pltpu.VMEM(values.shape, bf16)]
         + [pltpu.VMEM((blocks, span, block), bf16), pltpu.VMEM((slots, blocks, span, block), bf16)]
         + [pltpu.VMEM(s, bf16) for s in state]
@@ -1248,11 +1511,10 @@
             pltpu.VMEM((slots, 2, chips, rows, width), bf16),
         ]
         + [pltpu.VMEM((n, chips, rows, width), bf16) for n in (turns, slots, turns)]
-        + [pltpu.VMEM((span, block), bf16)]
-        + [sem((5,)), sem((7,)), sem((slots, 2)), sem((turns,)), sem((turns,)), sem((turns, chips)), sem((turns, chips))]
+        + [sem((4,)), sem((7,)), sem((slots, 2)), sem((turns,)), sem((turns,)), sem((turns, chips)), sem((turns, chips))]
         + Scatter.scratch(chips, rows, width)
         + Spread.scratch(chips, rows, width)
-        + Gather.scratch()
+        + own_rows
         + Deliver.scratch(1, rows, block)
         + [pltpu.VMEM((1, 2, chips, rows, block), bf16)]
     )
@@ -1282,6 +1544,8 @@
     width, hidden = low1_all.shape[1:]
     chips, rows = err_all.shape[2:4]
     n_scatter = len(Scatter.scratch(1, 8, 128))
+    kind = lane_gather()
+    own_rows = kind.scratch(span, block)
 
     def kernel(*refs):
         own_hbm, q_ins, k_ins, lengths_ref, gates_ref = refs[0], refs[1:5], refs[5:12], refs[12], refs[13]
@@ -1290,10 +1554,10 @@
         q_bufs, k_bufs, rest = rest[:4], rest[4:11], rest[11:]
         qbuf, low1, low2, qpre = q_bufs
         kbuf, m1, m2, g1, g2, errs, pre = k_bufs
-        rall, own_hold, cf, cs, cmf, cms, w1, w2, a1, a2, c1, c2 = rest[:12]
-        dh, khid, qpl, qhid, kpl, slow, sg, hk, qcots, kcots, vcots, sumrows, tile, mb1, mb2, result = rest[12:28]
-        q_sem, k_sem, end_sem, own_sem, tile_send, tile_recv = rest[28:34]
-        rest = rest[34:]
+        rall, cf, cs, cmf, cms, w1, w2, a1, a2, c1, c2 = rest[:11]
+        dh, khid, qpl, qhid, kpl, slow, sg, hk, qcots, kcots, vcots, sumrows, tile, mb1, mb2, result = rest[11:27]
+        q_sem, k_sem, end_sem, tile_send, tile_recv = rest[27:32]
+        rest = rest[32:]
         lane = Lane()
         grid = Grid()
         plan = Plan(lengths_ref, gates_ref, lengths.shape[0])
@@ -1301,8 +1565,9 @@
         qstream = Scatter.of(lane, rest[n_scatter : 2 * n_scatter])
         kstream = Scatter.of(lane, rest[2 * n_scatter : 3 * n_scatter])
         spread = Spread.of(lane, rest[3 * n_scatter : 3 * n_scatter + 5])
-        gather = Gather(grid, own_hbm, rall, rest[3 * n_scatter + 5 : 3 * n_scatter + 9])
-        rest = rest[3 * n_scatter + 9 :]
+        rest = rest[3 * n_scatter + 5 :]
+        gather = kind(grid, plan, own_hbm, rall, rest[: len(own_rows)])
+        rest = rest[len(own_rows) :]
         deliver = Deliver(grid, plan, chips, *rest[:2], rest[2:4])
 
         def q_loads(turn, slot):
@@ -1317,19 +1582,13 @@
                 for i, (source, target) in enumerate(zip(k_ins, k_bufs))
             ]
 
-        own = pltpu.make_async_copy(own_hbm, own_hold, own_sem.at[0])
-        own.start()
         grid.greet_all()()
         gather.begin()
         for copy in q_loads(turns - 1, 0) + q_loads(turns - 2, 1) + k_loads(turns - 2, 1):
             copy.start()
-        own.wait()
-        own_store = pltpu.make_async_copy(own_hold, rall.at[grid.wide, grid.narrow], own_sem.at[0])
-        own_store.start()
         for ref in (cf, cs, cmf, cms, a1, a2):
             ref[...] = jnp.zeros_like(ref)
         gather.middle()
-        own_store.wait()
         gather.finish()
 
         kcots[turns - 1] = jnp.zeros((rows, width), bf16)
@@ -1341,7 +1600,7 @@
             stream.wait_sends()
 
         def query_rows(turn, slot):
-            index = plan.span(turn)
+            index = gather.index(turn)
             back = inner_right(rall[index, 0], low2[slot, :, pl.ds(0, block)])
             for b in range(1, blocks):
                 back = back + inner_right(rall[index, b], low2[slot, :, pl.ds(b * block, block)])
@@ -1352,7 +1611,7 @@
             qstream.start_pair()
 
         def query_weights(turn, slot):
-            index = plan.span(turn)
+            index = gather.index(turn)
             valid = plan.valid(turn)
             for b in range(blocks):
                 w1[pl.ds(b * block, block), :] = inner_left(qbuf[slot, b], qpl[...])
@@ -1536,7 +1795,7 @@
     sem = pltpu.SemaphoreType.DMA
     scratch = (
         [pltpu.VMEM((2,) + s, t) for s, t in q_buffers + k_buffers]
-        + [pltpu.VMEM((wide, blocks, span, block), bf16), pltpu.VMEM((span, block), bf16)]
+        + [pltpu.VMEM(kind.shape(span, block), bf16)]
         + [pltpu.VMEM(s, f32) for s in state * 4]
         + [pltpu.VMEM((2,) + state[0], bf16), pltpu.VMEM(state[1], bf16)]
         + [pltpu.VMEM((span, hidden), bf16)] * 6
@@ -1545,10 +1804,10 @@
         + [pltpu.VMEM((turns, 8, 128), f32), pltpu.VMEM((wide, 128), f32)]
         + [pltpu.VMEM(s, bf16) for s in by_owner]
         + [pltpu.VMEM((3, 2, chips, rows, block), bf16)]
-        + [sem((2, 4)), sem((2, 7)), sem((3,)), sem((1,)), sem((1,)), sem((1,))]
+        + [sem((2, 4)), sem((2, 7)), sem((3,)), sem((1,)), sem((1,))]
         + Scatter.scratch(chips, rows, width) * 3
         + Spread.scratch(chips, rows, width)
-        + Gather.scratch()
+        + own_rows
         + Deliver.scratch(3, rows, block)
     )
     vmem = pl.BlockSpec(memory_space=pltpu.VMEM)
@@ -1708,7 +1967,7 @@
     gate_tile = jnp.broadcast_to(jnp.pad(gate_sig * gate_scale, (0, 125))[None], (8, 128))
 
     key_all, value_got, gate_got = rows_to_lanes(
-        key_low, value_low.reshape(shards, shard_rows, local_width), shard_of, gate_tile, 2
+        key_low, seq_spans, value_low.reshape(shards, shard_rows, local_width), shard_of, gate_tile, 2
     )
     later = (ffn_gate, ffn_up, ffn_down, jnp.concatenate([out_gate, out_proj.T], 1))
     key_all, *later = lax.optimization_barrier((key_all,) + later)
@@ -1719,7 +1978,7 @@
     gate_cols = out_weights[:, :local_width]
     proj_cols = out_weights[:, local_width:]
     gate_rows = gate_got[::narrow, 0, :3]
-    if wide > 8:
+    if not paired_lanes():
         long_start = (jnp.cumsum(seq_spans) - seq_spans)[jnp.argmax(seq_spans)]
         turn_order = jnp.arange(turns, dtype=jnp.int32)
         rest_order = jnp.where(turn_order < long_start, turn_order, turn_order + long_turns)

time: 954 us -> 904 us (0.948)
  Pallas kernels: 714 us -> 661 us
    pallas_call x1, Pallas kernels: 212 us -> 188 us  [chain_forward(): pl.pallas_call(kernel, out_shape=out_shape, in_specs=[ANY] * 3 + [smem] *...]
    pallas_call x1, Pallas kernels: 266 us -> 251 us  [chain_backward(): pl.pallas_call(kernel, out_shape=out_shape, in_specs=[ANY] * 12 + [smem]...]
    pallas_call x1, Pallas kernels: 60.1 us -> 45.3 us  [rows_to_lanes(): pl.pallas_call(kernel, out_shape=[jax.ShapeDtypeStruct(kind.shape(*rows.s...]
  transfers between devices with their start and end apart: 10 -> 10, of which waited for: 3 -> 2; matrix products, arithmetic and copies ran while one was open for 12% -> 13% of each run, Pallas kernels for 60% -> 60%
where the time goes in v4:
time: 904 us; the launch traced here: 886 us
  Pallas kernels  661 us (73%)
  matrix products  70.5 us (8%)
  local copies, waits for them, and re-layouts  67.5 us (7%)
  other arithmetic  48.1 us (5%)
  between operations  17.8 us (2%)
  waiting for transfers between devices  15.4 us (2%)
    pallas_call x1, Pallas kernels, chain_backward(): pl.pallas_call(kernel, out_shape=out_shape, in_specs=[ANY] * 12 + [smem]...  251 us
    pallas_call x1, Pallas kernels, chain_forward(): pl.pallas_call(kernel, out_shape=out_shape, in_specs=[ANY] * 3 + [smem] *...  188 us
    pallas_call x1, Pallas kernels, last_step(): pl.pallas_call(kernel, out_shape=[jax.ShapeDtypeStruct((narrow, rows, wid...  66.5 us
    pallas_call x2, Pallas kernels, narrow_step(): pl.pallas_call(kernel, out_shape=[jax.ShapeDtypeStruct((narrow, rows, wid...  55.3 us
    pallas_call x1, Pallas kernels, send_parameters(): pl.pallas_call(kernel, out_shape=[jax.ShapeDtypeStruct((devices,) + small...  54.7 us
    pallas_call x1, Pallas kernels, rows_to_lanes(): pl.pallas_call(kernel, out_shape=[jax.ShapeDtypeStruct(kind.shape(*rows.s...  45.3 us
    unnamed x189, local copies, waits for them, and re-layouts  24.6 us
    dot_general x6, matrix products, matmul(): return jnp.dot(left_side, right_side, preferred_element_type=jnp.float32)  18.2 us
  transfers between devices with their start and end apart: 10, of which 2 were waited for; matrix products, arithmetic and copies ran while one was open for 13% of the time, Pallas kernels for 60%

profile of v4, /device:TPU:0, one launch (start us, length us, event | category | flops | bytes accessed | tf_op | source)
XLA Modules:
  0.0 886.3 jit_solution(16846298662207275784)
XLA Ops:
  16.9 54.7 %send_parameters.1 = (bf16[32,16,128]{2,1,0:T(8,128)(2,1)}, bf16[8,4,32,768]{3,2,1,0:T(8,128)(2,1)}, bf16[8,128,256]{2,1,0:T(8,128)(2,1)}, bf16[8,256,128]{2,1,0:T(8,128)(2,1)}) custom-call(bf16[16,128]{1,0:T(8,128)(2,1)} %pad_bitcast_fusion.1.refs_0_, bf16[4,32,768]{2,1,0:T(8,128)(2,1)} %maximum_bitcast_fusion.refs_1_, bf16[4,128,256]{2,1,0:T(8,128)(2,1)} %bitcast.210, ...), custom_call_target="tpu_custom_call" | custom-call | tf_op jit(solution)/shard_map/send_parameters/pallas_call | solution.py:328
  72.8 2.5 fusion.89
  76.4 4.6 collective-permute-start
  86.6 5.3 fusion.27
  105.9 45.3 %rows_to_lanes.1 = (bf16[5,4,512,256]{3,2,1,0:T(8,128)(2,1)}, bf16[32,32,256]{2,1,0:T(8,128)(2,1)}, f32[32,8,128]{2,1,0:T(8,128)}) custom-call(bf16[512,256]{1,0:T(8,128)(2,1)} %get-tuple-element.192.rows_ref, s32[3]{0:T(128)} %refs_12_.1, bf16[16,32,256]{2,1,0:T(8,128)(2,1)} %bitcast.192, f32[8,128]{1,0:T(8,128)} %broadcast_in_dim.31.tile_ref), custom_call_target="tpu_custom_call" | custom-call | tf_op jit(solution)/shard_map/rows_to_lanes/pallas_call | solution.py:1017
  162.2 188.1 %chain_forward.1 = (bf16[2,8,32,256]{3,2,1,0:T(8,128)(2,1)}, bf16[5,1024,256]{2,1,0:T(8,128)(2,1)}, bf16[5,256,1024]{2,1,0:T(8,128)(2,1)}, bf16[4,1024,256]{2,1,...) custom-call(bf16[5,4,512,256]{3,2,1,0:T(8,128)(2,1)} %get-tuple-elem, ...), custom_call_target="tpu_custom_call" | custom-call | flops 53687091200 | bytes 209715200 | tf_op jit(solution)/shard_map/chain_forward/pallas_call | solution.py:1522
  354.0 2.9 fusion.96
  360.3 2.4 fusion.9
  362.8 2.7 fusion.52
  366.9 22.1 %narrow_step_7.1 = (bf16[4,128,1024]{2,1,0:T(8,128)(2,1)}, f32[128,1024]{1,0:T(8,128)}) custom-call(bf16[2,2,128,1024]{3,2,1,0:T(8,128)(2,1)} %bitcast.186, bf16[128,1024]{1,0:T(8,128)(2,1)} %constant_dynamic-slice_fusion.3.refs_1_.refs_5_, f32[1,1024]{1,0:T(1,128)} %reshape.419.refs_2_.refs_4_), custom_call_target="tpu_custom_call" | custom-call | tf_op jit(solution)/shard_map/narrow_step_7/pallas_call | solution.py:436
  389.0 4.5 fusion.98
  393.5 4.5 fusion.97
  398.0 10.0 %all-gather.11.cloned.1.call-done = bf16[1024,1024]{1,0:T(8,128)(2,1)} async-done(((bf16[1024,128]{1,0:T(8,128)(2,1)}), bf16[1024,1024]{1,0:T(8,128)(2,1)}) %all-gather.11.cloned.1.call-update) | async-done | bytes 2097168 | tf_op jit(solution)/shard_map/all_gather | solution.py:1977
  408.1 6.2 fusion.22
  415.3 2.6 convolution_convert_fusion
  417.9 4.2 convolution_convert_fusion.1
  422.1 4.2 convert_bitcast_fusion
  430.4 2.3 add_convert_fusion.1
  432.6 33.2 %narrow_step_9.1 = (bf16[4,128,1024]{2,1,0:T(8,128)(2,1)}, bf16[4,128,1024]{2,1,0:T(8,128)(2,1)}, f32[128,1024]{1,0:T(8,128)}, f32[1,1024]{1,0:T(1,128)}) custom-call(bf16[2,2,128,1024]{3,2,1,0:T(8,128)(2,1)} %bitcast.202, bf16[2,2,128,1024]{3,2,1,0:T(8,128)(2,1)} %bitcast.203, f32[128,1024]{1,0:T(8,128)} %get-tuple-element.78.refs_2_, ...), custom_call_target="tpu_custom_call" | custom-call | tf_op jit(solution)/shard_map/narrow_step_9/pallas_call | solution.py:436
  473.1 4.0 copy.174
  477.0 6.5 multiply_reduce_fusion
  483.6 10.3 %multiply_convert_fusion = bf16[4,512,1040]{1,2,0:T(8,128)(2,1)} fusion(f32[4,512,1040]{1,2,0:T(8,128)} %get-tuple-element.218, f32[4,512,1040]{1,2,0:T(8,128)} %copy-done.8, f32[4,512]{1,0:T(4,128)S(1)} %get-tuple-element.217, f32[4,512]{1,0:T(4,128)S(1)} %log_add_fusion), kind=kLoop, calls=%fused_computation.4 | loop fusion | flops 8519680 | bytes 21315584 | tf_op jit(solution)/shard_map/convert_element_type | solution.py:2093
  493.9 3.6 fusion.10
  497.6 5.4 fusion.11
  504.9 251.0 %chain_backward.1 = (bf16[3,2,8,32,256]{4,3,2,1,0:T(8,128)(2,1)}, f32[32,8,128]{2,1,0:T(8,128)}, bf16[8,128,256]{2,1,0:T(8,128)(2,1)}, bf16[8,256,128]{2,1,0:T(8,128)(2,1)}) custom-call(bf16[512,256]{1,0:T(8,128)(2,1)} %copy.156.refs_0_, bf16[5,4,512,256]{3,2,1,0:T(8,128)(2,1)} %get-tuple-element.81.refs_1_, ...), custom_call_target="tpu_custom_call" | custom-call | flops 107374182400 | bytes 314572800 | tf_op jit(solution)/shard_map/chain_backward/pallas_call | solution.py:1815
  764.0 3.2 fusion.32
  769.8 2.6 fusion.42
  774.8 3.4 multiply_reduce_fusion.3
  784.2 2.9 pad_add_fusion
  787.7 4.0 collective-permute-done.1
  791.7 2.3 convolution_convert_fusion.2
  795.6 66.5 %last_step.1 = (bf16[4,128,1024]{2,1,0:T(8,128)(2,1)S(1)}, f32[128,768]{1,0:T(8,128)S(1)}, f32[128,1024]{1,0:T(8,128)S(1)}, f32[1024,128]{1,0:T(8,128)S(1)}, f32...) custom-call(bf16[2,2,128,1024]{3,2,1,0:T(8,128)(2,1)S(1)} %bitcast.177, bf16[4,2,128,768]{3,2,1,0:T(8,128)(2,1)} %bitcast.199, ...), custom_call_target="tpu_custom_call" | custom-call | tf_op jit(solution)/shard_map/last_step/pallas_call | solution.py:622
  (366 shorter events, 100.5 us)
Async XLA Ops:
  7.2 148.3 %copy-start = (bf16[512,1024]{1,0:T(8,128)(2,1)S(1)}, bf16[512,1024]{1,0:T(8,128)(2,1)}, u32[]{:S(2)}) copy-start(bf16[512,1024]{1,0:T(8,128)(2,1)} %param.21) | copy-start | bytes 3145732
  7.2 65.5 %copy-start.16 = (bf16[512,1024]{1,0:T(8,128)(2,1)S(1)}, bf16[512,1024]{1,0:T(8,128)(2,1)}, u32[]{:S(2)}) copy-start(bf16[512,1024]{1,0:T(8,128)(2,1)} %param.20) | copy-start | bytes 3145732
  7.2 9.0 %copy-start.52 = (bf16[32,1024]{1,0:T(8,128)(2,1)S(1)}, bf16[32,1024]{1,0:T(8,128)(2,1)}, u32[]{:S(2)}) copy-start(bf16[32,1024]{1,0:T(8,128)(2,1)} %param.25) | copy-start | bytes 196612
  7.2 9.0 %copy-start.53 = (bf16[32,1024]{1,0:T(8,128)(2,1)S(1)}, bf16[32,1024]{1,0:T(8,128)(2,1)}, u32[]{:S(2)}) copy-start(bf16[32,1024]{1,0:T(8,128)(2,1)} %param.24) | copy-start | bytes 196612
  7.2 355.5 %all-gather.5.cloned.1.call-start = ((), (), s32[]{:S(2)}) async-start(), calls=%async_computation.4 | async-start | bytes 1179648 | tf_op jit(solution)/shard_map/all_gather | solution.py:1974
  10.5 70.6 %copy-start.71 = (f32[512]{0:T(512)}, f32[512]{0:T(512)S(1)}, u32[]{:S(2)}) copy-start(f32[512]{0:T(512)S(1)} %add_rsqrt_fusion.4) | copy-start | bytes 6148
  72.7 8.3 copy-start.69
  72.8 8.7 copy-start.51
  76.4 7.0 copy-start.77
  76.4 7.5 copy-start.73
  76.4 10.1 %collective-permute-start = (bf16[3,768]{1,0:T(4,128)(2,1)S(1)}, bf16[3,768]{1,0:T(4,128)(2,1)S(1)}, u32[]{:S(2)}, u32[]{:S(2)}) collective-permute-start(bf16[3,768]{1,0:T(4,128)(2,1)S(1)} %slice.302), channel_id=1, source_target_pairs={{0,4},{4,8},{8,12},{12,16},{16,20},{20,24},{24,28},{1,5},{5,9},{9,... | collective-permute-start | bytes 13832 | tf_op jit(solution)/shard_map/ppermute | solution.py:1837
  95.0 7.1 copy-start.19
  95.1 8.3 copy-start.49
  98.3 7.0 copy-start.47
  105.3 51.0 %copy-start.41 = (bf16[8,256,128]{2,1,0:T(8,128)(2,1)S(1)}, bf16[8,256,128]{2,1,0:T(8,128)(2,1)}, u32[]{:S(2)}) copy-start(bf16[8,256,128]{2,1,0:T(8,128)(2,1)} %get-tuple-element.69) | copy-start | bytes 1572868
  151.2 237.9 %all-gather.9.cloned.1.call-start = ((), (), s32[]{:S(2)}) async-start(), calls=%async_computation.6 | async-start | bytes 2359296 | tf_op jit(solution)/shard_map/all_gather | solution.py:1976
  151.9 241.6 %all-gather.7.cloned.1.call-start = ((), (), s32[]{:S(2)}) async-start(), calls=%async_computation.5 | async-start | bytes 2359296 | tf_op jit(solution)/shard_map/all_gather | solution.py:1975
  152.7 6.0 copy-start.27
  152.9 6.7 copy-start.28
  153.1 7.3 copy-start.33
  153.8 6.7 copy-start.35
  162.1 245.9 %all-gather.11.cloned.1.call-start = ((), (), s32[]{:S(2)}) async-start(), calls=%async_computation.7 | async-start | bytes 2359296 | tf_op jit(solution)/shard_map/all_gather | solution.py:1977
  352.1 516.4 %reduce-scatter.13.cloned.1.call-start = ((), (), s32[]{:S(2)}) async-start(), calls=%async_computation.10 | async-start | bytes 1179648
  408.1 7.3 copy-start.82
  472.1 399.0 %reduce-scatter.11.cloned.1.call-start = ((), (), s32[]{:S(2)}) async-start(), calls=%async_computation.9 | async-start | bytes 2359296 | tf_op jit(solution)/shard_map/reduce_scatter | solution.py:2065
  472.6 400.2 %reduce-scatter.15.cloned.1.call-start = ((), (), s32[]{:S(2)}) async-start(), calls=%async_computation.11 | async-start | bytes 2359296
  504.8 370.1 %reduce-scatter.9.cloned.1.call-start = ((), (), s32[]{:S(2)}) async-start(), calls=%async_computation.8 | async-start | bytes 2359296 | tf_op jit(solution)/shard_map/reduce_scatter | solution.py:2065
  504.9 252.9 %copy-start.74 = (f32[1,1024]{1,0:T(1,128)S(1)}, f32[1,1024]{1,0:T(1,128)}, u32[]{:S(2)}) copy-start(f32[1,1024]{1,0:T(1,128)} %get-tuple-element.95) | copy-start | bytes 12292
  504.9 253.7 %slice-start = ((f32[1040,4,64]{0,2,1:T(8,128)}), f32[16,4,64]{0,2,1:T(8,128)S(1)}, s32[]{:S(2)}) async-start(f32[1040,4,64]{0,2,1:T(8,128)} %copy-done.25), calls=%async_computation.12 | async-start | bytes 262144 | tf_op jit(solution)/shard_map/slice | solution.py:2105
  782.6 9.1 %collective-permute-start.1 = (bf16[3,768]{1,0:T(4,128)(2,1)S(1)}, bf16[3,768]{1,0:T(4,128)(2,1)S(1)}, u32[]{:S(2)}, u32[]{:S(2)}) collective-permute-start(bf16[3,768]{1,0:T(4,128)(2,1)S(1)} %fusion.79), channel_id=1, source_target_pairs={{4,0},{8,4},{12,8},{16,12},{20,16},{24,20},{28,24},{5,1},{9,5},{13... | collective-permute-start | bytes 13832 | tf_op jit(solution)/shard_map/ppermute | solution.py:1837
  787.7 6.3 copy-start.81
  869.5 7.1 copy-start.34
  (66 other events, 191.5 us)
Sparse Core Ops, SparseCore 0:
  151.3 50.0 all-gather.4
  203.5 64.5 all-gather.8
  270.2 80.6 all-gather.6
  352.7 55.2 all-gather.10
  472.2 62.7 reduce-scatter.12
  538.7 84.3 reduce-scatter.10
  627.1 90.2 reduce-scatter.14
  774.8 100.0 reduce-scatter.8

commit v5 on v4

--- a/solution.py
+++ b/solution.py
@@ -28,6 +28,8 @@
     )
 
 
+def sigmoid(values):
+    return 1.0 / (1.0 + jnp.exp(-values))
 class Grid:
     def __init__(self):
         wide, narrow = lax.axis_size("wide"), lax.axis_size("narrow")
@@ -213,19 +215,19 @@
                         ).wait_recv()
 
 
-def send_parameters(smalls, weights, blocks, ident):
+def send_parameters(smalls, weights, blocks, tokens, ident):
     wide, narrow = lax.axis_size("wide"), lax.axis_size("narrow")
     devices = wide * narrow
     count = len(blocks)
 
     def kernel(*refs):
         smalls_ref, weights_ref = refs[:2]
-        block_refs, refs = refs[2 : 2 + count], refs[2 + count :]
+        block_refs, tokens_ref, refs = refs[2 : 2 + count], refs[2 + count], refs[3 + count :]
         smalls_out, weights_out = refs[:2]
-        block_outs, refs = refs[2 : 2 + count], refs[2 + count :]
+        block_outs, tail_out, refs = refs[2 : 2 + count], refs[2 + count], refs[3 + count :]
         hold_small, hold_weight, refs = refs[0], refs[1], refs[2:]
         hold_blocks, refs = refs[:count], refs[count:]
-        local_sem, all_send, all_recv, near_send, near_recv, z_send, z_recv, x_send, x_recv, b_send, b_recv = refs
+        local_sem, all_send, all_recv, near_send, near_recv, z_send, z_recv, x_send, x_recv, b_send, b_recv, t_sem = refs
         g = Grid()
         me = g.wide * narrow + g.narrow
         wait_all = g.greet_all()
@@ -253,6 +255,14 @@
             )
             copy.start()
             near.append(copy)
+        tail = remote(
+            tokens_ref.at[pl.ds(tokens_ref.shape[0] - 8, 8)],
+            tail_out,
+            t_sem.at[0],
+            t_sem.at[1],
+            (lax.rem(g.wide + 1, wide), g.narrow),
+        )
+        tail.start()
 
         def send_small(step, carry):
             target = lax.rem(me + step, devices)
@@ -291,6 +301,10 @@
             push(g.z, g.device(z, g.x, g.y, g.c), z_send.at[i], z_recv.at[g.z])
         for i, x in enumerate(g.x_others()):
             push(g.z, g.device(g.z, x, g.y, g.c), x_send.at[0, i], x_recv.at[g.z, g.x])
+        for j, z in enumerate(g.z_others()):
+            remote(row(z, g.x), row(z, g.x), z_send.at[0], z_recv.at[z], g.partner).wait_recv()
+            for i, x in enumerate(g.x_others()):
+                push(z, g.device(g.z, x, g.y, g.c), x_send.at[1 + j, i], x_recv.at[z, g.x])
         for s in range(1, wide):
             target = lax.rem(g.wide + s, wide)
             for i in range(count):
@@ -303,10 +317,6 @@
                 )
                 copy.start()
                 sends.append(copy)
-        for j, z in enumerate(g.z_others()):
-            remote(row(z, g.x), row(z, g.x), z_send.at[0], z_recv.at[z], g.partner).wait_recv()
-            for i, x in enumerate(g.x_others()):
-                push(z, g.device(g.z, x, g.y, g.c), x_send.at[1 + j, i], x_recv.at[z, g.x])
         for x in g.x_others():
             for z in [g.z] + g.z_others():
                 remote(row(z, x), row(z, x), z_send.at[0], x_recv.at[z, x], g.partner).wait_recv()
@@ -317,6 +327,7 @@
                 remote(there, there, z_send.at[0], b_recv.at[i, source], g.partner).wait_recv()
         for copy in near + sends:
             copy.wait_send()
+        tail.wait()
         others = smalls_out.at[pl.ds(0, devices - 1)]
         whole = remote(others, others, all_send.at[0], all_recv.at[0], g.partner)
         whole.wait_send()
@@ -331,16 +342,17 @@
             jax.ShapeDtypeStruct((devices,) + smalls.shape, smalls.dtype),
             jax.ShapeDtypeStruct((wide, narrow) + weights.shape[1:], weights.dtype),
         ]
-        + [jax.ShapeDtypeStruct((wide,) + b.shape[1:], b.dtype) for b in blocks],
-        in_specs=[ANY] * (2 + count),
-        out_specs=[ANY] * (2 + count),
+        + [jax.ShapeDtypeStruct((wide,) + b.shape[1:], b.dtype) for b in blocks]
+        + [jax.ShapeDtypeStruct((8, tokens.shape[1]), tokens.dtype)],
+        in_specs=[ANY] * (3 + count),
+        out_specs=[ANY] * (3 + count),
         scratch_shapes=[pltpu.VMEM(smalls.shape, smalls.dtype), pltpu.VMEM(weights.shape[1:], weights.dtype)]
         + [pltpu.VMEM(b.shape[1:], b.dtype) for b in blocks]
         + [sem((2 + count,)), sem((1,)), sem((1,)), sem((narrow,)), sem((narrow,)), sem((zs,)), sem((zs,))]
-        + [sem((zs, xs)), sem((zs, xs)), sem((count, wide)), sem((count, wide))],
+        + [sem((zs, xs)), sem((zs, xs)), sem((count, wide)), sem((count, wide)), sem((2,))],
         compiler_params=pltpu.CompilerParams(collective_id=ident, has_side_effects=True),
         name="send_parameters",
-    )(smalls, weights, *blocks)
+    )(smalls, weights, *blocks, tokens)
 
 
 def narrow_step(parts, extras, work, spread_count, locals_like, ident):
@@ -377,7 +389,8 @@
         for i in range(count):
             loads[i].wait()
             pairs[i].wait_recv()
-            half[i] = (mine[i].astype(f32) + pair[i].astype(f32)).astype(bf16)
+            mine[i] += pair[i]
+            half[i] = mine[i].astype(bf16)
             for s, y in enumerate(g.y_others()):
                 copy = remote(
                     half.at[i, y], got.at[i, g.y], y_send.at[i, s], y_recv.at[i, g.y], g.device(g.z, g.x, y, g.c)
@@ -386,7 +399,7 @@
                 sends.append(copy)
         totals = []
         for i in range(count):
-            total = half[i, g.y].astype(f32)
+            total = mine[i, g.y]
             for y in g.y_others():
                 remote(got.at[i, y], got.at[i, y], y_send.at[i, 0], y_recv.at[i, y], g.partner).wait_recv()
                 total = total + got[i, y].astype(f32)
@@ -439,19 +452,25 @@
         + [jax.ShapeDtypeStruct(shape, dtype) for shape, dtype in locals_like],
         in_specs=[ANY] * count + [vmem] * extra_count,
         out_specs=[ANY] * spread_count + [vmem] * local_count,
-        scratch_shapes=[pltpu.VMEM((count, ys, rows, width), bf16)] * 4
+        scratch_shapes=[pltpu.VMEM((count, ys, rows, width), f32)] * 2
+        + [pltpu.VMEM((count, ys, rows, width), bf16)] * 2
         + [pltpu.VMEM((spread_count, rows, width), bf16)]
         + [sem((count,))] * 3
         + [sem((count, ys))] * 2
         + [sem((spread_count, ys))] * 4
         + [sem((spread_count,))],
         compiler_params=pltpu.CompilerParams(collective_id=ident, has_side_effects=True),
+        cost_estimate=pl.CostEstimate(flops=30 * 10**9, bytes_accessed=100 * 2**20, transcendentals=0),
         name=f"narrow_step_{ident}",
     )(*parts, *extras)
 
 
-def last_step(part, extras, work, grads, chunks, flat, ident):
-    narrow, rows, width = part.shape
+def last_step(heads, conv, lengths, gate_back, extras, work, early, chunks, flat, ident):
+    span, columns = conv[0].shape
+    block = columns // 3
+    width = conv[3].shape[0]
+    narrow = lax.axis_size("narrow")
+    rows = span // narrow
     wide = lax.axis_size("wide")
     devices = wide * narrow
     ys = narrow // 2
@@ -459,47 +478,77 @@
     xs = wide // zs
     lanes = wide // LANE_WIDE
     extra_count = len(extras)
-    part = part.reshape(ys, 2, rows, width)
-    own_grad = grads.shape[1:]
-    grads = grads.reshape((zs, xs) + own_grad)
+    own_grad, own_early = (width // wide, columns), (width // wide, early.shape[1])
+    early = early.reshape((zs, xs) + own_early)
+    compute = list(heads) + list(conv) + list(gate_back)
+    compute_count = len(compute)
+    count = 4
     first_shape, second_shape, flat_shape = chunks[0].shape[1:], chunks[1].shape[1:], flat.shape[1:]
 
     def kernel(*refs):
-        part_ref, grads_ref, first_ref, second_ref, flat_ref = refs[:5]
-        extra_refs, refs = refs[5 : 5 + extra_count], refs[5 + extra_count :]
-        spread_ref, grads_out, first_out, second_out, flat_out, row_out, refs = refs[:6] + (refs[6:],)
-        mine, pair, half, got, rowbuf, rowtile, rowgot, refs = refs[:7] + (refs[7:],)
-        gown, gx, ghalf, gz, fgot, sgot, flatgot, refs = refs[:7] + (refs[7:],)
+        first_ref, second_ref, flat_ref, early_ref, lengths_ref = refs[:5]
+        compute_refs, refs = refs[5 : 5 + compute_count], refs[5 + compute_count :]
+        extra_refs, refs = refs[:extra_count], refs[extra_count:]
+        spread_ref, grads_out, first_out, second_out, flat_out, row_out, taps_out, early_out = refs[:8]
+        refs = refs[8:]
+        part_ref, grads_ref, conv_grad, tap_rows, halo_out, halo_in, halo_sem, taps_sem, refs = refs[:8] + (refs[8:],)
+        pair, half, got, rowbuf, rowtile, rowgot, refs = refs[:6] + (refs[6:],)
+        gx, ghalf, gz, fgot, sgot, flatgot, refs = refs[:6] + (refs[6:],)
         load_sem, pair_sem, y_send, y_recv, s_send, s_recv, p_send, p_recv, refs = refs[:8] + (refs[8:],)
-        gx_send, gx_recv, gz_send, gz_recv, c_send, c_recv, all_send, all_recv = refs
+        gx_send, gx_recv, gz_send, gz_recv, c_send, c_recv, all_send, all_recv = refs[:8]
+        early_own, ex, ehalf, ez, e_sems = refs[8], refs[9], refs[10], refs[11], refs[12:16]
         g = Grid()
         me = g.wide * narrow + g.narrow
         wait_all = g.greet_all()
+        plan = Plan(lengths_ref, None, lengths.shape[0])
         loads = [
-            pltpu.make_async_copy(part_ref.at[:, g.c], mine, load_sem.at[0]),
-            pltpu.make_async_copy(grads_ref.at[:, g.x], gown, load_sem.at[1]),
-            pltpu.make_async_copy(first_ref.at[g.wide], fgot.at[g.wide], load_sem.at[2]),
-            pltpu.make_async_copy(second_ref.at[g.wide], sgot.at[g.wide], load_sem.at[3]),
-            pltpu.make_async_copy(flat_ref.at[me], flatgot.at[me], load_sem.at[4]),
+            pltpu.make_async_copy(first_ref.at[g.wide], fgot.at[g.wide], load_sem.at[0]),
+            pltpu.make_async_copy(second_ref.at[g.wide], sgot.at[g.wide], load_sem.at[1]),
+            pltpu.make_async_copy(flat_ref.at[me], flatgot.at[me], load_sem.at[2]),
+            pltpu.make_async_copy(early_ref.at[:, g.x], early_own, load_sem.at[3]),
         ]
         for copy in loads:
             copy.start()
         wait_all()
-        pair_copy = remote(part_ref.at[:, 1 - g.c], pair, pair_sem.at[0], pair_sem.at[1], g.partner)
-        pair_copy.start()
         sends = []
         order = g.z_others()[::-1] + [g.z]
-        for z in order:
-            for i, x in enumerate(g.x_others()):
-                copy = remote(
-                    grads_ref.at[z, x],
-                    gx.at[g.x, z],
-                    gx_send.at[i, z],
-                    gx_recv.at[g.x, z],
-                    g.device(g.z, x, g.y, g.c),
-                )
-                copy.start()
-                sends.append(copy)
+
+        def along_x(source, place, sems):
+            for z in order:
+                for i, x in enumerate(g.x_others()):
+                    copy = remote(
+                        source.at[z, x],
+                        place.at[g.x, z],
+                        sems[0].at[i, z],
+                        sems[1].at[g.x, z],
+                        g.device(g.z, x, g.y, g.c),
+                    )
+                    copy.start()
+                    sends.append(copy)
+
+        def join(z, own, place, joined, sems):
+            total = own.astype(f32)
+            for x in g.x_others():
+                there = place.at[x, z]
+                remote(there, there, sems[0].at[0, 0], sems[1].at[x, z], g.partner).wait_recv()
+                total = total + place[x, z].astype(f32)
+            joined[z] = total.astype(bf16)
+
+        def along_z(i, z, joined, place, sems):
+            copy = remote(joined.at[z], place.at[g.z], sems[2].at[i], sems[3].at[g.z], g.device(z, g.x, g.y, g.c))
+            copy.start()
+            sends.append(copy)
+
+        def whole_of(joined, place, sems):
+            total = joined[g.z].astype(f32)
+            for z in order[:-1]:
+                there = place.at[z]
+                remote(there, there, sems[2].at[0], sems[3].at[z], g.partner).wait_recv()
+                total = total + place[z].astype(f32)
+            return total
+
+        g_sems = (gx_send, gx_recv, gz_send, gz_recv)
+        along_x(early_ref, ex, e_sems)
         for s in range(1, wide):
             target = lax.rem(g.wide + s, wide)
             for i, (source, place) in enumerate(((first_ref, fgot), (second_ref, sgot))):
@@ -520,33 +569,68 @@
             return carry
 
         lax.fori_loop(1, devices, send_flat, 0)
-        loads[0].wait()
+        qmem, kmem, vmem_ref, qatt, katt, vatt = compute_refs[:6]
+        mixed_ref, ext_ref, taps_ref, weights_ref, normed_ref, gate_low, gate_cols = compute_refs[6:]
+        for third, (memory, attention) in enumerate(((qmem, qatt), (kmem, katt), (vmem_ref, vatt))):
+            place = pl.ds(third * block, block)
+            mixed = mixed_ref[:, place]
+            if third < 2:
+                grad = memory[...].astype(f32) + attention[...]
+                act = mixed * sigmoid(mixed)
+                factor = lax.rsqrt(head_sums(act * act) + eps_head)
+                normed = act * factor
+                grad = factor * (grad - normed * head_sums(normed * grad))
+            else:
+                grad = attention[...] - memory[...].astype(f32)
+            grad = grad * silu_slope(mixed)
+            conv_grad[pl.ds(0, span), place] = grad
+            for j in range(count):
+                tap_rows[pl.ds(j, 1), place] = jnp.sum(grad * ext_ref[pl.ds(8 - j, span), place], axis=0, keepdims=True)
+        begins = plan.begins(g.wide)
+        halo_out[...] = jnp.where(begins, 0.0, conv_grad[pl.ds(0, 8), :])
+        halo = remote(
+            halo_out, halo_in, halo_sem.at[0], halo_sem.at[1], (lax.rem(g.wide + wide - 1, wide), g.narrow)
+        )
+        halo.start()
+
+        def send_taps(step, carry):
+            target = lax.rem(me + step, devices)
+            where = lax.div(target, narrow), lax.rem(target, narrow)
+            remote(tap_rows, taps_out.at[me], taps_sem.at[0], taps_sem.at[1], where).start()
+            return carry
+
+        lax.fori_loop(1, devices, send_taps, 0)
+        taps_out[me] = tap_rows[...]
+        for copy in loads:
+            copy.wait()
+        for i, z in enumerate(order):
+            join(z, early_own[z], ex, ehalf, e_sems)
+            if i < len(order) - 1:
+                along_z(i, z, ehalf, ez, e_sems)
+        halo.wait()
+        conv_grad[pl.ds(span, 8), :] = halo_in[...]
+        projected = taps_ref[pl.ds(0, 1), :] * conv_grad[pl.ds(0, span), :]
+        for j in range(1, count):
+            projected = projected + taps_ref[pl.ds(j, 1), :] * conv_grad[pl.ds(j, span), :]
+        projected_low = projected.astype(bf16)
+        part = inner_right(projected_low, weights_ref[...]) + inner_right(gate_low[...], gate_cols[...])
+        part_ref[...] = part.reshape(ys, 2, rows, width)
+        pair_copy = remote(part_ref.at[:, 1 - g.c], pair, pair_sem.at[0], pair_sem.at[1], g.partner)
+        pair_copy.start()
+        grads_ref[...] = inner_left(normed_ref[...], projected_low).astype(bf16).reshape((zs, xs) + own_grad)
+        along_x(grads_ref, gx, g_sems)
         pair_copy.wait()
-        half[...] = (mine[...].astype(f32) + pair[...].astype(f32)).astype(bf16)
+        pair[...] += part_ref[:, g.c]
+        half[...] = pair[...].astype(bf16)
         for s, y in enumerate(g.y_others()):
             copy = remote(half.at[y], got.at[g.y], y_send.at[s], y_recv.at[g.y], g.device(g.z, g.x, y, g.c))
             copy.start()
             sends.append(copy)
-        for copy in loads[1:]:
-            copy.wait()
-
-        def grad_along_z(z):
-            total = gown[z].astype(f32)
-            for x in g.x_others():
-                place = gx.at[x, z]
-                remote(place, place, gx_send.at[0, 0], gx_recv.at[x, z], g.partner).wait_recv()
-                total = total + gx[x, z].astype(f32)
-            ghalf[z] = total.astype(bf16)
-
         for i, z in enumerate(order[:-1]):
-            grad_along_z(z)
-            copy = remote(
-                ghalf.at[z], gz.at[g.z], gz_send.at[i], gz_recv.at[g.z], g.device(z, g.x, g.y, g.c)
-            )
-            copy.start()
-            sends.append(copy)
+            join(z, grads_ref[z, g.x], gx, ghalf, g_sems)
+            along_z(i, z, ghalf, gz, g_sems)
             if i == 0:
-                total = half[g.y].astype(f32)
+                total = pair[g.y]
                 for y in g.y_others():
                     remote(got.at[y], got.at[y], y_send.at[0], y_recv.at[y], g.partner).wait_recv()
                     total = total + got[y].astype(f32)
@@ -584,7 +668,8 @@
             copy = remote(there, there, p_send.at[y], p_recv.at[y], g.partner)
             copy.start()
             sends.append(copy)
-        grad_along_z(g.z)
+        join(g.z, grads_ref[g.z, g.x], gx, ghalf, g_sems)
+        early_out[...] = whole_of(ehalf, ez, e_sems)
         for s in range(1, wide):
             source = lax.rem(g.wide + s, wide)
             for i, place in enumerate((fgot, sgot)):
@@ -597,15 +682,11 @@
                 second_sum = second_sum + sgot[lane * LANE_WIDE + p].astype(f32)
             first_out[:, p * first_shape[1] : (p + 1) * first_shape[1]] = first_sum
             second_out[p * second_shape[0] : (p + 1) * second_shape[0], :] = second_sum
-        total = ghalf[g.z].astype(f32)
-        for z in order[:-1]:
-            place = gz.at[z]
-            remote(place, place, gz_send.at[0], gz_recv.at[z], g.partner).wait_recv()
-            total = total + gz[z].astype(f32)
-        grads_out[...] = total
-        for i, place in enumerate((flatgot, rowgot)):
+        grads_out[...] = whole_of(ghalf, gz, g_sems)
+        ends = ((flatgot, all_send.at[0], all_recv.at[0]), (rowgot, all_send.at[1], all_recv.at[1]))
+        for place, send, recv in ends + ((taps_out, taps_sem.at[0], taps_sem.at[1]),):
             others = place.at[pl.ds(0, devices - 1)]
-            whole = remote(others, others, all_send.at[i], all_recv.at[i], g.partner)
+            whole = remote(others, others, send, recv, g.partner)
             whole.wait_send()
             whole.wait_recv()
         flat_out[...] = jnp.sum(flatgot[...], axis=0)
@@ -628,14 +709,28 @@
             jax.ShapeDtypeStruct((LANE_WIDE * second_shape[0], second_shape[1]), f32),
             jax.ShapeDtypeStruct(flat_shape, f32),
             jax.ShapeDtypeStruct((8, width // 8), f32),
+            jax.ShapeDtypeStruct((devices, count, columns), f32),
+            jax.ShapeDtypeStruct(own_early, f32),
         ],
-        in_specs=[ANY] * 5 + [vmem] * extra_count,
-        out_specs=[ANY] + [vmem] * 5,
-        scratch_shapes=[pltpu.VMEM((ys, rows, width), bf16)] * 4
+        in_specs=[ANY] * 4
+        + [pl.BlockSpec(memory_space=pltpu.SMEM)]
+        + [vmem] * (compute_count + extra_count),
+        out_specs=[ANY] + [vmem] * 7,
+        scratch_shapes=[
+            pltpu.VMEM((ys, 2, rows, width), f32),
+            pltpu.VMEM((zs, xs) + own_grad, bf16),
+            pltpu.VMEM((span + 8, columns), f32),
+            pltpu.VMEM((count, columns), f32),
+            pltpu.VMEM((8, columns), f32),
+            pltpu.VMEM((8, columns), f32),
+            sem((2,)),
+            sem((2,)),
+        ]
+        + [pltpu.VMEM((ys, rows, width), f32)]
+        + [pltpu.VMEM((ys, rows, width), bf16)] * 2
         + [pltpu.VMEM((rows, width), bf16)]
         + [pltpu.VMEM((8, width // 8), f32), pltpu.VMEM((devices, 8, width // 8), f32)]
         + [
-            pltpu.VMEM((zs,) + own_grad, bf16),
             pltpu.VMEM((xs, zs) + own_grad, bf16),
             pltpu.VMEM((zs,) + own_grad, bf16),
             pltpu.VMEM((zs,) + own_grad, bf16),
@@ -643,17 +738,25 @@
             pltpu.VMEM((wide,) + second_shape, bf16),
             pltpu.VMEM((devices,) + flat_shape, f32),
         ]
-        + [sem((5,)), sem((2,))]
+        + [sem((4,)), sem((2,))]
         + [sem((ys,))] * 6
         + [sem((xs, zs))] * 2
         + [sem((zs,))] * 2
         + [sem((2, wide))] * 2
-        + [sem((2,))] * 2,
+        + [sem((2,))] * 2
+        + [
+            pltpu.VMEM((zs,) + own_early, bf16),
+            pltpu.VMEM((xs, zs) + own_early, bf16),
+            pltpu.VMEM((zs,) + own_early, bf16),
+            pltpu.VMEM((zs,) + own_early, bf16),
+        ]
+        + [sem((xs, zs))] * 2
+        + [sem((zs,))] * 2,
         compiler_params=pltpu.CompilerParams(
-            collective_id=ident, has_side_effects=True, vmem_limit_bytes=48 * 1024 * 1024
+            collective_id=ident, has_side_effects=True, vmem_limit_bytes=60 * 1024 * 1024
         ),
         name="last_step",
-    )(part, grads, chunks[0], chunks[1], flat, *extras)
+    )(chunks[0], chunks[1], flat, early, lengths, *compute, *extras)
 
 
 class Plan:
@@ -688,6 +791,12 @@
             found = jnp.maximum(found, jnp.where(span == start, 1.0, 0.0))
         return jnp.maximum(found, 1.0 - self.valid(turn))
 
+    def begins(self, span):
+        found = span == self.starts[0]
+        for start in self.starts[1:]:
+            found = found | (span == start)
+        return found
+
     def rates(self, turn):
         span = self.span(turn)
         return self.gates[span, 0], self.gates[span, 1], self.gates[span, 2]
@@ -970,43 +1079,84 @@
     return LaneGather if paired_lanes() else SpanGather
 
 
-def rows_to_lanes(rows, lengths, chunks, pick, tile, ident):
+def head_sums(values):
+    width = values.shape[1]
+    row = lax.broadcasted_iota(jnp.int32, (width, width), 0) // HEAD
+    column = lax.broadcasted_iota(jnp.int32, (width, width), 1) // HEAD
+    same = jnp.where(row == column, 1.0, 0.0)
+    return jnp.dot(values, same, precision=lax.Precision.HIGHEST, preferred_element_type=f32)
+
+
+def front_step(tokens, tail, gain, weights, taps, rates, lengths, pick, ident):
+    span, width = tokens.shape
+    block = weights.shape[1] // 3
     wide, narrow = lax.axis_size("wide"), lax.axis_size("narrow")
     devices = wide * narrow
+    shards = LANE_WIDE * narrow
+    shard_rows = span // shards
     kind = lane_gather()
-
-    def kernel(rows_ref, lengths_ref, chunks_ref, tile_ref, rows_out, chunks_out, tile_out, *refs):
-        hold_chunk, hold_tile, local_sem, send, recv = refs[:5]
+    count = 4
+
+    def kernel(*refs):
+        tokens_ref, tail_ref, gain_ref, weights_ref, taps_ref, rates_ref, lengths_ref = refs[:7]
+        keys_out, chunks_out, tile_out, key_out, query_out, value_out = refs[7:13]
+        normed_out, ext_out, mixed_out, mean_out, gate_out = refs[13:18]
+        tail_low, tile, send, recv = refs[18:22]
         g = Grid()
         me = g.wide * narrow + g.narrow
+        plan = Plan(lengths_ref, None, lengths.shape[0])
         wait_all = g.greet_all()
-        own = [
-            (chunks_ref.at[pick(g.wide, g.narrow)], hold_chunk, chunks_out.at[me]),
-            (tile_ref, hold_tile, tile_out.at[me]),
-        ]
-        into = [pltpu.make_async_copy(a, b, local_sem.at[i]) for i, (a, b, _) in enumerate(own)]
-        back = [pltpu.make_async_copy(b, c, local_sem.at[i]) for i, (_, b, c) in enumerate(own)]
-        for copy in into:
-            copy.start()
+        gather = kind(g, plan, key_out, keys_out, refs[22:])
+
+        def normed_of(rows):
+            values = rows.astype(f32)
+            factor = lax.rsqrt(jnp.mean(values * values, axis=-1, keepdims=True) + eps_norm)
+            return values * factor * gain_ref[...]
+
+        normed = normed_of(tokens_ref[...])
+        normed_out[...] = normed.astype(bf16)
+        mean_out[...] = jnp.mean(normed, axis=0, keepdims=True)
+        tail_low[...] = normed_of(tail_ref[...]).astype(bf16)
+        begins = plan.begins(g.wide)
+
+        def activated(third):
+            columns = pl.ds(third * block, block)
+            ext_out[pl.ds(0, 8), columns] = jnp.where(begins, 0.0, matmul(tail_low[...], weights_ref[:, columns]))
+            ext_out[pl.ds(8, span), columns] = matmul(normed_out[...], weights_ref[:, columns])
+            mixed = taps_ref[pl.ds(0, 1), columns] * ext_out[pl.ds(8, span), columns]
+            for j in range(1, count):
+                mixed = mixed + taps_ref[pl.ds(j, 1), columns] * ext_out[pl.ds(8 - j, span), columns]
+            mixed_out[:, columns] = mixed
+            return mixed * sigmoid(mixed)
+
+        def normed_heads(values):
+            return (values * lax.rsqrt(head_sums(values * values) + eps_head)).astype(bf16)
+
+        key_out[...] = normed_heads(activated(1))
         wait_all()
-        gather = kind(g, Plan(lengths_ref, None, lengths.shape[0]), rows_ref, rows_out, refs[5:])
         gather.begin()
+        value_out[...] = activated(2).astype(bf16).reshape(shards, shard_rows, block)
+        column = lax.broadcasted_iota(jnp.int32, (8, 128), 1)
+        gates = jnp.zeros((8, 128), f32)
+        for i in range(3):
+            logit = jnp.sum(mean_out[...] * rates_ref[pl.ds(i, 1), :], axis=1, keepdims=True)
+            gates = jnp.where(column == i, sigmoid(logit), gates)
+        gate_out[...] = gates
+        scale = jnp.where(column == 0, decay_top, jnp.where(column == 1, moment_top, learn_top))
+        tile[...] = gates * scale
 
         def send_chunks(step, carry):
             target = lax.rem(me + step, devices)
             where = lax.div(target, narrow), lax.rem(target, narrow)
-            remote(chunks_ref.at[pick(*where)], chunks_out.at[me], send.at[0], recv.at[0], where).start()
-            remote(tile_ref, tile_out.at[me], send.at[1], recv.at[1], where).start()
+            remote(value_out.at[pick(*where)], chunks_out.at[me], send.at[0], recv.at[0], where).start()
+            remote(tile, tile_out.at[me], send.at[1], recv.at[1], where).start()
             return carry
 
         lax.fori_loop(1, devices, send_chunks, 0)
-        for copy in into:
-            copy.wait()
-        for copy in back:
-            copy.start()
+        chunks_out[me] = value_out[pick(g.wide, g.narrow)]
+        tile_out[me] = tile[...]
+        query_out[...] = normed_heads(activated(0))
         gather.middle()
-        for copy in back:
-            copy.wait()
         for i, out in enumerate((chunks_out, tile_out)):
             others = out.at[pl.ds(0, devices - 1)]
             whole = remote(others, others, send.at[i], recv.at[i], g.partner)
@@ -1014,26 +1164,36 @@
             whole.wait_recv()
         gather.finish()
 
+    vmem = pl.BlockSpec(memory_space=pltpu.VMEM)
     return pl.pallas_call(
         kernel,
         out_shape=[
-            jax.ShapeDtypeStruct(kind.shape(*rows.shape), rows.dtype),
-            jax.ShapeDtypeStruct((devices,) + chunks.shape[1:], chunks.dtype),
-            jax.ShapeDtypeStruct((devices,) + tile.shape, tile.dtype),
+            jax.ShapeDtypeStruct(kind.shape(span, block), bf16),
+            jax.ShapeDtypeStruct((devices, shard_rows, block), bf16),
+            jax.ShapeDtypeStruct((devices, 8, 128), f32),
+            jax.ShapeDtypeStruct((span, block), bf16),
+            jax.ShapeDtypeStruct((span, block), bf16),
+            jax.ShapeDtypeStruct((shards, shard_rows, block), bf16),
+            jax.ShapeDtypeStruct((span, width), bf16),
+            jax.ShapeDtypeStruct((8 + span, 3 * block), f32),
+            jax.ShapeDtypeStruct((span, 3 * block), f32),
+            jax.ShapeDtypeStruct((1, width), f32),
+            jax.ShapeDtypeStruct((8, 128), f32),
         ],
-        in_specs=[ANY, pl.BlockSpec(memory_space=pltpu.SMEM), ANY, ANY],
-        out_specs=[ANY] * 3,
+        in_specs=[vmem] * 6 + [pl.BlockSpec(memory_space=pltpu.SMEM)],
+        out_specs=[ANY] + [vmem] * 10,
         scratch_shapes=[
-            pltpu.VMEM(chunks.shape[1:], chunks.dtype),
-            pltpu.VMEM(tile.shape, tile.dtype),
-            pltpu.SemaphoreType.DMA((2,)),
+            pltpu.VMEM((8, width), bf16),
+            pltpu.VMEM((8, 128), f32),
             pltpu.SemaphoreType.DMA((2,)),
             pltpu.SemaphoreType.DMA((2,)),
         ]
-        + kind.scratch(*rows.shape),
-        compiler_params=pltpu.CompilerParams(collective_id=ident, has_side_effects=True),
-        name="rows_to_lanes",
-    )(rows, lengths, chunks, tile)
+        + kind.scratch(span, block),
+        compiler_params=pltpu.CompilerParams(
+            collective_id=ident, has_side_effects=True, vmem_limit_bytes=40 * 1024 * 1024
+        ),
+        name="front_step",
+    )(tokens, tail, gain, weights, taps, rates, lengths)
 
 
 def matmul(left_side, right_side):
@@ -1049,12 +1209,12 @@
 
 
 def silu_slope(values):
-    sigmoid_val = jax.nn.sigmoid(values)
+    sigmoid_val = sigmoid(values)
     return sigmoid_val * (1.0 + values * (1.0 - sigmoid_val))
 
 
 def silu_curve(values):
-    sigmoid_val = jax.nn.sigmoid(values)
+    sigmoid_val = sigmoid(values)
     return sigmoid_val * (1.0 - sigmoid_val) * (2.0 + values * (1.0 - 2.0 * sigmoid_val))
 
 
@@ -1084,15 +1244,16 @@
 
 
 class Scatter:
-    def __init__(self, lane, part, pair, half, got, sems):
-        self.lane, self.part, self.pair, self.half, self.got = lane, part, pair, half, got
+    def __init__(self, lane, part, pair, half, got, sems, own=None):
+        self.lane, self.part, self.pair, self.half, self.got, self.own = lane, part, pair, half, got, own
         self.pair_send, self.pair_recv, self.send, self.recv = sems
 
     @staticmethod
-    def scratch(chips, rows, width):
+    def scratch(chips, rows, width, pair_type=f32):
         return [
-            pltpu.VMEM((2, chips, rows, width), bf16),
-            pltpu.VMEM((chips, rows, width), bf16),
+            pltpu.VMEM((rows, width), f32),
+            pltpu.VMEM((2, chips, rows, width), pair_type),
+            pltpu.VMEM((chips, rows, width), pair_type),
             pltpu.VMEM((chips, rows, width), bf16),
             pltpu.VMEM((chips, rows, width), bf16),
             pltpu.SemaphoreType.DMA((1,)),
@@ -1103,7 +1264,7 @@
 
     @classmethod
     def of(cls, lane, refs):
-        return cls(lane, *refs[:4], refs[4:8])
+        return cls(lane, *refs[1:5], refs[5:9], refs[0])
 
     def pair_copy(self):
         return remote(
@@ -1119,10 +1280,12 @@
 
     def take_pair(self):
         self.pair_copy().wait()
-        self.half[...] = (
-            self.part[self.lane.colour].astype(f32) + self.pair[...].astype(f32)
-        ).astype(bf16)
-        self.got[self.lane.chip] = self.half[self.lane.chip]
+        self.half[...] = (self.part[self.lane.colour].astype(f32) + self.pair[...].astype(f32)).astype(bf16)
+        if self.own is None:
+            self.got[self.lane.chip] = self.half[self.lane.chip]
+        else:
+            chip = self.lane.chip
+            self.own[...] = self.part[self.lane.colour, chip].astype(f32) + self.pair[chip].astype(f32)
 
     def copy_to(self, step):
         chip = self.lane.other(step)
@@ -1139,7 +1302,7 @@
             self.copy_to(step).start()
 
     def total(self):
-        result = self.got[self.lane.chip].astype(f32)
+        result = self.got[self.lane.chip].astype(f32) if self.own is None else self.own[...]
         for step in range(1, self.lane.chips):
             chip = self.lane.other(step)
             remote(
@@ -1263,13 +1426,13 @@
 
     def kernel(*refs):
         keys_hbm, values_hbm, own_hbm, lengths_ref, gates_ref, first_hbm, second_hbm = refs[:7]
-        recalled_hbm, low1_hbm, low2_hbm, m1_hbm, m2_hbm, g1_hbm, g2_hbm = refs[7:14]
-        err_hbm, pre_hbm, qpre_hbm, klane_hbm, qlane_hbm = refs[14:19]
-        rest = refs[19:]
-        kall, qall, vall, kcur, qcur, i1, i2, s1, s2, m1, m2, low1, low2, mb1, mb2, gb1, gb2 = rest[:17]
-        pre, qpre, khid, rec, qpart, qpair, qhalf, qgot = rest[17:25]
-        in_sem, out_sem, q_sem, q_pair_send, q_pair_recv, q_send, q_recv = rest[25:32]
-        rest = rest[32:]
+        recalled_hbm, low1_hbm, low2_hbm, s1_hbm, s2_hbm, m1_hbm, m2_hbm, g1_hbm, g2_hbm = refs[7:16]
+        err_hbm, pre_hbm, qpre_hbm, klane_hbm, qlane_hbm = refs[16:21]
+        rest = refs[21:]
+        kall, qall, vall, kcur, qcur, i1, i2, s1, s2, m1, m2, gb1, gb2, low1, low2 = rest[:15]
+        pre, qpre, khid, rec, qpart, qpair, qhalf, qgot = rest[15:23]
+        in_sem, out_sem, q_sem, q_pair_send, q_pair_recv, q_send, q_recv = rest[23:30]
+        rest = rest[30:]
         lane = Lane()
         grid = Grid()
         plan = Plan(lengths_ref, gates_ref, sequences)
@@ -1288,12 +1451,12 @@
         def state_saves(turn):
             return [
                 pltpu.make_async_copy(source, target.at[turn], out_sem.at[i])
-                for i, (source, target) in enumerate(((mb1, m1_hbm), (mb2, m2_hbm), (kcur, klane_hbm)))
+                for i, (source, target) in enumerate(((m1, m1_hbm), (m2, m2_hbm), (kcur, klane_hbm), (s1, s1_hbm), (s2, s2_hbm)))
             ]
 
         def other_saves(turn):
             return [
-                pltpu.make_async_copy(source, target.at[turn], out_sem.at[3 + i])
+                pltpu.make_async_copy(source, target.at[turn], out_sem.at[5 + i])
                 for i, (source, target) in enumerate(
                     ((gb1, g1_hbm), (gb2, g2_hbm), (error.whole, err_hbm), (pre, pre_hbm))
                 )
@@ -1322,7 +1485,7 @@
         low2[0] = i2[...]
         s1[...] = i1[...].astype(f32)
         s2[...] = i2[...].astype(f32)
-        for ref in (m1, m2, mb1, mb2):
+        for ref in (m1, m2):
             ref[...] = jnp.zeros_like(ref)
 
         def lookup_blocks(buf, first):
@@ -1348,7 +1511,7 @@
             qpre[slot] = query_pre
             for copy in query_saves(q, slot):
                 copy.start()
-            query_hidden = (query_pre * jax.nn.sigmoid(query_pre)).astype(bf16)
+            query_hidden = (query_pre * sigmoid(query_pre)).astype(bf16)
             qpart[slot] = matmul(query_hidden, low2[q]).astype(bf16).reshape(2, chips, rows, width)
             recall(q, slot).start_pair()
 
@@ -1365,8 +1528,8 @@
                 copy.start()
             key_pre = lookup_blocks(kcur, low1.at[turn])
             pre[0] = key_pre
-            khid[...] = (key_pre * jax.nn.sigmoid(key_pre)).astype(bf16)
-            lookup.part[...] = matmul(khid[...], low2[turn]).astype(bf16).reshape(2, chips, rows, width)
+            khid[...] = (key_pre * sigmoid(key_pre)).astype(bf16)
+            lookup.part[...] = matmul(khid[...], low2[turn]).reshape(2, chips, rows, width)
             lookup.start_pair()
 
             @pl.when(turn == ask_from)
@@ -1420,23 +1583,22 @@
                 copy.wait()
             following = jnp.minimum(turn + 1, turns - 1)
 
-            def update(s, m, mb, init, low, grad, place):
+            def update(s, m, init, low, grad, place):
                 moment_new = moment * m[place] - rate * grad
                 state_new = (1.0 - decay) * s[place] + moment_new
                 state_new = reset * init[place].astype(f32) + (1.0 - reset) * state_new
                 moment_new = (1.0 - reset) * moment_new
                 m[place] = moment_new
-                mb[place] = moment_new.astype(bf16)
                 s[place] = state_new
                 low[(following,) + place] = state_new.astype(bf16)
 
-            gb2[...] = grad_second.astype(bf16)
-            update(s2, m2, mb2, i2, low2, grad_second, (slice(None), slice(None)))
+            gb2[...] = grad_second
+            update(s2, m2, i2, low2, grad_second, (slice(None), slice(None)))
             for b in range(blocks):
                 grad_first = inner_left(kcur[b], slope)
                 place = (pl.ds(b * block, block), slice(None))
-                gb1[place] = grad_first.astype(bf16)
-                update(s1, m1, mb1, i1, low1, grad_first, place)
+                gb1[place] = grad_first
+                update(s1, m1, i1, low1, grad_first, place)
             saves = other_saves(turn)
             for copy in saves:
                 copy.start()
@@ -1485,7 +1647,7 @@
     out_shape = (
         [jax.ShapeDtypeStruct((2, chips, rows, block), bf16)]
         + [jax.ShapeDtypeStruct((turns,) + s, bf16) for s in state]
-        + [jax.ShapeDtypeStruct((key_turns,) + s, bf16) for s in state * 2]
+        + [jax.ShapeDtypeStruct((key_turns,) + s, f32) for s in state * 3]
         + [
             jax.ShapeDtypeStruct((key_turns, 2, chips, rows, width), bf16),
             jax.ShapeDtypeStruct((key_turns, 2, span, hidden), f32),
@@ -1500,9 +1662,8 @@
         + [pltpu.VMEM(values.shape, bf16)]
         + [pltpu.VMEM((blocks, span, block), bf16), pltpu.VMEM((slots, blocks, span, block), bf16)]
         + [pltpu.VMEM(s, bf16) for s in state]
-        + [pltpu.VMEM(s, f32) for s in state * 2]
+        + [pltpu.VMEM(s, f32) for s in state * 3]
         + [pltpu.VMEM((turns,) + s, bf16) for s in state]
-        + [pltpu.VMEM(s, bf16) for s in state * 2]
         + [
             pltpu.VMEM((2, span, hidden), f32),
             pltpu.VMEM((slots, span, hidden), f32),
@@ -1511,7 +1672,7 @@
             pltpu.VMEM((slots, 2, chips, rows, width), bf16),
         ]
         + [pltpu.VMEM((n, chips, rows, width), bf16) for n in (turns, slots, turns)]
-        + [sem((4,)), sem((7,)), sem((slots, 2)), sem((turns,)), sem((turns,)), sem((turns, chips)), sem((turns, chips))]
+        + [sem((4,)), sem((9,)), sem((slots, 2)), sem((turns,)), sem((turns,)), sem((turns, chips)), sem((turns, chips))]
         + Scatter.scratch(chips, rows, width)
         + Spread.scratch(chips, rows, width)
         + own_rows
@@ -1536,7 +1697,7 @@
 
 
 def chain_backward(recall_grad, saved, lengths, gates, ident):
-    low1_all, low2_all, m1_all, m2_all, g1_all, g2_all, err_all, pre_all, qpre_all, keys, queries = saved
+    low1_all, low2_all, s1_all, s2_all, m1_all, m2_all, g1_all, g2_all, err_all, pre_all, qpre_all, keys, queries = saved
     wide = lax.axis_size("wide")
     devices = wide * lax.axis_size("narrow")
     key_turns, blocks, span, block = keys.shape
@@ -1548,12 +1709,12 @@
     own_rows = kind.scratch(span, block)
 
     def kernel(*refs):
-        own_hbm, q_ins, k_ins, lengths_ref, gates_ref = refs[0], refs[1:5], refs[5:12], refs[12], refs[13]
-        cots_hbm, sums_out, mg1_hbm, mg2_hbm = refs[14:18]
-        rest = refs[18:]
-        q_bufs, k_bufs, rest = rest[:4], rest[4:11], rest[11:]
+        own_hbm, q_ins, k_ins, lengths_ref, gates_ref = refs[0], refs[1:5], refs[5:14], refs[14], refs[15]
+        cots_hbm, sums_out, mg1_hbm, mg2_hbm = refs[16:20]
+        rest = refs[20:]
+        q_bufs, k_bufs, rest = rest[:4], rest[4:13], rest[13:]
         qbuf, low1, low2, qpre = q_bufs
-        kbuf, m1, m2, g1, g2, errs, pre = k_bufs
+        kbuf, s1, s2, m1, m2, g1, g2, errs, pre = k_bufs
         rall, cf, cs, cmf, cms, w1, w2, a1, a2, c1, c2 = rest[:11]
         dh, khid, qpl, qhid, kpl, slow, sg, hk, qcots, kcots, vcots, sumrows, tile, mb1, mb2, result = rest[11:27]
         q_sem, k_sem, end_sem, tile_send, tile_recv = rest[27:32]
@@ -1606,7 +1767,7 @@
                 back = back + inner_right(rall[index, b], low2[slot, :, pl.ds(b * block, block)])
             query_pre = qpre[slot]
             qpl[...] = (plan.valid(turn) * back * silu_slope(query_pre)).astype(bf16)
-            qhid[...] = (query_pre * jax.nn.sigmoid(query_pre)).astype(bf16)
+            qhid[...] = (query_pre * sigmoid(query_pre)).astype(bf16)
             qstream.part[...] = inner_right(qpl[...], low1[slot]).astype(bf16).reshape(2, chips, rows, width)
             qstream.start_pair()
 
@@ -1620,7 +1781,6 @@
         def key_rows(slot):
             kstream.part[...] = (
                 (inner_right(kpl[...], low1[slot]) + inner_right(slow[...], c1[slot]))
-                .astype(bf16)
                 .reshape(2, chips, rows, width)
             )
 
@@ -1649,10 +1809,10 @@
                 slope_grad = slope_grad + matmul(kbuf[slot, b], c1[slot, pl.ds(b * block, block), :])
             sg[...] = slope_grad
             key_pre = pre[slot, 0]
-            khid[...] = (key_pre * jax.nn.sigmoid(key_pre)).astype(bf16)
+            khid[...] = (key_pre * sigmoid(key_pre)).astype(bf16)
             dh[...] = (slope_grad * silu_slope(key_pre)).astype(bf16)
             lookup.part[...] = (
-                (matmul(khid[...], c2[...]) + matmul(dh[...], low2[slot])).astype(bf16).reshape(2, chips, rows, width)
+                (matmul(khid[...], c2[...]) + matmul(dh[...], low2[slot])).reshape(2, chips, rows, width)
             )
             lookup.start_pair()
             finish(qstream, qcots, turn + 1)
@@ -1681,12 +1841,12 @@
             w2[...] += inner_left(dh[...], err)
 
             def whole_sum(first_a, first_b, second_a, second_b):
-                first = jnp.sum(first_a * first_b.astype(f32), axis=0, keepdims=True)
-                second = jnp.sum(second_a * second_b.astype(f32), axis=0, keepdims=True)
+                first = jnp.sum(first_a * first_b, axis=0, keepdims=True)
+                second = jnp.sum(second_a * second_b, axis=0, keepdims=True)
                 return jnp.sum(first, axis=1, keepdims=True) + jnp.sum(second, axis=1, keepdims=True)
 
             kinds = (
-                whole_sum(cf[...], low1[slot], cs[...], low2[slot]),
+                whole_sum(cf[...], s1[slot], cs[...], s2[slot]),
                 whole_sum(cmf[...] + cf[...], m1[slot], cms[...] + cs[...], m2[slot]),
                 whole_sum(cmf[...] + cf[...], g1[slot], cms[...] + cs[...], g2[slot]),
             )
@@ -1739,6 +1899,7 @@
             lookup.half,
             lookup.got,
             (lookup.pair_send, lookup.pair_recv, lookup.send, lookup.recv),
+            lookup.own,
         )
         key_rows((turns - 1) % 2)
         tail.start_pair()
@@ -1784,7 +1945,7 @@
     q_buffers = [((blocks, span, block), bf16)] + [(s, bf16) for s in state] + [((span, hidden), f32)]
     k_buffers = (
         [((blocks, span, block), bf16)]
-        + [(s, bf16) for s in state * 2]
+        + [(s, f32) for s in state * 3]
         + [((2, chips, rows, width), bf16), ((2, span, hidden), f32)]
     )
     by_owner = [(wide, width // wide, hidden), (wide, hidden, width // wide)]
@@ -1804,8 +1965,10 @@
         + [pltpu.VMEM((turns, 8, 128), f32), pltpu.VMEM((wide, 128), f32)]
         + [pltpu.VMEM(s, bf16) for s in by_owner]
         + [pltpu.VMEM((3, 2, chips, rows, block), bf16)]
-        + [sem((2, 4)), sem((2, 7)), sem((3,)), sem((1,)), sem((1,))]
-        + Scatter.scratch(chips, rows, width) * 3
+        + [sem((2, 4)), sem((2, 9)), sem((3,)), sem((1,)), sem((1,))]
+        + Scatter.scratch(chips, rows, width)
+        + Scatter.scratch(chips, rows, width, bf16)
+        + Scatter.scratch(chips, rows, width)
         + Spread.scratch(chips, rows, width)
         + own_rows
         + Deliver.scratch(3, rows, block)
@@ -1815,18 +1978,18 @@
     return pl.pallas_call(
         kernel,
         out_shape=out_shape,
-        in_specs=[ANY] * 12 + [smem] * 2,
+        in_specs=[ANY] * 14 + [smem] * 2,
         out_specs=[ANY, vmem, ANY, ANY],
         scratch_shapes=scratch,
         compiler_params=pltpu.CompilerParams(
-            collective_id=ident, has_side_effects=True, vmem_limit_bytes=62 * 1024 * 1024
+            collective_id=ident, has_side_effects=True, vmem_limit_bytes=63 * 1024 * 1024
         ),
         cost_estimate=pl.CostEstimate(
             flops=80 * turns * 2 * span * width * hidden, bytes_accessed=turns * 60 * 2**20, transcendentals=0
         ),
         name="chain_backward",
     )(
-        recall_grad, queries, low1_all, low2_all, qpre_all, keys, m1_all, m2_all, g1_all, g2_all, err_all, pre_all,
+        recall_grad, queries, low1_all, low2_all, qpre_all, keys, s1_all, s2_all, m1_all, m2_all, g1_all, g2_all, err_all, pre_all,
         lengths, gates,
     )
 
@@ -1916,8 +2079,8 @@
     ).transpose(1, 0, 2)
     memory_cols = memory_in.reshape(memory_in.shape[0], LANE_WIDE, hidden).transpose(1, 0, 2)
     memory_rows = memory_out.reshape(LANE_WIDE, hidden, memory_out.shape[1])
-    small_all, weights_all, first_all, second_all = send_parameters(
-        packed, own_weights, [memory_cols, memory_rows], 1
+    small_all, weights_all, first_all, second_all, tail_tokens = send_parameters(
+        packed, own_weights, [memory_cols, memory_rows], tokens, 1
     )
     first_init = first_all.reshape(width, hidden)
     second_init = second_all.transpose(1, 0, 2).reshape(hidden, width)
@@ -1943,32 +2106,22 @@
     persist_f = own_cols(persist_all, 2).astype(f32)
     qkv_weights = weights_all.reshape(width, 3 * local_width)
 
-    inputs_f = tokens.astype(f32)
-    first_factor = lax.rsqrt(jnp.mean(inputs_f * inputs_f, axis=-1, keepdims=True) + eps_norm)
-    first_scaled = inputs_f * first_factor
-    normed = first_scaled * gain_one
-    normed_low = normed.astype(bf16)
-    projected = matmul(normed_low, qkv_weights)
-    tail_rows = from_behind(projected[span - taps + 1 :].astype(bf16), "wide", 1).astype(f32)
-    extended = jnp.concatenate([jnp.where(is_first, 0.0, tail_rows), projected], 0)
-    mixed_conv = kernel_f[0] * projected
-    for offset in range(1, taps):
-        start_row = taps - 1 - offset
-        mixed_conv = mixed_conv + kernel_f[offset] * extended[start_row : start_row + span]
-    activated = jax.nn.silu(mixed_conv)
-    query_act = activated[:, :local_width]
-    key_act = activated[:, local_width : 2 * local_width]
-    query_low = head_norm(query_act, HEAD).astype(bf16)
-    key_low = head_norm(key_act, HEAD).astype(bf16)
-    value_low = activated[:, 2 * local_width :].astype(bf16)
-    span_mean = jnp.mean(normed, axis=0)
+    key_all, value_got, gate_got, key_low, query_low, value_low, normed_low, extended, mixed_conv, span_mean, gate_tile = (
+        front_step(
+            tokens,
+            tail_tokens,
+            gain_one[None],
+            qkv_weights,
+            jnp.pad(kernel_f, ((0, 8 - taps), (0, 0))),
+            jnp.pad(rate_f.T, ((0, 5), (0, 0))),
+            seq_spans,
+            shard_of,
+            2,
+        )
+    )
+    value_low = value_low.reshape(span, local_width)
+    span_mean, gate_sig = span_mean[0], gate_tile[0, :3]
     gate_scale = jnp.array([decay_top, moment_top, learn_top], f32)
-    gate_sig = jax.nn.sigmoid(jnp.sum(span_mean[:, None] * rate_f, axis=0))
-    gate_tile = jnp.broadcast_to(jnp.pad(gate_sig * gate_scale, (0, 125))[None], (8, 128))
-
-    key_all, value_got, gate_got = rows_to_lanes(
-        key_low, seq_spans, value_low.reshape(shards, shard_rows, local_width), shard_of, gate_tile, 2
-    )
     later = (ffn_gate, ffn_up, ffn_down, jnp.concatenate([out_gate, out_proj.T], 1))
     key_all, *later = lax.optimization_barrier((key_all,) + later)
     out_weights = lax.all_gather(later[3], "wide", axis=0, tiled=True)
@@ -2022,7 +2175,7 @@
     gated_low = (attended * gate_sigmoid).astype(bf16)
 
     def by_rows(part):
-        return part.astype(bf16).reshape(narrow, own_rows, width)
+        return part.reshape(narrow, own_rows, width)
 
     tokens_own, cotangent_own = own_part(tokens), own_part(cotangent)
     rows_f32, row_f32 = ((own_rows, width), f32), ((1, width), f32)
@@ -2084,7 +2237,7 @@
     attended_grad_low = (gated_grad * gate_sigmoid).astype(bf16)
     gate_pre_low = (gated_grad * attended * gate_sigmoid * (1.0 - gate_sigmoid)).astype(bf16)
     early_grads = jnp.concatenate([inner_left(normed_low, gate_pre_low), inner_left(branch_low, gated_low)], 1)
-    early_out = scatter_wide(early_grads)
+    early_grads = early_grads.astype(bf16)
 
     weights_again = jnp.exp(score_block() - log_total)
     grad_heads = split_heads(attended_grad_low, HEAD)
@@ -2110,33 +2263,11 @@
     ).astype(bf16)
 
     cots, sums_got, first_chunks, second_chunks = chain_backward(recall_grad_low, saved, seq_spans, gate_rows, 12)
-    query_mem, key_mem, value_mem = [cots[i].reshape(span, local_width).astype(f32) for i in range(3)]
     gate_sums = jnp.sum(sums_got[:, :, :3], axis=0)[wide_pos] * jnp.array([-1.0, 1.0, -1.0], f32)
 
     logit_grad = gate_sums * gate_scale * gate_sig * (1.0 - gate_sig)
     rate_part = span_mean[:, None] * logit_grad[None, :]
     gate_row = jnp.sum(rate_f * logit_grad[None, :], axis=1)[None, :] / span
-    act_grad = jnp.concatenate(
-        [
-            head_norm_back(query_act, query_mem + query_att, HEAD),
-            head_norm_back(key_act, key_mem + keys_grad[recall_end:], HEAD),
-            values_grad[recall_end:] - value_mem,
-        ],
-        1,
-    )
-    conv_grad = act_grad * silu_slope(mixed_conv)
-    kernel_rows = []
-    extended_grad = jnp.zeros_like(extended)
-    for offset in range(taps):
-        start_row = taps - 1 - offset
-        kernel_rows.append(jnp.sum(conv_grad * extended[start_row : start_row + span], axis=0))
-        extended_grad = extended_grad + jnp.pad(kernel_f[offset] * conv_grad, ((start_row, offset), (0, 0)))
-    tail_back = from_behind(
-        jnp.where(is_first, 0.0, extended_grad[: taps - 1]).astype(bf16), "wide", -1
-    ).astype(f32)
-    projected_grad = extended_grad[taps - 1 :] + jnp.pad(tail_back, ((span - taps + 1, 0), (0, 0)))
-    projected_low = projected_grad.astype(bf16)
-    normed_part = inner_right(projected_low, qkv_weights) + inner_right(gate_pre_low, gate_cols)
 
     def after_all(totals, extras):
         tokens_rows, grad_rows, gain, row = extras
@@ -2145,17 +2276,13 @@
         gain_part = jnp.sum(normed_grad * scaled, axis=0, keepdims=True)
         return [(grad_rows + rms_back(scaled, factor, normed_grad * gain)).astype(bf16)], [gain_part]
 
-    weight_grads = inner_left(normed_low, projected_low).astype(bf16)
-
     def place_cols(piece, axis):
         full = piece.shape[:axis] + (width,) + piece.shape[axis + 1 :]
         return lax.dynamic_update_slice_in_dim(jnp.zeros(full, f32), piece, col_offset, axis)
 
-    kernel_full = place_cols(jnp.stack(kernel_rows).reshape(taps, 3, local_width), 2).reshape(taps, 3 * width)
     persist_full = place_cols(persist_part, 2)
     rate_part = jnp.where(narrow_pos == 0, rate_part, 0.0)
     chunks = [
-        kernel_full.reshape(taps, devices, -1).transpose(1, 0, 2),
         persist_full.reshape(2, persist_count, devices, -1).transpose(2, 0, 1, 3),
         gain_two_part.reshape(devices, -1),
         rate_part.reshape(devices, -1, 3),
@@ -2163,11 +2290,15 @@
     flat = jnp.concatenate([a.reshape(devices, -1) for a in chunks], 1)
     flat_size = -(-flat.shape[1] // 1024) * 1024
     flat = jnp.pad(flat, ((0, 0), (0, flat_size - flat.shape[1]))).reshape(devices, -1, 128)
-    tokens_grad, weight_out, first_out, second_out, flat_sum, gain_sum = last_step(
-        by_rows(normed_part),
+    cots = cots.reshape(3, span, local_width)
+    tokens_grad, weight_out, first_out, second_out, flat_sum, gain_sum, tap_rows, early_out = last_step(
+        [cots[0], cots[1], cots[2], query_att, keys_grad[recall_end:], values_grad[recall_end:]],
+        [mixed_conv, extended, jnp.pad(kernel_f, ((0, 8 - taps), (0, 0))), qkv_weights, normed_low],
+        seq_spans,
+        [gate_pre_low, gate_cols],
         [tokens_own, middle_grad, gain_one[None], gate_row],
         after_all,
-        weight_grads.reshape(wide, width // wide, 3 * local_width),
+        early_grads,
         [first_chunks, second_chunks],
         flat,
         15,
@@ -2181,7 +2312,12 @@
         size = a.size // devices
         small_outs.append(flat_sum[at : at + size].reshape(a.shape[1:]))
         at += size
-    kernel_grad, persist_grad, ffn_gain_grad, rate_grad = small_outs
+    persist_grad, ffn_gain_grad, rate_grad = small_outs
+    tap_sum = jnp.sum(tap_rows.reshape(wide, narrow, taps, 3, local_width), axis=0)
+    tap_sum = tap_sum.transpose(1, 2, 0, 3).reshape(taps, 3 * width)
+    kernel_grad = lax.dynamic_slice_in_dim(
+        tap_sum, (wide_pos * narrow + narrow_pos) * (3 * width // devices), 3 * width // devices, 1
+    )
     return (
         output,
         tokens_grad,

time: 904 us -> 870 us (0.962); the launches traced: 886 us -> 862 us
  Pallas kernels: 661 us -> 687 us
  other arithmetic: 48.1 us -> 23.9 us
  matrix products: 70.5 us -> 60.7 us
    pallas_call x1, Pallas kernels: 66.5 us -> 93.3 us  [last_step(): pl.pallas_call(kernel, out_shape=[jax.ShapeDtypeStruct((narrow, rows, wid...]
    unnamed x189 -> x133, local copies, waits for them, and re-layouts: 24.6 us -> 22.7 us
    dot_general x6 -> x5, matrix products: 18.2 us -> 16.4 us  [matmul(): return jnp.dot(left_side, right_side, preferred_element_type=jnp.float32)]
  transfers between devices with their start and end apart: 10 -> 7, of which waited for: 2 -> 1; matrix products, arithmetic and copies ran while one was open for 13% -> 12% of each run, Pallas kernels for 60% -> 68%
where the time goes in v5:
time: 870 us; the launch traced here: 862 us
  Pallas kernels  687 us (79%)
  local copies, waits for them, and re-layouts  67.4 us (8%)
  matrix products  60.7 us (7%)
  other arithmetic  23.9 us (3%)
  between operations  15.7 us (2%)
    pallas_call x1, Pallas kernels, chain_backward(): pl.pallas_call(kernel, out_shape=out_shape, in_specs=[ANY] * 14 + [smem]...  248 us
    pallas_call x1, Pallas kernels, chain_forward(): pl.pallas_call(kernel, out_shape=out_shape, in_specs=[ANY] * 3 + [smem] *...  189 us
    pallas_call x1, Pallas kernels, last_step(): pl.pallas_call(kernel, out_shape=[jax.ShapeDtypeStruct((narrow, rows, wid...  93.3 us
    pallas_call x2, Pallas kernels, narrow_step(): pl.pallas_call(kernel, out_shape=[jax.ShapeDtypeStruct((narrow, rows, wid...  59 us
    pallas_call x1, Pallas kernels, send_parameters(): pl.pallas_call(kernel, out_shape=[jax.ShapeDtypeStruct((devices,) + small...  52.1 us
    pallas_call x1, Pallas kernels, front_step(): pl.pallas_call(kernel, out_shape=[jax.ShapeDtypeStruct(kind.shape(span, b...  46.3 us
    unnamed x133, local copies, waits for them, and re-layouts  22.7 us
  transfers between devices with their start and end apart: 7, of which 1 were waited for; matrix products, arithmetic and copies ran while one was open for 12% of the time, Pallas kernels for 68%

profile of v5, /device:TPU:0, one launch (start us, length us, event | category | flops | bytes accessed | tf_op | source)
XLA Modules:
  0.0 862.4 jit_solution(9725548116465117529)
XLA Ops:
  16.1 52.1 %send_parameters.1 = (bf16[32,16,128]{2,1,0:T(8,128)(2,1)}, bf16[8,4,32,768]{3,2,1,0:T(8,128)(2,1)}, bf16[8,128,256]{2,1,0:T(8,128)(2,1)}, bf16[8,256,128]{2,1,0:T(8,128)(2,1)}, bf16[8,1024]{1,0:T(8,128)(2,1)}) custom-call(bf16[16,128]{1,0:T(8,128)(2,1)} %pad_bitcast_fusion.1.refs_0_, bf16[4,32,768]{2,1,0:T(8,128)(2,1)} %maximum_bitcast_fusion.refs_1_, ...), custom_call_target="tpu_custom_call" | custom-call | tf_op jit(solution)/shard_map/send_parameters/pallas_call | solution.py:339
  71.5 46.3 %front_step.1 = (bf16[5,4,512,256]{3,2,1,0:T(8,128)(2,1)S(1)}, bf16[32,32,256]{2,1,0:T(8,128)(2,1)S(1)}, f32[32,8,128]{2,1,0:T(8,128)S(1)}, bf16[512,256]{1,0:T(...) custom-call(bf16[512,1024]{1,0:T(8,128)(2,1)S(1)} %copy-done.1, ...), custom_call_target="tpu_custom_call" | custom-call | tf_op jit(solution)/shard_map/front_step/pallas_call | solution.py:1168
  121.9 2.3 copy-done.13
  133.7 188.6 %chain_forward.1 = (bf16[2,8,32,256]{3,2,1,0:T(8,128)(2,1)}, bf16[5,1024,256]{2,1,0:T(8,128)(2,1)}, bf16[5,256,1024]{2,1,0:T(8,128)(2,1)}, f32[4,1024,256]{2,1,0...) custom-call(bf16[5,4,512,256]{3,2,1,0:T(8,128)(2,1)} %copy-done.13, ...), custom_call_target="tpu_custom_call" | custom-call | flops 53687091200 | bytes 209715200 | tf_op jit(solution)/shard_map/chain_forward/pallas_call | solution.py:1683
  326.1 1.7 fusion.51
  329.0 2.2 fusion.7
  331.5 2.4 multiply_convert_fusion.4
  334.6 1.8 fusion.37
  336.4 24.9 %narrow_step_7.1 = (bf16[4,128,1024]{2,1,0:T(8,128)(2,1)}, f32[128,1024]{1,0:T(8,128)}) custom-call(f32[2,2,128,1024]{3,2,1,0:T(8,128)} %bitcast.187, bf16[128,1024]{1,0:T(8,128)(2,1)} %constant_dynamic-slice_fusion.4.refs_1_.refs_18_, f32[1,1024]{1,0:T(1,128)} %reshape.350.refs_2_.refs_4_), custom_call_target="tpu_custom_call" | custom-call | flops 30000001024 | bytes 104857600 | tf_op jit(solution)/shard_map/narrow_step_7/pallas_call | solution.py:449
  361.3 4.5 fusion.53
  365.8 4.6 fusion.52
  370.4 5.1 all-gather.11.cloned.1.call-done
  375.6 5.9 fusion.16
  381.5 2.6 convert_bitcast_fusion
  384.1 2.6 convolution_convert_fusion
  386.8 4.1 convolution_convert_fusion.1
  390.9 3.3 fusion.55
  394.3 2.6 fusion.54
  396.9 2.6 convolution_add_fusion
  404.0 4.1 copy.296
  408.1 34.0 %narrow_step_9.1 = (bf16[4,128,1024]{2,1,0:T(8,128)(2,1)}, bf16[4,128,1024]{2,1,0:T(8,128)(2,1)}, f32[128,1024]{1,0:T(8,128)}, f32[1,1024]{1,0:T(1,128)}) custom-call(f32[2,2,128,1024]{3,2,1,0:T(8,128)} %bitcast.226, f32[2,2,128,1024]{3,2,1,0:T(8,128)} %bitcast.227, f32[128,1024]{1,0:T(8,128)} %get-tuple-element.96.refs_2_, ...), custom_call_target="tpu_custom_call" | custom-call | flops 30000001024 | bytes 104857600 | tf_op jit(solution)/shard_map/narrow_step_9/pallas_call | solution.py:449
  442.2 2.4 multiply_convert_fusion.2
  444.7 6.5 multiply_reduce_fusion
  451.2 8.4 multiply_convert_fusion
  461.1 5.4 fusion.9
  468.4 248.2 %chain_backward.1 = (bf16[3,2,8,32,256]{4,3,2,1,0:T(8,128)(2,1)}, f32[32,8,128]{2,1,0:T(8,128)}, bf16[8,128,256]{2,1,0:T(8,128)(2,1)}, bf16[8,256,128]{2,1,0:T(8,128)(2,1)}) custom-call(bf16[512,256]{1,0:T(8,128)(2,1)} %copy.271.refs_0_, bf16[5,4,512,256]{3,2,1,0:T(8,128)(2,1)} %get-tuple-element.99.refs_1_, ...), custom_call_target="tpu_custom_call" | custom-call | flops 107374182400 | bytes 314572800 | tf_op jit(solution)/shard_map/chain_backward/pallas_call | solution.py:1978
  718.0 2.1 slice.149
  722.7 2.0 copy.283.refs_9_
  725.8 3.1 convolution_multiply_fusion.1
  741.2 93.3 %last_step.1 = (bf16[4,128,1024]{2,1,0:T(8,128)(2,1)}, f32[128,768]{1,0:T(8,128)}, f32[128,1024]{1,0:T(8,128)}, f32[1024,128]{1,0:T(8,128)}, f32[16,128]{1,0:T(8...) custom-call(bf16[8,128,256]{2,1,0:T(8,128)(2,1)} %get-tuple-element.112.refs_0_, ...), custom_call_target="tpu_custom_call" | custom-call | tf_op jit(solution)/shard_map/last_step/pallas_call | solution.py:703
  846.8 1.9 convert_element_type.157
  850.7 1.9 convert_element_type.156
  (268 shorter events, 73.2 us)
Async XLA Ops:
  7.2 62.3 %copy-start.45 = (bf16[256,128]{1,0:T(8,128)(2,1)S(1)}, bf16[256,128]{1,0:T(8,128)(2,1)}, u32[]{:S(2)}) copy-start(bf16[256,128]{1,0:T(8,128)(2,1)} %param.31) | copy-start | bytes 196612
  7.2 324.2 %all-gather.5.cloned.1.call-start = ((), (), s32[]{:S(2)}) async-start(), calls=%async_computation.3 | async-start | bytes 1179648 | tf_op jit(solution)/shard_map/all_gather | solution.py:2127
  15.4 55.4 %copy-start.47 = (bf16[128,256]{1,0:T(8,128)(2,1)S(1)}, bf16[128,256]{1,0:T(8,128)(2,1)}, u32[]{:S(2)}) copy-start(bf16[128,256]{1,0:T(8,128)(2,1)} %param.30) | copy-start | bytes 196612
  15.4 56.1 %copy-start.1 = (bf16[512,1024]{1,0:T(8,128)(2,1)S(1)}, bf16[512,1024]{1,0:T(8,128)(2,1)}, u32[]{:S(2)}) copy-start(bf16[512,1024]{1,0:T(8,128)(2,1)} %refs_0_.1) | copy-start | bytes 3145732
  15.4 56.1 %copy-start.11 = (s32[3]{0:T(128)S(1)}, s32[3]{0:T(128)}, u32[]{:S(2)}) copy-start(s32[3]{0:T(128)} %refs_4_.3) | copy-start | bytes 40
  69.9 55.2 %copy-start.8 = (f32[8,768]{1,0:T(8,128)}, f32[8,768]{1,0:T(8,128)S(1)}, u32[]{:S(2)}) copy-start(f32[8,768]{1,0:T(8,128)S(1)} %pad_convert_fusion.refs_4_.refs_13_) | copy-start | bytes 73732
  70.1 55.0 %copy-start.9 = (f32[1,1024]{1,0:T(1,128)}, f32[1,1024]{1,0:T(1,128)S(1)}, u32[]{:S(2)}) copy-start(f32[1,1024]{1,0:T(1,128)S(1)} %reshape.347.refs_2_.refs_20_) | copy-start | bytes 12292
  125.0 7.9 copy-start.7
  125.0 5.5 copy-start.37
  125.1 236.3 %all-gather.9.cloned.1.call-start = ((), (), s32[]{:S(2)}) async-start(), calls=%async_computation.5 | async-start | bytes 2359296 | tf_op jit(solution)/shard_map/all_gather | solution.py:2129
  125.8 240.0 %all-gather.7.cloned.1.call-start = ((), (), s32[]{:S(2)}) async-start(), calls=%async_computation.4 | async-start | bytes 2359296 | tf_op jit(solution)/shard_map/all_gather | solution.py:2128
  126.6 249.0 %all-gather.11.cloned.1.call-start = ((), (), s32[]{:S(2)}) async-start(), calls=%async_computation.6 | async-start | bytes 2359296 | tf_op jit(solution)/shard_map/all_gather | solution.py:2130
  127.1 719.7 %reduce-scatter.8.cloned.1.call-start = ((), (), s32[]{:S(2)}) async-start(), calls=%async_computation.8 | async-start | bytes 2359296 | tf_op jit(solution)/shard_map/reduce_scatter | solution.py:2218
  130.3 191.9 %copy-start.48 = (f32[16,4]{0,1:T(4,128)}, f32[16,4]{0,1:T(4,128)S(1)}, u32[]{:S(2)}) copy-start(f32[16,4]{0,1:T(4,128)S(1)} %add_rsqrt_fusion.1) | copy-start | bytes 772
  133.1 193.0 %copy-start.24 = (bf16[512,256]{0,1:T(8,128)(2,1)}, bf16[512,256]{0,1:T(8,128)(2,1)S(1)}, u32[]{:S(2)}) copy-start(bf16[512,256]{0,1:T(8,128)(2,1)S(1)} %copy.260) | copy-start | bytes 786436
  365.8 9.7 %copy-start.44 = (bf16[512,1024]{1,0:T(8,128)(2,1)S(1)}, bf16[512,1024]{1,0:T(8,128)(2,1)}, u32[]{:S(2)}) copy-start(bf16[512,1024]{1,0:T(8,128)(2,1)} %param.21) | copy-start | bytes 3145732
  399.5 449.2 %reduce-scatter.10.cloned.1.call-start = ((), (), s32[]{:S(2)}) async-start(), calls=%async_computation.9 | async-start | bytes 2359296
  408.1 442.6 %reduce-scatter.6.cloned.1.call-start = ((), (), s32[]{:S(2)}) async-start(), calls=%async_computation.7 | async-start | bytes 2359296 | tf_op jit(solution)/shard_map/reduce_scatter | solution.py:2218
  408.1 34.1 %copy-start.40 = (f32[512,256]{1,0:T(8,128)S(1)}, f32[512,256]{1,0:T(8,128)}, u32[]{:S(2)}) copy-start(f32[512,256]{1,0:T(8,128)} %get-tuple-element.255) | copy-start | bytes 1572868
  451.2 8.4 copy-start.25
  459.7 6.8 copy-start.16
  461.1 5.9 copy-start.22
  461.1 5.4 copy-start.27
  716.6 5.0 slice-start
  720.8 5.0 copy-start.18
  729.0 6.0 copy-start.46
  730.0 7.5 copy-start.20
  731.4 6.2 copy-start.6
  731.5 6.2 copy-start.30
  834.5 9.9 %copy-start.42 = (f32[128,768]{1,0:T(8,128)S(1)}, f32[128,768]{1,0:T(8,128)}, u32[]{:S(2)}) copy-start(f32[128,768]{1,0:T(8,128)} %get-tuple-element.123) | copy-start | bytes 1179652
  834.5 10.7 %copy-start.29 = (bf16[4,128,1024]{2,1,0:T(8,128)(2,1)S(1)}, bf16[4,128,1024]{2,1,0:T(8,128)(2,1)}, u32[]{:S(2)}) copy-start(bf16[4,128,1024]{2,1,0:T(8,128)(2,1)} %get-tuple-element.122) | copy-start | bytes 3145732
  846.8 5.8 copy-start.31
  (35 other events, 89.5 us)
Sparse Core Ops, SparseCore 0:
  125.2 49.5 all-gather.4
  176.9 63.8 all-gather.8
  242.9 80.4 all-gather.6
  325.4 50.1 all-gather.10
  399.6 67.0 reduce-scatter.7
  470.1 86.5 reduce-scatter.9
  560.2 85.8 reduce-scatter.5

commit v6 on v5

--- a/solution.py
+++ b/solution.py
@@ -465,7 +465,7 @@
     )(*parts, *extras)
 
 
-def last_step(heads, conv, lengths, gate_back, extras, work, early, chunks, flat, ident):
+def last_step(heads, conv, lengths, gate_back, extras, work, early, chunks, flat, ready, ident):
     span, columns = conv[0].shape
     block = columns // 3
     width = conv[3].shape[0]
@@ -486,17 +486,18 @@
     first_shape, second_shape, flat_shape = chunks[0].shape[1:], chunks[1].shape[1:], flat.shape[1:]
 
     def kernel(*refs):
-        first_ref, second_ref, flat_ref, early_ref, lengths_ref = refs[:5]
-        compute_refs, refs = refs[5 : 5 + compute_count], refs[5 + compute_count :]
+        first_ref, second_ref, flat_ref, early_ref, lengths_ref, ready_ref = refs[:6]
+        compute_refs, refs = refs[6 : 6 + compute_count], refs[6 + compute_count :]
         extra_refs, refs = refs[:extra_count], refs[extra_count:]
-        spread_ref, grads_out, first_out, second_out, flat_out, row_out, taps_out, early_out = refs[:8]
-        refs = refs[8:]
+        spread_ref, grads_out, first_out, second_out, flat_out, row_out, taps_out, early_out, ready_out = refs[:9]
+        refs = refs[9:]
         part_ref, grads_ref, conv_grad, tap_rows, halo_out, halo_in, halo_sem, taps_sem, refs = refs[:8] + (refs[8:],)
         pair, half, got, rowbuf, rowtile, rowgot, refs = refs[:6] + (refs[6:],)
         gx, ghalf, gz, fgot, sgot, flatgot, refs = refs[:6] + (refs[6:],)
         load_sem, pair_sem, y_send, y_recv, s_send, s_recv, p_send, p_recv, refs = refs[:8] + (refs[8:],)
         gx_send, gx_recv, gz_send, gz_recv, c_send, c_recv, all_send, all_recv = refs[:8]
         early_own, ex, ehalf, ez, e_sems = refs[8], refs[9], refs[10], refs[11], refs[12:16]
+        r_send, r_recv, rp_send, rp_recv, r_own = refs[16:21]
         g = Grid()
         me = g.wide * narrow + g.narrow
         wait_all = g.greet_all()
@@ -569,6 +570,18 @@
             return carry
 
         lax.fori_loop(1, devices, send_flat, 0)
+        ready_sends = []
+
+        def ready_to(source, place, send, recv, target):
+            copy = remote(source, ready_out.at[place], send, recv, target)
+            copy.start()
+            ready_sends.append(copy)
+
+        for s, y in enumerate(g.y_others()):
+            ready_to(ready_ref, g.narrow, r_send.at[s], r_recv.at[g.y], g.device(g.z, g.x, y, g.c))
+        ready_to(ready_ref, g.narrow, rp_send.at[g.y], rp_recv.at[g.y], g.partner)
+        ready_own = pltpu.make_async_copy(ready_ref, ready_out.at[g.narrow], r_own.at[0])
+        ready_own.start()
         qmem, kmem, vmem_ref, qatt, katt, vatt = compute_refs[:6]
         mixed_ref, ext_ref, taps_ref, weights_ref, normed_ref, gate_low, gate_cols = compute_refs[6:]
         for third, (memory, attention) in enumerate(((qmem, qatt), (kmem, katt), (vmem_ref, vatt))):
@@ -619,6 +632,10 @@
         pair_copy.start()
         grads_ref[...] = inner_left(normed_ref[...], projected_low).astype(bf16).reshape((zs, xs) + own_grad)
         along_x(grads_ref, gx, g_sems)
+        for y in g.y_others():
+            there = ready_out.at[2 * y + g.c]
+            remote(there, there, r_send.at[0], r_recv.at[y], g.partner).wait_recv()
+            ready_to(there, 2 * y + g.c, rp_send.at[y], rp_recv.at[y], g.partner)
         pair_copy.wait()
         pair[...] += part_ref[:, g.c]
         half[...] = pair[...].astype(bf16)
@@ -694,9 +711,13 @@
         for y in range(ys):
             there = spread_ref.at[2 * y + 1 - g.c]
             remote(there, there, s_send.at[0], p_recv.at[y], g.partner).wait_recv()
-        for copy in sends:
+        for y in range(ys):
+            there = ready_out.at[2 * y + 1 - g.c]
+            remote(there, there, r_send.at[0], rp_recv.at[y], g.partner).wait_recv()
+        for copy in sends + ready_sends:
             copy.wait_send()
         own.wait()
+        ready_own.wait()
 
     sem = pltpu.SemaphoreType.DMA
     vmem = pl.BlockSpec(memory_space=pltpu.VMEM)
@@ -711,11 +732,12 @@
             jax.ShapeDtypeStruct((8, width // 8), f32),
             jax.ShapeDtypeStruct((devices, count, columns), f32),
             jax.ShapeDtypeStruct(own_early, f32),
+            jax.ShapeDtypeStruct((narrow, rows, width), bf16),
         ],
         in_specs=[ANY] * 4
-        + [pl.BlockSpec(memory_space=pltpu.SMEM)]
+        + [pl.BlockSpec(memory_space=pltpu.SMEM), vmem]
         + [vmem] * (compute_count + extra_count),
-        out_specs=[ANY] + [vmem] * 7,
+        out_specs=[ANY] + [vmem] * 7 + [ANY],
         scratch_shapes=[
             pltpu.VMEM((ys, 2, rows, width), f32),
             pltpu.VMEM((zs, xs) + own_grad, bf16),
@@ -751,12 +773,14 @@
             pltpu.VMEM((zs,) + own_early, bf16),
         ]
         + [sem((xs, zs))] * 2
-        + [sem((zs,))] * 2,
+        + [sem((zs,))] * 2
+        + [sem((ys,))] * 4
+        + [sem((1,))],
         compiler_params=pltpu.CompilerParams(
             collective_id=ident, has_side_effects=True, vmem_limit_bytes=60 * 1024 * 1024
         ),
         name="last_step",
-    )(chunks[0], chunks[1], flat, early, lengths, *compute, *extras)
+    )(chunks[0], chunks[1], flat, early, lengths, ready, *compute, *extras)
 
 
 class Plan:
@@ -1345,11 +1369,13 @@
         place = self.whole.at[colour, chip]
         return remote(place, place, self.pair_send.at[chip], self.pair_recv.at[chip], self.lane.partner)
 
-    def run(self):
+    def run(self, meanwhile=None):
         lane = self.lane
         for step in range(1, lane.chips):
             self.copy_to(step).start()
         self.pair_copy(lane.chip, lane.colour).start()
+        if meanwhile is not None:
+            meanwhile()
         for step in range(1, lane.chips):
             chip = lane.other(step)
             place = self.whole.at[lane.colour, chip]
@@ -1845,22 +1871,24 @@
                 second = jnp.sum(second_a * second_b, axis=0, keepdims=True)
                 return jnp.sum(first, axis=1, keepdims=True) + jnp.sum(second, axis=1, keepdims=True)
 
-            kinds = (
-                whole_sum(cf[...], s1[slot], cs[...], s2[slot]),
-                whole_sum(cmf[...] + cf[...], m1[slot], cms[...] + cs[...], m2[slot]),
-                whole_sum(cmf[...] + cf[...], g1[slot], cms[...] + cs[...], g2[slot]),
-            )
-            column = lax.broadcasted_iota(jnp.int32, (8, 128), 1)
-            sumrow = jnp.zeros((8, 128), f32)
-            for i, kind in enumerate(kinds):
-                sumrow = jnp.where(column == i, kind, sumrow)
-            sumrows[turn] = sumrow
+            def gate_sums():
+                kinds = (
+                    whole_sum(cf[...], s1[slot], cs[...], s2[slot]),
+                    whole_sum(cmf[...] + cf[...], m1[slot], cms[...] + cs[...], m2[slot]),
+                    whole_sum(cmf[...] + cf[...], g1[slot], cms[...] + cs[...], g2[slot]),
+                )
+                column = lax.broadcasted_iota(jnp.int32, (8, 128), 1)
+                sumrow = jnp.zeros((8, 128), f32)
+                for i, kind in enumerate(kinds):
+                    sumrow = jnp.where(column == i, kind, sumrow)
+                sumrows[turn] = sumrow
+
             qstream.take_pair()
             total = lookup.total()
             mine = (total / span).astype(bf16)
             spread.whole[lane.colour, lane.chip] = mine
             vcots[turn] = mine
-            spread.run()
+            spread.run(gate_sums)
             lookup.wait_sends()
             qstream.start_sends()
 
@@ -2226,12 +2254,17 @@
         scaled, factor = scaled_of(middle_rows)
         grad = cotangent_rows.astype(f32) + rms_back(scaled, factor, totals[1] * gain)
         gain_part = jnp.sum(totals[1] * scaled, axis=0, keepdims=True)
-        return [grad.astype(bf16), (middle_rows + totals[0]).astype(bf16)], [grad, gain_part]
-
-    branch_low, output, middle_grad, gain_two_part = narrow_step(
-        list(ffn_sums), [middle, cotangent_own, gain_two[None]], after_ffn, 2, [rows_f32, row_f32], 9
+        return [grad.astype(bf16)], [grad, gain_part, (middle_rows + totals[0]).astype(bf16)]
+
+    branch_low, middle_grad, gain_two_part, output_own = narrow_step(
+        list(ffn_sums),
+        [middle, cotangent_own, gain_two[None]],
+        after_ffn,
+        1,
+        [rows_f32, row_f32, ((own_rows, width), bf16)],
+        9,
     )
-    branch_low, output = branch_low.reshape(span, width), output.reshape(span, width)
+    branch_low = branch_low.reshape(span, width)
 
     gated_grad = matmul(branch_low, proj_cols)
     attended_grad_low = (gated_grad * gate_sigmoid).astype(bf16)
@@ -2291,7 +2324,7 @@
     flat_size = -(-flat.shape[1] // 1024) * 1024
     flat = jnp.pad(flat, ((0, 0), (0, flat_size - flat.shape[1]))).reshape(devices, -1, 128)
     cots = cots.reshape(3, span, local_width)
-    tokens_grad, weight_out, first_out, second_out, flat_sum, gain_sum, tap_rows, early_out = last_step(
+    tokens_grad, weight_out, first_out, second_out, flat_sum, gain_sum, tap_rows, early_out, output = last_step(
         [cots[0], cots[1], cots[2], query_att, keys_grad[recall_end:], values_grad[recall_end:]],
         [mixed_conv, extended, jnp.pad(kernel_f, ((0, 8 - taps), (0, 0))), qkv_weights, normed_low],
         seq_spans,
@@ -2301,8 +2334,10 @@
         early_grads,
         [first_chunks, second_chunks],
         flat,
+        output_own,
         15,
     )
+    output = output.reshape(span, width)
     tokens_grad = tokens_grad.reshape(span, width).astype(f32)
     flat_sum = flat_sum.reshape(-1)
     own_start = (wide_pos * narrow + narrow_pos) * (width // devices)

time: 870 us -> 861 us (0.990)
  Pallas kernels: 687 us -> 678 us
where the time goes in v6:
time: 861 us; the launch traced here: 854 us
  Pallas kernels  678 us (79%)
  local copies, waits for them, and re-layouts  67.4 us (8%)
  matrix products  60.7 us (7%)
  other arithmetic  23.8 us (3%)
  between operations  15.7 us (2%)
    pallas_call x1, Pallas kernels, chain_backward(): pl.pallas_call(kernel, out_shape=out_shape, in_specs=[ANY] * 14 + [smem]...  247 us
    pallas_call x1, Pallas kernels, chain_forward(): pl.pallas_call(kernel, out_shape=out_shape, in_specs=[ANY] * 3 + [smem] *...  189 us
    pallas_call x1, Pallas kernels, last_step(): pl.pallas_call(kernel, out_shape=[jax.ShapeDtypeStruct((narrow, rows, wid...  91.3 us
    pallas_call x2, Pallas kernels, narrow_step(): pl.pallas_call(kernel, out_shape=[jax.ShapeDtypeStruct((narrow, rows, wid...  52.9 us
    pallas_call x1, Pallas kernels, send_parameters(): pl.pallas_call(kernel, out_shape=[jax.ShapeDtypeStruct((devices,) + small...  52.1 us
    pallas_call x1, Pallas kernels, front_step(): pl.pallas_call(kernel, out_shape=[jax.ShapeDtypeStruct(kind.shape(span, b...  46.3 us
    unnamed x133, local copies, waits for them, and re-layouts  22.7 us
  transfers between devices with their start and end apart: 7, of which 1 were waited for; matrix products, arithmetic and copies ran while one was open for 12% of the time, Pallas kernels for 68%

profile of v6, /device:TPU:0, one launch (start us, length us, event | category | flops | bytes accessed | tf_op | source)
XLA Modules:
  0.0 853.5 jit_solution(15399436816860168370)
XLA Ops:
  16.1 52.1 %send_parameters.1 = (bf16[32,16,128]{2,1,0:T(8,128)(2,1)}, bf16[8,4,32,768]{3,2,1,0:T(8,128)(2,1)}, bf16[8,128,256]{2,1,0:T(8,128)(2,1)}, bf16[8,256,128]{2,1,0:T(8,128)(2,1)}, bf16[8,1024]{1,0:T(8,128)(2,1)}) custom-call(bf16[16,128]{1,0:T(8,128)(2,1)} %pad_bitcast_fusion.1.refs_0_, bf16[4,32,768]{2,1,0:T(8,128)(2,1)} %maximum_bitcast_fusion.refs_1_, ...), custom_call_target="tpu_custom_call" | custom-call | tf_op jit(solution)/shard_map/send_parameters/pallas_call | solution.py:339
  71.5 46.3 %front_step.1 = (bf16[5,4,512,256]{3,2,1,0:T(8,128)(2,1)S(1)}, bf16[32,32,256]{2,1,0:T(8,128)(2,1)S(1)}, f32[32,8,128]{2,1,0:T(8,128)S(1)}, bf16[512,256]{1,0:T(...) custom-call(bf16[512,1024]{1,0:T(8,128)(2,1)S(1)} %copy-done.1, ...), custom_call_target="tpu_custom_call" | custom-call | tf_op jit(solution)/shard_map/front_step/pallas_call | solution.py:1192
  121.9 2.3 copy-done.13
  133.6 189.2 %chain_forward.1 = (bf16[2,8,32,256]{3,2,1,0:T(8,128)(2,1)}, bf16[5,1024,256]{2,1,0:T(8,128)(2,1)}, bf16[5,256,1024]{2,1,0:T(8,128)(2,1)}, f32[4,1024,256]{2,1,0...) custom-call(bf16[5,4,512,256]{3,2,1,0:T(8,128)(2,1)} %copy-done.13, ...), custom_call_target="tpu_custom_call" | custom-call | flops 53687091200 | bytes 209715200 | tf_op jit(solution)/shard_map/chain_forward/pallas_call | solution.py:1709
  326.7 1.7 fusion.51
  329.6 2.2 fusion.7
  332.1 2.4 multiply_convert_fusion.4
  335.2 1.8 fusion.37
  337.0 24.2 %narrow_step_7.1 = (bf16[4,128,1024]{2,1,0:T(8,128)(2,1)}, f32[128,1024]{1,0:T(8,128)}) custom-call(f32[2,2,128,1024]{3,2,1,0:T(8,128)} %bitcast.187, bf16[128,1024]{1,0:T(8,128)(2,1)} %constant_dynamic-slice_fusion.3.refs_1_.refs_19_, f32[1,1024]{1,0:T(1,128)} %reshape.353.refs_2_.refs_4_), custom_call_target="tpu_custom_call" | custom-call | flops 30000001024 | bytes 104857600 | tf_op jit(solution)/shard_map/narrow_step_7/pallas_call | solution.py:449
  361.2 4.5 fusion.53
  365.7 4.6 fusion.52
  370.3 5.4 all-gather.11.cloned.1.call-done
  375.7 5.9 fusion.16
  381.6 2.6 convert_bitcast_fusion
  384.3 2.6 convolution_convert_fusion
  386.9 4.1 convolution_convert_fusion.1
  391.1 3.3 fusion.55
  394.5 2.6 fusion.54
  397.0 2.6 convolution_add_fusion
  404.1 4.1 copy.296
  408.3 28.6 %narrow_step_9.1 = (bf16[4,128,1024]{2,1,0:T(8,128)(2,1)}, f32[128,1024]{1,0:T(8,128)}, f32[1,1024]{1,0:T(1,128)}, bf16[128,1024]{1,0:T(8,128)(2,1)}) custom-call(f32[2,2,128,1024]{3,2,1,0:T(8,128)} %bitcast.226, f32[2,2,128,1024]{3,2,1,0:T(8,128)} %bitcast.227, f32[128,1024]{1,0:T(8,128)} %get-tuple-element.97.refs_2_, ...), custom_call_target="tpu_custom_call" | custom-call | flops 30000001024 | bytes 104857600 | tf_op jit(solution)/shard_map/narrow_step_9/pallas_call | solution.py:449
  436.9 2.4 multiply_convert_fusion.2
  439.5 6.6 multiply_reduce_fusion
  446.0 8.2 multiply_convert_fusion
  455.8 5.3 fusion.9
  463.0 246.6 %chain_backward.1 = (bf16[3,2,8,32,256]{4,3,2,1,0:T(8,128)(2,1)}, f32[32,8,128]{2,1,0:T(8,128)}, bf16[8,128,256]{2,1,0:T(8,128)(2,1)}, bf16[8,256,128]{2,1,0:T(8,128)(2,1)}) custom-call(bf16[512,256]{1,0:T(8,128)(2,1)} %copy.271.refs_0_, bf16[5,4,512,256]{3,2,1,0:T(8,128)(2,1)} %get-tuple-element.99.refs_1_, ...), custom_call_target="tpu_custom_call" | custom-call | flops 107374182400 | bytes 314572800 | tf_op jit(solution)/shard_map/chain_backward/pallas_call | solution.py:2006
  711.0 2.1 slice.149
  715.7 2.0 copy.283.refs_10_
  718.9 3.1 convolution_multiply_fusion.1
  734.2 91.3 %last_step.1 = (bf16[4,128,1024]{2,1,0:T(8,128)(2,1)}, f32[128,768]{1,0:T(8,128)}, f32[128,1024]{1,0:T(8,128)}, f32[1024,128]{1,0:T(8,128)}, f32[16,128]{1,0:T(8...) custom-call(bf16[8,128,256]{2,1,0:T(8,128)(2,1)} %get-tuple-element.112.re, ...), custom_call_target="tpu_custom_call" | custom-call | tf_op jit(solution)/shard_map/last_step/pallas_call | solution.py:724
  837.9 1.9 convert_element_type.157
  841.8 1.9 convert_element_type.156
  (268 shorter events, 73.2 us)
Async XLA Ops:
  7.2 62.3 %copy-start.45 = (bf16[256,128]{1,0:T(8,128)(2,1)S(1)}, bf16[256,128]{1,0:T(8,128)(2,1)}, u32[]{:S(2)}) copy-start(bf16[256,128]{1,0:T(8,128)(2,1)} %param.31) | copy-start | bytes 196612
  7.2 324.8 %all-gather.5.cloned.1.call-start = ((), (), s32[]{:S(2)}) async-start(), calls=%async_computation.3 | async-start | bytes 1179648 | tf_op jit(solution)/shard_map/all_gather | solution.py:2155
  15.4 55.4 %copy-start.47 = (bf16[128,256]{1,0:T(8,128)(2,1)S(1)}, bf16[128,256]{1,0:T(8,128)(2,1)}, u32[]{:S(2)}) copy-start(bf16[128,256]{1,0:T(8,128)(2,1)} %param.30) | copy-start | bytes 196612
  15.4 56.1 %copy-start.1 = (bf16[512,1024]{1,0:T(8,128)(2,1)S(1)}, bf16[512,1024]{1,0:T(8,128)(2,1)}, u32[]{:S(2)}) copy-start(bf16[512,1024]{1,0:T(8,128)(2,1)} %refs_0_.1) | copy-start | bytes 3145732
  15.4 56.1 %copy-start.11 = (s32[3]{0:T(128)S(1)}, s32[3]{0:T(128)}, u32[]{:S(2)}) copy-start(s32[3]{0:T(128)} %refs_4_.3) | copy-start | bytes 40
  69.9 55.2 %copy-start.8 = (f32[8,768]{1,0:T(8,128)}, f32[8,768]{1,0:T(8,128)S(1)}, u32[]{:S(2)}) copy-start(f32[8,768]{1,0:T(8,128)S(1)} %pad_convert_fusion.refs_4_.refs_14_) | copy-start | bytes 73732
  70.1 55.0 %copy-start.9 = (f32[1,1024]{1,0:T(1,128)}, f32[1,1024]{1,0:T(1,128)S(1)}, u32[]{:S(2)}) copy-start(f32[1,1024]{1,0:T(1,128)S(1)} %reshape.350.refs_2_.refs_21_) | copy-start | bytes 12292
  125.0 7.9 copy-start.7
  125.0 5.5 copy-start.37
  125.1 236.2 %all-gather.9.cloned.1.call-start = ((), (), s32[]{:S(2)}) async-start(), calls=%async_computation.5 | async-start | bytes 2359296 | tf_op jit(solution)/shard_map/all_gather | solution.py:2157
  125.8 239.9 %all-gather.7.cloned.1.call-start = ((), (), s32[]{:S(2)}) async-start(), calls=%async_computation.4 | async-start | bytes 2359296 | tf_op jit(solution)/shard_map/all_gather | solution.py:2156
  126.6 249.2 %all-gather.11.cloned.1.call-start = ((), (), s32[]{:S(2)}) async-start(), calls=%async_computation.6 | async-start | bytes 2359296 | tf_op jit(solution)/shard_map/all_gather | solution.py:2158
  127.1 710.8 %reduce-scatter.8.cloned.1.call-start = ((), (), s32[]{:S(2)}) async-start(), calls=%async_computation.8 | async-start | bytes 2359296 | tf_op jit(solution)/shard_map/reduce_scatter | solution.py:2246
  130.3 192.5 %copy-start.48 = (f32[16,4]{0,1:T(4,128)}, f32[16,4]{0,1:T(4,128)S(1)}, u32[]{:S(2)}) copy-start(f32[16,4]{0,1:T(4,128)S(1)} %add_rsqrt_fusion.1) | copy-start | bytes 772
  133.1 193.6 %copy-start.24 = (bf16[512,256]{0,1:T(8,128)(2,1)}, bf16[512,256]{0,1:T(8,128)(2,1)S(1)}, u32[]{:S(2)}) copy-start(bf16[512,256]{0,1:T(8,128)(2,1)S(1)} %copy.257) | copy-start | bytes 786436
  365.7 10.0 %copy-start.44 = (bf16[512,1024]{1,0:T(8,128)(2,1)S(1)}, bf16[512,1024]{1,0:T(8,128)(2,1)}, u32[]{:S(2)}) copy-start(bf16[512,1024]{1,0:T(8,128)(2,1)} %param.21) | copy-start | bytes 3145732
  399.7 440.1 %reduce-scatter.10.cloned.1.call-start = ((), (), s32[]{:S(2)}) async-start(), calls=%async_computation.9 | async-start | bytes 2359296
  408.2 433.6 %reduce-scatter.6.cloned.1.call-start = ((), (), s32[]{:S(2)}) async-start(), calls=%async_computation.7 | async-start | bytes 2359296 | tf_op jit(solution)/shard_map/reduce_scatter | solution.py:2246
  408.3 28.7 %copy-start.40 = (f32[512,256]{1,0:T(8,128)S(1)}, f32[512,256]{1,0:T(8,128)}, u32[]{:S(2)}) copy-start(f32[512,256]{1,0:T(8,128)} %get-tuple-element.257) | copy-start | bytes 1572868
  446.0 8.2 copy-start.25
  454.3 6.8 copy-start.16
  455.7 5.9 copy-start.22
  455.7 5.4 copy-start.27
  709.6 5.0 slice-start
  713.8 5.0 copy-start.18
  722.0 6.0 copy-start.46
  723.0 7.5 copy-start.20
  724.5 6.2 copy-start.6
  724.5 6.2 copy-start.30
  825.6 10.0 %copy-start.42 = (f32[128,768]{1,0:T(8,128)S(1)}, f32[128,768]{1,0:T(8,128)}, u32[]{:S(2)}) copy-start(f32[128,768]{1,0:T(8,128)} %get-tuple-element.125) | copy-start | bytes 1179652
  825.6 10.7 %copy-start.29 = (bf16[4,128,1024]{2,1,0:T(8,128)(2,1)S(1)}, bf16[4,128,1024]{2,1,0:T(8,128)(2,1)}, u32[]{:S(2)}) copy-start(bf16[4,128,1024]{2,1,0:T(8,128)(2,1)} %get-tuple-element.124) | copy-start | bytes 3145732
  837.9 5.8 copy-start.31
  (35 other events, 89.5 us)
Sparse Core Ops, SparseCore 0:
  125.2 49.5 all-gather.4
  176.8 63.8 all-gather.8
  242.9 80.7 all-gather.6
  325.6 50.1 all-gather.10
  399.8 66.9 reduce-scatter.7
  470.2 85.7 reduce-scatter.9
  559.5 85.7 reduce-scatter.5
